TPU v7x, 1024 devices: a whole 4x8x16 slice. The times are simulated.
1024 devices in a mesh: gx: 16 (over z), gy: 8 (over y), gz: 8 (over x, core).
Axes of the slice: x: 4, y: 8, z: 16, core: 2. Of those that a mesh axis runs over, the one named last changes fastest.
Arguments:
- residual: float32 [256, 128, 1024], P('gx', 'gy', 'gz'), may hold values from -6 to 6
- solution: float32 [256, 128, 1024], P('gx', 'gy', 'gz'), may hold values from -6 to 6
- direction: float32 [256, 128, 1024], P('gx', 'gy', 'gz'), may hold values from -6 to 6
- conductance: float32 [3, 256, 128, 1024], P(None, 'gx', 'gy', 'gz'), may hold values from 0.3 to 3
- mass_term: float32 [256, 128, 1024], P('gx', 'gy', 'gz'), may hold values from 0.2 to 1
- eigen_basis: float32 [10, 10], replicated, may hold values from -2 to 2
- inverse_eigen_sums: float32 [320, 160, 1280], P('gx', 'gy', 'gz'), may hold values from 0.1 to 1
- element_coarse_index: int32 [32, 16, 128], P('gx', 'gy', 'gz'), may hold values from 0 to 63
- xxt_values: float32 [8192, 64, 128], P(('gx', 'gy', 'gz')), may hold values from -0.0625 to 0.0625
- xxt_blocks: int32 [8192], P(('gx', 'gy', 'gz')), may hold values from 0 to 511
- prior_inner: float32 [1], replicated, may hold values from 13107200 to 52428800
Outputs:
- new_solution: float32 [256, 128, 1024], P('gx', 'gy', 'gz')
- new_residual: float32 [256, 128, 1024], P('gx', 'gy', 'gz')
- new_direction: float32 [256, 128, 1024], P('gx', 'gy', 'gz')
Inputs may be any that keep to these rules, and one draw needn't show every extreme that they name: `element_coarse_index`: an element's coarse unknown is one of the 64 of the device that holds the element. `xxt_blocks`: block numbers of the coarse vector, repeats allowed.
All inputs are finite; a program needn't handle non-finite values.
Results may differ from a plain program's by a relative error of at most 0.00011.
Values sent between devices are 32-bit elements; how exact they have to be, the bound alone decides.
No kernel may reach another device: no remote copies, remote signals or barrier semaphores. Data moves between devices by JAX's collectives and lax.ppermute only.
A program may use at most 32 MiB of HBM per device.

v0:
```python
import jax
import jax.numpy as jnp
import numpy as np
from jax import lax
from jax.sharding import PartitionSpec as P

HIGH = lax.Precision.HIGHEST


def padded_2(block, sides, width):
    for axis, dim in sides:
        count = lax.axis_size(axis)
        forward = [(i, i + 1) for i in range(count - 1)]
        backward = [(target, source) for source, target in forward]
        low = lax.ppermute(
            lax.slice_in_dim(block, block.shape[dim] - width, None, axis=dim), axis, forward
        )
        high = lax.ppermute(lax.slice_in_dim(block, 0, width, axis=dim), axis, backward)
        block = jnp.concatenate([low, block, high], axis=dim)
    return block


def cheb_matrix():
    count = 8
    points = np.cos(np.pi * np.arange(count) / (count - 1))
    signs = np.array([2.0, 1, 1, 1, 1, 1, 1, 2.0]) * (-1.0) ** np.arange(count)
    differ = points[:, None] - points[None, :] + np.eye(count)
    matrix = np.outer(signs, 1.0 / signs) / differ
    matrix = matrix - np.eye(count) * np.sum(matrix, axis=1)[:, None]
    return (0.25 * matrix).astype(np.float32)


def extended_index(count):
    parts = [
        np.array(
            [8 * element] + list(range(8 * element + 2, 8 * element + 10)) + [8 * element + 11]
        )
        for element in range(count)
    ]
    return np.concatenate(parts).astype(np.int32)


def inside_index(count):
    parts = [np.arange(10 * element + 1, 10 * element + 9) for element in range(count)]
    return np.concatenate(parts).astype(np.int32)


def assemble_padded(padded):
    result = padded
    for which_axis in range(3):
        length = result.shape[which_axis] - 2
        position = np.arange(length) % 8
        shape_list = [1, 1, 1]
        shape_list[which_axis] = length
        upper = jnp.asarray((position == 7).astype(np.float32).reshape(shape_list))
        lower = jnp.asarray((position == 0).astype(np.float32).reshape(shape_list))
        centre = lax.slice_in_dim(result, 1, length + 1, axis=which_axis)
        above = lax.slice_in_dim(result, 2, length + 2, axis=which_axis)
        below = lax.slice_in_dim(result, 0, length, axis=which_axis)
        result = centre + upper * above + lower * below
    return result


def apply_big(matrix, values, which_axis):
    if which_axis == 0:
        return jnp.einsum("ij,jyz->iyz", matrix, values, precision=HIGH)
    if which_axis == 1:
        return jnp.einsum("ij,xjz->xiz", matrix, values, precision=HIGH)
    return jnp.einsum("ij,xyj->xyi", matrix, values, precision=HIGH)


def local_operator(values, conductance, mass_term, tables):
    total = mass_term * values
    for which_axis in range(3):
        grad = apply_big(tables[which_axis], values, which_axis)
        total = total + apply_big(tables[which_axis].T, conductance[which_axis] * grad, which_axis)
    return total


def aggregate_table(count):
    return jnp.asarray(
        (np.arange(8 * count)[:, None] // 8 == np.arange(count)[None, :]).astype(np.float32)
    )


def body(
    residual,
    solution,
    direction,
    conductance,
    mass_term,
    eigen_basis,
    inverse_eigen_sums,
    element_coarse_index,
    xxt_values,
    xxt_blocks,
    prior_inner,
):
    elems_x = residual.shape[0] // 8
    elems_y = residual.shape[1] // 8
    elems_z = residual.shape[2] // 8
    counts = (elems_x, elems_y, elems_z)
    base = cheb_matrix()
    tables = tuple(
        (jnp.asarray(np.kron(np.eye(count_one, dtype=np.float32), base)) for count_one in counts)
    )
    device_count = lax.axis_size("gx") * lax.axis_size("gy") * lax.axis_size("gz")
    padded = padded_2(residual, (("gx", 0), ("gy", 1), ("gz", 2)), 2)
    extended_element = jnp.take(padded, jnp.asarray(extended_index(elems_x)), axis=0)
    extended_element = jnp.take(extended_element, jnp.asarray(extended_index(elems_y)), axis=1)
    extended_element = jnp.take(extended_element, jnp.asarray(extended_index(elems_z)), axis=2)
    bases = tuple(
        (jnp.kron(jnp.eye(count_one, dtype=jnp.float32), eigen_basis) for count_one in counts)
    )
    spectral = extended_element
    for which_axis in range(3):
        spectral = apply_big(bases[which_axis].T, spectral, which_axis)
    spectral = inverse_eigen_sums * spectral
    for which_axis in range(3):
        spectral = apply_big(bases[which_axis], spectral, which_axis)
    device_portion = jnp.take(spectral, jnp.asarray(inside_index(elems_x)), axis=0)
    device_portion = jnp.take(device_portion, jnp.asarray(inside_index(elems_y)), axis=1)
    device_portion = jnp.take(device_portion, jnp.asarray(inside_index(elems_z)), axis=2)
    inner_local = jnp.sum(extended_element * spectral)
    agg_x = aggregate_table(elems_x)
    agg_y = aggregate_table(elems_y)
    agg_z = aggregate_table(elems_z)
    summed = jnp.einsum("xyz,zc->xyc", residual, agg_z, precision=HIGH)
    summed = jnp.einsum("xyc,yb->xbc", summed, agg_y, precision=HIGH)
    element_sum = jnp.einsum("xbc,xa->abc", summed, agg_x, precision=HIGH)
    coarse_count = xxt_values.shape[1]
    block_size = xxt_values.shape[2]
    onehot_ids = (
        element_coarse_index[..., None] == jnp.arange(coarse_count, dtype=jnp.int32)
    ).astype(jnp.float32)
    coarse_residual = jnp.einsum("abcn,abc->n", onehot_ids, element_sum, precision=HIGH)
    contrib = jnp.einsum("knb,n->kb", xxt_values, coarse_residual, precision=HIGH)
    block_count = coarse_count * device_count // block_size
    partial_inner = jnp.zeros((block_count, block_size), jnp.float32).at[xxt_blocks].add(contrib)
    coarse_inner, inner_sum = lax.psum((partial_inner, inner_local), ("gx", "gy", "gz"))
    coarse_solution = jnp.einsum("knb,kb->n", xxt_values, coarse_inner[xxt_blocks], precision=HIGH)
    element_coarse = jnp.einsum("abcn,n->abc", onehot_ids, coarse_solution, precision=HIGH)
    spread_values = jnp.einsum("abc,xa->xbc", element_coarse, agg_x, precision=HIGH)
    spread_values = jnp.einsum("xbc,yb->xyc", spread_values, agg_y, precision=HIGH)
    spread_values = jnp.einsum("xyc,zc->xyz", spread_values, agg_z, precision=HIGH)
    preconditioned = device_portion + spread_values
    inner = inner_sum + jnp.sum(coarse_inner * coarse_inner)
    ratio = inner / prior_inner[0]
    new_direction = preconditioned + ratio * direction
    image = local_operator(new_direction, conductance, mass_term, tables)
    curvature = lax.psum(jnp.sum(new_direction * image), ("gx", "gy", "gz"))
    alpha = inner / curvature
    new_solution = solution + alpha * new_direction
    image_padded = padded_2(image, (("gx", 0), ("gy", 1), ("gz", 2)), 1)
    new_residual = residual - alpha * assemble_padded(image_padded)
    return (new_solution, new_residual, new_direction)


def solution(mesh):
    in_specs = (
        P("gx", "gy", "gz"),
        P("gx", "gy", "gz"),
        P("gx", "gy", "gz"),
        P(None, "gx", "gy", "gz"),
        P("gx", "gy", "gz"),
        P(),
        P("gx", "gy", "gz"),
        P("gx", "gy", "gz"),
        P(("gx", "gy", "gz"), None, None),
        P(("gx", "gy", "gz")),
        P(),
    )
    out_specs = (P("gx", "gy", "gz"), P("gx", "gy", "gz"), P("gx", "gy", "gz"))
    return jax.shard_map(body, mesh=mesh, in_specs=in_specs, out_specs=out_specs, check_vma=False)
```

profile of v0, /device:TPU:1, one launch (start us, length us, event | category | flops | bytes accessed | tf_op | source)
XLA Modules:
  0.0 672.2 jit_solution(9950151250412404135)
XLA Ops:
  7.2 0.8 fusion.36
  8.0 1.3 collective-permute-start.1
  9.3 5.5 collective-permute-start
  14.8 0.7 compare_select_fusion
  15.4 2.0 convolution_bitcast_fusion.4
  17.4 1.7 convolution_bitcast_fusion.6
  19.1 0.8 convolution_bitcast_fusion.7
  20.0 0.9 convolution_bitcast_fusion.8
  21.1 1.3 scatter_custom_fusion
  22.8 3.2 collective-permute-start.2
  26.0 1.3 collective-permute-start.3
  27.4 3.2 collective-permute-done.3
  30.7 5.4 collective-permute-start.4
  36.1 10.3 %collective-permute-start.5 = (f32[20,20,2]{2,1,0:T(8,128)S(1)}, f32[20,20,2]{2,1,0:T(8,128)S(1)}, u32[]{:S(2)}, u32[]{:S(2)}) collective-permute-start(f32[20,20,2]{2,1,0:T(8,128)S(1)} %get-tuple-element.4), channel_id=1, source_target_pairs={{1,0},{2,1},{3,2},{4,3},{5,4},{6,5},{7,6},{9,8},{10,9},{11,10},{12... | collective-permute-start | bytes 9608 | tf_op jit(solution)/shard_map/ppermute | solution.py:18
  47.3 0.6 reshape.133
  48.3 0.6 gather_fusion
  49.0 0.6 gather_fusion.1
  49.6 2.2 copy.42
  51.8 2.1 gather_fusion.2
  53.9 0.8 copy.43
  54.7 1.0 copy.45
  55.7 0.6 fusion.25
  56.3 0.7 convolution_bitcast_fusion.1
  57.0 0.5 convolution_multiply_fusion
  57.5 0.6 fusion.5
  58.2 0.7 convolution_bitcast_fusion
  58.8 1.2 fusion.3
  60.0 129.9 %psum.21 = f32[]{:T(128)} all-reduce(f32[]{:T(128)} %get-tuple-element.15), channel_id=1, replica_groups=mesh['gx'=16,'gy'=8,'gz'=8] {'gx','gy','gz'}, use_global_device_ids=true, to_apply=%region_1.2 | all-reduce | flops 1 | bytes 8 | tf_op jit(solution)/shard_map/psum | solution.py:140
  189.9 0.6 gather_fusion.3
  190.6 0.6 gather_fusion.4
  191.2 0.7 copy.53
  191.9 0.8 gather_fusion.5
  193.2 314.6 %all-reduce.2.cloned.1.call-done = f32[512,128]{1,0:T(8,128)} async-done(((f32[512,128]{1,0:T(8,128)}), f32[512,128]{1,0:T(8,128)}) %all-reduce.2.cloned.1.call-update) | async-done | bytes 262160 | tf_op jit(solution)/shard_map/psum | solution.py:140
  507.8 1.5 gather_fusion.6
  510.5 1.6 multiply_reduce_fusion
  513.5 1.3 fusion.2
  516.4 0.9 multiply_reduce_fusion.1
  517.2 1.3 collective-permute-start.6
  518.5 1.3 collective-permute-start.7
  519.8 3.1 collective-permute-done.7
  522.9 3.1 collective-permute-start.8
  526.0 1.3 collective-permute-start.9
  527.3 124.5 %psum.23 = f32[]{:T(128)} all-reduce(f32[]{:T(128)} %get-tuple-element.17), channel_id=1, replica_groups=mesh['gx'=16,'gy'=8,'gz'=8] {'gx','gy','gz'}, use_global_device_ids=true, to_apply=%region_6.7 | all-reduce | flops 1 | bytes 8 | tf_op jit(solution)/shard_map/psum | solution.py:151
  652.7 3.6 collective-permute-start.10
  656.3 1.9 collective-permute-start.11
  658.3 0.7 multiply_add_fusion
  659.2 4.4 collective-permute-done.11
  664.6 0.8 fusion.14
  (92 shorter events, 6.1 us)
Async XLA Ops:
  7.2 13.7 %copy-start = (f32[8,64,128]{2,1,0:T(8,128)S(1)}, f32[8,64,128]{2,1,0:T(8,128)}, u32[]{:S(2)}) copy-start(f32[8,64,128]{2,1,0:T(8,128)} %param.37) | copy-start | bytes 786436
  7.2 15.3 %copy-start.10 = (f32[10,10]{1,0:T(8,128)S(1)}, f32[10,10]{1,0:T(8,128)}, u32[]{:S(2)}) copy-start(f32[10,10]{1,0:T(8,128)} %param.34) | copy-start | bytes 1204
  7.2 500.6 %all-reduce.2.cloned.1.call-start = ((), (), s32[]{:S(2)}) async-start(), calls=%async_computation | async-start | bytes 524288 | tf_op jit(solution)/shard_map/psum | solution.py:140
  8.0 14.8 %collective-permute-start.1 = (f32[2,16,128]{2,1,0:T(8,128)S(1)}, f32[2,16,128]{2,1,0:T(8,128)S(1)}, u32[]{:S(2)}, u32[]{:S(2)}) collective-permute-start(f32[2,16,128]{2,1,0:T(8,128)S(1)} %get-tuple-element.13), channel_id=1, source_target_pairs={{64,0},{128,64},{192,128},{256,192},{320,256},{384,320},{448,384},... | collective-permute-start | bytes 49160 | tf_op jit(solution)/shard_map/ppermute | solution.py:18
  9.3 13.4 %collective-permute-start = (f32[2,16,128]{2,1,0:T(8,128)S(1)}, f32[2,16,128]{2,1,0:T(8,128)S(1)}, u32[]{:S(2)}, u32[]{:S(2)}) collective-permute-start(f32[2,16,128]{2,1,0:T(8,128)S(1)} %get-tuple-element.14), channel_id=1, source_target_pairs={{0,64},{64,128},{128,192},{192,256},{256,320},{320,384},{384,448},... | collective-permute-start | bytes 49160 | tf_op jit(solution)/shard_map/ppermute | solution.py:15
  15.4 7.3 %copy-start.16 = (s32[128]{0:T(128)S(1)}, s32[128]{0:T(128)}, u32[]{:S(2)}) copy-start(s32[128]{0:T(128)} %constant.175) | copy-start | bytes 1540
  15.4 7.3 %copy-start.17 = (s32[16]{0:T(128)S(1)}, s32[16]{0:T(128)}, u32[]{:S(2)}) copy-start(s32[16]{0:T(128)} %constant.173) | copy-start | bytes 196
  17.4 5.4 copy-start.2
  20.8 6.5 copy-start.15
  22.5 23.9 %copy-start.14 = (s32[160]{0:T(256)S(1)}, s32[160]{0:T(256)}, u32[]{:S(2)}) copy-start(s32[160]{0:T(256)} %constant.172) | copy-start | bytes 1924
  22.8 4.5 collective-permute-start.2
  26.0 4.5 collective-permute-start.3
  30.7 17.2 %collective-permute-start.4 = (f32[20,20,2]{2,1,0:T(8,128)S(1)}, f32[20,20,2]{2,1,0:T(8,128)S(1)}, u32[]{:S(2)}, u32[]{:S(2)}) collective-permute-start(f32[20,20,2]{2,1,0:T(8,128)S(1)} %get-tuple-element.3), channel_id=1, source_target_pairs={{0,1},{1,2},{2,3},{3,4},{4,5},{5,6},{6,7},{8,9},{9,10},{10,11},{11... | collective-permute-start | bytes 9608 | tf_op jit(solution)/shard_map/ppermute | solution.py:15
  36.1 11.8 %collective-permute-start.5 = (f32[20,20,2]{2,1,0:T(8,128)S(1)}, f32[20,20,2]{2,1,0:T(8,128)S(1)}, u32[]{:S(2)}, u32[]{:S(2)}) collective-permute-start(f32[20,20,2]{2,1,0:T(8,128)S(1)} %get-tuple-element.4), channel_id=1, source_target_pairs={{1,0},{2,1},{3,2},{4,3},{5,4},{6,5},{7,6},{9,8},{10,9},{11,10},{12... | collective-permute-start | bytes 9608 | tf_op jit(solution)/shard_map/ppermute | solution.py:18
  55.7 1.3 copy-start.4
  191.2 318.4 %copy-start.20 = (s32[2,2,16]{2,1,0:T(2,128)S(1)}, s32[2,2,16]{2,1,0:T(2,128)}, u32[]{:S(2)}) copy-start(s32[2,2,16]{2,1,0:T(2,128)} %param.36) | copy-start | bytes 772
  191.9 318.0 %copy-start.11 = (f32[16,2,1]{0,1,2:T(2,128)S(1)}, f32[16,2,1]{0,1,2:T(2,128)}, u32[]{:S(2)}) copy-start(f32[16,2,1]{0,1,2:T(2,128)} %constant.176) | copy-start | bytes 388
  191.9 321.6 %copy-start.9 = (f32[128,16,1]{0,1,2:T(8,128)S(1)}, f32[128,16,1]{0,1,2:T(8,128)}, u32[]{:S(2)}) copy-start(f32[128,16,1]{0,1,2:T(8,128)} %constant.177) | copy-start | bytes 24580
  192.7 322.1 %copy-start.3 = (f32[3,16,16,128]{3,2,1,0:T(8,128)S(1)}, f32[3,16,16,128]{3,2,1,0:T(8,128)}, u32[]{:S(2)}) copy-start(f32[3,16,16,128]{3,2,1,0:T(8,128)} %param.32) | copy-start | bytes 1179652
  192.7 322.1 %copy-start.8 = (f32[16,16,1]{1,0,2:T(8,128)S(1)}, f32[16,16,1]{1,0,2:T(8,128)}, u32[]{:S(2)}) copy-start(f32[16,16,1]{1,0,2:T(8,128)} %constant.178) | copy-start | bytes 3076
  192.7 322.4 %slice-start = ((f32[3,16,16,128]{3,2,1,0:T(8,128)}), f32[1,16,16,128]{3,2,1,0:T(8,128)S(1)}, s32[]{:S(2)}) async-start(f32[3,16,16,128]{3,2,1,0:T(8,128)} %param.32), calls=%async_computation.1 | async-start | bytes 262144 | tf_op jit(solution)/shard_map/slice | solution.py:76
  193.2 322.6 %copy-start.5 = (f32[128,128,1]{1,0,2:T(8,128)S(1)}, f32[128,128,1]{1,0,2:T(8,128)}, u32[]{:S(2)}) copy-start(f32[128,128,1]{1,0,2:T(8,128)} %constant.179) | copy-start | bytes 196612
  509.5 6.5 copy-start.7
  514.8 143.4 %copy-start.1 = (f32[16,16,128]{2,1,0:T(8,128)}, f32[16,16,128]{2,1,0:T(8,128)S(1)}, u32[]{:S(2)}) copy-start(f32[16,16,128]{2,1,0:T(8,128)S(1)} %fusion.2) | copy-start | bytes 393220
  516.0 142.2 %copy-start.6 = (f32[16,16,128]{2,1,0:T(8,128)S(1)}, f32[16,16,128]{2,1,0:T(8,128)}, u32[]{:S(2)}) copy-start(f32[16,16,128]{2,1,0:T(8,128)} %param.30) | copy-start | bytes 393220
  517.2 2.6 collective-permute-start.6
  518.5 4.4 collective-permute-start.7
  522.9 129.6 %collective-permute-start.8 = (f32[18,1,128]{2,1,0:T(1,128)S(1)}, f32[18,1,128]{2,1,0:T(1,128)S(1)}, u32[]{:S(2)}, u32[]{:S(2)}) collective-permute-start(f32[18,1,128]{2,1,0:T(1,128)S(1)} %get-tuple-element.9), channel_id=1, source_target_pairs={{0,8},{8,16},{16,24},{24,32},{32,40},{40,48},{48,56},{1,9},{9,17},... | collective-permute-start | bytes 27656 | tf_op jit(solution)/shard_map/ppermute | solution.py:15
  526.0 126.5 %collective-permute-start.9 = (f32[18,1,128]{2,1,0:T(1,128)S(1)}, f32[18,1,128]{2,1,0:T(1,128)S(1)}, u32[]{:S(2)}, u32[]{:S(2)}) collective-permute-start(f32[18,1,128]{2,1,0:T(1,128)S(1)} %get-tuple-element.10), channel_id=1, source_target_pairs={{8,0},{16,8},{24,16},{32,24},{40,32},{48,40},{56,48},{9,1},{17,9},... | collective-permute-start | bytes 27656 | tf_op jit(solution)/shard_map/ppermute | solution.py:18
  652.5 11.4 %copy-start.12 = (f32[16]{0:T(128)S(1)}, f32[16]{0:T(128)}, u32[]{:S(2)}) copy-start(f32[16]{0:T(128)} %constant.161) | copy-start | bytes 196
  652.5 11.4 %copy-start.13 = (f32[16]{0:T(128)S(1)}, f32[16]{0:T(128)}, u32[]{:S(2)}) copy-start(f32[16]{0:T(128)} %constant.160) | copy-start | bytes 196
  652.7 6.5 collective-permute-start.10
  656.3 7.3 %collective-permute-start.11 = (f32[18,18,1]{2,1,0:T(8,128)S(1)}, f32[18,18,1]{2,1,0:T(8,128)S(1)}, u32[]{:S(2)}, u32[]{:S(2)}) collective-permute-start(f32[18,18,1]{2,1,0:T(8,128)S(1)} %get-tuple-element.6), channel_id=1, source_target_pairs={{1,0},{2,1},{3,2},{4,3},{5,4},{6,5},{7,6},{9,8},{10,9},{11,10},{12... | collective-permute-start | bytes 3896 | tf_op jit(solution)/shard_map/ppermute | solution.py:18
  663.9 0.7 copy-start.18
  663.9 0.7 copy-start.19
Sparse Core Ops, SparseCore 0:
  22.5 485.1 all-reduce.1
where the time goes:
time: 673 us; the launch traced here: 672 us
  waiting for transfers between devices  326 us (48%)
  blocking collectives  254 us (38%)
  starting transfers between devices  39.5 us (6%)
  between operations  17.5 us (3%)
  matrix products  14.8 us (2%)
  local copies, waits for them, and re-layouts  14.3 us (2%)
    psum x1, waiting for transfers between devices, body(): lax.psum((partial_inner, inner_local), ('gx', 'gy', 'gz'))  315 us
    psum x1, blocking collectives, body(): lax.psum((partial_inner, inner_local), ('gx', 'gy', 'gz'))  130 us
    psum x1, blocking collectives, body(): curvature = lax.psum(jnp.sum(new_direction * image), ('gx', 'gy', 'gz'))  124 us
    ppermute x6, starting transfers between devices, padded_2(): lax.ppermute(lax.slice_in_dim(block, block.shape[dim] - width, None, axis...  22 us
    ppermute x6, starting transfers between devices, padded_2(): lax.ppermute(lax.slice_in_dim(block, 0, width, axis=dim), axis, backward)  17.4 us
  transfers between devices with their start and end apart: 13, of which 5 were waited for; matrix products, arithmetic and copies ran while one was open for 4% of the time, Pallas kernels for 0%

commit v1 on v0

v1 whole, which is shorter than its diff:
```python
import jax
import jax.numpy as jnp
import numpy as np
from jax import lax
from jax.sharding import PartitionSpec as P

HIGH = lax.Precision.HIGHEST
N = 8
E = 10


def cheb_matrix():
    count = 8
    points = np.cos(np.pi * np.arange(count) / (count - 1))
    signs = np.array([2.0, 1, 1, 1, 1, 1, 1, 2.0]) * (-1.0) ** np.arange(count)
    differ = points[:, None] - points[None, :] + np.eye(count)
    matrix = np.outer(signs, 1.0 / signs) / differ
    matrix = matrix - np.eye(count) * np.sum(matrix, axis=1)[:, None]
    return (0.25 * matrix).astype(np.float32)


def extended_positions(count):
    length = N * count
    result = []
    for element in range(count):
        for node in [N * element - 2, *range(N * element, N * element + N), N * element + N + 1]:
            result.append(length if node < 0 else length + 1 if node >= length else node)
    return np.array(result)


def one_hot(index, size):
    return (np.asarray(index)[:, None] == np.arange(size)[None, :]).astype(np.float32)


def dot(a, b):
    return jnp.dot(a, b, precision=HIGH)


def shifts(axis):
    count = lax.axis_size(axis)
    forward = [(i, i + 1) for i in range(count - 1)]
    return forward, [(b, a) for a, b in forward]


def exchange(to_high, to_low, axis):
    forward, backward = shifts(axis)
    return lax.ppermute(to_high, axis, forward), lax.ppermute(to_low, axis, backward)


def spread(values, axes):
    return lax.all_to_all(values, axes, 0, 0, tiled=False)


def broadcast_sum(values, axes):
    count = lax.axis_size(axes)
    return jnp.sum(spread(jnp.broadcast_to(values[None], (count, *values.shape)), axes), axis=0)


def local_operator(values, conductance, mass_term, cheb, kx, ky, kz):
    rows = values.shape[0] * values.shape[1]
    flat = values.reshape(rows, -1)
    along_xy = dot(jnp.asarray(np.concatenate([kx, ky], axis=0)), flat)
    along_xy = along_xy * conductance[:2].reshape(2 * rows, -1)
    along_z = dot(flat, jnp.asarray(kz.T)) * conductance[2].reshape(rows, -1)
    total = mass_term.reshape(rows, -1) * flat
    total = total + dot(jnp.asarray(np.concatenate([kx.T, ky.T], axis=1)), along_xy)
    total = total + dot(along_z, jnp.asarray(kz))
    return total.reshape(values.shape)


def assemble_inside(values, axis, low, high):
    length = values.shape[axis]
    above = jnp.concatenate([lax.slice_in_dim(values, 1, length, axis=axis), high], axis=axis)
    below = jnp.concatenate([low, lax.slice_in_dim(values, 0, length - 1, axis=axis)], axis=axis)
    position = lax.broadcasted_iota(jnp.int32, values.shape, axis) % N
    return values + jnp.where(position == N - 1, above, jnp.where(position == 0, below, 0.0))


def body(
    residual,
    solution,
    direction,
    conductance,
    mass_term,
    eigen_basis,
    inverse_eigen_sums,
    element_coarse_index,
    xxt_values,
    xxt_blocks,
    prior_inner,
):
    nx, ny, nz = residual.shape
    ex, ey, ez = nx // N, ny // N, nz // N
    rows = nx * ny
    plane = ("gy", "gz")
    n_plane = lax.axis_size(plane)
    coarse_count, block = xxt_values.shape[1:]
    n_blocks = coarse_count * lax.axis_size(("gx", "gy", "gz")) // block
    own_blocks = n_blocks // n_plane
    flat = residual.reshape(rows, nz)

    x_low, x_high = exchange(residual[nx - 2], residual[1], "gx")

    agg_xy = one_hot((np.arange(rows) // ny // N) * ey + (np.arange(rows) % ny) // N, ex * ey)
    agg_z = one_hot(np.arange(nz) // N, ez)
    element_sum = dot(dot(jnp.asarray(agg_xy.T), flat), jnp.asarray(agg_z))
    ids = element_coarse_index.reshape(ex * ey, ez)
    onehot_ids = (ids[..., None] == jnp.arange(coarse_count, dtype=jnp.int32)).astype(jnp.float32)
    coarse_residual = jnp.sum(onehot_ids * element_sum[..., None], axis=(0, 1))
    contrib = jnp.sum(xxt_values * coarse_residual[None, :, None], axis=1)
    place = (xxt_blocks[None, :] == jnp.arange(n_blocks, dtype=jnp.int32)[:, None]).astype(
        jnp.float32
    )
    partial_inner = dot(place, contrib).reshape(n_plane, own_blocks, block)

    y_low, y_high = exchange(
        jnp.concatenate([residual[:, ny - 2], x_low[ny - 2][None], x_high[ny - 2][None]]),
        jnp.concatenate([residual[:, 1], x_low[1][None], x_high[1][None]]),
        "gy",
    )
    partial_inner = jnp.sum(spread(partial_inner, plane), axis=0)

    every = jnp.concatenate([flat, x_low, x_high, y_low, y_high])
    picks = one_hot([nz - 2, 1], nz)
    ends = jnp.einsum("kl,rl->kr", jnp.asarray(picks), every, precision=HIGH)
    z_low, z_high = exchange(ends[:1], ends[1:], "gz")
    partial_inner = broadcast_sum(partial_inner, "gx")
    coarse_inner = spread(
        jnp.broadcast_to(partial_inner[None], (n_plane, own_blocks, block)), plane
    ).reshape(n_blocks, block)

    cols_x = np.concatenate(
        [np.repeat(np.arange(nx), ny), np.full(ny, nx), np.full(ny, nx + 1), *[np.arange(nx + 2)] * 2]
    )
    cols_y = np.concatenate(
        [
            np.tile(np.arange(ny), nx),
            *[np.arange(ny)] * 2,
            np.full(nx + 2, ny),
            np.full(nx + 2, ny + 1),
        ]
    )

    def blocks_of(count, matrix):
        mask = np.kron(np.eye(count), np.ones((E, E))).astype(np.float32)
        return jnp.tile(matrix, (count, count)) * mask

    pos_x, pos_y, pos_z = extended_positions(ex), extended_positions(ey), extended_positions(ez)
    n_ext_x, n_ext_y, n_ext_z = E * ex, E * ey, E * ez
    row_x = one_hot(np.repeat(np.arange(n_ext_x), n_ext_y), n_ext_x)
    row_y = one_hot(np.tile(np.arange(n_ext_y), n_ext_x), n_ext_y)
    col_x = (pos_x[:, None] == cols_x[None, :]).astype(np.float32)
    col_y = (pos_y[:, None] == cols_y[None, :]).astype(np.float32)
    basis_x, basis_y = blocks_of(ex, eigen_basis), blocks_of(ey, eigen_basis)
    basis_z = blocks_of(ez, eigen_basis)
    to_x = dot(jnp.asarray(row_x), dot(basis_x.T, jnp.asarray(col_x)))
    to_y = dot(jnp.asarray(row_y), dot(basis_y.T, jnp.asarray(col_y)))
    to_spectral = to_x * to_y
    inside_x = np.concatenate([np.arange(E * e + 1, E * e + N + 1) for e in range(ex)])
    inside_y = np.concatenate([np.arange(E * e + 1, E * e + N + 1) for e in range(ey)])
    inside_z = np.concatenate([np.arange(E * e + 1, E * e + N + 1) for e in range(ez)])
    out_x = one_hot(np.repeat(inside_x, ny), n_ext_x)
    out_y = one_hot(np.tile(inside_y, nx), n_ext_y)
    from_spectral = dot(dot(jnp.asarray(out_x), basis_x), jnp.asarray(row_x.T)) * dot(
        dot(jnp.asarray(out_y), basis_y), jnp.asarray(row_y.T)
    )
    col_z = one_hot(pos_z, nz + 2)
    to_z = dot(jnp.asarray(col_z.T), basis_z)
    from_z = dot(basis_z.T, jnp.asarray(one_hot(inside_z, n_ext_z).T))
    ends_in = jnp.concatenate([z_low, z_high])
    spectral = dot(dot(to_spectral, every), to_z[:nz])
    ends_spectral = jnp.einsum("sr,kr->sk", to_spectral, ends_in, precision=HIGH)
    spectral = spectral + dot(ends_spectral, to_z[nz:])
    weighted = inverse_eigen_sums.reshape(n_ext_x * n_ext_y, n_ext_z) * spectral
    inner_local = jnp.sum(weighted * spectral)
    local_part = dot(dot(from_spectral, weighted), from_z)

    picked = dot(place.T, coarse_inner)
    coarse_solution = jnp.sum(xxt_values * picked[:, None, :], axis=(0, 2))
    element_coarse = jnp.sum(onehot_ids * coarse_solution, axis=-1)
    spread_values = dot(dot(jnp.asarray(agg_xy), element_coarse), jnp.asarray(agg_z.T))
    preconditioned = (local_part + spread_values).reshape(residual.shape)

    cheb = cheb_matrix()
    kx = np.kron(np.kron(np.eye(ex, dtype=np.float32), cheb), np.eye(ny, dtype=np.float32))
    ky = np.kron(np.eye(nx, dtype=np.float32), np.kron(np.eye(ey, dtype=np.float32), cheb))
    kz = np.kron(np.eye(ez, dtype=np.float32), cheb)
    image_direction = local_operator(direction, conductance, mass_term, cheb, kx, ky, kz)
    image = local_operator(preconditioned, conductance, mass_term, cheb, kx, ky, kz)

    images = jnp.stack([image, image_direction])
    low, high = exchange(images[:, nx - 1 :], images[:, :1], "gx")
    terms = jnp.stack(
        [
            inner_local,
            jnp.sum(preconditioned * image),
            jnp.sum(preconditioned * image_direction + direction * image),
            jnp.sum(direction * image_direction),
        ]
    )
    terms = broadcast_sum(jnp.broadcast_to(terms[:, None], (4, 128)), plane)
    images = assemble_inside(images, 1, low, high)
    low, high = exchange(images[:, :, ny - 1 :], images[:, :, :1], "gy")
    terms = broadcast_sum(terms, "gx")[:, 0]
    images = assemble_inside(images, 2, low, high)
    low, high = exchange(images[:, :, :, nz - 1], images[:, :, :, 0], "gz")
    images = assemble_inside(images, 3, low[..., None], high[..., None])

    inner = terms[0] + jnp.sum(coarse_inner * coarse_inner)
    ratio = inner / prior_inner[0]
    curvature = terms[1] + ratio * terms[2] + ratio * ratio * terms[3]
    alpha = inner / curvature
    new_direction = preconditioned + ratio * direction
    new_solution = solution + alpha * new_direction
    new_residual = residual - alpha * (images[0] + ratio * images[1])
    return (new_solution, new_residual, new_direction)


def solution(mesh):
    whole = P("gx", "gy", "gz")
    in_specs = (
        whole,
        whole,
        whole,
        P(None, "gx", "gy", "gz"),
        whole,
        P(),
        whole,
        whole,
        P(("gx", "gy", "gz"), None, None),
        P(("gx", "gy", "gz")),
        P(),
    )
    return jax.shard_map(
        body, mesh=mesh, in_specs=in_specs, out_specs=(whole, whole, whole), check_vma=False
    )
```

time: 673 us -> 221 us (0.33)
  waiting for transfers between devices: 326 us -> 27.3 us
  blocking collectives: 254 us -> 0 us
  starting transfers between devices: 39.5 us -> 87.8 us
  local copies, waits for them, and re-layouts: 14.3 us -> 47.9 us
  other arithmetic: 6.31 us -> 24.8 us
  between operations: 17.5 us -> 5.4 us
  matrix products: 14.8 us -> 26.2 us
    psum x1 -> x0, waiting for transfers between devices: 315 us -> none  [body(): lax.psum((partial_inner, inner_local), ('gx', 'gy', 'gz'))]
    psum x2 -> x0, blocking collectives: 254 us -> none  [the longest x1 130 us: body(): lax.psum((partial_inner, inner_local), ('gx', 'gy', 'gz'))]
    all_to_all x0 -> x5, starting transfers between devices: none -> 55.4 us  [spread(): return lax.all_to_all(values, axes, 0, 0, tiled=False)]
    all_to_all x0 -> x5, waiting for transfers between devices: none -> 27.3 us  [spread(): return lax.all_to_all(values, axes, 0, 0, tiled=False)]
    slice x7 -> x10, local copies, waits for them, and re-layouts: 1.03 us -> 13.3 us  [the longest x2 5.23 us: assemble_inside(): lax.slice_in_dim(values, 0, length - 1, axis=axis)]
    add x2 -> x4, other arithmetic: 0.25 us -> 12.3 us  [the longest x3 11.7 us: assemble_inside(): values + jnp.where(position == N - 1, above, jnp.where(position == 0, bel...]
    gather x14 -> x0, local copies, waits for them, and re-layouts: 12 us -> none  [the longest x3 3.9 us: body(): jnp.take(extended_element, jnp.asarray(extended_index(elems_z)), axis=2)]
    dot_general x22 -> x31, matrix products: 14.8 us -> 26.2 us  [the longest x29 25.3 us: dot(): return jnp.dot(a, b, precision=HIGH)]
  transfers between devices with their start and end apart: 13 -> 17, of which waited for: 5 -> 3; matrix products, arithmetic and copies ran while one was open for 4% -> 38% of each run, Pallas kernels for 0% -> 0%
where the time goes in v1:
time: 221 us; the launch traced here: 219 us
  starting transfers between devices  87.8 us (40%)
  local copies, waits for them, and re-layouts  47.9 us (22%)
  waiting for transfers between devices  27.3 us (12%)
  matrix products  26.2 us (12%)
  other arithmetic  24.8 us (11%)
  between operations  5.4 us (2%)
    all_to_all x5, starting transfers between devices, spread(): return lax.all_to_all(values, axes, 0, 0, tiled=False)  55.4 us
    all_to_all x5, waiting for transfers between devices, spread(): return lax.all_to_all(values, axes, 0, 0, tiled=False)  27.3 us
    dot_general x29, matrix products, dot(): return jnp.dot(a, b, precision=HIGH)  25.3 us
    ppermute x6, starting transfers between devices, exchange(): lax.ppermute(to_high, axis, forward)  22.4 us
    add x3, other arithmetic, assemble_inside(): values + jnp.where(position == N - 1, above, jnp.where(position == 0, bel...  11.7 us
    ppermute x6, starting transfers between devices, exchange(): lax.ppermute(to_low, axis, backward)  10.1 us
    unnamed x82, local copies, waits for them, and re-layouts  9.45 us
    slice x2, local copies, waits for them, and re-layouts, assemble_inside(): lax.slice_in_dim(values, 0, length - 1, axis=axis)  5.23 us
  transfers between devices with their start and end apart: 17, of which 3 were waited for; matrix products, arithmetic and copies ran while one was open for 38% of the time, Pallas kernels for 0%

profile of v1, /device:TPU:1, one launch (start us, length us, event | category | flops | bytes accessed | tf_op | source)
XLA Modules:
  0.0 219.5 jit_solution(15746941548502153262)
XLA Ops:
  0.7 1.4 slice_bitcast_fusion.2
  2.1 5.4 %collective-permute-start = (f32[16,128]{1,0:T(8,128)}, f32[16,128]{1,0:T(8,128)}, u32[]{:S(2)}, u32[]{:S(2)}) collective-permute-start(f32[16,128]{1,0:T(8,128)} %get-tuple-element.36), channel_id=1, source_target_pairs={{0,64},{64,128},{128,192},{192,256},{256,320},{320,384},{384,448},... | collective-permute-start | bytes 24584 | tf_op jit(solution)/shard_map/ppermute | solution.py:47
  7.5 1.3 collective-permute-start.1
  12.8 1.7 fusion.13
  14.5 15.4 %all-to-all-start = ((f32[64,8,128]{2,1,0:T(8,128)}), f32[64,8,128]{2,1,0:T(8,128)}, u32[]{:S(2)}, u32[]{:S(2)}) async-start(f32[64,8,128]{2,1,0:T(8,128)} %fusion.13), calls=%async_computation | async-start | bytes 524288 | tf_op jit(solution)/shard_map/all_to_all | solution.py:51
  29.9 1.5 fusion.34
  36.4 1.2 fusion.45
  37.6 1.2 fusion.47
  42.2 1.3 convolution_multiply_fusion.2
  47.8 3.3 %collective-permute-start.2 = (f32[18,128]{1,0:T(8,128)S(1)}, f32[18,128]{1,0:T(8,128)S(1)}, u32[]{:S(2)}, u32[]{:S(2)}) collective-permute-start(f32[18,128]{1,0:T(8,128)S(1)} %pad_maximum_fusion.3), channel_id=1, source_target_pairs={{0,8},{8,16},{16,24},{24,32},{32,40},{40,48},{48,56},{1,9},{9,17},... | collective-permute-start | bytes 27656 | tf_op jit(solution)/shard_map/ppermute | solution.py:47
  51.2 1.3 collective-permute-start.3
  53.5 1.8 reshape.73
  57.2 1.5 concatenate.32
  59.0 3.7 %collective-permute-start.4 = (f32[1,324]{1,0:T(1,128)S(1)}, f32[1,324]{1,0:T(1,128)S(1)}, u32[]{:S(2)}, u32[]{:S(2)}) collective-permute-start(f32[1,324]{1,0:T(1,128)S(1)} %get-tuple-element.41), channel_id=1, source_target_pairs={{0,1},{1,2},{2,3},{3,4},{4,5},{5,6},{6,7},{8,9},{9,10},{10,11},{11... | collective-permute-start | bytes 3896 | tf_op jit(solution)/shard_map/ppermute | solution.py:47
  62.6 1.9 collective-permute-start.5
  66.2 15.2 %all-to-all-start.1 = ((f32[16,8,128]{2,1,0:T(8,128)}), f32[16,8,128]{2,1,0:T(8,128)S(1)}, u32[]{:S(2)}, u32[]{:S(2)}) async-start(f32[16,8,128]{2,1,0:T(8,128)} %broadcast_in_dim.15), calls=%async_computation.1 | async-start | bytes 131072 | tf_op jit(solution)/shard_map/all_to_all | solution.py:51
  81.5 1.3 fusion.42
  83.4 10.0 %all-to-all-done.1 = f32[16,8,128]{2,1,0:T(8,128)S(1)} async-done(((f32[16,8,128]{2,1,0:T(8,128)}), f32[16,8,128]{2,1,0:T(8,128)S(1)}, u32[]{:S(2)}, u32[]{:S(2)}) %all-to-all-start.1) | async-done | bytes 65568 | tf_op jit(solution)/shard_map/all_to_all | solution.py:51
  94.2 13.9 %all-to-all-start.2 = ((f32[64,8,128]{2,1,0:T(8,128)}), f32[64,8,128]{2,1,0:T(8,128)S(1)}, u32[]{:S(2)}, u32[]{:S(2)}) async-start(f32[64,8,128]{2,1,0:T(8,128)} %broadcast_in_dim.16), calls=%async_computation.2 | async-start | bytes 524288 | tf_op jit(solution)/shard_map/all_to_all | solution.py:51
  109.3 2.2 %multiply_reduce_fusion = (f32[]{:T(128)}, f32[400,160]{0,1:T(8,128)S(1)}) fusion(f32[400,160]{0,1:T(8,128)S(1)} %copy.79, f32[400,160]{0,1:T(8,128)S(1)} %fusion.28, f32[400,128]{1,0:T(8,128)} %fusion.42, f32[130,160]{1,0:T(8,128)} %fusion.43), kind=kOutput, calls=%fused_computation.41 | convolution fusion | flops 98560000 | bytes 1103876 | tf_op jit(solution)/shard_map/dot_general | solution.py:36
  112.0 9.3 %all-to-all-done.2 = f32[64,8,128]{2,1,0:T(8,128)S(1)} async-done(((f32[64,8,128]{2,1,0:T(8,128)}), f32[64,8,128]{2,1,0:T(8,128)S(1)}, u32[]{:S(2)}, u32[]{:S(2)}) %all-to-all-start.2) | async-done | bytes 262176 | tf_op jit(solution)/shard_map/all_to_all | solution.py:51
  123.7 1.6 bitcast_multiply_fusion
  125.3 1.6 convolution_multiply_fusion.3
  127.5 1.2 multiply_reduce_fusion.5
  129.3 2.4 %collective-permute-start.7 = (f32[2,1,16,128]{3,2,1,0:T(8,128)S(1)}, f32[2,1,16,128]{3,2,1,0:T(8,128)S(1)}, u32[]{:S(2)}, u32[]{:S(2)}) collective-permute-start(f32[2,1,16,128]{3,2,1,0:T(8,128)S(1)} %get-tuple-element.27), channel_id=1, source_target_pairs={{0,64},{64,128},{128,192},{192,256},{256,320},{320,384},{384,448},... | collective-permute-start | bytes 49160 | tf_op jit(solution)/shard_map/ppermute | solution.py:47
  131.8 1.3 collective-permute-start.6
  133.7 2.7 %pad_maximum_fusion.5 = f32[4]{0:T(128)S(1)} fusion(f32[1]{0:T(128)} %bitcast.19, f32[1]{0:T(128)} %bitcast.18, f32[1]{0:T(128)} %bitcast.12, f32[1]{0:T(128)} %bitcast.5), kind=kLoop, calls=%fused_computation.89 | loop fusion | flops 12 | bytes 32 | tf_op jit(solution)/shard_map/stack | solution.py:193
  137.2 5.0 %all-to-all-start.3 = ((f32[64,4,128]{2,1,0:T(4,128)}), f32[64,4,128]{2,1,0:T(4,128)S(1)}, u32[]{:S(2)}, u32[]{:S(2)}) async-start(f32[64,4,128]{2,1,0:T(4,128)} %broadcast_in_dim_broadcast_in_dim_broadcast_in_dim.2), calls=%async_computation.3 | async-start | bytes 262144 | tf_op jit(solution)/shard_map/all_to_all | solution.py:51
  142.9 2.8 %copy.85 = f32[2,16,16,128]{2,1,0,3:T(8,128)} copy(f32[2,16,16,128]{3,2,1,0:T(8,128)S(1)} %pad_maximum_fusion) | data formatting | bytes 524288 | tf_op jit(solution)/shard_map/stack | solution.py:191
  145.8 2.9 %copy.83 = f32[2,16,16,128]{2,1,0,3:T(8,128)} copy(f32[2,16,16,128]{3,2,1,0:T(8,128)S(1)} %pad_maximum_fusion.2) | data formatting | bytes 524288 | tf_op jit(solution)/shard_map/concatenate | solution.py:74
  148.7 2.8 %copy.84 = f32[2,16,16,128]{2,1,0,3:T(8,128)} copy(f32[2,16,16,128]{3,2,1,0:T(8,128)S(1)} %pad_maximum_fusion.1) | data formatting | bytes 524288 | tf_op jit(solution)/shard_map/concatenate | solution.py:73
  151.5 3.7 %select_add_fusion = f32[2,16,16,128]{2,1,0,3:T(8,128)S(1)} fusion(f32[2,16,16,128]{2,1,0,3:T(8,128)} %copy.85, f32[2,16,16,128]{2,1,0,3:T(8,128)} %copy.84, f32[2,16,16,128]{2,1,0,3:T(8,128)} %copy.83, s32[16]{0:T(128)S(1)} %copy-done.35, s32[16]{0:T(128)S(1)} %copy-done.31, pred[16]{0:T(512)(128)(4,1)S(1)} %copy-done.33), kind=kLoop, calls=%fused_computation.12 | loop fusion | flops 393216 | bytes 1048720 | tf_op jit(solution)/shard_map/add | solution.py:76
  155.2 2.7 %fusion.32 = (f32[2,16,1,128]{2,1,0,3:T(8,128)}, f32[2,16,1,128]{2,1,0,3:T(8,128)}) fusion(f32[2,16,16,128]{2,1,0,3:T(8,128)S(1)} %select_add_fusion), kind=kLoop, calls=%fused_computation.96 | loop fusion | bytes 65536 | tf_op jit(solution)/shard_map/slice | solution.py:203
  157.9 2.7 %copy.99 = f32[2,16,1,128]{3,1,2,0:T(8,128)S(1)} copy(f32[2,16,1,128]{2,1,0,3:T(8,128)} %get-tuple-element.24) | data formatting | bytes 32768
  160.6 1.5 collective-permute-start.8
  162.1 3.3 %copy.100 = f32[2,16,1,128]{3,1,2,0:T(8,128)} copy(f32[2,16,1,128]{2,1,0,3:T(8,128)} %get-tuple-element.23) | data formatting | bytes 32768
  165.3 4.5 %collective-permute-start.9 = (f32[2,16,1,128]{3,1,2,0:T(8,128)}, f32[2,16,1,128]{3,1,2,0:T(8,128)}, u32[]{:S(2)}, u32[]{:S(2)}) collective-permute-start(f32[2,16,1,128]{3,1,2,0:T(8,128)} %copy.100), channel_id=1, source_target_pairs={{0,8},{8,16},{16,24},{24,32},{32,40},{40,48},{48,56},{1,9},{9,17},... | collective-permute-start | bytes 49160 | tf_op jit(solution)/shard_map/ppermute | solution.py:47
  169.8 2.7 %fusion.33 = (f32[2,16,15,128]{2,1,0,3:T(8,128)}, f32[2,16,15,128]{2,1,0,3:T(8,128)}) fusion(f32[2,16,16,128]{2,1,0,3:T(8,128)S(1)} %select_add_fusion), kind=kLoop, calls=%fused_computation.97 | loop fusion | bytes 983040 | tf_op jit(solution)/shard_map/slice | solution.py:74
  172.6 3.6 %copy.87 = f32[2,16,1,128]{2,1,0,3:T(8,128)} copy(f32[2,16,1,128]{3,1,2,0:T(8,128)} %collective-permute-done.8) | data formatting | bytes 32768 | tf_op jit(solution)/shard_map/ppermute | solution.py:47
  176.2 3.6 %copy.89 = f32[2,16,1,128]{2,1,0,3:T(8,128)} copy(f32[2,16,1,128]{3,1,2,0:T(8,128)} %collective-permute-done.9) | data formatting | bytes 32768 | tf_op jit(solution)/shard_map/ppermute | solution.py:47
  179.8 4.8 %fusion = f32[2,16,16,128]{2,1,0,3:T(8,128)S(1)} fusion(f32[2,16,16,128]{2,1,0,3:T(8,128)S(1)} %select_add_fusion, f32[2,16,1,128]{2,1,0,3:T(8,128)} %copy.87, f32[2,16,15,128]{2,1,0,3:T(8,128)} %get-tuple-element.26, f32[2,16,15,128]{2,1,0,3:T(8,128)} %get-tuple-element.25, f32[2,16,1,128]{2,1,0,3:T(8,128)} %copy.89, s32[16]{0:T(128)S(1)} %copy-done.36, ...), kind=kLoop, calls=%fused_computation.7 | loop fusion | flops 524288 | bytes 1048720 | tf_op jit(solution)/shard_map/add | solution.py:76
  184.6 2.8 %collective-permute-start.10 = (f32[2,16,16]{2,1,0:T(8,128)S(1)}, f32[2,16,16]{2,1,0:T(8,128)S(1)}, u32[]{:S(2)}, u32[]{:S(2)}) collective-permute-start(f32[2,16,16]{2,1,0:T(8,128)S(1)} %get-tuple-element.20), channel_id=1, source_target_pairs={{1,0},{2,1},{3,2},{4,3},{5,4},{6,5},{7,6},{9,8},{10,9},{11,10},{12... | collective-permute-start | bytes 6152 | tf_op jit(solution)/shard_map/ppermute | solution.py:47
  187.4 3.1 %collective-permute-start.11 = (f32[2,16,16]{2,1,0:T(8,128)S(1)}, f32[2,16,16]{2,1,0:T(8,128)S(1)}, u32[]{:S(2)}, u32[]{:S(2)}) collective-permute-start(f32[2,16,16]{2,1,0:T(8,128)S(1)} %get-tuple-element.19), channel_id=1, source_target_pairs={{0,1},{1,2},{2,3},{3,4},{4,5},{5,6},{6,7},{8,9},{9,10},{10,11},{11... | collective-permute-start | bytes 6152 | tf_op jit(solution)/shard_map/ppermute | solution.py:47
  190.5 2.5 %fusion.31 = (f32[2,16,16,127]{2,1,0,3:T(8,128)}, f32[2,16,16,127]{2,1,0,3:T(8,128)}) fusion(f32[2,16,16,128]{2,1,0,3:T(8,128)S(1)} %fusion), kind=kLoop, calls=%fused_computation.95 | loop fusion | bytes 1040384 | tf_op jit(solution)/shard_map/slice | solution.py:74
  193.7 5.8 %all-to-all-start.4 = ((f32[16,4,128]{2,1,0:T(4,128)}), f32[16,4,128]{2,1,0:T(4,128)S(1)}, u32[]{:S(2)}, u32[]{:S(2)}) async-start(f32[16,4,128]{2,1,0:T(4,128)} %broadcast_in_dim.18), calls=%async_computation.4 | async-start | bytes 65536 | tf_op jit(solution)/shard_map/all_to_all | solution.py:51
  200.1 3.3 %fusion.1 = f32[2,16,16,128]{2,1,0,3:T(8,128)S(1)} fusion(f32[2,16,16,128]{2,1,0,3:T(8,128)} %copy-done, f32[2,16,16,1]{2,1,0,3:T(8,128)S(1)} %bitcast.127, f32[2,16,16,127]{2,1,0,3:T(8,128)} %get-tuple-element.22, f32[2,16,16,127]{2,1,0,3:T(8,128)} %get-tuple-element.21, f32[2,16,16,1]{2,1,0,3:T(8,128)} %bitcast.128, s32[128]{0:T(128)} %get-tuple-element.52, ...), kind=kLoop, calls=%fused_computation.10 | loop fusion | flops 524288 | bytes 1049728 | tf_op jit(solution)/shard_map/add | solution.py:76
  203.5 8.0 %all-to-all-done.4 = f32[16,4,128]{2,1,0:T(4,128)S(1)} async-done(((f32[16,4,128]{2,1,0:T(4,128)}), f32[16,4,128]{2,1,0:T(4,128)S(1)}, u32[]{:S(2)}, u32[]{:S(2)}) %all-to-all-start.4) | async-done | bytes 32800 | tf_op jit(solution)/shard_map/all_to_all | solution.py:51
  216.5 2.3 %copy.91 = f32[16,16,128]{2,1,0:T(8,128)} copy(f32[16,16,128]{1,0,2:T(8,128)} %fusion.8) | data formatting | bytes 262144
  (156 shorter events, 33.0 us)
Async XLA Ops:
  0.6 34.3 %copy-start.27 = (f32[2,10,2,10]{3,2,1,0:T(2,128)S(1)}, f32[2,10,2,10]{3,2,1,0:T(2,128)}, u32[]{:S(2)}) copy-start(f32[2,10,2,10]{3,2,1,0:T(2,128)} %constant.99) | copy-start | bytes 4804
  0.6 34.4 %copy-start.24 = (f32[20,324]{1,0:T(8,128)S(1)}, f32[20,324]{1,0:T(8,128)}, u32[]{:S(2)}) copy-start(f32[20,324]{1,0:T(8,128)} %constant.80.clone) | copy-start | bytes 77764
  0.7 34.6 %copy-start.23 = (f32[20,324]{1,0:T(8,128)S(1)}, f32[20,324]{1,0:T(8,128)}, u32[]{:S(2)}) copy-start(f32[20,324]{1,0:T(8,128)} %constant.82.clone) | copy-start | bytes 77764
  0.7 34.8 %copy-start.5 = (f32[16,10,16,10]{3,2,1,0:T(8,128)S(1)}, f32[16,10,16,10]{3,2,1,0:T(8,128)}, u32[]{:S(2)}) copy-start(f32[16,10,16,10]{3,2,1,0:T(8,128)} %constant.100) | copy-start | bytes 307204
  0.7 34.2 %copy-start.25 = (f32[10,10]{1,0:T(8,128)S(1)}, f32[10,10]{1,0:T(8,128)}, u32[]{:S(2)}) copy-start(f32[10,10]{1,0:T(8,128)} %param.41) | copy-start | bytes 1204
  2.1 44.3 %collective-permute-start = (f32[16,128]{1,0:T(8,128)}, f32[16,128]{1,0:T(8,128)}, u32[]{:S(2)}, u32[]{:S(2)}) collective-permute-start(f32[16,128]{1,0:T(8,128)} %get-tuple-element.36), channel_id=1, source_target_pairs={{0,64},{64,128},{128,192},{192,256},{256,320},{320,384},{384,448},... | collective-permute-start | bytes 24584 | tf_op jit(solution)/shard_map/ppermute | solution.py:47
  7.5 39.6 %collective-permute-start.1 = (f32[16,128]{1,0:T(8,128)}, f32[16,128]{1,0:T(8,128)}, u32[]{:S(2)}, u32[]{:S(2)}) collective-permute-start(f32[16,128]{1,0:T(8,128)} %get-tuple-element.35), channel_id=1, source_target_pairs={{64,0},{128,64},{192,128},{256,192},{320,256},{384,320},{448,384},... | collective-permute-start | bytes 24584 | tf_op jit(solution)/shard_map/ppermute | solution.py:47
  14.5 50.1 %all-to-all-start = ((f32[64,8,128]{2,1,0:T(8,128)}), f32[64,8,128]{2,1,0:T(8,128)}, u32[]{:S(2)}, u32[]{:S(2)}) async-start(f32[64,8,128]{2,1,0:T(8,128)} %fusion.13), calls=%async_computation | async-start | bytes 524288 | tf_op jit(solution)/shard_map/all_to_all | solution.py:51
  33.3 10.2 %copy-start.6 = (f32[1,16,16,128]{3,2,1,0:T(8,128)}, f32[1,16,16,128]{3,2,1,0:T(8,128)S(1)}, u32[]{:S(2)}) copy-start(f32[1,16,16,128]{3,2,1,0:T(8,128)S(1)} %slice.120) | copy-start | bytes 393220
  35.7 5.9 %copy-start.22 = (f32[20,400]{1,0:T(8,128)S(1)}, f32[20,400]{1,0:T(8,128)}, u32[]{:S(2)}) copy-start(f32[20,400]{1,0:T(8,128)} %constant.84.clone) | copy-start | bytes 96004
  35.7 6.5 %copy-start.1 = (f32[16,16,128]{2,1,0:T(8,128)S(1)}, f32[16,16,128]{2,1,0:T(8,128)}, u32[]{:S(2)}) copy-start(f32[16,16,128]{2,1,0:T(8,128)} %param.38) | copy-start | bytes 393220
  35.7 6.5 %copy-start.3 = (f32[512,256]{1,0:T(8,128)S(1)}, f32[512,256]{1,0:T(8,128)}, u32[]{:S(2)}) copy-start(f32[512,256]{1,0:T(8,128)} %constant.91.clone) | copy-start | bytes 1572868
  36.3 7.1 %copy-start.13 = (f32[128,128]{1,0:T(8,128)S(1)}, f32[128,128]{1,0:T(8,128)}, u32[]{:S(2)}) copy-start(f32[128,128]{1,0:T(8,128)} %constant.92.clone) | copy-start | bytes 196612
  36.3 7.4 %copy-start.11 = (f32[128,128]{1,0:T(8,128)S(1)}, f32[128,128]{1,0:T(8,128)}, u32[]{:S(2)}) copy-start(f32[128,128]{1,0:T(8,128)} %constant.94.clone) | copy-start | bytes 196612
  37.6 7.1 %copy-start.15 = (f32[400,20]{1,0:T(8,128)S(1)}, f32[400,20]{1,0:T(8,128)}, u32[]{:S(2)}) copy-start(f32[400,20]{1,0:T(8,128)} %constant.81.clone) | copy-start | bytes 96004
  42.2 5.7 %copy-start.26 = (f32[16,1,128]{2,1,0:T(1,128)S(1)}, f32[16,1,128]{2,1,0:T(1,128)}, u32[]{:S(2)}) copy-start(f32[16,1,128]{2,1,0:T(1,128)} %get-tuple-element.34) | copy-start | bytes 24580
  42.2 10.9 %copy-start.4 = (f32[16,16,128]{2,1,0:T(8,128)S(1)}, f32[16,16,128]{2,1,0:T(8,128)}, u32[]{:S(2)}) copy-start(f32[16,16,128]{2,1,0:T(8,128)} %param.36) | copy-start | bytes 393220
  45.3 13.3 %copy-start.37 = (f32[2,128]{1,0:T(2,128)S(1)}, f32[2,128]{1,0:T(2,128)}, u32[]{:S(2)}) copy-start(f32[2,128]{1,0:T(2,128)} %constant.76.clone) | copy-start | bytes 3076
  47.8 9.3 %collective-permute-start.2 = (f32[18,128]{1,0:T(8,128)S(1)}, f32[18,128]{1,0:T(8,128)S(1)}, u32[]{:S(2)}, u32[]{:S(2)}) collective-permute-start(f32[18,128]{1,0:T(8,128)S(1)} %pad_maximum_fusion.3), channel_id=1, source_target_pairs={{0,8},{8,16},{16,24},{24,32},{32,40},{40,48},{48,56},{1,9},{9,17},... | collective-permute-start | bytes 27656 | tf_op jit(solution)/shard_map/ppermute | solution.py:47
  51.2 6.0 %collective-permute-start.3 = (f32[18,128]{1,0:T(8,128)S(1)}, f32[18,128]{1,0:T(8,128)S(1)}, u32[]{:S(2)}, u32[]{:S(2)}) collective-permute-start(f32[18,128]{1,0:T(8,128)S(1)} %pad_maximum_fusion.4), channel_id=1, source_target_pairs={{8,0},{16,8},{24,16},{32,24},{40,32},{48,40},{56,48},{9,1},{17,9},... | collective-permute-start | bytes 27656 | tf_op jit(solution)/shard_map/ppermute | solution.py:47
  59.0 23.8 %collective-permute-start.4 = (f32[1,324]{1,0:T(1,128)S(1)}, f32[1,324]{1,0:T(1,128)S(1)}, u32[]{:S(2)}, u32[]{:S(2)}) collective-permute-start(f32[1,324]{1,0:T(1,128)S(1)} %get-tuple-element.41), channel_id=1, source_target_pairs={{0,1},{1,2},{2,3},{3,4},{4,5},{5,6},{6,7},{8,9},{9,10},{10,11},{11... | collective-permute-start | bytes 3896 | tf_op jit(solution)/shard_map/ppermute | solution.py:47
  62.6 20.2 %collective-permute-start.5 = (f32[1,324]{1,0:T(1,128)S(1)}, f32[1,324]{1,0:T(1,128)S(1)}, u32[]{:S(2)}, u32[]{:S(2)}) collective-permute-start(f32[1,324]{1,0:T(1,128)S(1)} %get-tuple-element.42), channel_id=1, source_target_pairs={{1,0},{2,1},{3,2},{4,3},{5,4},{6,5},{7,6},{9,8},{10,9},{11,10},{12... | collective-permute-start | bytes 3896 | tf_op jit(solution)/shard_map/ppermute | solution.py:47
  66.2 27.2 %all-to-all-start.1 = ((f32[16,8,128]{2,1,0:T(8,128)}), f32[16,8,128]{2,1,0:T(8,128)S(1)}, u32[]{:S(2)}, u32[]{:S(2)}) async-start(f32[16,8,128]{2,1,0:T(8,128)} %broadcast_in_dim.15), calls=%async_computation.1 | async-start | bytes 131072 | tf_op jit(solution)/shard_map/all_to_all | solution.py:51
  82.8 38.6 %copy-start.38 = (s32[8]{0:T(128)S(1)}, s32[8]{0:T(128)}, u32[]{:S(2)}) copy-start(s32[8]{0:T(128)} %param.45) | copy-start | bytes 100
  93.5 29.3 %copy-start.30 = (s32[2,2,16]{2,1,0:T(2,128)S(1)}, s32[2,2,16]{2,1,0:T(2,128)}, u32[]{:S(2)}) copy-start(s32[2,2,16]{2,1,0:T(2,128)} %param.43) | copy-start | bytes 772
  93.5 29.5 %copy-start.19 = (f32[256,4]{1,0:T(8,128)S(1)}, f32[256,4]{1,0:T(8,128)}, u32[]{:S(2)}) copy-start(f32[256,4]{1,0:T(8,128)} %constant.89.clone) | copy-start | bytes 12292
  94.2 29.0 %copy-start.29 = (f32[16,128]{1,0:T(8,128)S(1)}, f32[16,128]{1,0:T(8,128)}, u32[]{:S(2)}) copy-start(f32[16,128]{1,0:T(8,128)} %constant.90.clone) | copy-start | bytes 24580
  94.2 29.4 %copy-start.10 = (f32[160,128]{1,0:T(8,128)S(1)}, f32[160,128]{1,0:T(8,128)}, u32[]{:S(2)}) copy-start(f32[160,128]{1,0:T(8,128)} %fusion.48) | copy-start | bytes 245764
  94.2 27.1 %all-to-all-start.2 = ((f32[64,8,128]{2,1,0:T(8,128)}), f32[64,8,128]{2,1,0:T(8,128)S(1)}, u32[]{:S(2)}, u32[]{:S(2)}) async-start(f32[64,8,128]{2,1,0:T(8,128)} %broadcast_in_dim.16), calls=%async_computation.2 | async-start | bytes 524288 | tf_op jit(solution)/shard_map/all_to_all | solution.py:51
  111.5 15.4 %copy-start.7 = (f32[1,16,16,128]{3,2,1,0:T(8,128)S(1)}, f32[1,16,16,128]{3,2,1,0:T(8,128)}, u32[]{:S(2)}) copy-start(f32[1,16,16,128]{3,2,1,0:T(8,128)} %copy-done.6) | copy-start | bytes 393220
  111.5 15.4 %copy-start.14 = (f32[128,128]{1,0:T(8,128)S(1)}, f32[128,128]{1,0:T(8,128)}, u32[]{:S(2)}) copy-start(f32[128,128]{1,0:T(8,128)} %constant.92.clone) | copy-start | bytes 196612
  111.5 15.7 %copy-start.12 = (f32[128,128]{1,0:T(8,128)S(1)}, f32[128,128]{1,0:T(8,128)}, u32[]{:S(2)}) copy-start(f32[128,128]{1,0:T(8,128)} %constant.94.clone) | copy-start | bytes 196612
  112.0 15.5 %copy-start.2 = (f32[256,512]{1,0:T(8,128)S(1)}, f32[256,512]{1,0:T(8,128)}, u32[]{:S(2)}) copy-start(f32[256,512]{1,0:T(8,128)} %constant.93.clone) | copy-start | bytes 1572868
  129.3 16.4 %collective-permute-start.7 = (f32[2,1,16,128]{3,2,1,0:T(8,128)S(1)}, f32[2,1,16,128]{3,2,1,0:T(8,128)S(1)}, u32[]{:S(2)}, u32[]{:S(2)}) collective-permute-start(f32[2,1,16,128]{3,2,1,0:T(8,128)S(1)} %get-tuple-element.27), channel_id=1, source_target_pairs={{0,64},{64,128},{128,192},{192,256},{256,320},{320,384},{384,448},... | collective-permute-start | bytes 49160 | tf_op jit(solution)/shard_map/ppermute | solution.py:47
  131.8 16.9 %collective-permute-start.6 = (f32[2,1,16,128]{3,2,1,0:T(8,128)S(1)}, f32[2,1,16,128]{3,2,1,0:T(8,128)S(1)}, u32[]{:S(2)}, u32[]{:S(2)}) collective-permute-start(f32[2,1,16,128]{3,2,1,0:T(8,128)S(1)} %get-tuple-element.28), channel_id=1, source_target_pairs={{64,0},{128,64},{192,128},{256,192},{320,256},{384,320},{448,384},... | collective-permute-start | bytes 49160 | tf_op jit(solution)/shard_map/ppermute | solution.py:47
  137.2 55.9 %all-to-all-start.3 = ((f32[64,4,128]{2,1,0:T(4,128)}), f32[64,4,128]{2,1,0:T(4,128)S(1)}, u32[]{:S(2)}, u32[]{:S(2)}) async-start(f32[64,4,128]{2,1,0:T(4,128)} %broadcast_in_dim_broadcast_in_dim_broadcast_in_dim.2), calls=%async_computation.3 | async-start | bytes 262144 | tf_op jit(solution)/shard_map/all_to_all | solution.py:51
  145.7 5.8 %copy-start.31 = (s32[16]{0:T(128)S(1)}, s32[16]{0:T(128)}, u32[]{:S(2)}) copy-start(s32[16]{0:T(128)} %broadcast_add_fusion.1) | copy-start | bytes 196
  145.7 5.8 %copy-start.33 = (pred[16]{0:T(512)(128)(4,1)S(1)}, pred[16]{0:T(512)(128)(4,1)}, u32[]{:S(2)}) copy-start(pred[16]{0:T(512)(128)(4,1)} %compare_and_fusion.1) | copy-start | bytes 52
  145.8 5.7 %copy-start.35 = (s32[16]{0:T(128)S(1)}, s32[16]{0:T(128)}, u32[]{:S(2)}) copy-start(s32[16]{0:T(128)} %iota_and_fusion.1) | copy-start | bytes 196
  160.6 12.0 %collective-permute-start.8 = (f32[2,16,1,128]{3,1,2,0:T(8,128)S(1)}, f32[2,16,1,128]{3,1,2,0:T(8,128)}, u32[]{:S(2)}, u32[]{:S(2)}) collective-permute-start(f32[2,16,1,128]{3,1,2,0:T(8,128)S(1)} %copy.99), channel_id=1, source_target_pairs={{8,0},{16,8},{24,16},{32,24},{40,32},{48,40},{56,48},{9,1},{17,9},... | collective-permute-start | bytes 49160 | tf_op jit(solution)/shard_map/ppermute | solution.py:47
  165.3 10.8 %collective-permute-start.9 = (f32[2,16,1,128]{3,1,2,0:T(8,128)}, f32[2,16,1,128]{3,1,2,0:T(8,128)}, u32[]{:S(2)}, u32[]{:S(2)}) collective-permute-start(f32[2,16,1,128]{3,1,2,0:T(8,128)} %copy.100), channel_id=1, source_target_pairs={{0,8},{8,16},{16,24},{24,32},{32,40},{40,48},{48,56},{1,9},{9,17},... | collective-permute-start | bytes 49160 | tf_op jit(solution)/shard_map/ppermute | solution.py:47
  172.5 7.3 %copy-start.32 = (s32[16]{0:T(128)S(1)}, s32[16]{0:T(128)}, u32[]{:S(2)}) copy-start(s32[16]{0:T(128)} %broadcast_add_fusion.1) | copy-start | bytes 196
  172.5 7.3 %copy-start.34 = (pred[16]{0:T(512)(128)(4,1)S(1)}, pred[16]{0:T(512)(128)(4,1)}, u32[]{:S(2)}) copy-start(pred[16]{0:T(512)(128)(4,1)} %compare_and_fusion.1) | copy-start | bytes 52
  172.5 7.3 %copy-start.36 = (s32[16]{0:T(128)S(1)}, s32[16]{0:T(128)}, u32[]{:S(2)}) copy-start(s32[16]{0:T(128)} %iota_and_fusion.1) | copy-start | bytes 196
  184.6 5.9 %copy-start = (f32[2,16,16,128]{2,1,0,3:T(8,128)}, f32[2,16,16,128]{2,1,0,3:T(8,128)S(1)}, u32[]{:S(2)}) copy-start(f32[2,16,16,128]{2,1,0,3:T(8,128)S(1)} %fusion) | copy-start | bytes 786436
  184.6 14.9 %collective-permute-start.10 = (f32[2,16,16]{2,1,0:T(8,128)S(1)}, f32[2,16,16]{2,1,0:T(8,128)S(1)}, u32[]{:S(2)}, u32[]{:S(2)}) collective-permute-start(f32[2,16,16]{2,1,0:T(8,128)S(1)} %get-tuple-element.20), channel_id=1, source_target_pairs={{1,0},{2,1},{3,2},{4,3},{5,4},{6,5},{7,6},{9,8},{10,9},{11,10},{12... | collective-permute-start | bytes 6152 | tf_op jit(solution)/shard_map/ppermute | solution.py:47
  187.4 12.1 %collective-permute-start.11 = (f32[2,16,16]{2,1,0:T(8,128)S(1)}, f32[2,16,16]{2,1,0:T(8,128)S(1)}, u32[]{:S(2)}, u32[]{:S(2)}) collective-permute-start(f32[2,16,16]{2,1,0:T(8,128)S(1)} %get-tuple-element.19), channel_id=1, source_target_pairs={{0,1},{1,2},{2,3},{3,4},{4,5},{5,6},{6,7},{8,9},{9,10},{10,11},{11... | collective-permute-start | bytes 6152 | tf_op jit(solution)/shard_map/ppermute | solution.py:47
  193.7 17.7 %all-to-all-start.4 = ((f32[16,4,128]{2,1,0:T(4,128)}), f32[16,4,128]{2,1,0:T(4,128)S(1)}, u32[]{:S(2)}, u32[]{:S(2)}) async-start(f32[16,4,128]{2,1,0:T(4,128)} %broadcast_in_dim.18), calls=%async_computation.4 | async-start | bytes 65536 | tf_op jit(solution)/shard_map/all_to_all | solution.py:51
  (8 other events, 30.5 us)

commit v2 on v1

v2 whole, which is shorter than its diff:
```python
import jax
import jax.numpy as jnp
import numpy as np
from jax import lax
from jax.experimental import pallas as pl
from jax.experimental.pallas import tpu as pltpu
from jax.sharding import PartitionSpec as P

HIGH = lax.Precision.HIGHEST
N = 8
E = 10
F32 = jnp.float32


def cheb_matrix():
    count = 8
    points = np.cos(np.pi * np.arange(count) / (count - 1))
    signs = np.array([2.0, 1, 1, 1, 1, 1, 1, 2.0]) * (-1.0) ** np.arange(count)
    differ = points[:, None] - points[None, :] + np.eye(count)
    matrix = np.outer(signs, 1.0 / signs) / differ
    matrix = matrix - np.eye(count) * np.sum(matrix, axis=1)[:, None]
    return (0.25 * matrix).astype(np.float32)


def extended_positions(count):
    length = N * count
    result = []
    for element in range(count):
        for node in [N * element - 2, *range(N * element, N * element + N), N * element + N + 1]:
            result.append(length if node < 0 else length + 1 if node >= length else node)
    return np.array(result)


def inside_positions(count):
    return np.concatenate([np.arange(E * e + 1, E * e + N + 1) for e in range(count)])


def one_hot(index, size):
    return (np.asarray(index)[:, None] == np.arange(size)[None, :]).astype(np.float32)


def up8(count):
    return -(-count // 8) * 8


def mm(a, b, ca=1, cb=0):
    return lax.dot_general(
        a, b, (((ca,), (cb,)), ((), ())), precision=HIGH, preferred_element_type=F32
    )


def call(kernel, name, outs, *args, smem=(), flops=0):
    specs = [
        pl.BlockSpec(memory_space=pltpu.SMEM if i in smem else pltpu.VMEM)
        for i in range(len(args))
    ]
    moved = sum(int(np.prod(a.shape)) * 4 for a in args)
    moved += sum(int(np.prod(s)) * 4 for s in outs)
    return pl.pallas_call(
        kernel,
        out_shape=[jax.ShapeDtypeStruct(s, F32) for s in outs],
        in_specs=specs,
        out_specs=[pl.BlockSpec(memory_space=pltpu.VMEM)] * len(outs),
        cost_estimate=pl.CostEstimate(flops=flops, bytes_accessed=moved, transcendentals=0),
        compiler_params=pltpu.CompilerParams(vmem_limit_bytes=16 * 2**20),
        name=name,
    )(*args)


def coarse_kernel(blocks, residual, ids, values, out, ids_wide):
    nx, ny, nz = residual.shape
    ex, ey = nx // N, ny // N
    ez = ids.shape[1]
    n_stored, coarse, _ = values.shape
    widen = (
        lax.broadcasted_iota(jnp.int32, (ez, nz), 1) // N
        == lax.broadcasted_iota(jnp.int32, (ez, nz), 0)
    ).astype(F32)
    wide = mm(ids[...].astype(F32), widen)
    ids_wide[...] = wide
    unknown = lax.broadcasted_iota(jnp.int32, (coarse, nz), 0).astype(F32)
    total = jnp.zeros((coarse, nz), F32)
    for a in range(ex):
        for b in range(ey):
            part = jnp.sum(residual[a * N : a * N + N, b * N : b * N + N, :], axis=(0, 1))[None]
            q = a * ey + b
            total = total + jnp.where(jnp.abs(unknown - wide[q : q + 1]) < 0.5, part, 0.0)
    coarse_residual = jnp.sum(total, axis=1, keepdims=True)
    out[...] = jnp.zeros_like(out)
    for k in range(n_stored):
        row = jnp.sum(values[k] * coarse_residual, axis=0, keepdims=True)
        at = pl.ds(blocks[k], 1)
        out[at, :] = out[at, :] + row


def sum_spread_kernel(parts, out):
    total = jnp.sum(parts[...], axis=0)
    for i in range(out.shape[0]):
        out[i] = total


def across_faces_kernel(residual, low, high, to_high, to_low):
    nx, ny, nz = residual.shape
    for out, y in ((to_high, ny - 2), (to_low, 1)):
        out[...] = jnp.zeros_like(out)
        out[:nx] = residual[:, y, :]
        out[nx : nx + 1] = low[y : y + 1]
        out[nx + 1 : nx + 2] = high[y : y + 1]


def depth_faces_kernel(residual, x_low, x_high, y_low, y_high, every, to_high, to_low):
    nx, ny, nz = residual.shape
    at = 0
    for ref, count in ((None, nx * ny), (x_low, ny), (x_high, ny), (y_low, None), (y_high, None)):
        block = residual[...].reshape(nx * ny, nz) if ref is None else ref[...]
        every[at : at + block.shape[0]] = block
        at += block.shape[0]
    row = lax.broadcasted_iota(jnp.int32, (8, nz), 0)
    lane = lax.broadcasted_iota(jnp.int32, (8, nz), 1)
    pick = ((row == 0) & (lane == nz - 2)) | ((row == 1) & (lane == 1))
    ends = mm(pick.astype(F32), every[...], 1, 1)
    to_high[...] = ends[0:1]
    to_low[...] = ends[1:2]


def matrices_kernel(
    basis, tile2, mask2, tilez, maskz, row_x, row_y, col_x, col_y, out_x, out_y, col_z, in_z,
    to_spectral, from_spectral, to_z, from_z,
):
    flat2 = mm(mm(tile2[...], basis[...]), tile2[...], 1, 1) * mask2[...]
    flatz = mm(mm(tilez[...], basis[...]), tilez[...], 1, 1) * maskz[...]
    to_x = mm(row_x[...], mm(flat2, col_x[...], 0, 0))
    to_y = mm(row_y[...], mm(flat2, col_y[...], 0, 0))
    to_spectral[...] = to_x * to_y
    from_x = mm(mm(out_x[...], flat2), row_x[...], 1, 1)
    from_y = mm(mm(out_y[...], flat2), row_y[...], 1, 1)
    from_spectral[...] = from_x * from_y
    to_z[...] = mm(col_z[...], flatz)
    from_z[...] = mm(flatz, in_z[...], 0, 0)


def solve_kernel(
    every, z_low, z_high, to_spectral, from_spectral, to_z, from_z, sums, local_part, inner, wide
):
    nz = every.shape[1]
    n_x, n_y, n_z = sums.shape
    wide[...] = jnp.zeros_like(wide)
    wide[:, :n_y, :] = sums[...]
    weights = wide[...].reshape(-1, n_z)
    row = lax.broadcasted_iota(jnp.int32, (8, every.shape[0]), 0)
    ends = jnp.where(row == 0, z_low[...], jnp.where(row == 1, z_high[...], 0.0))
    spectral = mm(mm(to_spectral[...], every[...]), to_z[:nz, :])
    spectral = spectral + mm(mm(to_spectral[...], ends, 1, 1), to_z[nz:, :])
    weighted = weights * spectral
    inner[...] = jnp.sum(jnp.sum(weighted * spectral, axis=0, keepdims=True), axis=1, keepdims=True)
    local_part[...] = mm(mm(from_spectral[...], weighted), from_z[...])


def operator(flat, conductance, mass, kxy, kz):
    rows = flat.shape[0]
    along = mm(kxy[...], flat)
    along_x = along[:rows] * conductance[0].reshape(rows, -1)
    along_y = along[rows:] * conductance[1].reshape(rows, -1)
    along_z = mm(flat, kz[...], 1, 1) * conductance[2].reshape(rows, -1)
    total = mass[...].reshape(rows, -1) * flat + mm(along_z, kz[...])
    total = total + mm(kxy[:rows, :], along_x, 0, 0)
    return total + mm(kxy[rows:, :], along_y, 0, 0)


def operator_kernel(direction, conductance, mass, kxy, kz, image):
    rows = kxy.shape[1]
    flat = direction[...].reshape(rows, -1)
    image[...] = operator(flat, conductance, mass, kxy, kz).reshape(image.shape)


def total_of(values):
    return jnp.sum(jnp.sum(values, axis=0, keepdims=True), axis=1, keepdims=True)


def correct_kernel(
    blocks, coarse_inner, values, ids_wide, local_part, inner_local, direction, image_direction,
    conductance, mass, kxy, kz,
    z_out, image_out, to_high, to_low, terms, square,
):
    nx, ny, nz = direction.shape
    rows = nx * ny
    n_stored, coarse, block = values.shape
    total = jnp.zeros((coarse, block), F32)
    for k in range(n_stored):
        total = total + values[k] * coarse_inner[pl.ds(blocks[k], 1), :]
    solution = jnp.sum(total, axis=1, keepdims=True)
    unknown = lax.broadcasted_iota(jnp.int32, (coarse, nz), 0).astype(F32)
    ey = ny // N
    for a in range(nx // N):
        for b in range(ey):
            q = a * ey + b
            hit = jnp.abs(unknown - ids_wide[q : q + 1, :]) < 0.5
            line = jnp.sum(jnp.where(hit, solution, 0.0), axis=0, keepdims=True)
            for x in range(N):
                at = (a * N + x) * ny + b * N
                z_out[a * N + x, b * N : b * N + N, :] = local_part[at : at + N, :] + line
    flat = z_out[...].reshape(rows, nz)
    image = operator(flat, conductance, mass, kxy, kz)
    image_out[...] = image.reshape(nx, ny, nz)
    to_high[0] = image[rows - ny :]
    to_high[1] = image_direction[nx - 1]
    to_low[0] = image[:ny]
    to_low[1] = image_direction[0]
    old = direction[...].reshape(rows, nz)
    old_image = image_direction[...].reshape(rows, nz)
    first = total_of(flat * image)
    second = total_of(flat * old_image + old * image)
    third = total_of(old * old_image)
    lane = lax.broadcasted_iota(jnp.int32, (1, nz), 1)
    line = jnp.where(
        lane == 0,
        inner_local[...],
        jnp.where(lane == 1, first, jnp.where(lane == 2, second, jnp.where(lane == 3, third, 0.0))),
    )
    for i in range(terms.shape[0]):
        terms[i] = line
    square[...] = total_of(coarse_inner[...] * coarse_inner[...])


def assemble_length_kernel(image, image_direction, low, high, out, to_high, to_low):
    nx, ny, nz = image.shape
    for i, ref in ((0, image), (1, image_direction)):
        out[i] = ref[...]
        for x in range(nx):
            if x % N == N - 1:
                out[i, x] = ref[x] + (ref[x + 1] if x + 1 < nx else high[i])
            elif x % N == 0:
                out[i, x] = ref[x] + (ref[x - 1] if x else low[i])
        to_high[i] = out[i, :, ny - 1, :]
        to_low[i] = out[i, :, 0, :]


def assemble_across_kernel(images, low, high, out, to_high, to_low):
    _, nx, ny, nz = images.shape
    out[...] = images[...]
    for i in range(2):
        for y in range(ny):
            if y % N == N - 1:
                other = images[i, :, y + 1, :] if y + 1 < ny else high[i]
            elif y % N == 0:
                other = images[i, :, y - 1, :] if y else low[i]
            else:
                continue
            out[i, :, y, :] = images[i, :, y, :] + other
    row = lax.broadcasted_iota(jnp.int32, (8, nz), 0)
    lane = lax.broadcasted_iota(jnp.int32, (8, nz), 1)
    pick = ((row == 0) & (lane == nz - 1)) | ((row == 1) & (lane == 0))
    ends = mm(pick.astype(F32), out[...].reshape(2 * nx * ny, nz), 1, 1)
    to_high[...] = ends[0:1]
    to_low[...] = ends[1:2]


def update_kernel(
    prior, terms, square, images, low, high, residual, solution, direction, z,
    new_solution, new_residual, new_direction,
):
    nx, ny, nz = residual.shape
    rows = nx * ny
    lane1 = lax.broadcasted_iota(jnp.int32, (1, nz), 1)
    sums = jnp.sum(terms[...], axis=0)

    def term(i):
        return jnp.sum(jnp.where(lane1 == i, sums, 0.0), axis=1, keepdims=True)

    inner = term(0) + square[...]
    ratio = inner / prior[0]
    alpha = inner / (term(1) + ratio * term(2) + ratio * ratio * term(3))
    new = z[...].reshape(rows, nz) + ratio * direction[...].reshape(rows, nz)
    new_direction[...] = new.reshape(nx, ny, nz)
    new_solution[...] = (solution[...].reshape(rows, nz) + alpha * new).reshape(nx, ny, nz)
    image = images[0].reshape(rows, nz) + ratio * images[1].reshape(rows, nz)
    row = lax.broadcasted_iota(jnp.int32, (8, rows), 0)
    low_line = low[:, :rows] + ratio * low[:, rows:]
    high_line = high[:, :rows] + ratio * high[:, rows:]
    ends = jnp.where(row == 0, low_line, jnp.where(row == 1, high_line, 0.0))
    row = lax.broadcasted_iota(jnp.int32, (8, nz), 0)
    lane = lax.broadcasted_iota(jnp.int32, (8, nz), 1)
    place = ((row == 0) & (lane == 0)) | ((row == 1) & (lane == nz - 1))
    outer = mm(jnp.transpose(ends), place.astype(F32))
    lane = lax.broadcasted_iota(jnp.int32, (rows, nz), 1)
    above = pltpu.roll(image, nz - 1, 1)
    below = pltpu.roll(image, 1, 1)
    above = jnp.where((lane % N == N - 1) & (lane < nz - 1), above, 0.0)
    below = jnp.where((lane % N == 0) & (lane > 0), below, 0.0)
    image = image + above + below + outer
    new_residual[...] = (residual[...].reshape(rows, nz) - alpha * image).reshape(nx, ny, nz)


def shifts(axis):
    count = lax.axis_size(axis)
    forward = [(i, i + 1) for i in range(count - 1)]
    return forward, [(b, a) for a, b in forward]


def exchange(to_high, to_low, axis):
    forward, backward = shifts(axis)
    return lax.ppermute(to_high, axis, forward), lax.ppermute(to_low, axis, backward)


def spread(values, axes):
    return lax.all_to_all(values, axes, 0, 0, tiled=False)


def body(
    residual,
    solution,
    direction,
    conductance,
    mass_term,
    eigen_basis,
    inverse_eigen_sums,
    element_coarse_index,
    xxt_values,
    xxt_blocks,
    prior_inner,
):
    nx, ny, nz = residual.shape
    ex, ey, ez = nx // N, ny // N, nz // N
    rows = nx * ny
    plane = ("gy", "gz")
    n_plane, n_line = lax.axis_size(plane), lax.axis_size("gx")
    coarse_count, block = xxt_values.shape[1:]
    n_blocks = coarse_count * n_plane * n_line // block
    own = n_blocks // n_plane

    x_low, x_high = exchange(residual[nx - 2], residual[1], "gx")

    ids = element_coarse_index.reshape(ex * ey, ez)
    partial_inner, ids_wide = call(
        coarse_kernel, "coarse_restrict", [(n_blocks, block), (ex * ey, nz)],
        xxt_blocks, residual, ids, xxt_values, smem=(0,),
    )
    parts = spread(partial_inner.reshape(n_plane, own, block), plane)
    to_high, to_low = call(
        across_faces_kernel, "across_faces", [(up8(nx + 2), nz)] * 2, residual, x_low, x_high
    )
    y_low, y_high = exchange(to_high, to_low, "gy")

    face = up8(nx + 2)
    n_every = rows + 2 * ny + 2 * face
    pad = [-1] * (face - nx - 2)
    line = [*range(nx), nx, nx + 1, *pad]
    cols_x = np.array([*np.repeat(np.arange(nx), ny), *[nx] * ny, *[nx + 1] * ny, *line, *line])
    cols_y = np.array(
        [*np.tile(np.arange(ny), nx), *range(ny), *range(ny), *[ny] * face, *[ny + 1] * face]
    )
    n_x, n_y, n_z = inverse_eigen_sums.shape
    high_y = up8(n_y)
    place_y = np.tile(np.arange(high_y), n_x)
    row_x = one_hot(np.repeat(np.arange(n_x), high_y), n_x) * (place_y < n_y)[:, None]
    row_y = one_hot(place_y, n_y)
    col_x = (extended_positions(ex)[:, None] == cols_x[None, :]).astype(np.float32)
    col_y = (extended_positions(ey)[:, None] == cols_y[None, :]).astype(np.float32)
    assert ex == ey
    to_spectral, from_spectral, to_z, from_z = call(
        matrices_kernel, "basis_matrices",
        [(n_x * high_y, n_every), (rows, n_x * high_y), (nz + 8, n_z), (n_z, nz)],
        eigen_basis,
        *map(
            jnp.asarray,
            (
                np.tile(np.eye(E, dtype=np.float32), (ex, 1)),
                np.kron(np.eye(ex), np.ones((E, E))).astype(np.float32),
                np.tile(np.eye(E, dtype=np.float32), (ez, 1)),
                np.kron(np.eye(ez), np.ones((E, E))).astype(np.float32),
                row_x.astype(np.float32),
                row_y,
                col_x,
                col_y,
                one_hot(np.repeat(inside_positions(ex), ny), n_x),
                one_hot(np.tile(inside_positions(ey), nx), n_y),
                np.ascontiguousarray(one_hot(extended_positions(ez), nz + 8).T),
                np.ascontiguousarray(one_hot(inside_positions(ez), n_z).T),
            ),
        ),
    )

    cheb = cheb_matrix()
    kx = np.kron(np.kron(np.eye(ex, dtype=np.float32), cheb), np.eye(ny, dtype=np.float32))
    ky = np.kron(np.eye(nx, dtype=np.float32), np.kron(np.eye(ey, dtype=np.float32), cheb))
    kxy = jnp.asarray(np.concatenate([kx, ky]))
    kz = jnp.asarray(np.kron(np.eye(ez, dtype=np.float32), cheb))
    (image_direction,) = call(
        operator_kernel, "operator_direction", [direction.shape],
        direction, conductance, mass_term, kxy, kz,
    )

    every, to_high, to_low = call(
        depth_faces_kernel, "depth_faces", [(n_every, nz), (1, n_every), (1, n_every)],
        residual, x_low, x_high, y_low, y_high,
    )
    z_low, z_high = exchange(to_high, to_low, "gz")
    (owned,) = call(sum_spread_kernel, "sum_plane", [(n_line, own, block)], parts)
    parts = spread(owned, "gx")
    local_part, inner_local = pl.pallas_call(
        solve_kernel,
        out_shape=[jax.ShapeDtypeStruct((rows, nz), F32), jax.ShapeDtypeStruct((1, 1), F32)],
        in_specs=[pl.BlockSpec(memory_space=pltpu.VMEM)] * 8,
        out_specs=[pl.BlockSpec(memory_space=pltpu.VMEM)] * 2,
        scratch_shapes=[pltpu.VMEM((n_x, high_y, n_z), F32)],
        cost_estimate=pl.CostEstimate(flops=10**8, bytes_accessed=3 * 10**6, transcendentals=0),
        compiler_params=pltpu.CompilerParams(vmem_limit_bytes=16 * 2**20),
        name="element_solve",
    )(every, z_low, z_high, to_spectral, from_spectral, to_z, from_z, inverse_eigen_sums)
    (owned,) = call(sum_spread_kernel, "sum_line", [(n_plane, own, block)], parts)
    coarse_inner = spread(owned, plane).reshape(n_blocks, block)

    z, image, to_high, to_low, terms, square = call(
        correct_kernel, "coarse_correct",
        [direction.shape, direction.shape, (2, ny, nz), (2, ny, nz), (n_plane, 1, nz), (1, 1)],
        xxt_blocks, coarse_inner, xxt_values, ids_wide, local_part, inner_local, direction,
        image_direction, conductance, mass_term, kxy, kz, smem=(0,),
    )
    low, high = exchange(to_high, to_low, "gx")
    parts = spread(terms, plane)
    images, to_high, to_low = call(
        assemble_length_kernel, "assemble_length", [(2, nx, ny, nz), (2, nx, nz), (2, nx, nz)],
        image, image_direction, low, high,
    )
    low, high = exchange(to_high, to_low, "gy")
    (terms,) = call(sum_spread_kernel, "sum_terms", [(n_line, 1, nz)], parts)
    parts = spread(terms, "gx")
    images, to_high, to_low = call(
        assemble_across_kernel, "assemble_across", [(2, nx, ny, nz), (1, 2 * rows), (1, 2 * rows)],
        images, low, high,
    )
    low, high = exchange(to_high, to_low, "gz")
    return tuple(
        call(
            update_kernel, "update", [direction.shape] * 3,
            prior_inner, parts, square, images, low, high, residual, solution, direction, z,
            smem=(0,),
        )
    )


def solution(mesh):
    whole = P("gx", "gy", "gz")
    in_specs = (
        whole,
        whole,
        whole,
        P(None, "gx", "gy", "gz"),
        whole,
        P(),
        whole,
        whole,
        P(("gx", "gy", "gz"), None, None),
        P(("gx", "gy", "gz")),
        P(),
    )
    return jax.shard_map(
        body, mesh=mesh, in_specs=in_specs, out_specs=(whole, whole, whole), check_vma=False
    )
```

time: 221 us -> 149 us (0.67)
  blocking collectives: 0 us -> 54.7 us
  local copies, waits for them, and re-layouts: 47.9 us -> 3.32 us
  starting transfers between devices: 87.8 us -> 52.6 us
  matrix products: 26.2 us -> 0 us
  other arithmetic: 24.8 us -> 0 us
  Pallas kernels: 0 us -> 17.6 us
  waiting for transfers between devices: 27.3 us -> 17.8 us
  between operations: 5.4 us -> 1.83 us
    all_to_all x0 -> x2, blocking collectives: none -> 54.7 us  [spread(): return lax.all_to_all(values, axes, 0, 0, tiled=False)]
    all_to_all x5 -> x3, starting transfers between devices: 55.4 us -> 22.4 us  [spread(): return lax.all_to_all(values, axes, 0, 0, tiled=False)]
    dot_general x31 -> x0, matrix products: 26.2 us -> none  [the longest x29 25.3 us: dot(): return jnp.dot(a, b, precision=HIGH)]
    all_to_all x5 -> x3, waiting for transfers between devices: 27.3 us -> 5.48 us  [spread(): return lax.all_to_all(values, axes, 0, 0, tiled=False)]
    pallas_call x0 -> x13, Pallas kernels: none -> 17.6 us  [the longest x12 13.2 us: call(): pl.pallas_call(kernel, out_shape=[jax.ShapeDtypeStruct(s, F32) for s in o...]
    slice x10 -> x0, local copies, waits for them, and re-layouts: 13.3 us -> none  [the longest x2 5.23 us: assemble_inside(): lax.slice_in_dim(values, 0, length - 1, axis=axis)]
    add x5 -> x0, other arithmetic: 13 us -> none  [the longest x3 11.7 us: assemble_inside(): values + jnp.where(position == N - 1, above, jnp.where(position == 0, bel...]
    ppermute x6, waiting for transfers between devices: 0.02 us -> 12.3 us  [exchange(): lax.ppermute(to_low, axis, backward)]
  transfers between devices with their start and end apart: 17 -> 15, of which waited for: 3 -> 5; matrix products, arithmetic and copies ran while one was open for 38% -> 0% of each run, Pallas kernels for 0% -> 7%
where the time goes in v2:
time: 149 us; the launch traced here: 148 us
  blocking collectives  54.7 us (37%)
  starting transfers between devices  52.6 us (35%)
  waiting for transfers between devices  17.8 us (12%)
  Pallas kernels  17.6 us (12%)
  local copies, waits for them, and re-layouts  3.32 us (2%)
  between operations  1.83 us (1%)
    all_to_all x2, blocking collectives, spread(): return lax.all_to_all(values, axes, 0, 0, tiled=False)  54.7 us
    all_to_all x3, starting transfers between devices, spread(): return lax.all_to_all(values, axes, 0, 0, tiled=False)  22.4 us
    ppermute x6, starting transfers between devices, exchange(): lax.ppermute(to_high, axis, forward)  20.7 us
    pallas_call x12, Pallas kernels, call(): pl.pallas_call(kernel, out_shape=[jax.ShapeDtypeStruct(s, F32) for s in o...  13.2 us
    ppermute x6, waiting for transfers between devices, exchange(): lax.ppermute(to_low, axis, backward)  12.3 us
    ppermute x6, starting transfers between devices, exchange(): lax.ppermute(to_low, axis, backward)  9.45 us
    all_to_all x3, waiting for transfers between devices, spread(): return lax.all_to_all(values, axes, 0, 0, tiled=False)  5.48 us
    pallas_call x1, Pallas kernels, body(): pl.pallas_call(solve_kernel, out_shape=[jax.ShapeDtypeStruct((rows, nz),...  4.42 us
  transfers between devices with their start and end apart: 15, of which 5 were waited for; matrix products, arithmetic and copies ran while one was open for 0% of the time, Pallas kernels for 7%

profile of v2, /device:TPU:1, one launch (start us, length us, event | category | flops | bytes accessed | tf_op | source)
XLA Modules:
  0.0 147.9 jit_solution(9348346898832640563)
XLA Ops:
  0.6 0.6 copy-done.25
  1.3 0.9 copy-done
  2.2 0.9 copy-done.5
  3.1 0.7 copy-done.24
  3.8 0.8 coarse_restrict.1
  4.6 30.6 %all_to_all.25.parts = f32[64,8,128]{2,1,0:T(8,128)S(1)} all-to-all(f32[64,8,128]{2,1,0:T(8,128)S(1)} %bitcast.8), channel_id=1, replica_groups=mesh['gx'=16,'gy'=8,'gz'=8] {'gy','gz'}, dimensions={0} | all-to-all | bytes 524288 | tf_op jit(solution)/shard_map/all_to_all | solution.py:306
  35.3 0.1 sum_plane.1
  35.4 24.0 %all_to_all.26.parts = f32[16,8,128]{2,1,0:T(8,128)S(1)} all-to-all(f32[16,8,128]{2,1,0:T(8,128)S(1)} %sum_plane.1), channel_id=1, replica_groups=mesh['gx'=16,'gy'=8,'gz'=8] {'gx'}, dimensions={0} | all-to-all | bytes 131072 | tf_op jit(solution)/shard_map/all_to_all | solution.py:306
  59.4 0.7 sum_line.1
  60.2 6.4 %all-to-all-start.2 = ((f32[64,8,128]{2,1,0:T(8,128)}), f32[64,8,128]{2,1,0:T(8,128)S(1)}, u32[]{:S(2)}, u32[]{:S(2)}) async-start(f32[64,8,128]{2,1,0:T(8,128)} %sum_line.1), calls=%async_computation.2 | async-start | bytes 524288 | tf_op jit(solution)/shard_map/all_to_all | solution.py:306
  66.6 2.6 %collective-permute-start = (f32[16,128]{1,0:T(8,128)S(1)}, f32[16,128]{1,0:T(8,128)S(1)}, u32[]{:S(2)}, u32[]{:S(2)}) collective-permute-start(f32[16,128]{1,0:T(8,128)S(1)} %get-tuple-element.54), channel_id=1, source_target_pairs={{0,64},{64,128},{128,192},{192,256},{256,320},{320,384},{384,448},... | collective-permute-start | bytes 24584 | tf_op jit(solution)/shard_map/ppermute | solution.py:302
  69.2 1.4 collective-permute-start.1
  70.7 3.4 %collective-permute-done.1.high.x_high = f32[16,128]{1,0:T(8,128)S(1)} collective-permute-done((f32[16,128]{1,0:T(8,128)S(1)}, f32[16,128]{1,0:T(8,128)S(1)}, u32[]{:S(2)}, u32[]{:S(2)}) %collective-permute-start.1) | collective-permute-done | bytes 8224 | tf_op jit(solution)/shard_map/ppermute | solution.py:302
  74.1 3.3 %collective-permute-start.2 = (f32[24,128]{1,0:T(8,128)S(1)}, f32[24,128]{1,0:T(8,128)S(1)}, u32[]{:S(2)}, u32[]{:S(2)}) collective-permute-start(f32[24,128]{1,0:T(8,128)S(1)} %get-tuple-element.30), channel_id=1, source_target_pairs={{0,8},{8,16},{16,24},{24,32},{32,40},{40,48},{48,56},{1,9},{9,17},... | collective-permute-start | bytes 36872 | tf_op jit(solution)/shard_map/ppermute | solution.py:302
  77.4 1.3 collective-permute-start.3
  78.7 3.1 %collective-permute-done.3.y_high = f32[24,128]{1,0:T(8,128)S(1)} collective-permute-done((f32[24,128]{1,0:T(8,128)S(1)}, f32[24,128]{1,0:T(8,128)S(1)}, u32[]{:S(2)}, u32[]{:S(2)}) %collective-permute-start.3) | collective-permute-done | bytes 12320 | tf_op jit(solution)/shard_map/ppermute | solution.py:302
  81.8 0.3 depth_faces.1
  82.1 5.9 %collective-permute-start.4 = (f32[1,336]{1,0:T(1,128)S(1)}, f32[1,336]{1,0:T(1,128)S(1)}, u32[]{:S(2)}, u32[]{:S(2)}) collective-permute-start(f32[1,336]{1,0:T(1,128)S(1)} %get-tuple-element.33), channel_id=1, source_target_pairs={{0,1},{1,2},{2,3},{3,4},{4,5},{5,6},{6,7},{8,9},{9,10},{10,11},{11... | collective-permute-start | bytes 4040 | tf_op jit(solution)/shard_map/ppermute | solution.py:302
  88.0 0.0 copy-start.10
  88.0 0.0 copy-start.11
  88.0 0.0 copy-start.12
  88.0 0.0 copy-start.13
  88.1 0.0 copy-start.15
  88.1 0.0 copy-start.16
  88.1 0.0 copy-start.17
  88.1 0.0 copy-start.19
  88.1 0.0 copy-start.20
  88.1 0.0 copy-start.21
  88.1 0.0 copy-start.22
  88.2 2.2 %collective-permute-start.5 = (f32[1,336]{1,0:T(1,128)S(1)}, f32[1,336]{1,0:T(1,128)S(1)}, u32[]{:S(2)}, u32[]{:S(2)}) collective-permute-start(f32[1,336]{1,0:T(1,128)S(1)} %get-tuple-element.34), channel_id=1, source_target_pairs={{1,0},{2,1},{3,2},{4,3},{5,4},{6,5},{7,6},{9,8},{10,9},{11,10},{12... | collective-permute-start | bytes 4040 | tf_op jit(solution)/shard_map/ppermute | solution.py:302
  90.5 1.3 operator_direction.1.image_direction
  91.9 3.6 %basis_matrices.1 = (f32[480,336]{1,0:T(8,128)S(1)}, f32[256,480]{1,0:T(8,128)S(1)}, f32[136,160]{1,0:T(8,128)S(1)}, f32[160,128]{1,0:T(8,128)S(1)}) custom-call(f32[10,10]{1,0:T(8,128)S(1)} %copy-done.23, f32[20,10]{1,0:T(8,128)S(1)} %copy-done.21, f32[20,20]{1,0:T(8,128)S(1)} %copy-done.22, f32[160,10]{1,0:T(8,128)S(1)} %copy-done.17, ...), custom_call_target="tpu_custom_call" | custom-call | bytes 1757680 | tf_op jit(solution)/shard_map/basis_matrices/pallas_call | solution.py:59
  95.6 4.4 %element_solve.1 = (f32[256,128]{1,0:T(8,128)S(1)}, f32[1,1]{1,0:T(1,128)}) custom-call(f32[336,128]{1,0:T(8,128)S(1)} %get-tuple-element.32.every, f32[1,336]{1,0:T(1,128)S(1)} %collective-permute-done.4.z_low, f32[1,336]{1,0:T(1,128)S(1)} %collective-permute-done.5.z_high, f32[480,336]{1,0:T(8,128)S(1)} %get-tuple-element.35.to_spectral, ...), custom_call_target="tpu_custom_call" | custom-call | flops 100000000 | bytes 3000000 | tf_op jit(solution)/shard_map/element_solve/pallas_call | solution.py:400
  100.1 3.4 %coarse_correct.1 = (f32[16,16,128]{2,1,0:T(8,128)S(1)}, f32[16,16,128]{2,1,0:T(8,128)S(1)}, f32[2,16,128]{2,1,0:T(8,128)S(1)}, f32[2,16,128]{2,1,0:T(8,128)S(1)...) custom-call(s32[8]{0:T(128)S(1)} %copy-done.25, f32[512,128]{1,0:T(8,128)S(1)} %bitcast.7, f32[8,64,128]{2,1,0:T(8,128)S(1)} %copy-done.6, ...), custom_call_target="tpu_custom_call" | custom-call | bytes 2361384 | tf_op jit(solution)/shard_map/coarse_correct/pallas_call | solution.py:59
  103.4 10.7 %all-to-all-start.3 = ((f32[64,1,128]{2,1,0:T(1,128)}), f32[64,1,128]{2,1,0:T(1,128)S(1)}, u32[]{:S(2)}, u32[]{:S(2)}) async-start(f32[64,1,128]{2,1,0:T(1,128)} %get-tuple-element.41), calls=%async_computation.3 | async-start | bytes 65536 | tf_op jit(solution)/shard_map/all_to_all | solution.py:306
  114.2 2.5 %collective-permute-start.6 = (f32[2,16,128]{2,1,0:T(8,128)S(1)}, f32[2,16,128]{2,1,0:T(8,128)S(1)}, u32[]{:S(2)}, u32[]{:S(2)}) collective-permute-start(f32[2,16,128]{2,1,0:T(8,128)S(1)} %get-tuple-element.44), channel_id=1, source_target_pairs={{0,64},{64,128},{128,192},{192,256},{256,320},{320,384},{384,448},... | collective-permute-start | bytes 49160 | tf_op jit(solution)/shard_map/ppermute | solution.py:302
  116.7 1.3 collective-permute-start.7
  118.0 5.5 %all-to-all-done.3.parts = f32[64,1,128]{2,1,0:T(1,128)S(1)} async-done(((f32[64,1,128]{2,1,0:T(1,128)}), f32[64,1,128]{2,1,0:T(1,128)S(1)}, u32[]{:S(2)}, u32[]{:S(2)}) %all-to-all-start.3) | async-done | bytes 32800 | tf_op jit(solution)/shard_map/all_to_all | solution.py:306
  123.5 0.7 sum_terms.1
  124.1 5.3 %all-to-all-start.4 = ((f32[16,1,128]{2,1,0:T(1,128)}), f32[16,1,128]{2,1,0:T(1,128)S(1)}, u32[]{:S(2)}, u32[]{:S(2)}) async-start(f32[16,1,128]{2,1,0:T(1,128)} %sum_terms.1), calls=%async_computation.4 | async-start | bytes 16384 | tf_op jit(solution)/shard_map/all_to_all | solution.py:306
  129.5 2.2 %collective-permute-start.8 = (f32[2,16,128]{2,1,0:T(8,128)S(1)}, f32[2,16,128]{2,1,0:T(8,128)S(1)}, u32[]{:S(2)}, u32[]{:S(2)}) collective-permute-start(f32[2,16,128]{2,1,0:T(8,128)S(1)} %get-tuple-element.47), channel_id=1, source_target_pairs={{0,8},{8,16},{16,24},{24,32},{32,40},{40,48},{48,56},{1,9},{9,17},... | collective-permute-start | bytes 49160 | tf_op jit(solution)/shard_map/ppermute | solution.py:302
  131.8 1.3 collective-permute-start.9
  133.1 3.5 %collective-permute-done.9.high = f32[2,16,128]{2,1,0:T(8,128)S(1)} collective-permute-done((f32[2,16,128]{2,1,0:T(8,128)S(1)}, f32[2,16,128]{2,1,0:T(8,128)S(1)}, u32[]{:S(2)}, u32[]{:S(2)}) %collective-permute-start.9) | collective-permute-done | bytes 16416 | tf_op jit(solution)/shard_map/ppermute | solution.py:302
  136.6 0.4 assemble_across.1
  137.0 4.2 %collective-permute-start.10 = (f32[1,512]{1,0:T(1,128)S(1)}, f32[1,512]{1,0:T(1,128)S(1)}, u32[]{:S(2)}, u32[]{:S(2)}) collective-permute-start(f32[1,512]{1,0:T(1,128)S(1)} %get-tuple-element.50), channel_id=1, source_target_pairs={{0,1},{1,2},{2,3},{3,4},{4,5},{5,6},{6,7},{8,9},{9,10},{10,11},{11... | collective-permute-start | bytes 6152 | tf_op jit(solution)/shard_map/ppermute | solution.py:302
  141.1 1.9 %collective-permute-start.11 = (f32[1,512]{1,0:T(1,128)S(1)}, f32[1,512]{1,0:T(1,128)S(1)}, u32[]{:S(2)}, u32[]{:S(2)}) collective-permute-start(f32[1,512]{1,0:T(1,128)S(1)} %get-tuple-element.51), channel_id=1, source_target_pairs={{1,0},{2,1},{3,2},{4,3},{5,4},{6,5},{7,6},{9,8},{10,9},{11,10},{12... | collective-permute-start | bytes 6152 | tf_op jit(solution)/shard_map/ppermute | solution.py:302
  143.7 2.3 %collective-permute-done.11.high = f32[1,512]{1,0:T(1,128)S(1)} collective-permute-done((f32[1,512]{1,0:T(1,128)S(1)}, f32[1,512]{1,0:T(1,128)S(1)}, u32[]{:S(2)}, u32[]{:S(2)}) %collective-permute-start.11) | collective-permute-done | bytes 2080 | tf_op jit(solution)/shard_map/ppermute | solution.py:302
  146.0 1.8 %update.1 = (f32[16,16,128]{2,1,0:T(8,128)}, f32[16,16,128]{2,1,0:T(8,128)}, f32[16,16,128]{2,1,0:T(8,128)}) custom-call(f32[1]{0:T(128)S(6)} %copy.28.prior, f32[16,1,128]{2,1,0:T(1,128)S(1)} %all-to-all-done.4.terms, f32[1,1]{1,0:T(1,128)} %get-tuple-element.42.square, f32[2,16,16,128]{3,2,1,0:T(8,128)S(1)} %get-tuple-element.49.images, ...), custom_call_target="tpu_custom_call" | custom-call | bytes 1191944 | tf_op jit(solution)/shard_map/update/pallas_call | solution.py:59
  (50 shorter events, 0.2 us)
Async XLA Ops:
  0.6 0.7 copy-start.25
  1.3 0.9 copy-start
  2.2 0.9 copy-start.5
  3.1 0.7 copy-start.24
  35.3 55.1 %copy-start.9 = (f32[128,128]{1,0:T(8,128)S(1)}, f32[128,128]{1,0:T(8,128)}, u32[]{:S(2)}) copy-start(f32[128,128]{1,0:T(8,128)} %constant.41.clone.kz) | copy-start | bytes 196612
  35.4 55.1 %copy-start.7 = (f32[16,16,128]{2,1,0:T(8,128)S(1)}, f32[16,16,128]{2,1,0:T(8,128)}, u32[]{:S(2)}) copy-start(f32[16,16,128]{2,1,0:T(8,128)} %mass.3) | copy-start | bytes 393220
  59.4 31.0 %copy-start.3 = (f32[3,16,16,128]{3,2,1,0:T(8,128)S(1)}, f32[3,16,16,128]{3,2,1,0:T(8,128)}, u32[]{:S(2)}) copy-start(f32[3,16,16,128]{3,2,1,0:T(8,128)} %conductance.3) | copy-start | bytes 1179652
  60.2 6.4 %copy-start.1 = (f32[16,16,128]{2,1,0:T(8,128)S(1)}, f32[16,16,128]{2,1,0:T(8,128)}, u32[]{:S(2)}) copy-start(f32[16,16,128]{2,1,0:T(8,128)} %residual.7) | copy-start | bytes 393220
  60.2 30.3 %copy-start.2 = (f32[512,256]{1,0:T(8,128)S(1)}, f32[512,256]{1,0:T(8,128)}, u32[]{:S(2)}) copy-start(f32[512,256]{1,0:T(8,128)} %constant.40.clone.kxy) | copy-start | bytes 1572868
  60.2 39.9 %all-to-all-start.2 = ((f32[64,8,128]{2,1,0:T(8,128)}), f32[64,8,128]{2,1,0:T(8,128)S(1)}, u32[]{:S(2)}, u32[]{:S(2)}) async-start(f32[64,8,128]{2,1,0:T(8,128)} %sum_line.1), calls=%async_computation.2 | async-start | bytes 524288 | tf_op jit(solution)/shard_map/all_to_all | solution.py:306
  66.6 4.1 %collective-permute-start = (f32[16,128]{1,0:T(8,128)S(1)}, f32[16,128]{1,0:T(8,128)S(1)}, u32[]{:S(2)}, u32[]{:S(2)}) collective-permute-start(f32[16,128]{1,0:T(8,128)S(1)} %get-tuple-element.54), channel_id=1, source_target_pairs={{0,64},{64,128},{128,192},{192,256},{256,320},{320,384},{384,448},... | collective-permute-start | bytes 24584 | tf_op jit(solution)/shard_map/ppermute | solution.py:302
  69.2 21.2 %copy-start.4 = (f32[16,16,128]{2,1,0:T(8,128)S(1)}, f32[16,16,128]{2,1,0:T(8,128)}, u32[]{:S(2)}) copy-start(f32[16,16,128]{2,1,0:T(8,128)} %direction.5) | copy-start | bytes 393220
  69.2 4.8 %collective-permute-start.1 = (f32[16,128]{1,0:T(8,128)S(1)}, f32[16,128]{1,0:T(8,128)S(1)}, u32[]{:S(2)}, u32[]{:S(2)}) collective-permute-start(f32[16,128]{1,0:T(8,128)S(1)} %get-tuple-element.53), channel_id=1, source_target_pairs={{64,0},{128,64},{192,128},{256,192},{320,256},{384,320},{448,384},... | collective-permute-start | bytes 24584 | tf_op jit(solution)/shard_map/ppermute | solution.py:302
  74.1 4.6 %collective-permute-start.2 = (f32[24,128]{1,0:T(8,128)S(1)}, f32[24,128]{1,0:T(8,128)S(1)}, u32[]{:S(2)}, u32[]{:S(2)}) collective-permute-start(f32[24,128]{1,0:T(8,128)S(1)} %get-tuple-element.30), channel_id=1, source_target_pairs={{0,8},{8,16},{16,24},{24,32},{32,40},{40,48},{48,56},{1,9},{9,17},... | collective-permute-start | bytes 36872 | tf_op jit(solution)/shard_map/ppermute | solution.py:302
  77.4 4.4 %collective-permute-start.3 = (f32[24,128]{1,0:T(8,128)S(1)}, f32[24,128]{1,0:T(8,128)S(1)}, u32[]{:S(2)}, u32[]{:S(2)}) collective-permute-start(f32[24,128]{1,0:T(8,128)S(1)} %get-tuple-element.31), channel_id=1, source_target_pairs={{8,0},{16,8},{24,16},{32,24},{40,32},{48,40},{56,48},{9,1},{17,9},... | collective-permute-start | bytes 36872 | tf_op jit(solution)/shard_map/ppermute | solution.py:302
  82.1 13.5 %collective-permute-start.4 = (f32[1,336]{1,0:T(1,128)S(1)}, f32[1,336]{1,0:T(1,128)S(1)}, u32[]{:S(2)}, u32[]{:S(2)}) collective-permute-start(f32[1,336]{1,0:T(1,128)S(1)} %get-tuple-element.33), channel_id=1, source_target_pairs={{0,1},{1,2},{2,3},{3,4},{4,5},{5,6},{6,7},{8,9},{9,10},{10,11},{11... | collective-permute-start | bytes 4040 | tf_op jit(solution)/shard_map/ppermute | solution.py:302
  88.0 3.8 %copy-start.10 = (f32[480,20]{1,0:T(8,128)S(1)}, f32[480,20]{1,0:T(8,128)}, u32[]{:S(2)}) copy-start(f32[480,20]{1,0:T(8,128)} %constant.32.clone.row_x) | copy-start | bytes 115204
  88.0 3.8 %copy-start.11 = (f32[480,20]{1,0:T(8,128)S(1)}, f32[480,20]{1,0:T(8,128)}, u32[]{:S(2)}) copy-start(f32[480,20]{1,0:T(8,128)} %constant.33.clone.row_y) | copy-start | bytes 115204
  88.0 3.8 %copy-start.12 = (f32[160,160]{1,0:T(8,128)S(1)}, f32[160,160]{1,0:T(8,128)}, u32[]{:S(2)}) copy-start(f32[160,160]{1,0:T(8,128)} %constant.31.clone.maskz) | copy-start | bytes 307204
  88.0 3.8 %copy-start.13 = (f32[136,160]{1,0:T(8,128)S(1)}, f32[136,160]{1,0:T(8,128)}, u32[]{:S(2)}) copy-start(f32[136,160]{1,0:T(8,128)} %constant.38.clone.col_z) | copy-start | bytes 261124
  88.1 3.8 %copy-start.15 = (f32[256,20]{1,0:T(8,128)S(1)}, f32[256,20]{1,0:T(8,128)}, u32[]{:S(2)}) copy-start(f32[256,20]{1,0:T(8,128)} %constant.36.clone.out_x) | copy-start | bytes 61444
  88.1 3.8 %copy-start.16 = (f32[256,20]{1,0:T(8,128)S(1)}, f32[256,20]{1,0:T(8,128)}, u32[]{:S(2)}) copy-start(f32[256,20]{1,0:T(8,128)} %constant.37.clone.out_y) | copy-start | bytes 61444
  88.1 3.8 %copy-start.17 = (f32[160,10]{1,0:T(8,128)S(1)}, f32[160,10]{1,0:T(8,128)}, u32[]{:S(2)}) copy-start(f32[160,10]{1,0:T(8,128)} %constant.30.clone.tilez) | copy-start | bytes 19204
  88.1 3.8 %copy-start.18 = (f32[160,128]{1,0:T(8,128)S(1)}, f32[160,128]{1,0:T(8,128)}, u32[]{:S(2)}) copy-start(f32[160,128]{1,0:T(8,128)} %constant.39.clone.in_z) | copy-start | bytes 245764
  88.1 3.8 %copy-start.19 = (f32[20,336]{1,0:T(8,128)S(1)}, f32[20,336]{1,0:T(8,128)}, u32[]{:S(2)}) copy-start(f32[20,336]{1,0:T(8,128)} %constant.34.clone.col_x) | copy-start | bytes 80644
  88.1 3.8 %copy-start.20 = (f32[20,336]{1,0:T(8,128)S(1)}, f32[20,336]{1,0:T(8,128)}, u32[]{:S(2)}) copy-start(f32[20,336]{1,0:T(8,128)} %constant.35.clone.col_y) | copy-start | bytes 80644
  88.1 3.8 %copy-start.21 = (f32[20,10]{1,0:T(8,128)S(1)}, f32[20,10]{1,0:T(8,128)}, u32[]{:S(2)}) copy-start(f32[20,10]{1,0:T(8,128)} %constant.28.clone.tile2) | copy-start | bytes 2404
  88.1 3.8 %copy-start.22 = (f32[20,20]{1,0:T(8,128)S(1)}, f32[20,20]{1,0:T(8,128)}, u32[]{:S(2)}) copy-start(f32[20,20]{1,0:T(8,128)} %constant.29.clone.mask2) | copy-start | bytes 4804
  88.2 3.8 %copy-start.23 = (f32[10,10]{1,0:T(8,128)S(1)}, f32[10,10]{1,0:T(8,128)}, u32[]{:S(2)}) copy-start(f32[10,10]{1,0:T(8,128)} %basis.1) | copy-start | bytes 1204
  88.2 7.4 %collective-permute-start.5 = (f32[1,336]{1,0:T(1,128)S(1)}, f32[1,336]{1,0:T(1,128)S(1)}, u32[]{:S(2)}, u32[]{:S(2)}) collective-permute-start(f32[1,336]{1,0:T(1,128)S(1)} %get-tuple-element.34), channel_id=1, source_target_pairs={{1,0},{2,1},{3,2},{4,3},{5,4},{6,5},{7,6},{9,8},{10,9},{11,10},{12... | collective-permute-start | bytes 4040 | tf_op jit(solution)/shard_map/ppermute | solution.py:302
  91.9 3.7 %copy-start.8 = (f32[20,20,160]{2,1,0:T(8,128)S(1)}, f32[20,20,160]{2,1,0:T(8,128)}, u32[]{:S(2)}) copy-start(f32[20,20,160]{2,1,0:T(8,128)} %sums.1) | copy-start | bytes 768004
  95.6 4.5 %copy-start.6 = (f32[8,64,128]{2,1,0:T(8,128)S(1)}, f32[8,64,128]{2,1,0:T(8,128)}, u32[]{:S(2)}) copy-start(f32[8,64,128]{2,1,0:T(8,128)} %values.3) | copy-start | bytes 786436
  103.4 20.0 %all-to-all-start.3 = ((f32[64,1,128]{2,1,0:T(1,128)}), f32[64,1,128]{2,1,0:T(1,128)S(1)}, u32[]{:S(2)}, u32[]{:S(2)}) async-start(f32[64,1,128]{2,1,0:T(1,128)} %get-tuple-element.41), calls=%async_computation.3 | async-start | bytes 65536 | tf_op jit(solution)/shard_map/all_to_all | solution.py:306
  114.2 15.3 %collective-permute-start.6 = (f32[2,16,128]{2,1,0:T(8,128)S(1)}, f32[2,16,128]{2,1,0:T(8,128)S(1)}, u32[]{:S(2)}, u32[]{:S(2)}) collective-permute-start(f32[2,16,128]{2,1,0:T(8,128)S(1)} %get-tuple-element.44), channel_id=1, source_target_pairs={{0,64},{64,128},{128,192},{192,256},{256,320},{320,384},{384,448},... | collective-permute-start | bytes 49160 | tf_op jit(solution)/shard_map/ppermute | solution.py:302
  116.7 12.8 %collective-permute-start.7 = (f32[2,16,128]{2,1,0:T(8,128)S(1)}, f32[2,16,128]{2,1,0:T(8,128)S(1)}, u32[]{:S(2)}, u32[]{:S(2)}) collective-permute-start(f32[2,16,128]{2,1,0:T(8,128)S(1)} %get-tuple-element.45), channel_id=1, source_target_pairs={{64,0},{128,64},{192,128},{256,192},{320,256},{384,320},{448,384},... | collective-permute-start | bytes 49160 | tf_op jit(solution)/shard_map/ppermute | solution.py:302
  124.1 21.9 %all-to-all-start.4 = ((f32[16,1,128]{2,1,0:T(1,128)}), f32[16,1,128]{2,1,0:T(1,128)S(1)}, u32[]{:S(2)}, u32[]{:S(2)}) async-start(f32[16,1,128]{2,1,0:T(1,128)} %sum_terms.1), calls=%async_computation.4 | async-start | bytes 16384 | tf_op jit(solution)/shard_map/all_to_all | solution.py:306
  129.5 3.6 %collective-permute-start.8 = (f32[2,16,128]{2,1,0:T(8,128)S(1)}, f32[2,16,128]{2,1,0:T(8,128)S(1)}, u32[]{:S(2)}, u32[]{:S(2)}) collective-permute-start(f32[2,16,128]{2,1,0:T(8,128)S(1)} %get-tuple-element.47), channel_id=1, source_target_pairs={{0,8},{8,16},{16,24},{24,32},{32,40},{40,48},{48,56},{1,9},{9,17},... | collective-permute-start | bytes 49160 | tf_op jit(solution)/shard_map/ppermute | solution.py:302
  131.8 4.8 %collective-permute-start.9 = (f32[2,16,128]{2,1,0:T(8,128)S(1)}, f32[2,16,128]{2,1,0:T(8,128)S(1)}, u32[]{:S(2)}, u32[]{:S(2)}) collective-permute-start(f32[2,16,128]{2,1,0:T(8,128)S(1)} %get-tuple-element.48), channel_id=1, source_target_pairs={{8,0},{16,8},{24,16},{32,24},{40,32},{48,40},{56,48},{9,1},{17,9},... | collective-permute-start | bytes 49160 | tf_op jit(solution)/shard_map/ppermute | solution.py:302
  136.6 9.5 %copy-start.14 = (f32[16,16,128]{2,1,0:T(8,128)S(1)}, f32[16,16,128]{2,1,0:T(8,128)}, u32[]{:S(2)}) copy-start(f32[16,16,128]{2,1,0:T(8,128)} %solution.1) | copy-start | bytes 393220
  137.0 6.7 %collective-permute-start.10 = (f32[1,512]{1,0:T(1,128)S(1)}, f32[1,512]{1,0:T(1,128)S(1)}, u32[]{:S(2)}, u32[]{:S(2)}) collective-permute-start(f32[1,512]{1,0:T(1,128)S(1)} %get-tuple-element.50), channel_id=1, source_target_pairs={{0,1},{1,2},{2,3},{3,4},{4,5},{5,6},{6,7},{8,9},{9,10},{10,11},{11... | collective-permute-start | bytes 6152 | tf_op jit(solution)/shard_map/ppermute | solution.py:302
  141.1 4.9 %collective-permute-start.11 = (f32[1,512]{1,0:T(1,128)S(1)}, f32[1,512]{1,0:T(1,128)S(1)}, u32[]{:S(2)}, u32[]{:S(2)}) collective-permute-start(f32[1,512]{1,0:T(1,128)S(1)} %get-tuple-element.51), channel_id=1, source_target_pairs={{1,0},{2,1},{3,2},{4,3},{5,4},{6,5},{7,6},{9,8},{10,9},{11,10},{12... | collective-permute-start | bytes 6152 | tf_op jit(solution)/shard_map/ppermute | solution.py:302

commit v3 on v2

--- a/solution.py
+++ b/solution.py
@@ -67,7 +67,18 @@
     )(*args)
 
 
-def coarse_kernel(blocks, residual, ids, values, out, ids_wide):
+def coarse_kernel(
+    blocks, residual_hbm, ids_hbm, values_hbm, out, ids_wide, to_high, to_low, residual, ids, values, sems
+):
+    copies = [
+        pltpu.make_async_copy(source, target, sems.at[i])
+        for i, (source, target) in enumerate(
+            ((residual_hbm, residual), (ids_hbm, ids), (values_hbm, values))
+        )
+    ]
+    for copy in copies:
+        copy.start()
+    out[...] = jnp.zeros_like(out)
     nx, ny, nz = residual.shape
     ex, ey = nx // N, ny // N
     ez = ids.shape[1]
@@ -76,30 +87,34 @@
         lax.broadcasted_iota(jnp.int32, (ez, nz), 1) // N
         == lax.broadcasted_iota(jnp.int32, (ez, nz), 0)
     ).astype(F32)
+    copies[1].wait()
     wide = mm(ids[...].astype(F32), widen)
     ids_wide[...] = wide
     unknown = lax.broadcasted_iota(jnp.int32, (coarse, nz), 0).astype(F32)
     total = jnp.zeros((coarse, nz), F32)
+    copies[0].wait()
+    to_high[...] = residual[nx - 2]
+    to_low[...] = residual[1]
     for a in range(ex):
         for b in range(ey):
             part = jnp.sum(residual[a * N : a * N + N, b * N : b * N + N, :], axis=(0, 1))[None]
             q = a * ey + b
             total = total + jnp.where(jnp.abs(unknown - wide[q : q + 1]) < 0.5, part, 0.0)
     coarse_residual = jnp.sum(total, axis=1, keepdims=True)
-    out[...] = jnp.zeros_like(out)
+    copies[2].wait()
     for k in range(n_stored):
         row = jnp.sum(values[k] * coarse_residual, axis=0, keepdims=True)
         at = pl.ds(blocks[k], 1)
         out[at, :] = out[at, :] + row
 
 
-def sum_spread_kernel(parts, out):
+def sum_spread_kernel(parts, after, out):
     total = jnp.sum(parts[...], axis=0)
     for i in range(out.shape[0]):
         out[i] = total
 
 
-def across_faces_kernel(residual, low, high, to_high, to_low):
+def across_faces_kernel(residual, low, high, after, to_high, to_low):
     nx, ny, nz = residual.shape
     for out, y in ((to_high, ny - 2), (to_low, 1)):
         out[...] = jnp.zeros_like(out)
@@ -108,7 +123,9 @@
         out[nx + 1 : nx + 2] = high[y : y + 1]
 
 
-def depth_faces_kernel(residual, x_low, x_high, y_low, y_high, every, to_high, to_low):
+def depth_faces_kernel(
+    residual, x_low, x_high, y_low, y_high, after, every, to_high, to_low
+):
     nx, ny, nz = residual.shape
     at = 0
     for ref, count in ((None, nx * ny), (x_low, ny), (x_high, ny), (y_low, None), (y_high, None)):
@@ -156,21 +173,32 @@
     local_part[...] = mm(mm(from_spectral[...], weighted), from_z[...])
 
 
-def operator(flat, conductance, mass, kxy, kz):
-    rows = flat.shape[0]
-    along = mm(kxy[...], flat)
-    along_x = along[:rows] * conductance[0].reshape(rows, -1)
-    along_y = along[rows:] * conductance[1].reshape(rows, -1)
-    along_z = mm(flat, kz[...], 1, 1) * conductance[2].reshape(rows, -1)
-    total = mass[...].reshape(rows, -1) * flat + mm(along_z, kz[...])
-    total = total + mm(kxy[:rows, :], along_x, 0, 0)
-    return total + mm(kxy[rows:, :], along_y, 0, 0)
-
-
-def operator_kernel(direction, conductance, mass, kxy, kz, image):
-    rows = kxy.shape[1]
-    flat = direction[...].reshape(rows, -1)
-    image[...] = operator(flat, conductance, mass, kxy, kz).reshape(image.shape)
+def derive(matrix, slabs):
+    result = []
+    for first in range(0, len(slabs), N):
+        for i in range(N):
+            terms = [float(matrix[i, j]) * slabs[first + j] for j in range(N)]
+            while len(terms) > 1:
+                terms = [a + b for a, b in zip(terms[::2], terms[1::2])]
+            result.append(terms[0])
+    return result
+
+
+def operator(source, conductance, mass, ky, ky_t, kz, kz_t, target):
+    nx, ny, nz = source.shape
+    rows = nx * ny
+    cheb = cheb_matrix()
+    flat = source[...].reshape(rows, nz)
+    along_y = mm(ky[...], flat) * conductance[1].reshape(rows, nz)
+    along_z = mm(flat, kz_t[...]) * conductance[2].reshape(rows, nz)
+    along_x = [g * conductance[0, x] for x, g in enumerate(derive(cheb, [source[x] for x in range(nx)]))]
+    yz = mm(ky_t[...], along_y) + mm(along_z, kz[...])
+    for x, value in enumerate(derive(cheb.T, along_x)):
+        target[x] = mass[x] * source[x] + value + yz[x * ny : (x + 1) * ny]
+
+
+def operator_kernel(direction, conductance, mass, ky, ky_t, kz, kz_t, image):
+    operator(direction, conductance, mass, ky, ky_t, kz, kz_t, image)
 
 
 def total_of(values):
@@ -179,7 +207,7 @@
 
 def correct_kernel(
     blocks, coarse_inner, values, ids_wide, local_part, inner_local, direction, image_direction,
-    conductance, mass, kxy, kz,
+    conductance, mass, ky, ky_t, kz, kz_t,
     z_out, image_out, to_high, to_low, terms, square,
 ):
     nx, ny, nz = direction.shape
@@ -199,12 +227,12 @@
             for x in range(N):
                 at = (a * N + x) * ny + b * N
                 z_out[a * N + x, b * N : b * N + N, :] = local_part[at : at + N, :] + line
+    operator(z_out, conductance, mass, ky, ky_t, kz, kz_t, image_out)
     flat = z_out[...].reshape(rows, nz)
-    image = operator(flat, conductance, mass, kxy, kz)
-    image_out[...] = image.reshape(nx, ny, nz)
-    to_high[0] = image[rows - ny :]
+    image = image_out[...].reshape(rows, nz)
+    to_high[0] = image_out[nx - 1]
     to_high[1] = image_direction[nx - 1]
-    to_low[0] = image[:ny]
+    to_low[0] = image_out[0]
     to_low[1] = image_direction[0]
     old = direction[...].reshape(rows, nz)
     old_image = image_direction[...].reshape(rows, nz)
@@ -328,16 +356,40 @@
     n_blocks = coarse_count * n_plane * n_line // block
     own = n_blocks // n_plane
 
-    x_low, x_high = exchange(residual[nx - 2], residual[1], "gx")
-
     ids = element_coarse_index.reshape(ex * ey, ez)
-    partial_inner, ids_wide = call(
-        coarse_kernel, "coarse_restrict", [(n_blocks, block), (ex * ey, nz)],
-        xxt_blocks, residual, ids, xxt_values, smem=(0,),
-    )
+    vmem, hbm = pl.BlockSpec(memory_space=pltpu.VMEM), pl.BlockSpec(memory_space=pl.ANY)
+    partial_inner, ids_wide, to_high, to_low = pl.pallas_call(
+        coarse_kernel,
+        out_shape=[
+            jax.ShapeDtypeStruct(shape, F32)
+            for shape in ((n_blocks, block), (ex * ey, nz), (ny, nz), (ny, nz))
+        ],
+        in_specs=[pl.BlockSpec(memory_space=pltpu.SMEM), hbm, hbm, hbm],
+        out_specs=[vmem] * 4,
+        scratch_shapes=[
+            pltpu.VMEM(residual.shape, F32),
+            pltpu.VMEM(ids.shape, jnp.int32),
+            pltpu.VMEM(xxt_values.shape, F32),
+            pltpu.SemaphoreType.DMA((3,)),
+        ],
+        cost_estimate=pl.CostEstimate(flops=10**6, bytes_accessed=10**6, transcendentals=0),
+        compiler_params=pltpu.CompilerParams(vmem_limit_bytes=16 * 2**20),
+        name="coarse_restrict",
+    )(xxt_blocks, residual, ids, xxt_values)
     parts = spread(partial_inner.reshape(n_plane, own, block), plane)
+    x_low, x_high = exchange(to_high, to_low, "gx")
+    cheb = cheb_matrix()
+    ky = np.kron(np.eye(nx, dtype=np.float32), np.kron(np.eye(ey, dtype=np.float32), cheb))
+    kz = np.kron(np.eye(ez, dtype=np.float32), cheb)
+    tables = [jnp.asarray(np.ascontiguousarray(t)) for t in (ky, ky.T, kz, kz.T)]
+    (image_direction,) = call(
+        operator_kernel, "operator_direction", [direction.shape],
+        direction, conductance, mass_term, *tables,
+    )
+
     to_high, to_low = call(
-        across_faces_kernel, "across_faces", [(up8(nx + 2), nz)] * 2, residual, x_low, x_high
+        across_faces_kernel, "across_faces", [(up8(nx + 2), nz)] * 2, residual, x_low, x_high,
+        image_direction,
     )
     y_low, y_high = exchange(to_high, to_low, "gy")
 
@@ -380,23 +432,15 @@
         ),
     )
 
-    cheb = cheb_matrix()
-    kx = np.kron(np.kron(np.eye(ex, dtype=np.float32), cheb), np.eye(ny, dtype=np.float32))
-    ky = np.kron(np.eye(nx, dtype=np.float32), np.kron(np.eye(ey, dtype=np.float32), cheb))
-    kxy = jnp.asarray(np.concatenate([kx, ky]))
-    kz = jnp.asarray(np.kron(np.eye(ez, dtype=np.float32), cheb))
-    (image_direction,) = call(
-        operator_kernel, "operator_direction", [direction.shape],
-        direction, conductance, mass_term, kxy, kz,
-    )
-
+    (owned,) = call(sum_spread_kernel, "sum_plane", [(n_line, own, block)], parts, to_high)
+    parts = spread(owned, "gx")
     every, to_high, to_low = call(
         depth_faces_kernel, "depth_faces", [(n_every, nz), (1, n_every), (1, n_every)],
-        residual, x_low, x_high, y_low, y_high,
-    )
+        residual, x_low, x_high, y_low, y_high, from_z,
+    )
+    (owned,) = call(sum_spread_kernel, "sum_line", [(n_plane, own, block)], parts, to_high)
+    coarse_inner = spread(owned, plane).reshape(n_blocks, block)
     z_low, z_high = exchange(to_high, to_low, "gz")
-    (owned,) = call(sum_spread_kernel, "sum_plane", [(n_line, own, block)], parts)
-    parts = spread(owned, "gx")
     local_part, inner_local = pl.pallas_call(
         solve_kernel,
         out_shape=[jax.ShapeDtypeStruct((rows, nz), F32), jax.ShapeDtypeStruct((1, 1), F32)],
@@ -407,14 +451,11 @@
         compiler_params=pltpu.CompilerParams(vmem_limit_bytes=16 * 2**20),
         name="element_solve",
     )(every, z_low, z_high, to_spectral, from_spectral, to_z, from_z, inverse_eigen_sums)
-    (owned,) = call(sum_spread_kernel, "sum_line", [(n_plane, own, block)], parts)
-    coarse_inner = spread(owned, plane).reshape(n_blocks, block)
-
     z, image, to_high, to_low, terms, square = call(
         correct_kernel, "coarse_correct",
         [direction.shape, direction.shape, (2, ny, nz), (2, ny, nz), (n_plane, 1, nz), (1, 1)],
         xxt_blocks, coarse_inner, xxt_values, ids_wide, local_part, inner_local, direction,
-        image_direction, conductance, mass_term, kxy, kz, smem=(0,),
+        image_direction, conductance, mass_term, *tables, smem=(0,),
     )
     low, high = exchange(to_high, to_low, "gx")
     parts = spread(terms, plane)
@@ -422,9 +463,10 @@
         assemble_length_kernel, "assemble_length", [(2, nx, ny, nz), (2, nx, nz), (2, nx, nz)],
         image, image_direction, low, high,
     )
-    low, high = exchange(to_high, to_low, "gy")
-    (terms,) = call(sum_spread_kernel, "sum_terms", [(n_line, 1, nz)], parts)
+    across = to_high, to_low
+    (terms,) = call(sum_spread_kernel, "sum_terms", [(n_line, 1, nz)], parts, to_high)
     parts = spread(terms, "gx")
+    low, high = exchange(*across, "gy")
     images, to_high, to_low = call(
         assemble_across_kernel, "assemble_across", [(2, nx, ny, nz), (1, 2 * rows), (1, 2 * rows)],
         images, low, high,

time: 149 us -> 150 us (level); the launches traced: 148 us -> 147 us
  blocking collectives: 54.7 us -> 0 us
  starting transfers between devices: 52.6 us -> 93.5 us
  local copies, waits for them, and re-layouts: 3.32 us -> 18.9 us
  waiting for transfers between devices: 17.8 us -> 14.3 us
    all_to_all x2 -> x0, blocking collectives: 54.7 us -> none  [spread(): return lax.all_to_all(values, axes, 0, 0, tiled=False)]
    all_to_all x3 -> x5, starting transfers between devices: 22.4 us -> 62.7 us  [spread(): return lax.all_to_all(values, axes, 0, 0, tiled=False)]
    unnamed x52 -> x80, local copies, waits for them, and re-layouts: 3.31 us -> 18.9 us
    ppermute x6, waiting for transfers between devices: 12.3 us -> 5.8 us  [exchange(): lax.ppermute(to_low, axis, backward)]
    pallas_call x0 -> x1, Pallas kernels: none -> 1.75 us  [body(): pl.pallas_call(coarse_kernel, out_shape=[jax.ShapeDtypeStruct(shape, F32)...]
    all_to_all x3 -> x5, waiting for transfers between devices: 5.48 us -> 7.17 us  [spread(): return lax.all_to_all(values, axes, 0, 0, tiled=False)]
    pallas_call x12 -> x11, Pallas kernels: 13.2 us -> 12.8 us  [call(): pl.pallas_call(kernel, out_shape=[jax.ShapeDtypeStruct(s, F32) for s in o...]
  transfers between devices with their start and end apart: 15 -> 17, of which waited for: 5 -> 6; matrix products, arithmetic and copies ran while one was open for 0% -> 0% of each run, Pallas kernels for 7% -> 7%
where the time goes in v3:
time: 150 us; the launch traced here: 147 us
  starting transfers between devices  93.5 us (62%)
  local copies, waits for them, and re-layouts  18.9 us (13%)
  Pallas kernels  18.9 us (13%)
  waiting for transfers between devices  14.3 us (10%)
  between operations  1.72 us (1%)
    all_to_all x5, starting transfers between devices, spread(): return lax.all_to_all(values, axes, 0, 0, tiled=False)  62.7 us
    ppermute x6, starting transfers between devices, exchange(): lax.ppermute(to_high, axis, forward)  21.2 us
    unnamed x80, local copies, waits for them, and re-layouts  18.9 us
    pallas_call x11, Pallas kernels, call(): pl.pallas_call(kernel, out_shape=[jax.ShapeDtypeStruct(s, F32) for s in o...  12.8 us
    ppermute x6, starting transfers between devices, exchange(): lax.ppermute(to_low, axis, backward)  9.58 us
    all_to_all x5, waiting for transfers between devices, spread(): return lax.all_to_all(values, axes, 0, 0, tiled=False)  7.17 us
    ppermute x6, waiting for transfers between devices, exchange(): lax.ppermute(to_low, axis, backward)  5.8 us
    pallas_call x1, Pallas kernels, body(): pl.pallas_call(solve_kernel, out_shape=[jax.ShapeDtypeStruct((rows, nz),...  4.41 us
  transfers between devices with their start and end apart: 17, of which 6 were waited for; matrix products, arithmetic and copies ran while one was open for 0% of the time, Pallas kernels for 7%

profile of v3, /device:TPU:1, one launch (start us, length us, event | category | flops | bytes accessed | tf_op | source)
XLA Modules:
  0.0 147.4 jit_solution(15990577272999240659)
XLA Ops:
  1.3 0.9 copy-done
  2.2 0.9 copy-done.4
  3.8 1.7 %coarse_restrict.1 = (f32[512,128]{1,0:T(8,128)}, f32[4,128]{1,0:T(4,128)S(1)}, f32[16,128]{1,0:T(8,128)S(1)}, f32[16,128]{1,0:T(8,128)S(1)}) custom-call(s32[8]{0:T(128)S(1)} %copy-done.38, f32[16,16,128]{2,1,0:T(8,128)S(1)} %copy-done, s32[4,16]{1,0:T(4,128)S(1)} %bitcast.4, f32[8,64,128]{2,1,0:T(8,128)S(1)} %copy-done.4), custom_call_target="tpu_custom_call" | custom-call | flops 1000000 | bytes 1000000 | tf_op jit(solution)/shard_map/coarse_restrict/pallas_call | solution.py:361
  6.2 18.3 %all-to-all-start = ((f32[64,8,128]{2,1,0:T(8,128)}), f32[64,8,128]{2,1,0:T(8,128)S(1)}, u32[]{:S(2)}, u32[]{:S(2)}) async-start(f32[64,8,128]{2,1,0:T(8,128)} %bitcast.1), calls=%async_computation | async-start | bytes 524288 | tf_op jit(solution)/shard_map/all_to_all | solution.py:334
  24.5 1.3 collective-permute-start
  25.8 1.4 collective-permute-start.1
  27.3 0.9 copy-done.7
  28.2 0.8 copy-done.11
  29.1 0.8 copy-done.13
  29.9 0.9 operator_direction.1.after.image_direction
  31.5 6.2 %all-to-all-done.parts = f32[64,8,128]{2,1,0:T(8,128)S(1)} async-done(((f32[64,8,128]{2,1,0:T(8,128)}), f32[64,8,128]{2,1,0:T(8,128)S(1)}, u32[]{:S(2)}, u32[]{:S(2)}) %all-to-all-start) | async-done | bytes 262176 | tf_op jit(solution)/shard_map/all_to_all | solution.py:334
  37.8 0.7 sum_plane.1
  38.5 12.1 %all-to-all-start.1 = ((f32[16,8,128]{2,1,0:T(8,128)}), f32[16,8,128]{2,1,0:T(8,128)S(1)}, u32[]{:S(2)}, u32[]{:S(2)}) async-start(f32[16,8,128]{2,1,0:T(8,128)} %sum_plane.1), calls=%async_computation.1 | async-start | bytes 131072 | tf_op jit(solution)/shard_map/all_to_all | solution.py:334
  50.5 1.3 collective-permute-start.3
  51.8 4.0 %collective-permute-start.2 = (f32[24,128]{1,0:T(8,128)S(1)}, f32[24,128]{1,0:T(8,128)S(1)}, u32[]{:S(2)}, u32[]{:S(2)}) collective-permute-start(f32[24,128]{1,0:T(8,128)S(1)} %get-tuple-element.33.after), channel_id=1, source_target_pairs={{0,8},{8,16},{16,24},{24,32},{32,40},{40,48},{48,56},{1,9},{9,17},... | collective-permute-start | bytes 36872 | tf_op jit(solution)/shard_map/ppermute | solution.py:330
  55.9 0.9 copy-done.22
  56.8 0.9 copy-done.26
  57.7 0.9 copy-done.27
  58.6 0.9 copy-done.28
  59.5 0.9 copy-done.29
  60.4 0.8 copy-done.31
  61.1 0.7 copy-done.32
  61.8 0.7 copy-done.33
  62.5 3.6 %basis_matrices.1 = (f32[480,336]{1,0:T(8,128)S(1)}, f32[256,480]{1,0:T(8,128)S(1)}, f32[136,160]{1,0:T(8,128)S(1)}, f32[160,128]{1,0:T(8,128)S(1)}) custom-call(f32[10,10]{1,0:T(8,128)S(1)} %copy-done.34, f32[20,10]{1,0:T(8,128)S(1)} %copy-done.33, f32[20,20]{1,0:T(8,128)S(1)} %copy-done.32, f32[160,10]{1,0:T(8,128)S(1)} %copy-done.29, ...), custom_call_target="tpu_custom_call" | custom-call | bytes 1757680 | tf_op jit(solution)/shard_map/basis_matrices/pallas_call | solution.py:59
  66.5 0.7 copy-done.17
  67.2 0.7 sum_line.1
  67.9 9.4 %all-to-all-start.2 = ((f32[64,8,128]{2,1,0:T(8,128)}), f32[64,8,128]{2,1,0:T(8,128)S(1)}, u32[]{:S(2)}, u32[]{:S(2)}) async-start(f32[64,8,128]{2,1,0:T(8,128)} %sum_line.1), calls=%async_computation.2 | async-start | bytes 524288 | tf_op jit(solution)/shard_map/all_to_all | solution.py:334
  77.4 2.4 %collective-permute-start.5 = (f32[1,336]{1,0:T(1,128)S(1)}, f32[1,336]{1,0:T(1,128)S(1)}, u32[]{:S(2)}, u32[]{:S(2)}) collective-permute-start(f32[1,336]{1,0:T(1,128)S(1)} %get-tuple-element.39), channel_id=1, source_target_pairs={{1,0},{2,1},{3,2},{4,3},{5,4},{6,5},{7,6},{9,8},{10,9},{11,10},{12... | collective-permute-start | bytes 4040 | tf_op jit(solution)/shard_map/ppermute | solution.py:330
  79.7 3.4 %collective-permute-start.4 = (f32[1,336]{1,0:T(1,128)S(1)}, f32[1,336]{1,0:T(1,128)S(1)}, u32[]{:S(2)}, u32[]{:S(2)}) collective-permute-start(f32[1,336]{1,0:T(1,128)S(1)} %get-tuple-element.36.after), channel_id=1, source_target_pairs={{0,1},{1,2},{2,3},{3,4},{4,5},{5,6},{6,7},{8,9},{9,10},{10,11},{11... | collective-permute-start | bytes 4040 | tf_op jit(solution)/shard_map/ppermute | solution.py:330
  83.7 1.0 copy-done.10
  84.7 0.9 copy-done.18
  85.6 0.9 copy-done.21
  86.5 4.4 %element_solve.1 = (f32[256,128]{1,0:T(8,128)S(1)}, f32[1,1]{1,0:T(1,128)}) custom-call(f32[336,128]{1,0:T(8,128)S(1)} %copy-done.18, f32[1,336]{1,0:T(1,128)S(1)} %collective-permute-done.4.z_low, f32[1,336]{1,0:T(1,128)S(1)} %collective-permute-done.5.z_high, f32[480,336]{1,0:T(8,128)S(1)} %get-tuple-element.40.to_spectral, ...), custom_call_target="tpu_custom_call" | custom-call | flops 100000000 | bytes 3000000 | tf_op jit(solution)/shard_map/element_solve/pallas_call | solution.py:444
  92.3 0.9 copy-done.25
  93.2 3.0 %coarse_correct.1 = (f32[16,16,128]{2,1,0:T(8,128)S(1)}, f32[16,16,128]{2,1,0:T(8,128)S(1)}, f32[2,16,128]{2,1,0:T(8,128)S(1)}, f32[2,16,128]{2,1,0:T(8,128)S(1)...) custom-call(s32[8]{0:T(128)S(1)} %copy-done.39, f32[512,128]{1,0:T(8,128)S(1)} %bitcast.3, f32[8,64,128]{2,1,0:T(8,128)S(1)} %copy-done.5, ...), custom_call_target="tpu_custom_call" | custom-call | bytes 2426920 | tf_op jit(solution)/shard_map/coarse_correct/pallas_call | solution.py:59
  96.2 11.1 %all-to-all-start.3 = ((f32[64,1,128]{2,1,0:T(1,128)}), f32[64,1,128]{2,1,0:T(1,128)S(1)}, u32[]{:S(2)}, u32[]{:S(2)}) async-start(f32[64,1,128]{2,1,0:T(1,128)} %get-tuple-element.45), calls=%async_computation.3 | async-start | bytes 65536 | tf_op jit(solution)/shard_map/all_to_all | solution.py:334
  107.3 3.5 %collective-permute-start.6 = (f32[2,16,128]{2,1,0:T(8,128)S(1)}, f32[2,16,128]{2,1,0:T(8,128)S(1)}, u32[]{:S(2)}, u32[]{:S(2)}) collective-permute-start(f32[2,16,128]{2,1,0:T(8,128)S(1)} %get-tuple-element.47), channel_id=1, source_target_pairs={{0,64},{64,128},{128,192},{192,256},{256,320},{320,384},{384,448},... | collective-permute-start | bytes 49160 | tf_op jit(solution)/shard_map/ppermute | solution.py:330
  110.8 1.3 collective-permute-start.7
  112.2 3.5 %collective-permute-done.7.high = f32[2,16,128]{2,1,0:T(8,128)S(1)} collective-permute-done((f32[2,16,128]{2,1,0:T(8,128)S(1)}, f32[2,16,128]{2,1,0:T(8,128)S(1)}, u32[]{:S(2)}, u32[]{:S(2)}) %collective-permute-start.7) | collective-permute-done | bytes 16416 | tf_op jit(solution)/shard_map/ppermute | solution.py:330
  115.7 0.9 all-to-all-done.3.parts
  117.3 11.7 %all-to-all-start.4 = ((f32[16,1,128]{2,1,0:T(1,128)}), f32[16,1,128]{2,1,0:T(1,128)S(1)}, u32[]{:S(2)}, u32[]{:S(2)}) async-start(f32[16,1,128]{2,1,0:T(1,128)} %sum_terms.1), calls=%async_computation.4 | async-start | bytes 16384 | tf_op jit(solution)/shard_map/all_to_all | solution.py:334
  129.0 1.3 collective-permute-start.9
  130.3 4.0 %collective-permute-start.8 = (f32[2,16,128]{2,1,0:T(8,128)S(1)}, f32[2,16,128]{2,1,0:T(8,128)S(1)}, u32[]{:S(2)}, u32[]{:S(2)}) collective-permute-start(f32[2,16,128]{2,1,0:T(8,128)S(1)} %get-tuple-element.49.after), channel_id=1, source_target_pairs={{0,8},{8,16},{16,24},{24,32},{32,40},{40,48},{48,56},{1,9},{9,17},... | collective-permute-start | bytes 49160 | tf_op jit(solution)/shard_map/ppermute | solution.py:330
  134.3 0.8 collective-permute-done.8.low
  135.6 5.0 %collective-permute-start.10 = (f32[1,512]{1,0:T(1,128)S(1)}, f32[1,512]{1,0:T(1,128)S(1)}, u32[]{:S(2)}, u32[]{:S(2)}) collective-permute-start(f32[1,512]{1,0:T(1,128)S(1)} %get-tuple-element.54), channel_id=1, source_target_pairs={{0,1},{1,2},{2,3},{3,4},{4,5},{5,6},{6,7},{8,9},{9,10},{10,11},{11... | collective-permute-start | bytes 6152 | tf_op jit(solution)/shard_map/ppermute | solution.py:330
  140.6 1.9 %collective-permute-start.11 = (f32[1,512]{1,0:T(1,128)S(1)}, f32[1,512]{1,0:T(1,128)S(1)}, u32[]{:S(2)}, u32[]{:S(2)}) collective-permute-start(f32[1,512]{1,0:T(1,128)S(1)} %get-tuple-element.55), channel_id=1, source_target_pairs={{1,0},{2,1},{3,2},{4,3},{5,4},{6,5},{7,6},{9,8},{10,9},{11,10},{12... | collective-permute-start | bytes 6152 | tf_op jit(solution)/shard_map/ppermute | solution.py:330
  143.2 2.3 %collective-permute-done.11.high = f32[1,512]{1,0:T(1,128)S(1)} collective-permute-done((f32[1,512]{1,0:T(1,128)S(1)}, f32[1,512]{1,0:T(1,128)S(1)}, u32[]{:S(2)}, u32[]{:S(2)}) %collective-permute-start.11) | collective-permute-done | bytes 2080 | tf_op jit(solution)/shard_map/ppermute | solution.py:330
  145.5 1.8 %update.1 = (f32[16,16,128]{2,1,0:T(8,128)}, f32[16,16,128]{2,1,0:T(8,128)}, f32[16,16,128]{2,1,0:T(8,128)}) custom-call(f32[1]{0:T(128)S(6)} %copy.30.prior, f32[16,1,128]{2,1,0:T(1,128)S(1)} %all-to-all-done.4.terms, f32[1,1]{1,0:T(1,128)} %get-tuple-element.50.square, f32[2,16,16,128]{3,2,1,0:T(8,128)S(1)} %get-tuple-element.53.images, ...), custom_call_target="tpu_custom_call" | custom-call | bytes 1191944 | tf_op jit(solution)/shard_map/update/pallas_call | solution.py:59
  (79 shorter events, 5.8 us)
Async XLA Ops:
  1.3 0.9 copy-start
  2.2 0.9 copy-start.4
  3.8 23.4 %copy-start.2 = (f32[3,16,16,128]{3,2,1,0:T(8,128)S(1)}, f32[3,16,16,128]{3,2,1,0:T(8,128)}, u32[]{:S(2)}) copy-start(f32[3,16,16,128]{3,2,1,0:T(8,128)} %conductance.3) | copy-start | bytes 1179652
  6.2 21.1 %copy-start.3 = (f32[16,16,128]{2,1,0:T(8,128)S(1)}, f32[16,16,128]{2,1,0:T(8,128)}, u32[]{:S(2)}) copy-start(f32[16,16,128]{2,1,0:T(8,128)} %direction.5) | copy-start | bytes 393220
  6.2 21.1 %copy-start.6 = (f32[256,256]{1,0:T(8,128)S(1)}, f32[256,256]{1,0:T(8,128)}, u32[]{:S(2)}) copy-start(f32[256,256]{1,0:T(8,128)} %constant.33.clone.ky_t) | copy-start | bytes 786436
  6.2 21.1 %copy-start.9 = (f32[16,16,128]{2,1,0:T(8,128)S(1)}, f32[16,16,128]{2,1,0:T(8,128)}, u32[]{:S(2)}) copy-start(f32[16,16,128]{2,1,0:T(8,128)} %mass.3) | copy-start | bytes 393220
  6.2 31.6 %all-to-all-start = ((f32[64,8,128]{2,1,0:T(8,128)}), f32[64,8,128]{2,1,0:T(8,128)S(1)}, u32[]{:S(2)}, u32[]{:S(2)}) async-start(f32[64,8,128]{2,1,0:T(8,128)} %bitcast.1), calls=%async_computation | async-start | bytes 524288 | tf_op jit(solution)/shard_map/all_to_all | solution.py:334
  24.5 6.4 %collective-permute-start = (f32[16,128]{1,0:T(8,128)S(1)}, f32[16,128]{1,0:T(8,128)S(1)}, u32[]{:S(2)}, u32[]{:S(2)}) collective-permute-start(f32[16,128]{1,0:T(8,128)S(1)} %get-tuple-element.31), channel_id=1, source_target_pairs={{0,64},{64,128},{128,192},{192,256},{256,320},{320,384},{384,448},... | collective-permute-start | bytes 24584 | tf_op jit(solution)/shard_map/ppermute | solution.py:330
  25.8 5.1 %copy-start.1 = (f32[16,16,128]{2,1,0:T(8,128)S(1)}, f32[16,16,128]{2,1,0:T(8,128)}, u32[]{:S(2)}) copy-start(f32[16,16,128]{2,1,0:T(8,128)} %residual.5) | copy-start | bytes 393220
  25.8 5.1 %collective-permute-start.1 = (f32[16,128]{1,0:T(8,128)S(1)}, f32[16,128]{1,0:T(8,128)S(1)}, u32[]{:S(2)}, u32[]{:S(2)}) collective-permute-start(f32[16,128]{1,0:T(8,128)S(1)} %get-tuple-element.32), channel_id=1, source_target_pairs={{64,0},{128,64},{192,128},{256,192},{320,256},{384,320},{448,384},... | collective-permute-start | bytes 24584 | tf_op jit(solution)/shard_map/ppermute | solution.py:330
  27.3 1.0 copy-start.7
  28.2 0.8 copy-start.11
  29.1 0.8 copy-start.13
  30.9 24.9 %copy-start.16 = (f32[480,20]{1,0:T(8,128)S(1)}, f32[480,20]{1,0:T(8,128)}, u32[]{:S(2)}) copy-start(f32[480,20]{1,0:T(8,128)} %constant.40.clone.row_x) | copy-start | bytes 115204
  31.5 24.3 %copy-start.15 = (f32[480,20]{1,0:T(8,128)S(1)}, f32[480,20]{1,0:T(8,128)}, u32[]{:S(2)}) copy-start(f32[480,20]{1,0:T(8,128)} %constant.41.clone.row_y) | copy-start | bytes 115204
  37.8 18.1 %copy-start.19 = (f32[160,160]{1,0:T(8,128)S(1)}, f32[160,160]{1,0:T(8,128)}, u32[]{:S(2)}) copy-start(f32[160,160]{1,0:T(8,128)} %constant.39.clone.maskz) | copy-start | bytes 307204
  38.5 17.4 %copy-start.30 = (f32[20,336]{1,0:T(8,128)S(1)}, f32[20,336]{1,0:T(8,128)}, u32[]{:S(2)}) copy-start(f32[20,336]{1,0:T(8,128)} %constant.43.clone.col_y) | copy-start | bytes 80644
  38.5 17.4 %copy-start.34 = (f32[10,10]{1,0:T(8,128)S(1)}, f32[10,10]{1,0:T(8,128)}, u32[]{:S(2)}) copy-start(f32[10,10]{1,0:T(8,128)} %basis.1) | copy-start | bytes 1204
  38.5 28.7 %all-to-all-start.1 = ((f32[16,8,128]{2,1,0:T(8,128)}), f32[16,8,128]{2,1,0:T(8,128)S(1)}, u32[]{:S(2)}, u32[]{:S(2)}) async-start(f32[16,8,128]{2,1,0:T(8,128)} %sum_plane.1), calls=%async_computation.1 | async-start | bytes 131072 | tf_op jit(solution)/shard_map/all_to_all | solution.py:334
  50.5 15.7 %collective-permute-start.3 = (f32[24,128]{1,0:T(8,128)}, f32[24,128]{1,0:T(8,128)S(1)}, u32[]{:S(2)}, u32[]{:S(2)}) collective-permute-start(f32[24,128]{1,0:T(8,128)} %get-tuple-element.34), channel_id=1, source_target_pairs={{8,0},{16,8},{24,16},{32,24},{40,32},{48,40},{56,48},{9,1},{17,9},... | collective-permute-start | bytes 36872 | tf_op jit(solution)/shard_map/ppermute | solution.py:330
  51.8 14.4 %collective-permute-start.2 = (f32[24,128]{1,0:T(8,128)S(1)}, f32[24,128]{1,0:T(8,128)S(1)}, u32[]{:S(2)}, u32[]{:S(2)}) collective-permute-start(f32[24,128]{1,0:T(8,128)S(1)} %get-tuple-element.33.after), channel_id=1, source_target_pairs={{0,8},{8,16},{16,24},{24,32},{32,40},{40,48},{48,56},{1,9},{9,17},... | collective-permute-start | bytes 36872 | tf_op jit(solution)/shard_map/ppermute | solution.py:330
  55.9 0.9 copy-start.22
  56.8 0.9 copy-start.26
  57.7 0.9 copy-start.27
  58.6 0.9 copy-start.28
  59.5 0.9 copy-start.29
  60.4 0.8 copy-start.31
  66.2 1.7 %copy-start.20 = (f32[136,160]{1,0:T(8,128)}, f32[136,160]{1,0:T(8,128)S(1)}, u32[]{:S(2)}) copy-start(f32[136,160]{1,0:T(8,128)S(1)} %get-tuple-element.42.to_z) | copy-start | bytes 261124
  67.9 23.7 %all-to-all-start.2 = ((f32[64,8,128]{2,1,0:T(8,128)}), f32[64,8,128]{2,1,0:T(8,128)S(1)}, u32[]{:S(2)}, u32[]{:S(2)}) async-start(f32[64,8,128]{2,1,0:T(8,128)} %sum_line.1), calls=%async_computation.2 | async-start | bytes 524288 | tf_op jit(solution)/shard_map/all_to_all | solution.py:334
  77.4 5.8 %collective-permute-start.5 = (f32[1,336]{1,0:T(1,128)S(1)}, f32[1,336]{1,0:T(1,128)S(1)}, u32[]{:S(2)}, u32[]{:S(2)}) collective-permute-start(f32[1,336]{1,0:T(1,128)S(1)} %get-tuple-element.39), channel_id=1, source_target_pairs={{1,0},{2,1},{3,2},{4,3},{5,4},{6,5},{7,6},{9,8},{10,9},{11,10},{12... | collective-permute-start | bytes 4040 | tf_op jit(solution)/shard_map/ppermute | solution.py:330
  79.7 3.9 %collective-permute-start.4 = (f32[1,336]{1,0:T(1,128)S(1)}, f32[1,336]{1,0:T(1,128)S(1)}, u32[]{:S(2)}, u32[]{:S(2)}) collective-permute-start(f32[1,336]{1,0:T(1,128)S(1)} %get-tuple-element.36.after), channel_id=1, source_target_pairs={{0,1},{1,2},{2,3},{3,4},{4,5},{5,6},{6,7},{8,9},{9,10},{10,11},{11... | collective-permute-start | bytes 4040 | tf_op jit(solution)/shard_map/ppermute | solution.py:330
  83.7 1.0 copy-start.10
  84.7 0.9 copy-start.18
  85.6 0.9 copy-start.21
  86.5 5.1 %copy-start.5 = (f32[8,64,128]{2,1,0:T(8,128)S(1)}, f32[8,64,128]{2,1,0:T(8,128)}, u32[]{:S(2)}) copy-start(f32[8,64,128]{2,1,0:T(8,128)} %values.1) | copy-start | bytes 786436
  86.5 5.1 %copy-start.8 = (f32[256,256]{1,0:T(8,128)S(1)}, f32[256,256]{1,0:T(8,128)}, u32[]{:S(2)}) copy-start(f32[256,256]{1,0:T(8,128)} %constant.32.clone.ky) | copy-start | bytes 786436
  86.5 5.1 %copy-start.12 = (f32[128,128]{1,0:T(8,128)S(1)}, f32[128,128]{1,0:T(8,128)}, u32[]{:S(2)}) copy-start(f32[128,128]{1,0:T(8,128)} %constant.35.clone.kz_t) | copy-start | bytes 196612
  86.5 5.1 %copy-start.14 = (f32[128,128]{1,0:T(8,128)S(1)}, f32[128,128]{1,0:T(8,128)}, u32[]{:S(2)}) copy-start(f32[128,128]{1,0:T(8,128)} %constant.34.clone.kz) | copy-start | bytes 196612
  92.3 0.9 copy-start.25
  96.2 20.5 %all-to-all-start.3 = ((f32[64,1,128]{2,1,0:T(1,128)}), f32[64,1,128]{2,1,0:T(1,128)S(1)}, u32[]{:S(2)}, u32[]{:S(2)}) async-start(f32[64,1,128]{2,1,0:T(1,128)} %get-tuple-element.45), calls=%async_computation.3 | async-start | bytes 65536 | tf_op jit(solution)/shard_map/all_to_all | solution.py:334
  107.3 4.8 %collective-permute-start.6 = (f32[2,16,128]{2,1,0:T(8,128)S(1)}, f32[2,16,128]{2,1,0:T(8,128)S(1)}, u32[]{:S(2)}, u32[]{:S(2)}) collective-permute-start(f32[2,16,128]{2,1,0:T(8,128)S(1)} %get-tuple-element.47), channel_id=1, source_target_pairs={{0,64},{64,128},{128,192},{192,256},{256,320},{320,384},{384,448},... | collective-permute-start | bytes 49160 | tf_op jit(solution)/shard_map/ppermute | solution.py:330
  110.8 4.8 %collective-permute-start.7 = (f32[2,16,128]{2,1,0:T(8,128)S(1)}, f32[2,16,128]{2,1,0:T(8,128)S(1)}, u32[]{:S(2)}, u32[]{:S(2)}) collective-permute-start(f32[2,16,128]{2,1,0:T(8,128)S(1)} %get-tuple-element.48), channel_id=1, source_target_pairs={{64,0},{128,64},{192,128},{256,192},{320,256},{384,320},{448,384},... | collective-permute-start | bytes 49160 | tf_op jit(solution)/shard_map/ppermute | solution.py:330
  117.3 28.2 %all-to-all-start.4 = ((f32[16,1,128]{2,1,0:T(1,128)}), f32[16,1,128]{2,1,0:T(1,128)S(1)}, u32[]{:S(2)}, u32[]{:S(2)}) async-start(f32[16,1,128]{2,1,0:T(1,128)} %sum_terms.1), calls=%async_computation.4 | async-start | bytes 16384 | tf_op jit(solution)/shard_map/all_to_all | solution.py:334
  129.0 5.3 %collective-permute-start.9 = (f32[2,16,128]{2,1,0:T(8,128)S(1)}, f32[2,16,128]{2,1,0:T(8,128)S(1)}, u32[]{:S(2)}, u32[]{:S(2)}) collective-permute-start(f32[2,16,128]{2,1,0:T(8,128)S(1)} %get-tuple-element.52), channel_id=1, source_target_pairs={{8,0},{16,8},{24,16},{32,24},{40,32},{48,40},{56,48},{9,1},{17,9},... | collective-permute-start | bytes 49160 | tf_op jit(solution)/shard_map/ppermute | solution.py:330
  130.3 4.8 %collective-permute-start.8 = (f32[2,16,128]{2,1,0:T(8,128)S(1)}, f32[2,16,128]{2,1,0:T(8,128)S(1)}, u32[]{:S(2)}, u32[]{:S(2)}) collective-permute-start(f32[2,16,128]{2,1,0:T(8,128)S(1)} %get-tuple-element.49.after), channel_id=1, source_target_pairs={{0,8},{8,16},{16,24},{24,32},{32,40},{40,48},{48,56},{1,9},{9,17},... | collective-permute-start | bytes 49160 | tf_op jit(solution)/shard_map/ppermute | solution.py:330
  135.2 10.3 %copy-start.23 = (f32[16,16,128]{2,1,0:T(8,128)S(1)}, f32[16,16,128]{2,1,0:T(8,128)}, u32[]{:S(2)}) copy-start(f32[16,16,128]{2,1,0:T(8,128)} %solution.1) | copy-start | bytes 393220
  135.6 7.6 %collective-permute-start.10 = (f32[1,512]{1,0:T(1,128)S(1)}, f32[1,512]{1,0:T(1,128)S(1)}, u32[]{:S(2)}, u32[]{:S(2)}) collective-permute-start(f32[1,512]{1,0:T(1,128)S(1)} %get-tuple-element.54), channel_id=1, source_target_pairs={{0,1},{1,2},{2,3},{3,4},{4,5},{5,6},{6,7},{8,9},{9,10},{10,11},{11... | collective-permute-start | bytes 6152 | tf_op jit(solution)/shard_map/ppermute | solution.py:330
  140.6 4.9 %collective-permute-start.11 = (f32[1,512]{1,0:T(1,128)S(1)}, f32[1,512]{1,0:T(1,128)S(1)}, u32[]{:S(2)}, u32[]{:S(2)}) collective-permute-start(f32[1,512]{1,0:T(1,128)S(1)} %get-tuple-element.55), channel_id=1, source_target_pairs={{1,0},{2,1},{3,2},{4,3},{5,4},{6,5},{7,6},{9,8},{10,9},{11,10},{12... | collective-permute-start | bytes 6152 | tf_op jit(solution)/shard_map/ppermute | solution.py:330
  (9 other events, 6.1 us)

commit v4 on v3

--- a/solution.py
+++ b/solution.py
@@ -49,86 +49,141 @@
     )
 
 
-def call(kernel, name, outs, *args, smem=(), flops=0):
-    specs = [
-        pl.BlockSpec(memory_space=pltpu.SMEM if i in smem else pltpu.VMEM)
-        for i in range(len(args))
+def call(kernel, name, outs, *args, smem=(), load=(), keep=(), scratch=(), pin=()):
+    count, n_out, n_keep = len(args), len(outs), len(keep)
+    moved = sorted((*load, *keep))
+    vmem = pl.BlockSpec(memory_space=pltpu.VMEM)
+
+    def whole(*refs):
+        inside, results = list(refs[:count]), refs[count : count + n_out]
+        kept = refs[count + n_out : count + n_out + n_keep]
+        rest = list(refs[count + n_out + n_keep :])
+        sems = rest.pop() if moved else None
+        copies = {}
+        for at, i in enumerate(moved):
+            target = kept[keep.index(i)] if i in keep else rest.pop()
+            copies[i] = pltpu.make_async_copy(inside[i], target, sems.at[at])
+            copies[i].start()
+            inside[i] = target
+        waiting = dict(copies)
+
+        def ready(*which):
+            for i in which:
+                if i in waiting:
+                    waiting.pop(i).wait()
+
+        kernel(ready, *inside, *results, *rest)
+        ready(*moved)
+
+    buffers = [pltpu.VMEM(args[i].shape, args[i].dtype) for i in moved if i not in keep]
+    specs = []
+    for i in range(count):
+        space = pltpu.SMEM if i in smem else pltpu.HBM if i in moved else pltpu.VMEM
+        specs.append(pl.BlockSpec(memory_space=space))
+    args = [
+        pltpu.with_memory_space_constraint(a, pltpu.HBM) if i in moved else a
+        for i, a in enumerate(args)
     ]
-    moved = sum(int(np.prod(a.shape)) * 4 for a in args)
-    moved += sum(int(np.prod(s)) * 4 for s in outs)
+    size = sum(int(np.prod(a.shape)) * 4 for a in args) + sum(int(np.prod(o)) * 4 for o in outs)
     return pl.pallas_call(
-        kernel,
-        out_shape=[jax.ShapeDtypeStruct(s, F32) for s in outs],
+        whole,
+        out_shape=[
+            pltpu.VMEM(o, F32) if i in pin else jax.ShapeDtypeStruct(o, F32)
+            for i, o in enumerate(outs)
+        ]
+        + [pltpu.VMEM(args[i].shape, args[i].dtype) for i in keep],
         in_specs=specs,
-        out_specs=[pl.BlockSpec(memory_space=pltpu.VMEM)] * len(outs),
-        cost_estimate=pl.CostEstimate(flops=flops, bytes_accessed=moved, transcendentals=0),
-        compiler_params=pltpu.CompilerParams(vmem_limit_bytes=16 * 2**20),
+        out_specs=[vmem] * (n_out + n_keep),
+        scratch_shapes=[
+            *scratch,
+            *buffers[::-1],
+            *([pltpu.SemaphoreType.DMA((len(moved),))] if moved else []),
+        ],
+        cost_estimate=pl.CostEstimate(flops=0, bytes_accessed=size, transcendentals=0),
+        compiler_params=pltpu.CompilerParams(vmem_limit_bytes=24 * 2**20),
         name=name,
     )(*args)
 
 
-def coarse_kernel(
-    blocks, residual_hbm, ids_hbm, values_hbm, out, ids_wide, to_high, to_low, residual, ids, values, sems
-):
-    copies = [
-        pltpu.make_async_copy(source, target, sems.at[i])
-        for i, (source, target) in enumerate(
-            ((residual_hbm, residual), (ids_hbm, ids), (values_hbm, values))
-        )
-    ]
-    for copy in copies:
-        copy.start()
-    out[...] = jnp.zeros_like(out)
+def coarse_kernel(ready, blocks, me, residual, ids, values, payload, ids_wide):
     nx, ny, nz = residual.shape
     ex, ey = nx // N, ny // N
     ez = ids.shape[1]
     n_stored, coarse, _ = values.shape
+    n_line, head = payload.shape[0], payload.shape[1] - ny
     widen = (
         lax.broadcasted_iota(jnp.int32, (ez, nz), 1) // N
         == lax.broadcasted_iota(jnp.int32, (ez, nz), 0)
     ).astype(F32)
-    copies[1].wait()
+    payload[...] = jnp.zeros_like(payload)
+    at = me[0]
+    lane = lax.broadcasted_iota(jnp.int32, (1, nz), 1)
+    numbers = jnp.zeros((1, nz), F32)
+    for k in range(n_stored):
+        numbers = jnp.where(lane == n_stored * at + k, blocks[k].astype(F32), numbers)
+    ready(3)
     wide = mm(ids[...].astype(F32), widen)
     ids_wide[...] = wide
     unknown = lax.broadcasted_iota(jnp.int32, (coarse, nz), 0).astype(F32)
     total = jnp.zeros((coarse, nz), F32)
-    copies[0].wait()
-    to_high[...] = residual[nx - 2]
-    to_low[...] = residual[1]
+    ready(2)
+
+    @pl.when(at + 1 < n_line)
+    def _():
+        payload[at + 1, head:, :] = residual[nx - 2]
+
+    @pl.when(at > 0)
+    def _():
+        payload[at - 1, head:, :] = residual[1]
+
     for a in range(ex):
         for b in range(ey):
             part = jnp.sum(residual[a * N : a * N + N, b * N : b * N + N, :], axis=(0, 1))[None]
             q = a * ey + b
             total = total + jnp.where(jnp.abs(unknown - wide[q : q + 1]) < 0.5, part, 0.0)
     coarse_residual = jnp.sum(total, axis=1, keepdims=True)
-    copies[2].wait()
+    ready(4)
+    row = lax.broadcasted_iota(jnp.int32, (head, nz), 0)
+    lines = jnp.where(row == n_stored, numbers, 0.0)
     for k in range(n_stored):
-        row = jnp.sum(values[k] * coarse_residual, axis=0, keepdims=True)
-        at = pl.ds(blocks[k], 1)
-        out[at, :] = out[at, :] + row
-
-
-def sum_spread_kernel(parts, after, out):
-    total = jnp.sum(parts[...], axis=0)
-    for i in range(out.shape[0]):
-        out[i] = total
-
-
-def across_faces_kernel(residual, low, high, after, to_high, to_low):
+        lines = jnp.where(
+            row == k, jnp.sum(values[k] * coarse_residual, axis=0, keepdims=True), lines
+        )
+    for i in range(n_line):
+        payload[i, :head, :] = lines
+
+
+def line_kernel(ready, me, parts, residual, after1, after2, dense, x_low, x_high, to_high, to_low):
     nx, ny, nz = residual.shape
+    n_line = parts.shape[0]
+    head, n_stored = parts.shape[1] - ny, 8
+    at = me[0]
+    rows = parts[:, :n_stored, :].reshape(n_line * n_stored, nz)
+    rows = jnp.concatenate([rows] + [jnp.zeros((nz - n_line * n_stored, nz), F32)]) if n_line * n_stored < nz else rows
+    numbers = jnp.sum(parts[:, n_stored : n_stored + 1, :], axis=0)
+    n_blocks = dense.shape[0] * dense.shape[1]
+    block = lax.broadcasted_iota(jnp.int32, (n_blocks, nz), 0).astype(F32)
+    place = (jnp.abs(block - numbers) < 0.5).astype(F32)
+    dense[...] = mm(place, rows).reshape(dense.shape)
+    before, behind = jnp.maximum(at - 1, 0), jnp.minimum(at + 1, n_line - 1)
+    x_low[...] = jnp.where(at > 0, parts[before, head:, :], 0.0)
+    x_high[...] = jnp.where(at + 1 < n_line, parts[behind, head:, :], 0.0)
     for out, y in ((to_high, ny - 2), (to_low, 1)):
         out[...] = jnp.zeros_like(out)
         out[:nx] = residual[:, y, :]
-        out[nx : nx + 1] = low[y : y + 1]
-        out[nx + 1 : nx + 2] = high[y : y + 1]
-
-
-def depth_faces_kernel(
-    residual, x_low, x_high, y_low, y_high, after, every, to_high, to_low
-):
+        out[nx : nx + 1] = x_low[y : y + 1]
+        out[nx + 1 : nx + 2] = x_high[y : y + 1]
+
+
+def plane_kernel(
+    ready, parts, residual, x_low, x_high, y_low, y_high, owned, every, to_high, to_low
+):
+    total = jnp.sum(parts[...], axis=0)
+    for i in range(owned.shape[0]):
+        owned[i] = total
     nx, ny, nz = residual.shape
     at = 0
-    for ref, count in ((None, nx * ny), (x_low, ny), (x_high, ny), (y_low, None), (y_high, None)):
+    for ref in (None, x_low, x_high, y_low, y_high):
         block = residual[...].reshape(nx * ny, nz) if ref is None else ref[...]
         every[at : at + block.shape[0]] = block
         at += block.shape[0]
@@ -141,9 +196,10 @@
 
 
 def matrices_kernel(
-    basis, tile2, mask2, tilez, maskz, row_x, row_y, col_x, col_y, out_x, out_y, col_z, in_z,
+    ready, basis, tile2, mask2, tilez, maskz, row_x, row_y, col_x, col_y, out_x, out_y, col_z, in_z,
     to_spectral, from_spectral, to_z, from_z,
 ):
+    ready(*range(13))
     flat2 = mm(mm(tile2[...], basis[...]), tile2[...], 1, 1) * mask2[...]
     flatz = mm(mm(tilez[...], basis[...]), tilez[...], 1, 1) * maskz[...]
     to_x = mm(row_x[...], mm(flat2, col_x[...], 0, 0))
@@ -157,18 +213,19 @@
 
 
 def solve_kernel(
-    every, z_low, z_high, to_spectral, from_spectral, to_z, from_z, sums, local_part, inner, wide
+    ready, every, z_low, z_high, to_spectral, from_spectral, to_z, from_z, sums, local_part, inner, wide
 ):
     nz = every.shape[1]
     n_x, n_y, n_z = sums.shape
     wide[...] = jnp.zeros_like(wide)
-    wide[:, :n_y, :] = sums[...]
-    weights = wide[...].reshape(-1, n_z)
     row = lax.broadcasted_iota(jnp.int32, (8, every.shape[0]), 0)
     ends = jnp.where(row == 0, z_low[...], jnp.where(row == 1, z_high[...], 0.0))
+    ready(3, 4, 5, 6)
     spectral = mm(mm(to_spectral[...], every[...]), to_z[:nz, :])
     spectral = spectral + mm(mm(to_spectral[...], ends, 1, 1), to_z[nz:, :])
-    weighted = weights * spectral
+    ready(7)
+    wide[:, :n_y, :] = sums[...]
+    weighted = wide[...].reshape(-1, n_z) * spectral
     inner[...] = jnp.sum(jnp.sum(weighted * spectral, axis=0, keepdims=True), axis=1, keepdims=True)
     local_part[...] = mm(mm(from_spectral[...], weighted), from_z[...])
 
@@ -197,7 +254,8 @@
         target[x] = mass[x] * source[x] + value + yz[x * ny : (x + 1) * ny]
 
 
-def operator_kernel(direction, conductance, mass, ky, ky_t, kz, kz_t, image):
+def operator_kernel(ready, direction, conductance, mass, ky, ky_t, kz, kz_t, image):
+    ready(0, 1, 2, 3, 4, 5, 6)
     operator(direction, conductance, mass, ky, ky_t, kz, kz_t, image)
 
 
@@ -206,7 +264,7 @@
 
 
 def correct_kernel(
-    blocks, coarse_inner, values, ids_wide, local_part, inner_local, direction, image_direction,
+    ready, blocks, coarse_inner, values, ids_wide, local_part, inner_local, direction, image_direction,
     conductance, mass, ky, ky_t, kz, kz_t,
     z_out, image_out, to_high, to_low, terms, square,
 ):
@@ -227,6 +285,7 @@
             for x in range(N):
                 at = (a * N + x) * ny + b * N
                 z_out[a * N + x, b * N : b * N + N, :] = local_part[at : at + N, :] + line
+    ready(10, 11)
     operator(z_out, conductance, mass, ky, ky_t, kz, kz_t, image_out)
     flat = z_out[...].reshape(rows, nz)
     image = image_out[...].reshape(rows, nz)
@@ -250,8 +309,13 @@
     square[...] = total_of(coarse_inner[...] * coarse_inner[...])
 
 
-def assemble_length_kernel(image, image_direction, low, high, out, to_high, to_low):
+def assemble_length_kernel(
+    ready, image, image_direction, low, high, parts, out, to_high, to_low, terms
+):
     nx, ny, nz = image.shape
+    total = jnp.sum(parts[...], axis=0)
+    for i in range(terms.shape[0]):
+        terms[i] = total
     for i, ref in ((0, image), (1, image_direction)):
         out[i] = ref[...]
         for x in range(nx):
@@ -263,7 +327,7 @@
         to_low[i] = out[i, :, 0, :]
 
 
-def assemble_across_kernel(images, low, high, out, to_high, to_low):
+def assemble_across_kernel(ready, images, low, high, solution, out, to_high, to_low):
     _, nx, ny, nz = images.shape
     out[...] = images[...]
     for i in range(2):
@@ -284,7 +348,7 @@
 
 
 def update_kernel(
-    prior, terms, square, images, low, high, residual, solution, direction, z,
+    ready, prior, terms, square, images, low, high, residual, solution, direction, z,
     new_solution, new_residual, new_direction,
 ):
     nx, ny, nz = residual.shape
@@ -357,41 +421,23 @@
     own = n_blocks // n_plane
 
     ids = element_coarse_index.reshape(ex * ey, ez)
-    vmem, hbm = pl.BlockSpec(memory_space=pltpu.VMEM), pl.BlockSpec(memory_space=pl.ANY)
-    partial_inner, ids_wide, to_high, to_low = pl.pallas_call(
-        coarse_kernel,
-        out_shape=[
-            jax.ShapeDtypeStruct(shape, F32)
-            for shape in ((n_blocks, block), (ex * ey, nz), (ny, nz), (ny, nz))
-        ],
-        in_specs=[pl.BlockSpec(memory_space=pltpu.SMEM), hbm, hbm, hbm],
-        out_specs=[vmem] * 4,
-        scratch_shapes=[
-            pltpu.VMEM(residual.shape, F32),
-            pltpu.VMEM(ids.shape, jnp.int32),
-            pltpu.VMEM(xxt_values.shape, F32),
-            pltpu.SemaphoreType.DMA((3,)),
-        ],
-        cost_estimate=pl.CostEstimate(flops=10**6, bytes_accessed=10**6, transcendentals=0),
-        compiler_params=pltpu.CompilerParams(vmem_limit_bytes=16 * 2**20),
-        name="coarse_restrict",
-    )(xxt_blocks, residual, ids, xxt_values)
-    parts = spread(partial_inner.reshape(n_plane, own, block), plane)
-    x_low, x_high = exchange(to_high, to_low, "gx")
+    me = lax.axis_index("gx").astype(jnp.int32).reshape(1)
+    head = up8(xxt_values.shape[0] + 1)
+    assert xxt_values.shape[0] * n_line <= nz
+    payload, ids_wide, residual, xxt_values = call(
+        coarse_kernel, "coarse_restrict", [(n_line, head + ny, nz), (ex * ey, nz)],
+        xxt_blocks, me, residual, ids, xxt_values, smem=(0, 1), load=(3,), keep=(2, 4), pin=(1,),
+    )
+    parts = spread(payload, "gx")
+
     cheb = cheb_matrix()
     ky = np.kron(np.eye(nx, dtype=np.float32), np.kron(np.eye(ey, dtype=np.float32), cheb))
     kz = np.kron(np.eye(ez, dtype=np.float32), cheb)
     tables = [jnp.asarray(np.ascontiguousarray(t)) for t in (ky, ky.T, kz, kz.T)]
-    (image_direction,) = call(
+    image_direction, direction, conductance, mass_term, kz, kz_t = call(
         operator_kernel, "operator_direction", [direction.shape],
-        direction, conductance, mass_term, *tables,
-    )
-
-    to_high, to_low = call(
-        across_faces_kernel, "across_faces", [(up8(nx + 2), nz)] * 2, residual, x_low, x_high,
-        image_direction,
-    )
-    y_low, y_high = exchange(to_high, to_low, "gy")
+        direction, conductance, mass_term, *tables, load=(3, 4), keep=(0, 1, 2, 5, 6), pin=(0,),
+    )
 
     face = up8(nx + 2)
     n_every = rows + 2 * ny + 2 * face
@@ -430,46 +476,47 @@
                 np.ascontiguousarray(one_hot(inside_positions(ez), n_z).T),
             ),
         ),
-    )
-
-    (owned,) = call(sum_spread_kernel, "sum_plane", [(n_line, own, block)], parts, to_high)
-    parts = spread(owned, "gx")
-    every, to_high, to_low = call(
-        depth_faces_kernel, "depth_faces", [(n_every, nz), (1, n_every), (1, n_every)],
-        residual, x_low, x_high, y_low, y_high, from_z,
-    )
-    (owned,) = call(sum_spread_kernel, "sum_line", [(n_plane, own, block)], parts, to_high)
+        load=tuple(range(13)),
+    )
+
+    dense, x_low, x_high, to_high, to_low = call(
+        line_kernel, "line_sum",
+        [(n_plane, own, block), (ny, nz), (ny, nz), (face, nz), (face, nz)],
+        me, parts, residual, image_direction, from_z, smem=(0,), pin=(1, 2),
+    )
+    parts = spread(dense, plane)
+    y_low, y_high = exchange(to_high, to_low, "gy")
+    owned, every, to_high, to_low = call(
+        plane_kernel, "plane_sum",
+        [(n_plane, own, block), (n_every, nz), (1, n_every), (1, n_every)],
+        parts, residual, x_low, x_high, y_low, y_high, pin=(1,),
+    )
     coarse_inner = spread(owned, plane).reshape(n_blocks, block)
     z_low, z_high = exchange(to_high, to_low, "gz")
-    local_part, inner_local = pl.pallas_call(
-        solve_kernel,
-        out_shape=[jax.ShapeDtypeStruct((rows, nz), F32), jax.ShapeDtypeStruct((1, 1), F32)],
-        in_specs=[pl.BlockSpec(memory_space=pltpu.VMEM)] * 8,
-        out_specs=[pl.BlockSpec(memory_space=pltpu.VMEM)] * 2,
-        scratch_shapes=[pltpu.VMEM((n_x, high_y, n_z), F32)],
-        cost_estimate=pl.CostEstimate(flops=10**8, bytes_accessed=3 * 10**6, transcendentals=0),
-        compiler_params=pltpu.CompilerParams(vmem_limit_bytes=16 * 2**20),
-        name="element_solve",
-    )(every, z_low, z_high, to_spectral, from_spectral, to_z, from_z, inverse_eigen_sums)
+    local_part, inner_local = call(
+        solve_kernel, "element_solve", [(rows, nz), (1, 1)],
+        every, z_low, z_high, to_spectral, from_spectral, to_z, from_z, inverse_eigen_sums,
+        load=(3, 4, 5, 6, 7), pin=(0, 1), scratch=(pltpu.VMEM((n_x, high_y, n_z), F32),),
+    )
+
     z, image, to_high, to_low, terms, square = call(
         correct_kernel, "coarse_correct",
         [direction.shape, direction.shape, (2, ny, nz), (2, ny, nz), (n_plane, 1, nz), (1, 1)],
         xxt_blocks, coarse_inner, xxt_values, ids_wide, local_part, inner_local, direction,
-        image_direction, conductance, mass_term, *tables, smem=(0,),
+        image_direction, conductance, mass_term, *tables[:2], kz, kz_t, smem=(0,), load=(10, 11), pin=(0, 1, 5),
     )
     low, high = exchange(to_high, to_low, "gx")
     parts = spread(terms, plane)
-    images, to_high, to_low = call(
-        assemble_length_kernel, "assemble_length", [(2, nx, ny, nz), (2, nx, nz), (2, nx, nz)],
-        image, image_direction, low, high,
-    )
-    across = to_high, to_low
-    (terms,) = call(sum_spread_kernel, "sum_terms", [(n_line, 1, nz)], parts, to_high)
+    images, to_high, to_low, terms = call(
+        assemble_length_kernel, "assemble_length",
+        [(2, nx, ny, nz), (2, nx, nz), (2, nx, nz), (n_line, 1, nz)],
+        image, image_direction, low, high, parts, pin=(0,),
+    )
     parts = spread(terms, "gx")
-    low, high = exchange(*across, "gy")
-    images, to_high, to_low = call(
+    low, high = exchange(to_high, to_low, "gy")
+    images, to_high, to_low, solution = call(
         assemble_across_kernel, "assemble_across", [(2, nx, ny, nz), (1, 2 * rows), (1, 2 * rows)],
-        images, low, high,
+        images, low, high, solution, keep=(3,), pin=(0,),
     )
     low, high = exchange(to_high, to_low, "gz")
     return tuple(

time: 150 us -> 142 us (0.947)
  local copies, waits for them, and re-layouts: 18.9 us -> 3.03 us
  waiting for transfers between devices: 14.3 us -> 25.6 us
  starting transfers between devices: 93.5 us -> 84.3 us
  Pallas kernels: 18.9 us -> 25.7 us
    unnamed x80 -> x10, local copies, waits for them, and re-layouts: 18.9 us -> 3.03 us
    ppermute x6 -> x5, waiting for transfers between devices: 5.8 us -> 15.9 us  [exchange(): lax.ppermute(to_low, axis, backward)]
    pallas_call x13 -> x10, Pallas kernels: 18.9 us -> 25.7 us  [call(): pl.pallas_call(whole, out_shape=[pltpu.VMEM(o, F32) if i in pin else jax....]
    all_to_all x5, starting transfers between devices: 62.7 us -> 57 us  [spread(): return lax.all_to_all(values, axes, 0, 0, tiled=False)]
    all_to_all x5, waiting for transfers between devices: 7.17 us -> 9.61 us  [spread(): return lax.all_to_all(values, axes, 0, 0, tiled=False)]
    ppermute x6 -> x5, starting transfers between devices: 21.2 us -> 19.4 us  [exchange(): lax.ppermute(to_high, axis, forward)]
    ppermute x6 -> x5, starting transfers between devices: 9.58 us -> 7.9 us  [exchange(): lax.ppermute(to_low, axis, backward)]
  transfers between devices with their start and end apart: 17 -> 15, of which waited for: 6 -> 8; matrix products, arithmetic and copies ran while one was open for 0% -> 0% of each run, Pallas kernels for 7% -> 11%
where the time goes in v4:
time: 142 us; the launch traced here: 140 us
  starting transfers between devices  84.3 us (59%)
  Pallas kernels  25.7 us (18%)
  waiting for transfers between devices  25.6 us (18%)
  local copies, waits for them, and re-layouts  3.03 us (2%)
  between operations  1.52 us (1%)
    all_to_all x5, starting transfers between devices, spread(): return lax.all_to_all(values, axes, 0, 0, tiled=False)  57 us
    pallas_call x10, Pallas kernels, call(): pl.pallas_call(whole, out_shape=[pltpu.VMEM(o, F32) if i in pin else jax....  25.7 us
    ppermute x5, starting transfers between devices, exchange(): lax.ppermute(to_high, axis, forward)  19.4 us
    ppermute x5, waiting for transfers between devices, exchange(): lax.ppermute(to_low, axis, backward)  15.9 us
    all_to_all x5, waiting for transfers between devices, spread(): return lax.all_to_all(values, axes, 0, 0, tiled=False)  9.61 us
    ppermute x5, starting transfers between devices, exchange(): lax.ppermute(to_low, axis, backward)  7.9 us
    unnamed x10, local copies, waits for them, and re-layouts  3.03 us
  transfers between devices with their start and end apart: 15, of which 8 were waited for; matrix products, arithmetic and copies ran while one was open for 0% of the time, Pallas kernels for 11%

profile of v4, /device:TPU:1, one launch (start us, length us, event | category | flops | bytes accessed | tf_op | source)
XLA Modules:
  0.0 140.1 jit_solution(18420573695879219137)
XLA Ops:
  0.6 0.0 copy-start.4
  0.6 0.6 copy-done.4
  1.3 2.4 %coarse_restrict.1 = (f32[16,32,128]{2,1,0:T(8,128)}, f32[4,128]{1,0:T(4,128)S(1)}, f32[16,16,128]{2,1,0:T(8,128)S(1)}, f32[8,64,128]{2,1,0:T(8,128)S(1)}) custom-call(s32[8]{0:T(128)S(1)} %copy-done.4, s32[1]{0:T(128)} %bitcast.refs_1_.refs_0_, f32[16,16,128]{2,1,0:T(8,128)} %refs_2_.3, s32[4,16]{1,0:T(4,128)} %bitcast.4, f32[8,64,128]{2,1,0:T(8,128)} %refs_4_.3), custom_call_target="tpu_custom_call" | custom-call | bytes 657700 | tf_op jit(solution)/shard_map/coarse_restrict/pallas_call | solution.py:88
  3.7 19.4 %all-to-all-start = ((f32[16,32,128]{2,1,0:T(8,128)}), f32[16,32,128]{2,1,0:T(8,128)S(1)}, u32[]{:S(2)}, u32[]{:S(2)}) async-start(f32[16,32,128]{2,1,0:T(8,128)} %get-tuple-element.42), calls=%async_computation | async-start | bytes 524288 | tf_op jit(solution)/shard_map/all_to_all | solution.py:398
  23.1 2.3 %operator_direction.1 = (f32[16,16,128]{2,1,0:T(8,128)S(1)}, f32[16,16,128]{2,1,0:T(8,128)S(1)}, f32[3,16,16,128]{3,2,1,0:T(8,128)S(1)}, f32[16,16,128]{2,1,0:T(...) custom-call(f32[16,16,128]{2,1,0:T(8,128)} %refs_0_.6, f32[3,16,16,128]{3,2,1,0:T(8,128)} %refs_1_.2, ...), custom_call_target="tpu_custom_call" | custom-call | bytes 1441792 | tf_op jit(solution)/shard_map/operator_direction/pallas_call | solution.py:88
  25.4 5.2 %basis_matrices.1 = (f32[480,336]{1,0:T(8,128)S(1)}, f32[256,480]{1,0:T(8,128)S(1)}, f32[136,160]{1,0:T(8,128)S(1)}, f32[160,128]{1,0:T(8,128)S(1)}) custom-call(f32[10,10]{1,0:T(8,128)} %refs_0_.7, f32[20,10]{1,0:T(8,128)} %constant.42.clone.refs_1_, f32[20,20]{1,0:T(8,128)} %constant.43.clone.refs_2_, f32[160,10]{1,0:T(8,128)} %constant.44.clone.refs_3_, ...), custom_call_target="tpu_custom_call" | custom-call | bytes 1757680 | tf_op jit(solution)/shard_map/basis_matrices/pallas_call | solution.py:88
  30.6 0.0 copy-start
  30.6 0.9 copy-done
  31.5 0.0 copy-start.1
  31.5 0.8 copy-done.1
  32.3 0.7 copy-done.3
  33.0 3.3 %all-to-all-done.refs_1_ = f32[16,32,128]{2,1,0:T(8,128)S(1)} async-done(((f32[16,32,128]{2,1,0:T(8,128)}), f32[16,32,128]{2,1,0:T(8,128)S(1)}, u32[]{:S(2)}, u32[]{:S(2)}) %all-to-all-start) | async-done | bytes 262176 | tf_op jit(solution)/shard_map/all_to_all | solution.py:398
  36.2 1.1 line_sum.1
  37.3 0.0 copy-done.2
  37.3 16.3 %all-to-all-start.1 = ((f32[64,8,128]{2,1,0:T(8,128)}), f32[64,8,128]{2,1,0:T(8,128)S(1)}, u32[]{:S(2)}, u32[]{:S(2)}) async-start(f32[64,8,128]{2,1,0:T(8,128)} %get-tuple-element.46), calls=%async_computation.1 | async-start | bytes 524288 | tf_op jit(solution)/shard_map/all_to_all | solution.py:398
  53.6 3.3 %collective-permute-start = (f32[24,128]{1,0:T(8,128)S(1)}, f32[24,128]{1,0:T(8,128)S(1)}, u32[]{:S(2)}, u32[]{:S(2)}) collective-permute-start(f32[24,128]{1,0:T(8,128)S(1)} %get-tuple-element.49), channel_id=1, source_target_pairs={{0,8},{8,16},{16,24},{24,32},{32,40},{40,48},{48,56},{1,9},{9,17},... | collective-permute-start | bytes 36872 | tf_op jit(solution)/shard_map/ppermute | solution.py:394
  56.9 1.3 collective-permute-start.1
  58.2 0.0 collective-permute-done.refs_4_
  58.2 3.6 %collective-permute-done.1.refs_5_ = f32[24,128]{1,0:T(8,128)S(1)} collective-permute-done((f32[24,128]{1,0:T(8,128)S(1)}, f32[24,128]{1,0:T(8,128)S(1)}, u32[]{:S(2)}, u32[]{:S(2)}) %collective-permute-start.1) | collective-permute-done | bytes 12320 | tf_op jit(solution)/shard_map/ppermute | solution.py:394
  61.9 4.9 %all-to-all-done.1.refs_0_ = f32[64,8,128]{2,1,0:T(8,128)S(1)} async-done(((f32[64,8,128]{2,1,0:T(8,128)}), f32[64,8,128]{2,1,0:T(8,128)S(1)}, u32[]{:S(2)}, u32[]{:S(2)}) %all-to-all-start.1) | async-done | bytes 262176 | tf_op jit(solution)/shard_map/all_to_all | solution.py:398
  66.8 1.0 plane_sum.1
  67.8 6.4 %all-to-all-start.2 = ((f32[64,8,128]{2,1,0:T(8,128)}), f32[64,8,128]{2,1,0:T(8,128)S(1)}, u32[]{:S(2)}, u32[]{:S(2)}) async-start(f32[64,8,128]{2,1,0:T(8,128)} %get-tuple-element.51), calls=%async_computation.2 | async-start | bytes 524288 | tf_op jit(solution)/shard_map/all_to_all | solution.py:398
  74.2 3.5 %collective-permute-start.2 = (f32[1,336]{1,0:T(1,128)S(1)}, f32[1,336]{1,0:T(1,128)S(1)}, u32[]{:S(2)}, u32[]{:S(2)}) collective-permute-start(f32[1,336]{1,0:T(1,128)S(1)} %get-tuple-element.55), channel_id=1, source_target_pairs={{0,1},{1,2},{2,3},{3,4},{4,5},{5,6},{6,7},{8,9},{9,10},{10,11},{11... | collective-permute-start | bytes 4040 | tf_op jit(solution)/shard_map/ppermute | solution.py:394
  77.7 2.1 %collective-permute-start.3 = (f32[1,336]{1,0:T(1,128)S(1)}, f32[1,336]{1,0:T(1,128)S(1)}, u32[]{:S(2)}, u32[]{:S(2)}) collective-permute-start(f32[1,336]{1,0:T(1,128)S(1)} %get-tuple-element.56), channel_id=1, source_target_pairs={{1,0},{2,1},{3,2},{4,3},{5,4},{6,5},{7,6},{9,8},{10,9},{11,10},{12... | collective-permute-start | bytes 4040 | tf_op jit(solution)/shard_map/ppermute | solution.py:394
  79.8 0.0 collective-permute-done.2.refs_1_
  79.9 3.1 %collective-permute-done.3.refs_2_ = f32[1,336]{1,0:T(1,128)S(1)} collective-permute-done((f32[1,336]{1,0:T(1,128)S(1)}, f32[1,336]{1,0:T(1,128)S(1)}, u32[]{:S(2)}, u32[]{:S(2)}) %collective-permute-start.3) | collective-permute-done | bytes 1376 | tf_op jit(solution)/shard_map/ppermute | solution.py:394
  82.9 6.3 %element_solve.1 = (f32[256,128]{1,0:T(8,128)S(1)}, f32[1,1]{1,0:T(1,128)}) custom-call(f32[336,128]{1,0:T(8,128)S(1)} %get-tuple-element.54.refs_0_, f32[1,336]{1,0:T(1,128)S(1)} %collective-permute-done.2.refs_1_, f32[1,336]{1,0:T(1,128)S(1)} %collective-permute-done.3.refs_2_, f32[480,336]{1,0:T(8,128)} %copy-done, f32[256,480]{1,0:T(8,128)} %copy-done.1, ...), custom_call_target="tpu_custom_call" | custom-call | bytes 1867396 | tf_op jit(solution)/shard_map/element_solve/pallas_call | solution.py:88
  89.2 0.0 all-to-all-done.2
  89.2 4.0 %coarse_correct.1 = (f32[16,16,128]{2,1,0:T(8,128)S(1)}, f32[16,16,128]{2,1,0:T(8,128)S(1)}, f32[2,16,128]{2,1,0:T(8,128)S(1)}, f32[2,16,128]{2,1,0:T(8,128)S(1)...) custom-call(s32[8]{0:T(128)S(1)} %copy-done.4, f32[512,128]{1,0:T(8,128)S(1)} %bitcast.3, ...), custom_call_target="tpu_custom_call" | custom-call | bytes 2426920 | tf_op jit(solution)/shard_map/coarse_correct/pallas_call | solution.py:88
  93.2 9.3 %all-to-all-start.3 = ((f32[64,1,128]{2,1,0:T(1,128)}), f32[64,1,128]{2,1,0:T(1,128)S(1)}, u32[]{:S(2)}, u32[]{:S(2)}) async-start(f32[64,1,128]{2,1,0:T(1,128)} %get-tuple-element.70), calls=%async_computation.3 | async-start | bytes 65536 | tf_op jit(solution)/shard_map/all_to_all | solution.py:398
  102.5 3.1 %collective-permute-start.4 = (f32[2,16,128]{2,1,0:T(8,128)S(1)}, f32[2,16,128]{2,1,0:T(8,128)S(1)}, u32[]{:S(2)}, u32[]{:S(2)}) collective-permute-start(f32[2,16,128]{2,1,0:T(8,128)S(1)} %get-tuple-element.68), channel_id=1, source_target_pairs={{0,64},{64,128},{128,192},{192,256},{256,320},{320,384},{384,448},... | collective-permute-start | bytes 49160 | tf_op jit(solution)/shard_map/ppermute | solution.py:394
  105.6 1.3 collective-permute-start.5
  106.9 0.0 collective-permute-done.4.refs_2_
  106.9 3.5 %collective-permute-done.5.refs_3_ = f32[2,16,128]{2,1,0:T(8,128)S(1)} collective-permute-done((f32[2,16,128]{2,1,0:T(8,128)S(1)}, f32[2,16,128]{2,1,0:T(8,128)S(1)}, u32[]{:S(2)}, u32[]{:S(2)}) %collective-permute-start.5) | collective-permute-done | bytes 16416 | tf_op jit(solution)/shard_map/ppermute | solution.py:394
  110.4 1.4 %all-to-all-done.3.refs_4_ = f32[64,1,128]{2,1,0:T(1,128)S(1)} async-done(((f32[64,1,128]{2,1,0:T(1,128)}), f32[64,1,128]{2,1,0:T(1,128)S(1)}, u32[]{:S(2)}, u32[]{:S(2)}) %all-to-all-start.3) | async-done | bytes 32800 | tf_op jit(solution)/shard_map/all_to_all | solution.py:398
  111.8 0.7 assemble_length.1
  112.5 5.6 %all-to-all-start.4 = ((f32[16,1,128]{2,1,0:T(1,128)}), f32[16,1,128]{2,1,0:T(1,128)S(1)}, u32[]{:S(2)}, u32[]{:S(2)}) async-start(f32[16,1,128]{2,1,0:T(1,128)} %get-tuple-element.71), calls=%async_computation.4 | async-start | bytes 16384 | tf_op jit(solution)/shard_map/all_to_all | solution.py:398
  118.1 3.3 %collective-permute-start.6 = (f32[2,16,128]{2,1,0:T(8,128)S(1)}, f32[2,16,128]{2,1,0:T(8,128)S(1)}, u32[]{:S(2)}, u32[]{:S(2)}) collective-permute-start(f32[2,16,128]{2,1,0:T(8,128)S(1)} %get-tuple-element.74), channel_id=1, source_target_pairs={{0,8},{8,16},{16,24},{24,32},{32,40},{40,48},{48,56},{1,9},{9,17},... | collective-permute-start | bytes 49160 | tf_op jit(solution)/shard_map/ppermute | solution.py:394
  121.4 1.3 collective-permute-start.7
  122.7 0.0 collective-permute-done.6.refs_1_
  122.7 3.5 %collective-permute-done.7.refs_2_ = f32[2,16,128]{2,1,0:T(8,128)S(1)} collective-permute-done((f32[2,16,128]{2,1,0:T(8,128)S(1)}, f32[2,16,128]{2,1,0:T(8,128)S(1)}, u32[]{:S(2)}, u32[]{:S(2)}) %collective-permute-start.7) | collective-permute-done | bytes 16416 | tf_op jit(solution)/shard_map/ppermute | solution.py:394
  126.2 1.0 assemble_across.1
  127.1 6.2 %collective-permute-start.8 = (f32[1,512]{1,0:T(1,128)S(1)}, f32[1,512]{1,0:T(1,128)S(1)}, u32[]{:S(2)}, u32[]{:S(2)}) collective-permute-start(f32[1,512]{1,0:T(1,128)S(1)} %get-tuple-element.77), channel_id=1, source_target_pairs={{0,1},{1,2},{2,3},{3,4},{4,5},{5,6},{6,7},{8,9},{9,10},{10,11},{11... | collective-permute-start | bytes 6152 | tf_op jit(solution)/shard_map/ppermute | solution.py:394
  133.3 1.9 %collective-permute-start.9 = (f32[1,512]{1,0:T(1,128)S(1)}, f32[1,512]{1,0:T(1,128)S(1)}, u32[]{:S(2)}, u32[]{:S(2)}) collective-permute-start(f32[1,512]{1,0:T(1,128)S(1)} %get-tuple-element.78), channel_id=1, source_target_pairs={{1,0},{2,1},{3,2},{4,3},{5,4},{6,5},{7,6},{9,8},{10,9},{11,10},{12... | collective-permute-start | bytes 6152 | tf_op jit(solution)/shard_map/ppermute | solution.py:394
  135.9 0.0 collective-permute-done.8.refs_4_
  135.9 2.3 %collective-permute-done.9.refs_5_ = f32[1,512]{1,0:T(1,128)S(1)} collective-permute-done((f32[1,512]{1,0:T(1,128)S(1)}, f32[1,512]{1,0:T(1,128)S(1)}, u32[]{:S(2)}, u32[]{:S(2)}) %collective-permute-start.9) | collective-permute-done | bytes 2080 | tf_op jit(solution)/shard_map/ppermute | solution.py:394
  138.2 0.0 all-to-all-done.4.refs_1_
  138.2 1.8 %update.1 = (f32[16,16,128]{2,1,0:T(8,128)}, f32[16,16,128]{2,1,0:T(8,128)}, f32[16,16,128]{2,1,0:T(8,128)}) custom-call(f32[1]{0:T(128)S(6)} %copy.30.refs_0_, f32[16,1,128]{2,1,0:T(1,128)S(1)} %all-to-all-done.4.refs_1_, f32[1,1]{1,0:T(1,128)} %get-tuple-element.72.refs_2_, f32[2,16,16,128]{3,2,1,0:T(8,128)S(1)} %get-tuple-element.76.refs_3_, ...), custom_call_target="tpu_custom_call" | custom-call | bytes 1191944 | tf_op jit(solution)/shard_map/update/pallas_call | solution.py:88
  (2 shorter events, 0.0 us)
Async XLA Ops:
  0.6 0.7 copy-start.4
  3.7 32.6 %all-to-all-start = ((f32[16,32,128]{2,1,0:T(8,128)}), f32[16,32,128]{2,1,0:T(8,128)S(1)}, u32[]{:S(2)}, u32[]{:S(2)}) async-start(f32[16,32,128]{2,1,0:T(8,128)} %get-tuple-element.42), calls=%async_computation | async-start | bytes 524288 | tf_op jit(solution)/shard_map/all_to_all | solution.py:398
  30.6 0.9 copy-start
  31.5 0.8 copy-start.1
  32.3 0.7 copy-start.3
  33.0 4.4 %copy-start.2 = (f32[160,128]{1,0:T(8,128)}, f32[160,128]{1,0:T(8,128)S(1)}, u32[]{:S(2)}) copy-start(f32[160,128]{1,0:T(8,128)S(1)} %get-tuple-element.45.refs_4_.refs_6_) | copy-start | bytes 245764
  37.3 29.5 %all-to-all-start.1 = ((f32[64,8,128]{2,1,0:T(8,128)}), f32[64,8,128]{2,1,0:T(8,128)S(1)}, u32[]{:S(2)}, u32[]{:S(2)}) async-start(f32[64,8,128]{2,1,0:T(8,128)} %get-tuple-element.46), calls=%async_computation.1 | async-start | bytes 524288 | tf_op jit(solution)/shard_map/all_to_all | solution.py:398
  53.6 4.6 %collective-permute-start = (f32[24,128]{1,0:T(8,128)S(1)}, f32[24,128]{1,0:T(8,128)S(1)}, u32[]{:S(2)}, u32[]{:S(2)}) collective-permute-start(f32[24,128]{1,0:T(8,128)S(1)} %get-tuple-element.49), channel_id=1, source_target_pairs={{0,8},{8,16},{16,24},{24,32},{32,40},{40,48},{48,56},{1,9},{9,17},... | collective-permute-start | bytes 36872 | tf_op jit(solution)/shard_map/ppermute | solution.py:394
  56.9 4.9 %collective-permute-start.1 = (f32[24,128]{1,0:T(8,128)S(1)}, f32[24,128]{1,0:T(8,128)S(1)}, u32[]{:S(2)}, u32[]{:S(2)}) collective-permute-start(f32[24,128]{1,0:T(8,128)S(1)} %get-tuple-element.50), channel_id=1, source_target_pairs={{8,0},{16,8},{24,16},{32,24},{40,32},{48,40},{56,48},{9,1},{17,9},... | collective-permute-start | bytes 36872 | tf_op jit(solution)/shard_map/ppermute | solution.py:394
  67.8 21.5 %all-to-all-start.2 = ((f32[64,8,128]{2,1,0:T(8,128)}), f32[64,8,128]{2,1,0:T(8,128)S(1)}, u32[]{:S(2)}, u32[]{:S(2)}) async-start(f32[64,8,128]{2,1,0:T(8,128)} %get-tuple-element.51), calls=%async_computation.2 | async-start | bytes 524288 | tf_op jit(solution)/shard_map/all_to_all | solution.py:398
  74.2 5.7 %collective-permute-start.2 = (f32[1,336]{1,0:T(1,128)S(1)}, f32[1,336]{1,0:T(1,128)S(1)}, u32[]{:S(2)}, u32[]{:S(2)}) collective-permute-start(f32[1,336]{1,0:T(1,128)S(1)} %get-tuple-element.55), channel_id=1, source_target_pairs={{0,1},{1,2},{2,3},{3,4},{4,5},{5,6},{6,7},{8,9},{9,10},{10,11},{11... | collective-permute-start | bytes 4040 | tf_op jit(solution)/shard_map/ppermute | solution.py:394
  77.7 5.2 %collective-permute-start.3 = (f32[1,336]{1,0:T(1,128)S(1)}, f32[1,336]{1,0:T(1,128)S(1)}, u32[]{:S(2)}, u32[]{:S(2)}) collective-permute-start(f32[1,336]{1,0:T(1,128)S(1)} %get-tuple-element.56), channel_id=1, source_target_pairs={{1,0},{2,1},{3,2},{4,3},{5,4},{6,5},{7,6},{9,8},{10,9},{11,10},{12... | collective-permute-start | bytes 4040 | tf_op jit(solution)/shard_map/ppermute | solution.py:394
  93.2 18.6 %all-to-all-start.3 = ((f32[64,1,128]{2,1,0:T(1,128)}), f32[64,1,128]{2,1,0:T(1,128)S(1)}, u32[]{:S(2)}, u32[]{:S(2)}) async-start(f32[64,1,128]{2,1,0:T(1,128)} %get-tuple-element.70), calls=%async_computation.3 | async-start | bytes 65536 | tf_op jit(solution)/shard_map/all_to_all | solution.py:398
  102.5 4.4 %collective-permute-start.4 = (f32[2,16,128]{2,1,0:T(8,128)S(1)}, f32[2,16,128]{2,1,0:T(8,128)S(1)}, u32[]{:S(2)}, u32[]{:S(2)}) collective-permute-start(f32[2,16,128]{2,1,0:T(8,128)S(1)} %get-tuple-element.68), channel_id=1, source_target_pairs={{0,64},{64,128},{128,192},{192,256},{256,320},{320,384},{384,448},... | collective-permute-start | bytes 49160 | tf_op jit(solution)/shard_map/ppermute | solution.py:394
  105.6 4.8 %collective-permute-start.5 = (f32[2,16,128]{2,1,0:T(8,128)S(1)}, f32[2,16,128]{2,1,0:T(8,128)S(1)}, u32[]{:S(2)}, u32[]{:S(2)}) collective-permute-start(f32[2,16,128]{2,1,0:T(8,128)S(1)} %get-tuple-element.69), channel_id=1, source_target_pairs={{64,0},{128,64},{192,128},{256,192},{320,256},{384,320},{448,384},... | collective-permute-start | bytes 49160 | tf_op jit(solution)/shard_map/ppermute | solution.py:394
  112.5 25.7 %all-to-all-start.4 = ((f32[16,1,128]{2,1,0:T(1,128)}), f32[16,1,128]{2,1,0:T(1,128)S(1)}, u32[]{:S(2)}, u32[]{:S(2)}) async-start(f32[16,1,128]{2,1,0:T(1,128)} %get-tuple-element.71), calls=%async_computation.4 | async-start | bytes 16384 | tf_op jit(solution)/shard_map/all_to_all | solution.py:398
  118.1 4.6 %collective-permute-start.6 = (f32[2,16,128]{2,1,0:T(8,128)S(1)}, f32[2,16,128]{2,1,0:T(8,128)S(1)}, u32[]{:S(2)}, u32[]{:S(2)}) collective-permute-start(f32[2,16,128]{2,1,0:T(8,128)S(1)} %get-tuple-element.74), channel_id=1, source_target_pairs={{0,8},{8,16},{16,24},{24,32},{32,40},{40,48},{48,56},{1,9},{9,17},... | collective-permute-start | bytes 49160 | tf_op jit(solution)/shard_map/ppermute | solution.py:394
  121.4 4.8 %collective-permute-start.7 = (f32[2,16,128]{2,1,0:T(8,128)S(1)}, f32[2,16,128]{2,1,0:T(8,128)S(1)}, u32[]{:S(2)}, u32[]{:S(2)}) collective-permute-start(f32[2,16,128]{2,1,0:T(8,128)S(1)} %get-tuple-element.75), channel_id=1, source_target_pairs={{8,0},{16,8},{24,16},{32,24},{40,32},{48,40},{56,48},{9,1},{17,9},... | collective-permute-start | bytes 49160 | tf_op jit(solution)/shard_map/ppermute | solution.py:394
  127.1 8.8 %collective-permute-start.8 = (f32[1,512]{1,0:T(1,128)S(1)}, f32[1,512]{1,0:T(1,128)S(1)}, u32[]{:S(2)}, u32[]{:S(2)}) collective-permute-start(f32[1,512]{1,0:T(1,128)S(1)} %get-tuple-element.77), channel_id=1, source_target_pairs={{0,1},{1,2},{2,3},{3,4},{4,5},{5,6},{6,7},{8,9},{9,10},{10,11},{11... | collective-permute-start | bytes 6152 | tf_op jit(solution)/shard_map/ppermute | solution.py:394
  133.3 4.9 %collective-permute-start.9 = (f32[1,512]{1,0:T(1,128)S(1)}, f32[1,512]{1,0:T(1,128)S(1)}, u32[]{:S(2)}, u32[]{:S(2)}) collective-permute-start(f32[1,512]{1,0:T(1,128)S(1)} %get-tuple-element.78), channel_id=1, source_target_pairs={{1,0},{2,1},{3,2},{4,3},{5,4},{6,5},{7,6},{9,8},{10,9},{11,10},{12... | collective-permute-start | bytes 6152 | tf_op jit(solution)/shard_map/ppermute | solution.py:394

commit v5 on v4

--- a/solution.py
+++ b/solution.py
@@ -1,3 +1,5 @@
+import functools
+
 import jax
 import jax.numpy as jnp
 import numpy as np
@@ -49,7 +51,7 @@
     )
 
 
-def call(kernel, name, outs, *args, smem=(), load=(), keep=(), scratch=(), pin=()):
+def call(kernel, name, outs, *args, smem=(), load=(), keep=(), scratch=(), pin=(), store=(), idle=()):
     count, n_out, n_keep = len(args), len(outs), len(keep)
     moved = sorted((*load, *keep))
     vmem = pl.BlockSpec(memory_space=pltpu.VMEM)
@@ -58,7 +60,10 @@
         inside, results = list(refs[:count]), refs[count : count + n_out]
         kept = refs[count + n_out : count + n_out + n_keep]
         rest = list(refs[count + n_out + n_keep :])
-        sems = rest.pop() if moved else None
+        sems = rest.pop() if moved or store else None
+        written = list(results)
+        for i in store:
+            written[i] = rest.pop()
         copies = {}
         for at, i in enumerate(moved):
             target = kept[keep.index(i)] if i in keep else rest.pop()
@@ -72,32 +77,48 @@
                 if i in waiting:
                     waiting.pop(i).wait()
 
-        kernel(ready, *inside, *results, *rest)
+        kernel(ready, *inside, *written, *rest)
         ready(*moved)
+        copies = [
+            pltpu.make_async_copy(written[i], results[i], sems.at[len(moved) + at])
+            for at, i in enumerate(store)
+        ]
+        for copy in copies:
+            copy.start()
+        for copy in copies:
+            copy.wait()
 
     buffers = [pltpu.VMEM(args[i].shape, args[i].dtype) for i in moved if i not in keep]
     specs = []
     for i in range(count):
-        space = pltpu.SMEM if i in smem else pltpu.HBM if i in moved else pltpu.VMEM
+        space = pltpu.SMEM if i in smem else pltpu.HBM if i in (*moved, *idle) else pltpu.VMEM
         specs.append(pl.BlockSpec(memory_space=space))
     args = [
-        pltpu.with_memory_space_constraint(a, pltpu.HBM) if i in moved else a
+        pltpu.with_memory_space_constraint(a, pltpu.HBM) if i in (*moved, *idle) else a
         for i, a in enumerate(args)
     ]
     size = sum(int(np.prod(a.shape)) * 4 for a in args) + sum(int(np.prod(o)) * 4 for o in outs)
     return pl.pallas_call(
         whole,
         out_shape=[
-            pltpu.VMEM(o, F32) if i in pin else jax.ShapeDtypeStruct(o, F32)
+            pltpu.VMEM(o, F32)
+            if i in pin
+            else pltpu.HBM(o, F32)
+            if i in store
+            else jax.ShapeDtypeStruct(o, F32)
             for i, o in enumerate(outs)
         ]
         + [pltpu.VMEM(args[i].shape, args[i].dtype) for i in keep],
         in_specs=specs,
-        out_specs=[vmem] * (n_out + n_keep),
+        out_specs=[
+            pl.BlockSpec(memory_space=pltpu.HBM) if i in store else vmem
+            for i in range(n_out + n_keep)
+        ],
         scratch_shapes=[
             *scratch,
             *buffers[::-1],
-            *([pltpu.SemaphoreType.DMA((len(moved),))] if moved else []),
+            *[pltpu.VMEM(outs[i], F32) for i in store[::-1]],
+            *([pltpu.SemaphoreType.DMA((len(moved) + len(store),))] if moved or store else []),
         ],
         cost_estimate=pl.CostEstimate(flops=0, bytes_accessed=size, transcendentals=0),
         compiler_params=pltpu.CompilerParams(vmem_limit_bytes=24 * 2**20),
@@ -153,13 +174,16 @@
         payload[i, :head, :] = lines
 
 
-def line_kernel(ready, me, parts, residual, after1, after2, dense, x_low, x_high, to_high, to_low):
+def line_kernel(
+    n_stored, ready, me, parts, residual, after1, after2, dense, x_low, x_high, to_high, to_low
+):
     nx, ny, nz = residual.shape
     n_line = parts.shape[0]
-    head, n_stored = parts.shape[1] - ny, 8
+    head = parts.shape[1] - ny
     at = me[0]
     rows = parts[:, :n_stored, :].reshape(n_line * n_stored, nz)
-    rows = jnp.concatenate([rows] + [jnp.zeros((nz - n_line * n_stored, nz), F32)]) if n_line * n_stored < nz else rows
+    if rows.shape[0] < nz:
+        rows = jnp.concatenate([rows, jnp.zeros((nz - rows.shape[0], nz), F32)])
     numbers = jnp.sum(parts[:, n_stored : n_stored + 1, :], axis=0)
     n_blocks = dense.shape[0] * dense.shape[1]
     block = lax.broadcasted_iota(jnp.int32, (n_blocks, nz), 0).astype(F32)
@@ -173,6 +197,12 @@
         out[:nx] = residual[:, y, :]
         out[nx : nx + 1] = x_low[y : y + 1]
         out[nx + 1 : nx + 2] = x_high[y : y + 1]
+
+
+def spread_sum_kernel(ready, parts, after, out):
+    total = jnp.sum(parts[...], axis=0)
+    for i in range(out.shape[0]):
+        out[i] = total
 
 
 def plane_kernel(
@@ -212,21 +242,26 @@
     from_z[...] = mm(flatz, in_z[...], 0, 0)
 
 
+def spectral_kernel(ready, every, to_spectral, to_z, spectral):
+    ready(1, 2)
+    spectral[...] = mm(mm(to_spectral[...], every[...]), to_z[: every.shape[1], :])
+
+
 def solve_kernel(
-    ready, every, z_low, z_high, to_spectral, from_spectral, to_z, from_z, sums, local_part, inner, wide
-):
-    nz = every.shape[1]
+    ready, inside, z_low, z_high, to_spectral, from_spectral, to_z, from_z, sums, local_part,
+    inner, wide
+):
     n_x, n_y, n_z = sums.shape
     wide[...] = jnp.zeros_like(wide)
-    row = lax.broadcasted_iota(jnp.int32, (8, every.shape[0]), 0)
+    row = lax.broadcasted_iota(jnp.int32, (8, z_low.shape[1]), 0)
     ends = jnp.where(row == 0, z_low[...], jnp.where(row == 1, z_high[...], 0.0))
-    ready(3, 4, 5, 6)
-    spectral = mm(mm(to_spectral[...], every[...]), to_z[:nz, :])
-    spectral = spectral + mm(mm(to_spectral[...], ends, 1, 1), to_z[nz:, :])
+    ready(3, 5)
+    spectral = inside[...] + mm(mm(to_spectral[...], ends, 1, 1), to_z[to_z.shape[0] - 8 :, :])
     ready(7)
     wide[:, :n_y, :] = sums[...]
     weighted = wide[...].reshape(-1, n_z) * spectral
     inner[...] = jnp.sum(jnp.sum(weighted * spectral, axis=0, keepdims=True), axis=1, keepdims=True)
+    ready(4, 6)
     local_part[...] = mm(mm(from_spectral[...], weighted), from_z[...])
 
 
@@ -264,9 +299,9 @@
 
 
 def correct_kernel(
-    ready, blocks, coarse_inner, values, ids_wide, local_part, inner_local, direction, image_direction,
+    ready, blocks, coarse_inner, values, ids_wide, local_part, direction, image_direction,
     conductance, mass, ky, ky_t, kz, kz_t,
-    z_out, image_out, to_high, to_low, terms, square,
+    z_out, image_out, to_high, to_low,
 ):
     nx, ny, nz = direction.shape
     rows = nx * ny
@@ -285,46 +320,40 @@
             for x in range(N):
                 at = (a * N + x) * ny + b * N
                 z_out[a * N + x, b * N : b * N + N, :] = local_part[at : at + N, :] + line
-    ready(10, 11)
     operator(z_out, conductance, mass, ky, ky_t, kz, kz_t, image_out)
-    flat = z_out[...].reshape(rows, nz)
-    image = image_out[...].reshape(rows, nz)
-    to_high[0] = image_out[nx - 1]
-    to_high[1] = image_direction[nx - 1]
-    to_low[0] = image_out[0]
-    to_low[1] = image_direction[0]
-    old = direction[...].reshape(rows, nz)
-    old_image = image_direction[...].reshape(rows, nz)
-    first = total_of(flat * image)
-    second = total_of(flat * old_image + old * image)
-    third = total_of(old * old_image)
-    lane = lax.broadcasted_iota(jnp.int32, (1, nz), 1)
-    line = jnp.where(
-        lane == 0,
-        inner_local[...],
-        jnp.where(lane == 1, first, jnp.where(lane == 2, second, jnp.where(lane == 3, third, 0.0))),
-    )
+    for out, x in ((to_high, nx - 1), (to_low, 0)):
+        out[0, :ny] = image_out[x]
+        out[1, :ny] = image_direction[x]
+
+
+def terms_kernel(
+    ready, z, image, direction, image_direction, inner_local, coarse_inner, after, terms, square
+):
+    first = jnp.sum(z[...] * image[...], axis=0)
+    second = jnp.sum(z[...] * image_direction[...] + direction[...] * image[...], axis=0)
+    third = jnp.sum(direction[...] * image_direction[...], axis=0)
+    lane = lax.broadcasted_iota(jnp.int32, (1, terms.shape[2]), 1)
+    line = jnp.where(lane == 0, inner_local[...], 0.0)
+    for i, value in enumerate((first, second, third)):
+        line = jnp.where(lane == i + 1, total_of(value), line)
     for i in range(terms.shape[0]):
         terms[i] = line
     square[...] = total_of(coarse_inner[...] * coarse_inner[...])
 
 
 def assemble_length_kernel(
-    ready, image, image_direction, low, high, parts, out, to_high, to_low, terms
+    ready, image, image_direction, low, high, out, to_high, to_low
 ):
     nx, ny, nz = image.shape
-    total = jnp.sum(parts[...], axis=0)
-    for i in range(terms.shape[0]):
-        terms[i] = total
     for i, ref in ((0, image), (1, image_direction)):
         out[i] = ref[...]
         for x in range(nx):
             if x % N == N - 1:
-                out[i, x] = ref[x] + (ref[x + 1] if x + 1 < nx else high[i])
+                out[i, x] = ref[x] + (ref[x + 1] if x + 1 < nx else high[i, :ny])
             elif x % N == 0:
-                out[i, x] = ref[x] + (ref[x - 1] if x else low[i])
-        to_high[i] = out[i, :, ny - 1, :]
-        to_low[i] = out[i, :, 0, :]
+                out[i, x] = ref[x] + (ref[x - 1] if x else low[i, :ny])
+        to_high[i, :nx] = out[i, :, ny - 1, :]
+        to_low[i, :nx] = out[i, :, 0, :]
 
 
 def assemble_across_kernel(ready, images, low, high, solution, out, to_high, to_low):
@@ -333,9 +362,9 @@
     for i in range(2):
         for y in range(ny):
             if y % N == N - 1:
-                other = images[i, :, y + 1, :] if y + 1 < ny else high[i]
+                other = images[i, :, y + 1, :] if y + 1 < ny else high[i, :nx]
             elif y % N == 0:
-                other = images[i, :, y - 1, :] if y else low[i]
+                other = images[i, :, y - 1, :] if y else low[i, :nx]
             else:
                 continue
             out[i, :, y, :] = images[i, :, y, :] + other
@@ -434,9 +463,9 @@
     ky = np.kron(np.eye(nx, dtype=np.float32), np.kron(np.eye(ey, dtype=np.float32), cheb))
     kz = np.kron(np.eye(ez, dtype=np.float32), cheb)
     tables = [jnp.asarray(np.ascontiguousarray(t)) for t in (ky, ky.T, kz, kz.T)]
-    image_direction, direction, conductance, mass_term, kz, kz_t = call(
+    image_direction, direction, conductance, mass_term, *tables = call(
         operator_kernel, "operator_direction", [direction.shape],
-        direction, conductance, mass_term, *tables, load=(3, 4), keep=(0, 1, 2, 5, 6), pin=(0,),
+        direction, conductance, mass_term, *tables, keep=tuple(range(7)), pin=(0,),
     )
 
     face = up8(nx + 2)
@@ -476,13 +505,13 @@
                 np.ascontiguousarray(one_hot(inside_positions(ez), n_z).T),
             ),
         ),
-        load=tuple(range(13)),
+        load=tuple(range(13)), store=(0, 1, 2, 3),
     )
 
     dense, x_low, x_high, to_high, to_low = call(
-        line_kernel, "line_sum",
+        functools.partial(line_kernel, xxt_values.shape[0]), "line_sum",
         [(n_plane, own, block), (ny, nz), (ny, nz), (face, nz), (face, nz)],
-        me, parts, residual, image_direction, from_z, smem=(0,), pin=(1, 2),
+        me, parts, residual, image_direction, from_z, smem=(0,), pin=(1, 2), idle=(4,),
     )
     parts = spread(dense, plane)
     y_low, y_high = exchange(to_high, to_low, "gy")
@@ -493,27 +522,35 @@
     )
     coarse_inner = spread(owned, plane).reshape(n_blocks, block)
     z_low, z_high = exchange(to_high, to_low, "gz")
+    (spectral,) = call(
+        spectral_kernel, "element_spectral", [(n_x * high_y, n_z)],
+        every, to_spectral, to_z, load=(1, 2), pin=(0,),
+    )
     local_part, inner_local = call(
         solve_kernel, "element_solve", [(rows, nz), (1, 1)],
-        every, z_low, z_high, to_spectral, from_spectral, to_z, from_z, inverse_eigen_sums,
+        spectral, z_low, z_high, to_spectral, from_spectral, to_z, from_z, inverse_eigen_sums,
         load=(3, 4, 5, 6, 7), pin=(0, 1), scratch=(pltpu.VMEM((n_x, high_y, n_z), F32),),
     )
 
-    z, image, to_high, to_low, terms, square = call(
+    z, image, to_high, to_low = call(
         correct_kernel, "coarse_correct",
-        [direction.shape, direction.shape, (2, ny, nz), (2, ny, nz), (n_plane, 1, nz), (1, 1)],
-        xxt_blocks, coarse_inner, xxt_values, ids_wide, local_part, inner_local, direction,
-        image_direction, conductance, mass_term, *tables[:2], kz, kz_t, smem=(0,), load=(10, 11), pin=(0, 1, 5),
+        [direction.shape, direction.shape, (2, 4 * ny, nz), (2, 4 * ny, nz)],
+        xxt_blocks, coarse_inner, xxt_values, ids_wide, local_part, direction,
+        image_direction, conductance, mass_term, *tables, smem=(0,), pin=(0, 1),
     )
     low, high = exchange(to_high, to_low, "gx")
+    terms, square = call(
+        terms_kernel, "terms", [(n_plane, 1, nz), (1, 1)],
+        z, image, direction, image_direction, inner_local, coarse_inner, low, pin=(1,),
+    )
     parts = spread(terms, plane)
-    images, to_high, to_low, terms = call(
-        assemble_length_kernel, "assemble_length",
-        [(2, nx, ny, nz), (2, nx, nz), (2, nx, nz), (n_line, 1, nz)],
-        image, image_direction, low, high, parts, pin=(0,),
-    )
+    images, to_high, to_low = call(
+        assemble_length_kernel, "assemble_length", [(2, nx, ny, nz), (2, 2 * nx, nz), (2, 2 * nx, nz)],
+        image, image_direction, low, high, pin=(0,),
+    )
+    low, high = exchange(to_high, to_low, "gy")
+    (terms,) = call(spread_sum_kernel, "sum_terms", [(n_line, 1, nz)], parts, low)
     parts = spread(terms, "gx")
-    low, high = exchange(to_high, to_low, "gy")
     images, to_high, to_low, solution = call(
         assemble_across_kernel, "assemble_across", [(2, nx, ny, nz), (1, 2 * rows), (1, 2 * rows)],
         images, low, high, solution, keep=(3,), pin=(0,),

time: 142 us -> 137 us (0.965); the launches traced: 140 us -> 137 us
  waiting for transfers between devices: 25.6 us -> 23 us
  local copies, waits for them, and re-layouts: 3.03 us -> 0.65 us
    ppermute x5, waiting for transfers between devices: 15.9 us -> 6.47 us  [exchange(): lax.ppermute(to_low, axis, backward)]
    all_to_all x5, waiting for transfers between devices: 9.61 us -> 16.5 us  [spread(): return lax.all_to_all(values, axes, 0, 0, tiled=False)]
    all_to_all x5, starting transfers between devices: 57 us -> 60.8 us  [spread(): return lax.all_to_all(values, axes, 0, 0, tiled=False)]
    ppermute x5, starting transfers between devices: 19.4 us -> 16.3 us  [exchange(): lax.ppermute(to_high, axis, forward)]
    unnamed x10 -> x2, local copies, waits for them, and re-layouts: 3.03 us -> 0.65 us
    pallas_call x10 -> x13, Pallas kernels: 25.7 us -> 26.4 us  [call(): pl.pallas_call(whole, out_shape=[pltpu.VMEM(o, F32) if i in pin else pltp...]
  transfers between devices with their start and end apart: 15 -> 15, of which waited for: 8 -> 7; matrix products, arithmetic and copies ran while one was open for 0% -> 0% of each run, Pallas kernels for 11% -> 14%
where the time goes in v5:
time: 137 us
  starting transfers between devices  84.9 us (62%)
  Pallas kernels  26.4 us (19%)
  waiting for transfers between devices  23 us (17%)
  between operations  1.53 us (1%)
    all_to_all x5, starting transfers between devices, spread(): return lax.all_to_all(values, axes, 0, 0, tiled=False)  60.8 us
    pallas_call x13, Pallas kernels, call(): pl.pallas_call(whole, out_shape=[pltpu.VMEM(o, F32) if i in pin else pltp...  26.4 us
    all_to_all x5, waiting for transfers between devices, spread(): return lax.all_to_all(values, axes, 0, 0, tiled=False)  16.5 us
    ppermute x5, starting transfers between devices, exchange(): lax.ppermute(to_high, axis, forward)  16.3 us
    ppermute x5, starting transfers between devices, exchange(): lax.ppermute(to_low, axis, backward)  7.9 us
    ppermute x5, waiting for transfers between devices, exchange(): lax.ppermute(to_low, axis, backward)  6.47 us
  transfers between devices with their start and end apart: 15, of which 7 were waited for; matrix products, arithmetic and copies ran while one was open for 0% of the time, Pallas kernels for 14%

profile of v5, /device:TPU:1, one launch (start us, length us, event | category | flops | bytes accessed | tf_op | source)
XLA Modules:
  0.0 136.5 jit_solution(11750945448331837447)
XLA Ops:
  0.6 0.0 copy-start
  0.6 0.6 copy-done
  1.3 2.3 %coarse_restrict.1 = (f32[16,32,128]{2,1,0:T(8,128)}, f32[4,128]{1,0:T(4,128)S(1)}, f32[16,16,128]{2,1,0:T(8,128)S(1)}, f32[8,64,128]{2,1,0:T(8,128)S(1)}) custom-call(s32[8]{0:T(128)S(1)} %copy-done, s32[1]{0:T(128)} %bitcast.refs_1_.refs_0_, f32[16,16,128]{2,1,0:T(8,128)} %refs_2_.3, s32[4,16]{1,0:T(4,128)} %bitcast.5, f32[8,64,128]{2,1,0:T(8,128)} %refs_4_.3), custom_call_target="tpu_custom_call" | custom-call | bytes 657700 | tf_op jit(solution)/shard_map/coarse_restrict/pallas_call | solution.py:101
  3.6 19.4 %all-to-all-start = ((f32[16,32,128]{2,1,0:T(8,128)}), f32[16,32,128]{2,1,0:T(8,128)S(1)}, u32[]{:S(2)}, u32[]{:S(2)}) async-start(f32[16,32,128]{2,1,0:T(8,128)} %get-tuple-element.43), calls=%async_computation | async-start | bytes 524288 | tf_op jit(solution)/shard_map/all_to_all | solution.py:427
  23.1 2.3 %operator_direction.1 = (f32[16,16,128]{2,1,0:T(8,128)S(1)}, f32[16,16,128]{2,1,0:T(8,128)S(1)}, f32[3,16,16,128]{3,2,1,0:T(8,128)S(1)}, f32[16,16,128]{2,1,0:T(...) custom-call(f32[16,16,128]{2,1,0:T(8,128)} %refs_0_.6, ...), custom_call_target="tpu_custom_call" | custom-call | bytes 1441792 | tf_op jit(solution)/shard_map/operator_direction/pallas_call | solution.py:101
  25.4 5.9 %basis_matrices.1 = (f32[480,336]{1,0:T(8,128)}, f32[256,480]{1,0:T(8,128)}, f32[136,160]{1,0:T(8,128)}, f32[160,128]{1,0:T(8,128)}) custom-call(f32[10,10]{1,0:T(8,128)} %refs_0_.7, f32[20,10]{1,0:T(8,128)} %constant.42.clone.refs_1_, f32[20,20]{1,0:T(8,128)} %constant.43.clone.refs_2_, f32[160,10]{1,0:T(8,128)} %constant.44.clone.refs_3_, ...), custom_call_target="tpu_custom_call" | custom-call | bytes 1757680 | tf_op jit(solution)/shard_map/basis_matrices/pallas_call | solution.py:101
  31.3 4.9 %all-to-all-done.refs_1_ = f32[16,32,128]{2,1,0:T(8,128)S(1)} async-done(((f32[16,32,128]{2,1,0:T(8,128)}), f32[16,32,128]{2,1,0:T(8,128)S(1)}, u32[]{:S(2)}, u32[]{:S(2)}) %all-to-all-start) | async-done | bytes 262176 | tf_op jit(solution)/shard_map/all_to_all | solution.py:427
  36.2 1.1 line_sum.1
  37.3 16.3 %all-to-all-start.1 = ((f32[64,8,128]{2,1,0:T(8,128)}), f32[64,8,128]{2,1,0:T(8,128)S(1)}, u32[]{:S(2)}, u32[]{:S(2)}) async-start(f32[64,8,128]{2,1,0:T(8,128)} %get-tuple-element.47), calls=%async_computation.1 | async-start | bytes 524288 | tf_op jit(solution)/shard_map/all_to_all | solution.py:427
  53.6 3.3 %collective-permute-start = (f32[24,128]{1,0:T(8,128)S(1)}, f32[24,128]{1,0:T(8,128)S(1)}, u32[]{:S(2)}, u32[]{:S(2)}) collective-permute-start(f32[24,128]{1,0:T(8,128)S(1)} %get-tuple-element.50), channel_id=1, source_target_pairs={{0,8},{8,16},{16,24},{24,32},{32,40},{40,48},{48,56},{1,9},{9,17},... | collective-permute-start | bytes 36872 | tf_op jit(solution)/shard_map/ppermute | solution.py:423
  56.9 1.3 collective-permute-start.1
  58.2 0.0 collective-permute-done.refs_4_
  58.2 3.6 %collective-permute-done.1.refs_5_ = f32[24,128]{1,0:T(8,128)S(1)} collective-permute-done((f32[24,128]{1,0:T(8,128)S(1)}, f32[24,128]{1,0:T(8,128)S(1)}, u32[]{:S(2)}, u32[]{:S(2)}) %collective-permute-start.1) | collective-permute-done | bytes 12320 | tf_op jit(solution)/shard_map/ppermute | solution.py:423
  61.8 4.9 %all-to-all-done.1.refs_0_ = f32[64,8,128]{2,1,0:T(8,128)S(1)} async-done(((f32[64,8,128]{2,1,0:T(8,128)}), f32[64,8,128]{2,1,0:T(8,128)S(1)}, u32[]{:S(2)}, u32[]{:S(2)}) %all-to-all-start.1) | async-done | bytes 262176 | tf_op jit(solution)/shard_map/all_to_all | solution.py:427
  66.8 0.9 plane_sum.1
  67.7 6.4 %all-to-all-start.2 = ((f32[64,8,128]{2,1,0:T(8,128)}), f32[64,8,128]{2,1,0:T(8,128)S(1)}, u32[]{:S(2)}, u32[]{:S(2)}) async-start(f32[64,8,128]{2,1,0:T(8,128)} %get-tuple-element.52), calls=%async_computation.2 | async-start | bytes 524288 | tf_op jit(solution)/shard_map/all_to_all | solution.py:427
  74.1 3.5 %collective-permute-start.2 = (f32[1,336]{1,0:T(1,128)S(1)}, f32[1,336]{1,0:T(1,128)S(1)}, u32[]{:S(2)}, u32[]{:S(2)}) collective-permute-start(f32[1,336]{1,0:T(1,128)S(1)} %get-tuple-element.58), channel_id=1, source_target_pairs={{0,1},{1,2},{2,3},{3,4},{4,5},{5,6},{6,7},{8,9},{9,10},{10,11},{11... | collective-permute-start | bytes 4040 | tf_op jit(solution)/shard_map/ppermute | solution.py:423
  77.7 2.1 %collective-permute-start.3 = (f32[1,336]{1,0:T(1,128)S(1)}, f32[1,336]{1,0:T(1,128)S(1)}, u32[]{:S(2)}, u32[]{:S(2)}) collective-permute-start(f32[1,336]{1,0:T(1,128)S(1)} %get-tuple-element.59), channel_id=1, source_target_pairs={{1,0},{2,1},{3,2},{4,3},{5,4},{6,5},{7,6},{9,8},{10,9},{11,10},{12... | collective-permute-start | bytes 4040 | tf_op jit(solution)/shard_map/ppermute | solution.py:423
  79.8 2.8 %element_spectral.1.refs_0_ = f32[480,160]{1,0:T(8,128)S(1)} custom-call(f32[336,128]{1,0:T(8,128)S(1)} %get-tuple-element.55.refs_0_, f32[480,336]{1,0:T(8,128)} %get-tuple-element.56.refs_1_.refs_3_, f32[136,160]{1,0:T(8,128)} %get-tuple-element.57.refs_2_.refs_5_), custom_call_target="tpu_custom_call" | custom-call | bytes 1211392 | tf_op jit(solution)/shard_map/element_spectral/pallas_call | solution.py:101
  82.6 0.0 collective-permute-done.2.refs_1_
  82.6 0.2 collective-permute-done.3.refs_2_
  82.9 4.6 %element_solve.1 = (f32[256,128]{1,0:T(8,128)S(1)}, f32[1,1]{1,0:T(1,128)}) custom-call(f32[480,160]{1,0:T(8,128)S(1)} %element_spectral.1.refs_0_, f32[1,336]{1,0:T(1,128)S(1)} %collective-permute-done.2.refs_1_, f32[1,336]{1,0:T(1,128)S(1)} %collective-permute-done.3.refs_2_, f32[480,336]{1,0:T(8,128)} %get-tuple-element.56.refs_1_.refs_3_, ...), custom_call_target="tpu_custom_call" | custom-call | bytes 2002564 | tf_op jit(solution)/shard_map/element_solve/pallas_call | solution.py:101
  87.5 0.0 all-to-all-done.2
  87.5 1.6 %coarse_correct.1 = (f32[16,16,128]{2,1,0:T(8,128)S(1)}, f32[16,16,128]{2,1,0:T(8,128)S(1)}, f32[2,64,128]{2,1,0:T(8,128)S(1)}, f32[2,64,128]{2,1,0:T(8,128)S(1)}) custom-call(s32[8]{0:T(128)S(1)} %copy-done, f32[512,128]{1,0:T(8,128)S(1)} %bitcast.3, f32[8,64,128]{2,1,0:T(8,128)S(1)} %get-tuple-element.53.refs_2_, f32[4,128]{1,0:T(4,128)S(1)} %get-tuple-element.54.refs_3_, ...), custom_call_target="tpu_custom_call" | custom-call | bytes 2492448 | tf_op jit(solution)/shard_map/coarse_correct/pallas_call | solution.py:101
  89.0 3.1 %collective-permute-start.4 = (f32[2,64,128]{2,1,0:T(8,128)S(1)}, f32[2,64,128]{2,1,0:T(8,128)S(1)}, u32[]{:S(2)}, u32[]{:S(2)}) collective-permute-start(f32[2,64,128]{2,1,0:T(8,128)S(1)} %get-tuple-element.72), channel_id=1, source_target_pairs={{0,64},{64,128},{128,192},{192,256},{256,320},{320,384},{384,448},... | collective-permute-start | bytes 196616 | tf_op jit(solution)/shard_map/ppermute | solution.py:423
  92.2 1.3 collective-permute-start.5
  93.5 0.0 collective-permute-done.4.refs_6_.refs_2_
  93.5 1.4 %terms.1 = (f32[64,1,128]{2,1,0:T(1,128)}, f32[1,1]{1,0:T(1,128)}) custom-call(f32[16,16,128]{2,1,0:T(8,128)S(1)} %get-tuple-element.69.refs_0_.refs_9_, f32[16,16,128]{2,1,0:T(8,128)S(1)} %get-tuple-element.70.refs_1_.refs_0_, f32[16,16,128]{2,1,0:T(8,128)S(1)} %get-tuple-element.62.refs_5_.refs_2_.refs_8_, ...), custom_call_target="tpu_custom_call" | custom-call | bytes 884744 | tf_op jit(solution)/shard_map/terms/pallas_call | solution.py:101
  94.9 11.0 %all-to-all-start.3 = ((f32[64,1,128]{2,1,0:T(1,128)}), f32[64,1,128]{2,1,0:T(1,128)S(1)}, u32[]{:S(2)}, u32[]{:S(2)}) async-start(f32[64,1,128]{2,1,0:T(1,128)} %get-tuple-element.73), calls=%async_computation.3 | async-start | bytes 65536 | tf_op jit(solution)/shard_map/all_to_all | solution.py:427
  105.9 0.0 collective-permute-done.5.refs_3_
  106.0 3.3 %collective-permute-start.6 = (f32[2,32,128]{2,1,0:T(8,128)S(1)}, f32[2,32,128]{2,1,0:T(8,128)S(1)}, u32[]{:S(2)}, u32[]{:S(2)}) collective-permute-start(f32[2,32,128]{2,1,0:T(8,128)S(1)} %get-tuple-element.75), channel_id=1, source_target_pairs={{0,8},{8,16},{16,24},{24,32},{32,40},{40,48},{48,56},{1,9},{9,17},... | collective-permute-start | bytes 98312 | tf_op jit(solution)/shard_map/ppermute | solution.py:423
  109.3 1.3 collective-permute-start.7
  110.6 0.0 collective-permute-done.6.refs_1_
  110.6 4.6 %all-to-all-done.3.refs_0_ = f32[64,1,128]{2,1,0:T(1,128)S(1)} async-done(((f32[64,1,128]{2,1,0:T(1,128)}), f32[64,1,128]{2,1,0:T(1,128)S(1)}, u32[]{:S(2)}, u32[]{:S(2)}) %all-to-all-start.3) | async-done | bytes 32800 | tf_op jit(solution)/shard_map/all_to_all | solution.py:427
  115.2 0.7 sum_terms.1
  115.9 7.6 %all-to-all-start.4 = ((f32[16,1,128]{2,1,0:T(1,128)}), f32[16,1,128]{2,1,0:T(1,128)S(1)}, u32[]{:S(2)}, u32[]{:S(2)}) async-start(f32[16,1,128]{2,1,0:T(1,128)} %sum_terms.1), calls=%async_computation.4 | async-start | bytes 16384 | tf_op jit(solution)/shard_map/all_to_all | solution.py:427
  123.5 0.0 collective-permute-done.7.refs_2_
  123.5 1.0 assemble_across.1
  124.5 3.0 %collective-permute-start.8 = (f32[1,512]{1,0:T(1,128)S(1)}, f32[1,512]{1,0:T(1,128)S(1)}, u32[]{:S(2)}, u32[]{:S(2)}) collective-permute-start(f32[1,512]{1,0:T(1,128)S(1)} %get-tuple-element.80), channel_id=1, source_target_pairs={{0,1},{1,2},{2,3},{3,4},{4,5},{5,6},{6,7},{8,9},{9,10},{10,11},{11... | collective-permute-start | bytes 6152 | tf_op jit(solution)/shard_map/ppermute | solution.py:423
  127.5 1.9 %collective-permute-start.9 = (f32[1,512]{1,0:T(1,128)S(1)}, f32[1,512]{1,0:T(1,128)S(1)}, u32[]{:S(2)}, u32[]{:S(2)}) collective-permute-start(f32[1,512]{1,0:T(1,128)S(1)} %get-tuple-element.81), channel_id=1, source_target_pairs={{1,0},{2,1},{3,2},{4,3},{5,4},{6,5},{7,6},{9,8},{10,9},{11,10},{12... | collective-permute-start | bytes 6152 | tf_op jit(solution)/shard_map/ppermute | solution.py:423
  130.1 0.0 collective-permute-done.8.refs_4_
  130.1 2.6 %collective-permute-done.9.refs_5_ = f32[1,512]{1,0:T(1,128)S(1)} collective-permute-done((f32[1,512]{1,0:T(1,128)S(1)}, f32[1,512]{1,0:T(1,128)S(1)}, u32[]{:S(2)}, u32[]{:S(2)}) %collective-permute-start.9) | collective-permute-done | bytes 2080 | tf_op jit(solution)/shard_map/ppermute | solution.py:423
  132.7 2.0 %all-to-all-done.4.refs_1_ = f32[16,1,128]{2,1,0:T(1,128)S(1)} async-done(((f32[16,1,128]{2,1,0:T(1,128)}), f32[16,1,128]{2,1,0:T(1,128)S(1)}, u32[]{:S(2)}, u32[]{:S(2)}) %all-to-all-start.4) | async-done | bytes 8224 | tf_op jit(solution)/shard_map/all_to_all | solution.py:427
  134.7 1.8 %update.1 = (f32[16,16,128]{2,1,0:T(8,128)}, f32[16,16,128]{2,1,0:T(8,128)}, f32[16,16,128]{2,1,0:T(8,128)}) custom-call(f32[1]{0:T(128)S(6)} %copy.30.refs_0_, f32[16,1,128]{2,1,0:T(1,128)S(1)} %all-to-all-done.4.refs_1_, f32[1,1]{1,0:T(1,128)} %get-tuple-element.76.refs_2_, f32[2,16,16,128]{3,2,1,0:T(8,128)S(1)} %get-tuple-element.79.refs_3_, ...), custom_call_target="tpu_custom_call" | custom-call | bytes 1191944 | tf_op jit(solution)/shard_map/update/pallas_call | solution.py:101
  (1 shorter events, 0.0 us)
Async XLA Ops:
  0.6 0.7 copy-start
  3.6 32.6 %all-to-all-start = ((f32[16,32,128]{2,1,0:T(8,128)}), f32[16,32,128]{2,1,0:T(8,128)S(1)}, u32[]{:S(2)}, u32[]{:S(2)}) async-start(f32[16,32,128]{2,1,0:T(8,128)} %get-tuple-element.43), calls=%async_computation | async-start | bytes 524288 | tf_op jit(solution)/shard_map/all_to_all | solution.py:427
  37.3 29.5 %all-to-all-start.1 = ((f32[64,8,128]{2,1,0:T(8,128)}), f32[64,8,128]{2,1,0:T(8,128)S(1)}, u32[]{:S(2)}, u32[]{:S(2)}) async-start(f32[64,8,128]{2,1,0:T(8,128)} %get-tuple-element.47), calls=%async_computation.1 | async-start | bytes 524288 | tf_op jit(solution)/shard_map/all_to_all | solution.py:427
  53.6 4.6 %collective-permute-start = (f32[24,128]{1,0:T(8,128)S(1)}, f32[24,128]{1,0:T(8,128)S(1)}, u32[]{:S(2)}, u32[]{:S(2)}) collective-permute-start(f32[24,128]{1,0:T(8,128)S(1)} %get-tuple-element.50), channel_id=1, source_target_pairs={{0,8},{8,16},{16,24},{24,32},{32,40},{40,48},{48,56},{1,9},{9,17},... | collective-permute-start | bytes 36872 | tf_op jit(solution)/shard_map/ppermute | solution.py:423
  56.9 4.9 %collective-permute-start.1 = (f32[24,128]{1,0:T(8,128)S(1)}, f32[24,128]{1,0:T(8,128)S(1)}, u32[]{:S(2)}, u32[]{:S(2)}) collective-permute-start(f32[24,128]{1,0:T(8,128)S(1)} %get-tuple-element.51), channel_id=1, source_target_pairs={{8,0},{16,8},{24,16},{32,24},{40,32},{48,40},{56,48},{9,1},{17,9},... | collective-permute-start | bytes 36872 | tf_op jit(solution)/shard_map/ppermute | solution.py:423
  67.7 19.7 %all-to-all-start.2 = ((f32[64,8,128]{2,1,0:T(8,128)}), f32[64,8,128]{2,1,0:T(8,128)S(1)}, u32[]{:S(2)}, u32[]{:S(2)}) async-start(f32[64,8,128]{2,1,0:T(8,128)} %get-tuple-element.52), calls=%async_computation.2 | async-start | bytes 524288 | tf_op jit(solution)/shard_map/all_to_all | solution.py:427
  74.1 8.5 %collective-permute-start.2 = (f32[1,336]{1,0:T(1,128)S(1)}, f32[1,336]{1,0:T(1,128)S(1)}, u32[]{:S(2)}, u32[]{:S(2)}) collective-permute-start(f32[1,336]{1,0:T(1,128)S(1)} %get-tuple-element.58), channel_id=1, source_target_pairs={{0,1},{1,2},{2,3},{3,4},{4,5},{5,6},{6,7},{8,9},{9,10},{10,11},{11... | collective-permute-start | bytes 4040 | tf_op jit(solution)/shard_map/ppermute | solution.py:423
  77.7 5.2 %collective-permute-start.3 = (f32[1,336]{1,0:T(1,128)S(1)}, f32[1,336]{1,0:T(1,128)S(1)}, u32[]{:S(2)}, u32[]{:S(2)}) collective-permute-start(f32[1,336]{1,0:T(1,128)S(1)} %get-tuple-element.59), channel_id=1, source_target_pairs={{1,0},{2,1},{3,2},{4,3},{5,4},{6,5},{7,6},{9,8},{10,9},{11,10},{12... | collective-permute-start | bytes 4040 | tf_op jit(solution)/shard_map/ppermute | solution.py:423
  89.0 4.4 %collective-permute-start.4 = (f32[2,64,128]{2,1,0:T(8,128)S(1)}, f32[2,64,128]{2,1,0:T(8,128)S(1)}, u32[]{:S(2)}, u32[]{:S(2)}) collective-permute-start(f32[2,64,128]{2,1,0:T(8,128)S(1)} %get-tuple-element.72), channel_id=1, source_target_pairs={{0,64},{64,128},{128,192},{192,256},{256,320},{320,384},{384,448},... | collective-permute-start | bytes 196616 | tf_op jit(solution)/shard_map/ppermute | solution.py:423
  92.2 13.7 %collective-permute-start.5 = (f32[2,64,128]{2,1,0:T(8,128)S(1)}, f32[2,64,128]{2,1,0:T(8,128)S(1)}, u32[]{:S(2)}, u32[]{:S(2)}) collective-permute-start(f32[2,64,128]{2,1,0:T(8,128)S(1)} %get-tuple-element.74), channel_id=1, source_target_pairs={{64,0},{128,64},{192,128},{256,192},{320,256},{384,320},{448,384},... | collective-permute-start | bytes 196616 | tf_op jit(solution)/shard_map/ppermute | solution.py:423
  94.9 20.3 %all-to-all-start.3 = ((f32[64,1,128]{2,1,0:T(1,128)}), f32[64,1,128]{2,1,0:T(1,128)S(1)}, u32[]{:S(2)}, u32[]{:S(2)}) async-start(f32[64,1,128]{2,1,0:T(1,128)} %get-tuple-element.73), calls=%async_computation.3 | async-start | bytes 65536 | tf_op jit(solution)/shard_map/all_to_all | solution.py:427
  106.0 4.6 %collective-permute-start.6 = (f32[2,32,128]{2,1,0:T(8,128)S(1)}, f32[2,32,128]{2,1,0:T(8,128)S(1)}, u32[]{:S(2)}, u32[]{:S(2)}) collective-permute-start(f32[2,32,128]{2,1,0:T(8,128)S(1)} %get-tuple-element.75), channel_id=1, source_target_pairs={{0,8},{8,16},{16,24},{24,32},{32,40},{40,48},{48,56},{1,9},{9,17},... | collective-permute-start | bytes 98312 | tf_op jit(solution)/shard_map/ppermute | solution.py:423
  109.3 14.2 %collective-permute-start.7 = (f32[2,32,128]{2,1,0:T(8,128)S(1)}, f32[2,32,128]{2,1,0:T(8,128)S(1)}, u32[]{:S(2)}, u32[]{:S(2)}) collective-permute-start(f32[2,32,128]{2,1,0:T(8,128)S(1)} %get-tuple-element.78), channel_id=1, source_target_pairs={{8,0},{16,8},{24,16},{32,24},{40,32},{48,40},{56,48},{9,1},{17,9},... | collective-permute-start | bytes 98312 | tf_op jit(solution)/shard_map/ppermute | solution.py:423
  115.9 18.8 %all-to-all-start.4 = ((f32[16,1,128]{2,1,0:T(1,128)}), f32[16,1,128]{2,1,0:T(1,128)S(1)}, u32[]{:S(2)}, u32[]{:S(2)}) async-start(f32[16,1,128]{2,1,0:T(1,128)} %sum_terms.1), calls=%async_computation.4 | async-start | bytes 16384 | tf_op jit(solution)/shard_map/all_to_all | solution.py:427
  124.5 5.6 %collective-permute-start.8 = (f32[1,512]{1,0:T(1,128)S(1)}, f32[1,512]{1,0:T(1,128)S(1)}, u32[]{:S(2)}, u32[]{:S(2)}) collective-permute-start(f32[1,512]{1,0:T(1,128)S(1)} %get-tuple-element.80), channel_id=1, source_target_pairs={{0,1},{1,2},{2,3},{3,4},{4,5},{5,6},{6,7},{8,9},{9,10},{10,11},{11... | collective-permute-start | bytes 6152 | tf_op jit(solution)/shard_map/ppermute | solution.py:423
  127.5 5.2 %collective-permute-start.9 = (f32[1,512]{1,0:T(1,128)S(1)}, f32[1,512]{1,0:T(1,128)S(1)}, u32[]{:S(2)}, u32[]{:S(2)}) collective-permute-start(f32[1,512]{1,0:T(1,128)S(1)} %get-tuple-element.81), channel_id=1, source_target_pairs={{1,0},{2,1},{3,2},{4,3},{5,4},{6,5},{7,6},{9,8},{10,9},{11,10},{12... | collective-permute-start | bytes 6152 | tf_op jit(solution)/shard_map/ppermute | solution.py:423

commit v6 on v5

--- a/solution.py
+++ b/solution.py
@@ -1,5 +1,3 @@
-import functools
-
 import jax
 import jax.numpy as jnp
 import numpy as np
@@ -126,91 +124,61 @@
     )(*args)
 
 
-def coarse_kernel(ready, blocks, me, residual, ids, values, payload, ids_wide):
+def coarse_kernel(ready, blocks, residual, ids, values, dense, ids_wide, to_high, to_low):
     nx, ny, nz = residual.shape
     ex, ey = nx // N, ny // N
     ez = ids.shape[1]
     n_stored, coarse, _ = values.shape
-    n_line, head = payload.shape[0], payload.shape[1] - ny
     widen = (
         lax.broadcasted_iota(jnp.int32, (ez, nz), 1) // N
         == lax.broadcasted_iota(jnp.int32, (ez, nz), 0)
     ).astype(F32)
-    payload[...] = jnp.zeros_like(payload)
-    at = me[0]
-    lane = lax.broadcasted_iota(jnp.int32, (1, nz), 1)
-    numbers = jnp.zeros((1, nz), F32)
-    for k in range(n_stored):
-        numbers = jnp.where(lane == n_stored * at + k, blocks[k].astype(F32), numbers)
-    ready(3)
+    dense[...] = jnp.zeros_like(dense)
+    ready(2)
     wide = mm(ids[...].astype(F32), widen)
     ids_wide[...] = wide
     unknown = lax.broadcasted_iota(jnp.int32, (coarse, nz), 0).astype(F32)
     total = jnp.zeros((coarse, nz), F32)
-    ready(2)
-
-    @pl.when(at + 1 < n_line)
-    def _():
-        payload[at + 1, head:, :] = residual[nx - 2]
-
-    @pl.when(at > 0)
-    def _():
-        payload[at - 1, head:, :] = residual[1]
-
+    ready(1)
+    to_high[...] = residual[nx - 2]
+    to_low[...] = residual[1]
     for a in range(ex):
         for b in range(ey):
             part = jnp.sum(residual[a * N : a * N + N, b * N : b * N + N, :], axis=(0, 1))[None]
             q = a * ey + b
             total = total + jnp.where(jnp.abs(unknown - wide[q : q + 1]) < 0.5, part, 0.0)
     coarse_residual = jnp.sum(total, axis=1, keepdims=True)
-    ready(4)
-    row = lax.broadcasted_iota(jnp.int32, (head, nz), 0)
-    lines = jnp.where(row == n_stored, numbers, 0.0)
+    ready(3)
     for k in range(n_stored):
-        lines = jnp.where(
-            row == k, jnp.sum(values[k] * coarse_residual, axis=0, keepdims=True), lines
-        )
-    for i in range(n_line):
-        payload[i, :head, :] = lines
-
-
-def line_kernel(
-    n_stored, ready, me, parts, residual, after1, after2, dense, x_low, x_high, to_high, to_low
-):
+        at = pl.ds(blocks[k], 1)
+        row = jnp.sum(values[k] * coarse_residual, axis=0, keepdims=True)
+        dense[at, :] = dense[at, :] + row
+
+
+def spread_sum(parts, out):
+    total = jnp.sum(parts[...], axis=0)
+    for i in range(out.shape[0]):
+        out[i] = total
+
+
+def across_kernel(ready, parts, residual, low, high, after1, after2, owned, to_high, to_low):
+    spread_sum(parts, owned)
     nx, ny, nz = residual.shape
-    n_line = parts.shape[0]
-    head = parts.shape[1] - ny
-    at = me[0]
-    rows = parts[:, :n_stored, :].reshape(n_line * n_stored, nz)
-    if rows.shape[0] < nz:
-        rows = jnp.concatenate([rows, jnp.zeros((nz - rows.shape[0], nz), F32)])
-    numbers = jnp.sum(parts[:, n_stored : n_stored + 1, :], axis=0)
-    n_blocks = dense.shape[0] * dense.shape[1]
-    block = lax.broadcasted_iota(jnp.int32, (n_blocks, nz), 0).astype(F32)
-    place = (jnp.abs(block - numbers) < 0.5).astype(F32)
-    dense[...] = mm(place, rows).reshape(dense.shape)
-    before, behind = jnp.maximum(at - 1, 0), jnp.minimum(at + 1, n_line - 1)
-    x_low[...] = jnp.where(at > 0, parts[before, head:, :], 0.0)
-    x_high[...] = jnp.where(at + 1 < n_line, parts[behind, head:, :], 0.0)
     for out, y in ((to_high, ny - 2), (to_low, 1)):
         out[...] = jnp.zeros_like(out)
         out[:nx] = residual[:, y, :]
-        out[nx : nx + 1] = x_low[y : y + 1]
-        out[nx + 1 : nx + 2] = x_high[y : y + 1]
+        out[nx : nx + 1] = low[y : y + 1]
+        out[nx + 1 : nx + 2] = high[y : y + 1]
 
 
 def spread_sum_kernel(ready, parts, after, out):
-    total = jnp.sum(parts[...], axis=0)
-    for i in range(out.shape[0]):
-        out[i] = total
-
-
-def plane_kernel(
-    ready, parts, residual, x_low, x_high, y_low, y_high, owned, every, to_high, to_low
-):
-    total = jnp.sum(parts[...], axis=0)
-    for i in range(owned.shape[0]):
-        owned[i] = total
+    spread_sum(parts, out)
+
+
+def depth_kernel(
+    ready, parts, residual, x_low, x_high, y_low, y_high, after, owned, every, to_high, to_low
+):
+    spread_sum(parts, owned)
     nx, ny, nz = residual.shape
     at = 0
     for ref in (None, x_low, x_high, y_low, y_high):
@@ -225,21 +193,31 @@
     to_low[...] = ends[1:2]
 
 
-def matrices_kernel(
-    ready, basis, tile2, mask2, tilez, maskz, row_x, row_y, col_x, col_y, out_x, out_y, col_z, in_z,
-    to_spectral, from_spectral, to_z, from_z,
-):
-    ready(*range(13))
-    flat2 = mm(mm(tile2[...], basis[...]), tile2[...], 1, 1) * mask2[...]
-    flatz = mm(mm(tilez[...], basis[...]), tilez[...], 1, 1) * maskz[...]
+def tiled(tile, basis, mask):
+    return mm(mm(tile[...], basis[...]), tile[...], 1, 1) * mask[...]
+
+
+def to_spectral_kernel(
+    ready, basis, tile2, mask2, tilez, maskz, row_x, row_y, col_x, col_y, col_z, to_spectral, to_z
+):
+    ready(*range(10))
+    flat2 = tiled(tile2, basis, mask2)
     to_x = mm(row_x[...], mm(flat2, col_x[...], 0, 0))
     to_y = mm(row_y[...], mm(flat2, col_y[...], 0, 0))
     to_spectral[...] = to_x * to_y
+    to_z[...] = mm(col_z[...], tiled(tilez, basis, maskz))
+
+
+def from_spectral_kernel(
+    ready, basis, tile2, mask2, tilez, maskz, row_x, row_y, out_x, out_y, in_z, from_spectral,
+    from_z,
+):
+    ready(*range(10))
+    flat2 = tiled(tile2, basis, mask2)
     from_x = mm(mm(out_x[...], flat2), row_x[...], 1, 1)
     from_y = mm(mm(out_y[...], flat2), row_y[...], 1, 1)
     from_spectral[...] = from_x * from_y
-    to_z[...] = mm(col_z[...], flatz)
-    from_z[...] = mm(flatz, in_z[...], 0, 0)
+    from_z[...] = mm(tiled(tilez, basis, maskz), in_z[...], 0, 0)
 
 
 def spectral_kernel(ready, every, to_spectral, to_z, spectral):
@@ -289,9 +267,10 @@
         target[x] = mass[x] * source[x] + value + yz[x * ny : (x + 1) * ny]
 
 
-def operator_kernel(ready, direction, conductance, mass, ky, ky_t, kz, kz_t, image):
+def operator_kernel(ready, direction, conductance, mass, ky, ky_t, kz, kz_t, image, third):
     ready(0, 1, 2, 3, 4, 5, 6)
     operator(direction, conductance, mass, ky, ky_t, kz, kz_t, image)
+    third[...] = total_of(jnp.sum(direction[...] * image[...], axis=0))
 
 
 def total_of(values):
@@ -327,23 +306,23 @@
 
 
 def terms_kernel(
-    ready, z, image, direction, image_direction, inner_local, coarse_inner, after, terms, square
-):
-    first = jnp.sum(z[...] * image[...], axis=0)
-    second = jnp.sum(z[...] * image_direction[...] + direction[...] * image[...], axis=0)
-    third = jnp.sum(direction[...] * image_direction[...], axis=0)
+    ready, z, image, direction, image_direction, inner_local, third, after, terms
+):
+    first = total_of(jnp.sum(z[...] * image[...], axis=0))
+    second = z[...] * image_direction[...] + direction[...] * image[...]
+    second = total_of(jnp.sum(second, axis=0))
     lane = lax.broadcasted_iota(jnp.int32, (1, terms.shape[2]), 1)
     line = jnp.where(lane == 0, inner_local[...], 0.0)
-    for i, value in enumerate((first, second, third)):
-        line = jnp.where(lane == i + 1, total_of(value), line)
+    for i, value in enumerate((first, second, third[...])):
+        line = jnp.where(lane == i + 1, value, line)
     for i in range(terms.shape[0]):
         terms[i] = line
+
+
+def assemble_length_kernel(
+    ready, image, image_direction, low, high, coarse_inner, out, to_high, to_low, square
+):
     square[...] = total_of(coarse_inner[...] * coarse_inner[...])
-
-
-def assemble_length_kernel(
-    ready, image, image_direction, low, high, out, to_high, to_low
-):
     nx, ny, nz = image.shape
     for i, ref in ((0, image), (1, image_direction)):
         out[i] = ref[...]
@@ -376,40 +355,40 @@
     to_low[...] = ends[1:2]
 
 
-def update_kernel(
-    ready, prior, terms, square, images, low, high, residual, solution, direction, z,
-    new_solution, new_residual, new_direction,
-):
-    nx, ny, nz = residual.shape
-    rows = nx * ny
-    lane1 = lax.broadcasted_iota(jnp.int32, (1, nz), 1)
-    sums = jnp.sum(terms[...], axis=0)
-
-    def term(i):
-        return jnp.sum(jnp.where(lane1 == i, sums, 0.0), axis=1, keepdims=True)
-
-    inner = term(0) + square[...]
-    ratio = inner / prior[0]
-    alpha = inner / (term(1) + ratio * term(2) + ratio * ratio * term(3))
-    new = z[...].reshape(rows, nz) + ratio * direction[...].reshape(rows, nz)
-    new_direction[...] = new.reshape(nx, ny, nz)
-    new_solution[...] = (solution[...].reshape(rows, nz) + alpha * new).reshape(nx, ny, nz)
-    image = images[0].reshape(rows, nz) + ratio * images[1].reshape(rows, nz)
+def assemble_depth_kernel(ready, images, low, high, out):
+    _, nx, ny, nz = images.shape
+    rows = 2 * nx * ny
+    image = images[...].reshape(rows, nz)
     row = lax.broadcasted_iota(jnp.int32, (8, rows), 0)
-    low_line = low[:, :rows] + ratio * low[:, rows:]
-    high_line = high[:, :rows] + ratio * high[:, rows:]
-    ends = jnp.where(row == 0, low_line, jnp.where(row == 1, high_line, 0.0))
+    ends = jnp.where(row == 0, low[...], jnp.where(row == 1, high[...], 0.0))
     row = lax.broadcasted_iota(jnp.int32, (8, nz), 0)
     lane = lax.broadcasted_iota(jnp.int32, (8, nz), 1)
     place = ((row == 0) & (lane == 0)) | ((row == 1) & (lane == nz - 1))
     outer = mm(jnp.transpose(ends), place.astype(F32))
     lane = lax.broadcasted_iota(jnp.int32, (rows, nz), 1)
-    above = pltpu.roll(image, nz - 1, 1)
-    below = pltpu.roll(image, 1, 1)
-    above = jnp.where((lane % N == N - 1) & (lane < nz - 1), above, 0.0)
-    below = jnp.where((lane % N == 0) & (lane > 0), below, 0.0)
-    image = image + above + below + outer
-    new_residual[...] = (residual[...].reshape(rows, nz) - alpha * image).reshape(nx, ny, nz)
+    above = jnp.where((lane % N == N - 1) & (lane < nz - 1), pltpu.roll(image, nz - 1, 1), 0.0)
+    below = jnp.where((lane % N == 0) & (lane > 0), pltpu.roll(image, 1, 1), 0.0)
+    out[...] = (image + above + below + outer).reshape(out.shape)
+
+
+def update_kernel(
+    ready, prior, terms, square, images, residual, solution, direction, z,
+    new_solution, new_residual, new_direction,
+):
+    lane = lax.broadcasted_iota(jnp.int32, (1, terms.shape[2]), 1)
+    sums = jnp.sum(terms[...], axis=0)
+
+    def term(i):
+        return jnp.sum(jnp.where(lane == i, sums, 0.0), axis=1, keepdims=True)
+
+    inner = term(0) + square[...]
+    ratio = inner / prior[0]
+    alpha = inner / (term(1) + ratio * term(2) + ratio * ratio * term(3))
+    ratio, alpha = ratio[None], alpha[None]
+    new = z[...] + ratio * direction[...]
+    new_direction[...] = new
+    new_solution[...] = solution[...] + alpha * new
+    new_residual[...] = residual[...] - alpha * (images[0] + ratio * images[1])
 
 
 def shifts(axis):
@@ -450,22 +429,20 @@
     own = n_blocks // n_plane
 
     ids = element_coarse_index.reshape(ex * ey, ez)
-    me = lax.axis_index("gx").astype(jnp.int32).reshape(1)
-    head = up8(xxt_values.shape[0] + 1)
-    assert xxt_values.shape[0] * n_line <= nz
-    payload, ids_wide, residual, xxt_values = call(
-        coarse_kernel, "coarse_restrict", [(n_line, head + ny, nz), (ex * ey, nz)],
-        xxt_blocks, me, residual, ids, xxt_values, smem=(0, 1), load=(3,), keep=(2, 4), pin=(1,),
-    )
-    parts = spread(payload, "gx")
+    dense, ids_wide, to_high, to_low, residual, xxt_values = call(
+        coarse_kernel, "coarse_restrict", [(n_blocks, block), (ex * ey, nz), (ny, nz), (ny, nz)],
+        xxt_blocks, residual, ids, xxt_values, smem=(0,), load=(2,), keep=(1, 3), pin=(1,),
+    )
+    parts = spread(dense.reshape(n_plane, own, block), plane)
+    x_low, x_high = exchange(to_high, to_low, "gx")
 
     cheb = cheb_matrix()
     ky = np.kron(np.eye(nx, dtype=np.float32), np.kron(np.eye(ey, dtype=np.float32), cheb))
     kz = np.kron(np.eye(ez, dtype=np.float32), cheb)
     tables = [jnp.asarray(np.ascontiguousarray(t)) for t in (ky, ky.T, kz, kz.T)]
-    image_direction, direction, conductance, mass_term, *tables = call(
-        operator_kernel, "operator_direction", [direction.shape],
-        direction, conductance, mass_term, *tables, keep=tuple(range(7)), pin=(0,),
+    image_direction, third, direction, conductance, mass_term, *tables = call(
+        operator_kernel, "operator_direction", [direction.shape, (1, 1)],
+        direction, conductance, mass_term, *tables, keep=tuple(range(7)), pin=(0, 1),
     )
 
     face = up8(nx + 2)
@@ -484,41 +461,38 @@
     col_x = (extended_positions(ex)[:, None] == cols_x[None, :]).astype(np.float32)
     col_y = (extended_positions(ey)[:, None] == cols_y[None, :]).astype(np.float32)
     assert ex == ey
-    to_spectral, from_spectral, to_z, from_z = call(
-        matrices_kernel, "basis_matrices",
-        [(n_x * high_y, n_every), (rows, n_x * high_y), (nz + 8, n_z), (n_z, nz)],
-        eigen_basis,
-        *map(
-            jnp.asarray,
-            (
-                np.tile(np.eye(E, dtype=np.float32), (ex, 1)),
-                np.kron(np.eye(ex), np.ones((E, E))).astype(np.float32),
-                np.tile(np.eye(E, dtype=np.float32), (ez, 1)),
-                np.kron(np.eye(ez), np.ones((E, E))).astype(np.float32),
-                row_x.astype(np.float32),
-                row_y,
-                col_x,
-                col_y,
-                one_hot(np.repeat(inside_positions(ex), ny), n_x),
-                one_hot(np.tile(inside_positions(ey), nx), n_y),
-                np.ascontiguousarray(one_hot(extended_positions(ez), nz + 8).T),
-                np.ascontiguousarray(one_hot(inside_positions(ez), n_z).T),
-            ),
-        ),
-        load=tuple(range(13)), store=(0, 1, 2, 3),
-    )
-
-    dense, x_low, x_high, to_high, to_low = call(
-        functools.partial(line_kernel, xxt_values.shape[0]), "line_sum",
-        [(n_plane, own, block), (ny, nz), (ny, nz), (face, nz), (face, nz)],
-        me, parts, residual, image_direction, from_z, smem=(0,), pin=(1, 2), idle=(4,),
-    )
-    parts = spread(dense, plane)
+    shared = [
+        np.tile(np.eye(E, dtype=np.float32), (ex, 1)),
+        np.kron(np.eye(ex), np.ones((E, E))).astype(np.float32),
+        np.tile(np.eye(E, dtype=np.float32), (ez, 1)),
+        np.kron(np.eye(ez), np.ones((E, E))).astype(np.float32),
+        row_x.astype(np.float32),
+        row_y,
+    ]
+    shared = [eigen_basis, *map(jnp.asarray, shared)]
+    to_spectral, to_z = call(
+        to_spectral_kernel, "to_spectral", [(n_x * high_y, n_every), (nz + 8, n_z)],
+        *shared, jnp.asarray(col_x), jnp.asarray(col_y),
+        jnp.asarray(np.ascontiguousarray(one_hot(extended_positions(ez), nz + 8).T)),
+        load=tuple(range(10)), store=(0, 1),
+    )
+    from_spectral, from_z = call(
+        from_spectral_kernel, "from_spectral", [(rows, n_x * high_y), (n_z, nz)],
+        *shared, jnp.asarray(one_hot(np.repeat(inside_positions(ex), ny), n_x)),
+        jnp.asarray(one_hot(np.tile(inside_positions(ey), nx), n_y)),
+        jnp.asarray(np.ascontiguousarray(one_hot(inside_positions(ez), n_z).T)),
+        load=tuple(range(10)), store=(0, 1),
+    )
+    owned, to_high, to_low = call(
+        across_kernel, "plane_sum", [(n_line, own, block), (face, nz), (face, nz)],
+        parts, residual, x_low, x_high, image_direction, to_z, idle=(5,),
+    )
+    parts = spread(owned, "gx")
     y_low, y_high = exchange(to_high, to_low, "gy")
     owned, every, to_high, to_low = call(
-        plane_kernel, "plane_sum",
+        depth_kernel, "line_sum",
         [(n_plane, own, block), (n_every, nz), (1, n_every), (1, n_every)],
-        parts, residual, x_low, x_high, y_low, y_high, pin=(1,),
+        parts, residual, x_low, x_high, y_low, y_high, from_z, pin=(1,), idle=(6,),
     )
     coarse_inner = spread(owned, plane).reshape(n_blocks, block)
     z_low, z_high = exchange(to_high, to_low, "gz")
@@ -539,14 +513,15 @@
         image_direction, conductance, mass_term, *tables, smem=(0,), pin=(0, 1),
     )
     low, high = exchange(to_high, to_low, "gx")
-    terms, square = call(
-        terms_kernel, "terms", [(n_plane, 1, nz), (1, 1)],
-        z, image, direction, image_direction, inner_local, coarse_inner, low, pin=(1,),
+    (terms,) = call(
+        terms_kernel, "terms", [(n_plane, 1, nz)],
+        z, image, direction, image_direction, inner_local, third, low,
     )
     parts = spread(terms, plane)
-    images, to_high, to_low = call(
-        assemble_length_kernel, "assemble_length", [(2, nx, ny, nz), (2, 2 * nx, nz), (2, 2 * nx, nz)],
-        image, image_direction, low, high, pin=(0,),
+    images, to_high, to_low, square = call(
+        assemble_length_kernel, "assemble_length",
+        [(2, nx, ny, nz), (2, 2 * nx, nz), (2, 2 * nx, nz), (1, 1)],
+        image, image_direction, low, high, coarse_inner, pin=(0, 3),
     )
     low, high = exchange(to_high, to_low, "gy")
     (terms,) = call(spread_sum_kernel, "sum_terms", [(n_line, 1, nz)], parts, low)
@@ -556,11 +531,13 @@
         images, low, high, solution, keep=(3,), pin=(0,),
     )
     low, high = exchange(to_high, to_low, "gz")
+    (images,) = call(
+        assemble_depth_kernel, "assemble_depth", [images.shape], images, low, high, pin=(0,)
+    )
     return tuple(
         call(
             update_kernel, "update", [direction.shape] * 3,
-            prior_inner, parts, square, images, low, high, residual, solution, direction, z,
-            smem=(0,),
+            prior_inner, parts, square, images, residual, solution, direction, z, smem=(0,),
         )
     )
 

time: 137 us -> 143 us (1.044)
  waiting for transfers between devices: 23 us -> 13.6 us
  starting transfers between devices: 84.9 us -> 94.2 us
  Pallas kernels: 26.4 us -> 31.7 us
    all_to_all x5, starting transfers between devices: 60.8 us -> 67.8 us  [spread(): return lax.all_to_all(values, axes, 0, 0, tiled=False)]
    all_to_all x5, waiting for transfers between devices: 16.5 us -> 10.7 us  [spread(): return lax.all_to_all(values, axes, 0, 0, tiled=False)]
    pallas_call x13 -> x15, Pallas kernels: 26.4 us -> 31.7 us  [call(): pl.pallas_call(whole, out_shape=[pltpu.VMEM(o, F32) if i in pin else pltp...]
    ppermute x5 -> x6, waiting for transfers between devices: 6.47 us -> 2.86 us  [exchange(): lax.ppermute(to_low, axis, backward)]
    ppermute x5 -> x6, starting transfers between devices: 7.9 us -> 9.19 us  [exchange(): lax.ppermute(to_low, axis, backward)]
    ppermute x5 -> x6, starting transfers between devices: 16.3 us -> 17.2 us  [exchange(): lax.ppermute(to_high, axis, forward)]
  transfers between devices with their start and end apart: 15 -> 17, of which waited for: 7 -> 6; matrix products, arithmetic and copies ran while one was open for 0% -> 0% of each run, Pallas kernels for 14% -> 17%
where the time goes in v6:
time: 143 us; the launch traced here: 142 us
  starting transfers between devices  94.2 us (66%)
  Pallas kernels  31.7 us (22%)
  waiting for transfers between devices  13.6 us (10%)
  between operations  1.57 us (1%)
    all_to_all x5, starting transfers between devices, spread(): return lax.all_to_all(values, axes, 0, 0, tiled=False)  67.8 us
    pallas_call x15, Pallas kernels, call(): pl.pallas_call(whole, out_shape=[pltpu.VMEM(o, F32) if i in pin else pltp...  31.7 us
    ppermute x6, starting transfers between devices, exchange(): lax.ppermute(to_high, axis, forward)  17.2 us
    all_to_all x5, waiting for transfers between devices, spread(): return lax.all_to_all(values, axes, 0, 0, tiled=False)  10.7 us
    ppermute x6, starting transfers between devices, exchange(): lax.ppermute(to_low, axis, backward)  9.19 us
    ppermute x6, waiting for transfers between devices, exchange(): lax.ppermute(to_low, axis, backward)  2.86 us
  transfers between devices with their start and end apart: 17, of which 6 were waited for; matrix products, arithmetic and copies ran while one was open for 0% of the time, Pallas kernels for 17%

profile of v6, /device:TPU:1, one launch (start us, length us, event | category | flops | bytes accessed | tf_op | source)
XLA Modules:
  0.0 141.7 jit_solution(16767108792142781991)
XLA Ops:
  0.6 0.6 copy-done
  1.3 2.4 %coarse_restrict.1 = (f32[512,128]{1,0:T(8,128)}, f32[4,128]{1,0:T(4,128)S(1)}, f32[16,128]{1,0:T(8,128)S(1)}, f32[16,128]{1,0:T(8,128)S(1)}, f32[16,16,128]{2,1,0:T(8,128)S(1)}, /*index=5*/f32[8,64,128]{2,1,0:T(8,128)S(1)}) custom-call(s32[8]{0:T(128)S(1)} %copy-done, f32[16,16,128]{2,1,0:T(8,128)} %refs_1_.4, s32[4,16]{1,0:T(4,128)} %bitcast.5, ...), custom_call_target="tpu_custom_call" | custom-call | bytes 674080 | tf_op jit(solution)/shard_map/coarse_restrict/pallas_call | solution.py:99
  3.7 18.2 %all-to-all-start = ((f32[64,8,128]{2,1,0:T(8,128)}), f32[64,8,128]{2,1,0:T(8,128)S(1)}, u32[]{:S(2)}, u32[]{:S(2)}) async-start(f32[64,8,128]{2,1,0:T(8,128)} %bitcast.1), calls=%async_computation | async-start | bytes 524288 | tf_op jit(solution)/shard_map/all_to_all | solution.py:406
  21.9 1.3 collective-permute-start
  23.2 1.3 collective-permute-start.1
  24.5 2.9 %operator_direction.1 = (f32[16,16,128]{2,1,0:T(8,128)S(1)}, f32[1,1]{1,0:T(1,128)}, f32[16,16,128]{2,1,0:T(8,128)S(1)}, f32[3,16,16,128]{3,2,1,0:T(8,128)S(1)},...) custom-call(f32[16,16,128]{2,1,0:T(8,128)} %refs_0_.7, ...), custom_call_target="tpu_custom_call" | custom-call | bytes 1441796 | tf_op jit(solution)/shard_map/operator_direction/pallas_call | solution.py:99
  27.4 4.8 %to_spectral.1 = (f32[480,336]{1,0:T(8,128)}, f32[136,160]{1,0:T(8,128)}) custom-call(f32[10,10]{1,0:T(8,128)} %refs_0_.9, f32[20,10]{1,0:T(8,128)} %constant.36.clone.refs_1_, f32[20,20]{1,0:T(8,128)} %constant.37.clone.refs_2_, f32[160,10]{1,0:T(8,128)} %constant.38.clone.refs_3_, f32[160,160]{1,0:T(8,128)} %constant.39.clone.refs_4_, ...), custom_call_target="tpu_custom_call" | custom-call | bytes 1061360 | tf_op jit(solution)/shard_map/to_spectral/pallas_call | solution.py:99
  32.1 0.0 collective-permute-done.refs_2_
  32.1 0.0 collective-permute-done.1.refs_3_
  32.1 3.0 %all-to-all-done.refs_0_ = f32[64,8,128]{2,1,0:T(8,128)S(1)} async-done(((f32[64,8,128]{2,1,0:T(8,128)}), f32[64,8,128]{2,1,0:T(8,128)S(1)}, u32[]{:S(2)}, u32[]{:S(2)}) %all-to-all-start) | async-done | bytes 262176 | tf_op jit(solution)/shard_map/all_to_all | solution.py:406
  35.1 0.7 plane_sum.1
  35.8 12.9 %all-to-all-start.1 = ((f32[16,8,128]{2,1,0:T(8,128)}), f32[16,8,128]{2,1,0:T(8,128)S(1)}, u32[]{:S(2)}, u32[]{:S(2)}) async-start(f32[16,8,128]{2,1,0:T(8,128)} %get-tuple-element.49), calls=%async_computation.1 | async-start | bytes 131072 | tf_op jit(solution)/shard_map/all_to_all | solution.py:406
  48.8 3.3 %collective-permute-start.2 = (f32[24,128]{1,0:T(8,128)S(1)}, f32[24,128]{1,0:T(8,128)S(1)}, u32[]{:S(2)}, u32[]{:S(2)}) collective-permute-start(f32[24,128]{1,0:T(8,128)S(1)} %get-tuple-element.50), channel_id=1, source_target_pairs={{0,8},{8,16},{16,24},{24,32},{32,40},{40,48},{48,56},{1,9},{9,17},... | collective-permute-start | bytes 36872 | tf_op jit(solution)/shard_map/ppermute | solution.py:402
  52.1 1.3 collective-permute-start.3
  53.4 4.9 %from_spectral.1 = (f32[256,480]{1,0:T(8,128)}, f32[160,128]{1,0:T(8,128)}) custom-call(f32[10,10]{1,0:T(8,128)} %refs_0_.9, f32[20,10]{1,0:T(8,128)} %constant.36.clone.refs_1_, f32[20,20]{1,0:T(8,128)} %constant.37.clone.refs_2_, f32[160,10]{1,0:T(8,128)} %constant.38.clone.refs_3_, f32[160,160]{1,0:T(8,128)} %constant.39.clone.refs_4_, ...), custom_call_target="tpu_custom_call" | custom-call | bytes 884720 | tf_op jit(solution)/shard_map/from_spectral/pallas_call | solution.py:99
  58.2 0.0 collective-permute-done.3.refs_5_
  58.3 2.1 %all-to-all-done.1.refs_0_ = f32[16,8,128]{2,1,0:T(8,128)S(1)} async-done(((f32[16,8,128]{2,1,0:T(8,128)}), f32[16,8,128]{2,1,0:T(8,128)S(1)}, u32[]{:S(2)}, u32[]{:S(2)}) %all-to-all-start.1) | async-done | bytes 65568 | tf_op jit(solution)/shard_map/all_to_all | solution.py:406
  60.4 0.9 line_sum.1
  61.3 12.3 %all-to-all-start.2 = ((f32[64,8,128]{2,1,0:T(8,128)}), f32[64,8,128]{2,1,0:T(8,128)S(1)}, u32[]{:S(2)}, u32[]{:S(2)}) async-start(f32[64,8,128]{2,1,0:T(8,128)} %get-tuple-element.53), calls=%async_computation.2 | async-start | bytes 524288 | tf_op jit(solution)/shard_map/all_to_all | solution.py:406
  73.6 3.5 %collective-permute-start.4 = (f32[1,336]{1,0:T(1,128)S(1)}, f32[1,336]{1,0:T(1,128)S(1)}, u32[]{:S(2)}, u32[]{:S(2)}) collective-permute-start(f32[1,336]{1,0:T(1,128)S(1)} %get-tuple-element.58), channel_id=1, source_target_pairs={{0,1},{1,2},{2,3},{3,4},{4,5},{5,6},{6,7},{8,9},{9,10},{10,11},{11... | collective-permute-start | bytes 4040 | tf_op jit(solution)/shard_map/ppermute | solution.py:402
  77.1 2.1 %collective-permute-start.5 = (f32[1,336]{1,0:T(1,128)S(1)}, f32[1,336]{1,0:T(1,128)S(1)}, u32[]{:S(2)}, u32[]{:S(2)}) collective-permute-start(f32[1,336]{1,0:T(1,128)S(1)} %get-tuple-element.59), channel_id=1, source_target_pairs={{1,0},{2,1},{3,2},{4,3},{5,4},{6,5},{7,6},{9,8},{10,9},{11,10},{12... | collective-permute-start | bytes 4040 | tf_op jit(solution)/shard_map/ppermute | solution.py:402
  79.2 2.8 %element_spectral.1.refs_0_ = f32[480,160]{1,0:T(8,128)S(1)} custom-call(f32[336,128]{1,0:T(8,128)S(1)} %get-tuple-element.56.refs_0_, f32[480,336]{1,0:T(8,128)} %get-tuple-element.57.refs_1_.refs_3_, f32[136,160]{1,0:T(8,128)} %get-tuple-element.48.refs_5_.refs_2_), custom_call_target="tpu_custom_call" | custom-call | bytes 1211392 | tf_op jit(solution)/shard_map/element_spectral/pallas_call | solution.py:99
  82.0 0.0 collective-permute-done.4.refs_1_
  82.1 0.2 collective-permute-done.5.refs_2_
  82.3 4.6 %element_solve.1 = (f32[256,128]{1,0:T(8,128)S(1)}, f32[1,1]{1,0:T(1,128)}) custom-call(f32[480,160]{1,0:T(8,128)S(1)} %element_spectral.1.refs_0_, f32[1,336]{1,0:T(1,128)S(1)} %collective-permute-done.4.refs_1_, f32[1,336]{1,0:T(1,128)S(1)} %collective-permute-done.5.refs_2_, f32[480,336]{1,0:T(8,128)} %get-tuple-element.57.refs_1_.refs_3_, ...), custom_call_target="tpu_custom_call" | custom-call | bytes 2002564 | tf_op jit(solution)/shard_map/element_solve/pallas_call | solution.py:99
  86.9 0.0 all-to-all-done.2
  86.9 1.6 %coarse_correct.1 = (f32[16,16,128]{2,1,0:T(8,128)S(1)}, f32[16,16,128]{2,1,0:T(8,128)S(1)}, f32[2,64,128]{2,1,0:T(8,128)S(1)}, f32[2,64,128]{2,1,0:T(8,128)S(1)}) custom-call(s32[8]{0:T(128)S(1)} %copy-done, f32[512,128]{1,0:T(8,128)S(1)} %bitcast.3, f32[8,64,128]{2,1,0:T(8,128)S(1)} %get-tuple-element.54.refs_2_, f32[4,128]{1,0:T(4,128)S(1)} %get-tuple-element.55.refs_3_, ...), custom_call_target="tpu_custom_call" | custom-call | bytes 2492448 | tf_op jit(solution)/shard_map/coarse_correct/pallas_call | solution.py:99
  88.5 2.8 %collective-permute-start.6 = (f32[2,64,128]{2,1,0:T(8,128)S(1)}, f32[2,64,128]{2,1,0:T(8,128)S(1)}, u32[]{:S(2)}, u32[]{:S(2)}) collective-permute-start(f32[2,64,128]{2,1,0:T(8,128)S(1)} %get-tuple-element.73), channel_id=1, source_target_pairs={{0,64},{64,128},{128,192},{192,256},{256,320},{320,384},{384,448},... | collective-permute-start | bytes 196616 | tf_op jit(solution)/shard_map/ppermute | solution.py:402
  91.3 1.3 collective-permute-start.7
  92.6 0.0 collective-permute-done.6.refs_6_.refs_2_
  92.6 2.0 %terms.1 = f32[64,1,128]{2,1,0:T(1,128)} custom-call(f32[16,16,128]{2,1,0:T(8,128)S(1)} %get-tuple-element.69.refs_0_.refs_7_, f32[16,16,128]{2,1,0:T(8,128)S(1)} %get-tuple-element.70.refs_1_.refs_0_, f32[16,16,128]{2,1,0:T(8,128)S(1)} %get-tuple-element.62.refs_5_.refs_2_.refs_6_, f32[16,16,128]{2,1,0:T(8,128)S(1)} %get-tuple-element.47.refs_4_.refs_6_.refs_3_.refs_1_, ...), custom_call_target="tpu_custom_call" | custom-call | bytes 622600 | tf_op jit(solution)/shard_map/terms/pallas_call | solution.py:99
  94.6 11.0 %all-to-all-start.3 = ((f32[64,1,128]{2,1,0:T(1,128)}), f32[64,1,128]{2,1,0:T(1,128)S(1)}, u32[]{:S(2)}, u32[]{:S(2)}) async-start(f32[64,1,128]{2,1,0:T(1,128)} %terms.1), calls=%async_computation.3 | async-start | bytes 65536 | tf_op jit(solution)/shard_map/all_to_all | solution.py:406
  105.6 0.7 assemble_length.1
  106.3 3.3 %collective-permute-start.8 = (f32[2,32,128]{2,1,0:T(8,128)S(1)}, f32[2,32,128]{2,1,0:T(8,128)S(1)}, u32[]{:S(2)}, u32[]{:S(2)}) collective-permute-start(f32[2,32,128]{2,1,0:T(8,128)S(1)} %get-tuple-element.75), channel_id=1, source_target_pairs={{0,8},{8,16},{16,24},{24,32},{32,40},{40,48},{48,56},{1,9},{9,17},... | collective-permute-start | bytes 98312 | tf_op jit(solution)/shard_map/ppermute | solution.py:402
  109.6 1.3 collective-permute-start.9
  110.9 0.0 collective-permute-done.8.refs_1_
  110.9 4.0 %all-to-all-done.3.refs_0_ = f32[64,1,128]{2,1,0:T(1,128)S(1)} async-done(((f32[64,1,128]{2,1,0:T(1,128)}), f32[64,1,128]{2,1,0:T(1,128)S(1)}, u32[]{:S(2)}, u32[]{:S(2)}) %all-to-all-start.3) | async-done | bytes 32800 | tf_op jit(solution)/shard_map/all_to_all | solution.py:406
  114.9 0.7 sum_terms.1
  115.6 13.4 %all-to-all-start.4 = ((f32[16,1,128]{2,1,0:T(1,128)}), f32[16,1,128]{2,1,0:T(1,128)S(1)}, u32[]{:S(2)}, u32[]{:S(2)}) async-start(f32[16,1,128]{2,1,0:T(1,128)} %sum_terms.1), calls=%async_computation.4 | async-start | bytes 16384 | tf_op jit(solution)/shard_map/all_to_all | solution.py:406
  129.0 0.0 collective-permute-done.9.refs_2_
  129.0 1.0 assemble_across.1
  130.0 3.0 %collective-permute-start.10 = (f32[1,512]{1,0:T(1,128)S(1)}, f32[1,512]{1,0:T(1,128)S(1)}, u32[]{:S(2)}, u32[]{:S(2)}) collective-permute-start(f32[1,512]{1,0:T(1,128)S(1)} %get-tuple-element.80), channel_id=1, source_target_pairs={{0,1},{1,2},{2,3},{3,4},{4,5},{5,6},{6,7},{8,9},{9,10},{10,11},{11... | collective-permute-start | bytes 6152 | tf_op jit(solution)/shard_map/ppermute | solution.py:402
  133.0 1.9 %collective-permute-start.11 = (f32[1,512]{1,0:T(1,128)S(1)}, f32[1,512]{1,0:T(1,128)S(1)}, u32[]{:S(2)}, u32[]{:S(2)}) collective-permute-start(f32[1,512]{1,0:T(1,128)S(1)} %get-tuple-element.81), channel_id=1, source_target_pairs={{1,0},{2,1},{3,2},{4,3},{5,4},{6,5},{7,6},{9,8},{10,9},{11,10},{12... | collective-permute-start | bytes 6152 | tf_op jit(solution)/shard_map/ppermute | solution.py:402
  135.6 0.0 collective-permute-done.10.refs_1_
  135.6 2.6 %collective-permute-done.11.refs_2_ = f32[1,512]{1,0:T(1,128)S(1)} collective-permute-done((f32[1,512]{1,0:T(1,128)S(1)}, f32[1,512]{1,0:T(1,128)S(1)}, u32[]{:S(2)}, u32[]{:S(2)}) %collective-permute-start.11) | collective-permute-done | bytes 2080 | tf_op jit(solution)/shard_map/ppermute | solution.py:402
  138.2 0.4 assemble_depth.1.refs_3_
  138.7 1.6 %all-to-all-done.4.refs_1_ = f32[16,1,128]{2,1,0:T(1,128)S(1)} async-done(((f32[16,1,128]{2,1,0:T(1,128)}), f32[16,1,128]{2,1,0:T(1,128)S(1)}, u32[]{:S(2)}, u32[]{:S(2)}) %all-to-all-start.4) | async-done | bytes 8224 | tf_op jit(solution)/shard_map/all_to_all | solution.py:406
  140.2 1.5 %update.1 = (f32[16,16,128]{2,1,0:T(8,128)}, f32[16,16,128]{2,1,0:T(8,128)}, f32[16,16,128]{2,1,0:T(8,128)}) custom-call(f32[1]{0:T(128)S(6)} %copy.30.refs_0_, f32[16,1,128]{2,1,0:T(1,128)S(1)} %all-to-all-done.4.refs_1_, f32[1,1]{1,0:T(1,128)} %get-tuple-element.76.refs_2_, f32[2,16,16,128]{3,2,1,0:T(8,128)S(1)} %assemble_depth.1.refs_3_, ...), custom_call_target="tpu_custom_call" | custom-call | bytes 1187848 | tf_op jit(solution)/shard_map/update/pallas_call | solution.py:99
  (3 shorter events, 0.0 us)
Async XLA Ops:
  0.6 0.7 copy-start
  3.7 31.5 %all-to-all-start = ((f32[64,8,128]{2,1,0:T(8,128)}), f32[64,8,128]{2,1,0:T(8,128)S(1)}, u32[]{:S(2)}, u32[]{:S(2)}) async-start(f32[64,8,128]{2,1,0:T(8,128)} %bitcast.1), calls=%async_computation | async-start | bytes 524288 | tf_op jit(solution)/shard_map/all_to_all | solution.py:406
  21.9 10.3 %collective-permute-start = (f32[16,128]{1,0:T(8,128)S(1)}, f32[16,128]{1,0:T(8,128)S(1)}, u32[]{:S(2)}, u32[]{:S(2)}) collective-permute-start(f32[16,128]{1,0:T(8,128)S(1)} %get-tuple-element.45), channel_id=1, source_target_pairs={{0,64},{64,128},{128,192},{192,256},{256,320},{320,384},{384,448},... | collective-permute-start | bytes 24584 | tf_op jit(solution)/shard_map/ppermute | solution.py:402
  23.2 9.0 %collective-permute-start.1 = (f32[16,128]{1,0:T(8,128)S(1)}, f32[16,128]{1,0:T(8,128)S(1)}, u32[]{:S(2)}, u32[]{:S(2)}) collective-permute-start(f32[16,128]{1,0:T(8,128)S(1)} %get-tuple-element.46), channel_id=1, source_target_pairs={{64,0},{128,64},{192,128},{256,192},{320,256},{384,320},{448,384},... | collective-permute-start | bytes 24584 | tf_op jit(solution)/shard_map/ppermute | solution.py:402
  35.8 24.6 %all-to-all-start.1 = ((f32[16,8,128]{2,1,0:T(8,128)}), f32[16,8,128]{2,1,0:T(8,128)S(1)}, u32[]{:S(2)}, u32[]{:S(2)}) async-start(f32[16,8,128]{2,1,0:T(8,128)} %get-tuple-element.49), calls=%async_computation.1 | async-start | bytes 131072 | tf_op jit(solution)/shard_map/all_to_all | solution.py:406
  48.8 9.5 %collective-permute-start.2 = (f32[24,128]{1,0:T(8,128)S(1)}, f32[24,128]{1,0:T(8,128)S(1)}, u32[]{:S(2)}, u32[]{:S(2)}) collective-permute-start(f32[24,128]{1,0:T(8,128)S(1)} %get-tuple-element.50), channel_id=1, source_target_pairs={{0,8},{8,16},{16,24},{24,32},{32,40},{40,48},{48,56},{1,9},{9,17},... | collective-permute-start | bytes 36872 | tf_op jit(solution)/shard_map/ppermute | solution.py:402
  52.1 6.2 %collective-permute-start.3 = (f32[24,128]{1,0:T(8,128)S(1)}, f32[24,128]{1,0:T(8,128)S(1)}, u32[]{:S(2)}, u32[]{:S(2)}) collective-permute-start(f32[24,128]{1,0:T(8,128)S(1)} %get-tuple-element.51), channel_id=1, source_target_pairs={{8,0},{16,8},{24,16},{32,24},{40,32},{48,40},{56,48},{9,1},{17,9},... | collective-permute-start | bytes 36872 | tf_op jit(solution)/shard_map/ppermute | solution.py:402
  61.3 25.6 %all-to-all-start.2 = ((f32[64,8,128]{2,1,0:T(8,128)}), f32[64,8,128]{2,1,0:T(8,128)S(1)}, u32[]{:S(2)}, u32[]{:S(2)}) async-start(f32[64,8,128]{2,1,0:T(8,128)} %get-tuple-element.53), calls=%async_computation.2 | async-start | bytes 524288 | tf_op jit(solution)/shard_map/all_to_all | solution.py:406
  73.6 8.5 %collective-permute-start.4 = (f32[1,336]{1,0:T(1,128)S(1)}, f32[1,336]{1,0:T(1,128)S(1)}, u32[]{:S(2)}, u32[]{:S(2)}) collective-permute-start(f32[1,336]{1,0:T(1,128)S(1)} %get-tuple-element.58), channel_id=1, source_target_pairs={{0,1},{1,2},{2,3},{3,4},{4,5},{5,6},{6,7},{8,9},{9,10},{10,11},{11... | collective-permute-start | bytes 4040 | tf_op jit(solution)/shard_map/ppermute | solution.py:402
  77.1 5.2 %collective-permute-start.5 = (f32[1,336]{1,0:T(1,128)S(1)}, f32[1,336]{1,0:T(1,128)S(1)}, u32[]{:S(2)}, u32[]{:S(2)}) collective-permute-start(f32[1,336]{1,0:T(1,128)S(1)} %get-tuple-element.59), channel_id=1, source_target_pairs={{1,0},{2,1},{3,2},{4,3},{5,4},{6,5},{7,6},{9,8},{10,9},{11,10},{12... | collective-permute-start | bytes 4040 | tf_op jit(solution)/shard_map/ppermute | solution.py:402
  88.5 4.1 %collective-permute-start.6 = (f32[2,64,128]{2,1,0:T(8,128)S(1)}, f32[2,64,128]{2,1,0:T(8,128)S(1)}, u32[]{:S(2)}, u32[]{:S(2)}) collective-permute-start(f32[2,64,128]{2,1,0:T(8,128)S(1)} %get-tuple-element.73), channel_id=1, source_target_pairs={{0,64},{64,128},{128,192},{192,256},{256,320},{320,384},{384,448},... | collective-permute-start | bytes 196616 | tf_op jit(solution)/shard_map/ppermute | solution.py:402
  91.3 14.4 %collective-permute-start.7 = (f32[2,64,128]{2,1,0:T(8,128)S(1)}, f32[2,64,128]{2,1,0:T(8,128)S(1)}, u32[]{:S(2)}, u32[]{:S(2)}) collective-permute-start(f32[2,64,128]{2,1,0:T(8,128)S(1)} %get-tuple-element.74), channel_id=1, source_target_pairs={{64,0},{128,64},{192,128},{256,192},{320,256},{384,320},{448,384},... | collective-permute-start | bytes 196616 | tf_op jit(solution)/shard_map/ppermute | solution.py:402
  94.6 20.3 %all-to-all-start.3 = ((f32[64,1,128]{2,1,0:T(1,128)}), f32[64,1,128]{2,1,0:T(1,128)S(1)}, u32[]{:S(2)}, u32[]{:S(2)}) async-start(f32[64,1,128]{2,1,0:T(1,128)} %terms.1), calls=%async_computation.3 | async-start | bytes 65536 | tf_op jit(solution)/shard_map/all_to_all | solution.py:406
  106.3 4.6 %collective-permute-start.8 = (f32[2,32,128]{2,1,0:T(8,128)S(1)}, f32[2,32,128]{2,1,0:T(8,128)S(1)}, u32[]{:S(2)}, u32[]{:S(2)}) collective-permute-start(f32[2,32,128]{2,1,0:T(8,128)S(1)} %get-tuple-element.75), channel_id=1, source_target_pairs={{0,8},{8,16},{16,24},{24,32},{32,40},{40,48},{48,56},{1,9},{9,17},... | collective-permute-start | bytes 98312 | tf_op jit(solution)/shard_map/ppermute | solution.py:402
  109.6 19.4 %collective-permute-start.9 = (f32[2,32,128]{2,1,0:T(8,128)S(1)}, f32[2,32,128]{2,1,0:T(8,128)S(1)}, u32[]{:S(2)}, u32[]{:S(2)}) collective-permute-start(f32[2,32,128]{2,1,0:T(8,128)S(1)} %get-tuple-element.78), channel_id=1, source_target_pairs={{8,0},{16,8},{24,16},{32,24},{40,32},{48,40},{56,48},{9,1},{17,9},... | collective-permute-start | bytes 98312 | tf_op jit(solution)/shard_map/ppermute | solution.py:402
  115.6 24.6 %all-to-all-start.4 = ((f32[16,1,128]{2,1,0:T(1,128)}), f32[16,1,128]{2,1,0:T(1,128)S(1)}, u32[]{:S(2)}, u32[]{:S(2)}) async-start(f32[16,1,128]{2,1,0:T(1,128)} %sum_terms.1), calls=%async_computation.4 | async-start | bytes 16384 | tf_op jit(solution)/shard_map/all_to_all | solution.py:406
  130.0 5.6 %collective-permute-start.10 = (f32[1,512]{1,0:T(1,128)S(1)}, f32[1,512]{1,0:T(1,128)S(1)}, u32[]{:S(2)}, u32[]{:S(2)}) collective-permute-start(f32[1,512]{1,0:T(1,128)S(1)} %get-tuple-element.80), channel_id=1, source_target_pairs={{0,1},{1,2},{2,3},{3,4},{4,5},{5,6},{6,7},{8,9},{9,10},{10,11},{11... | collective-permute-start | bytes 6152 | tf_op jit(solution)/shard_map/ppermute | solution.py:402
  133.0 5.2 %collective-permute-start.11 = (f32[1,512]{1,0:T(1,128)S(1)}, f32[1,512]{1,0:T(1,128)S(1)}, u32[]{:S(2)}, u32[]{:S(2)}) collective-permute-start(f32[1,512]{1,0:T(1,128)S(1)} %get-tuple-element.81), channel_id=1, source_target_pairs={{1,0},{2,1},{3,2},{4,3},{5,4},{6,5},{7,6},{9,8},{10,9},{11,10},{12... | collective-permute-start | bytes 6152 | tf_op jit(solution)/shard_map/ppermute | solution.py:402

commit v7 on v5

--- a/solution.py
+++ b/solution.py
@@ -51,9 +51,23 @@
     )
 
 
-def call(kernel, name, outs, *args, smem=(), load=(), keep=(), scratch=(), pin=(), store=(), idle=()):
+def halves(a):
+    high = a.astype(jnp.bfloat16)
+    return high, (a - high.astype(F32)).astype(jnp.bfloat16)
+
+
+def mm3(a, b):
+    (a_high, a_low), (b_high, b_low) = halves(a), halves(b)
+
+    def product(x, y):
+        return jnp.dot(x, y, preferred_element_type=F32)
+
+    return product(a_high, b_high) + (product(a_high, b_low) + product(a_low, b_high))
+
+
+def call(kernel, name, outs, *args, smem=(), load=(), keep=(), scratch=(), pin=(), store=(), idle=(), numbers=()):
     count, n_out, n_keep = len(args), len(outs), len(keep)
-    moved = sorted((*load, *keep))
+    moved = sorted((*load, *keep, *numbers))
     vmem = pl.BlockSpec(memory_space=pltpu.VMEM)
 
     def whole(*refs):
@@ -88,7 +102,11 @@
         for copy in copies:
             copy.wait()
 
-    buffers = [pltpu.VMEM(args[i].shape, args[i].dtype) for i in moved if i not in keep]
+    buffers = [
+        (pltpu.SMEM if i in numbers else pltpu.VMEM)(args[i].shape, args[i].dtype)
+        for i in moved
+        if i not in keep
+    ]
     specs = []
     for i in range(count):
         space = pltpu.SMEM if i in smem else pltpu.HBM if i in (*moved, *idle) else pltpu.VMEM
@@ -126,7 +144,7 @@
     )(*args)
 
 
-def coarse_kernel(ready, blocks, me, residual, ids, values, payload, ids_wide):
+def coarse_kernel(ready, blocks, me, residual, ids, values, kept, payload, ids_wide):
     nx, ny, nz = residual.shape
     ex, ey = nx // N, ny // N
     ez = ids.shape[1]
@@ -138,10 +156,6 @@
     ).astype(F32)
     payload[...] = jnp.zeros_like(payload)
     at = me[0]
-    lane = lax.broadcasted_iota(jnp.int32, (1, nz), 1)
-    numbers = jnp.zeros((1, nz), F32)
-    for k in range(n_stored):
-        numbers = jnp.where(lane == n_stored * at + k, blocks[k].astype(F32), numbers)
     ready(3)
     wide = mm(ids[...].astype(F32), widen)
     ids_wide[...] = wide
@@ -164,6 +178,11 @@
             total = total + jnp.where(jnp.abs(unknown - wide[q : q + 1]) < 0.5, part, 0.0)
     coarse_residual = jnp.sum(total, axis=1, keepdims=True)
     ready(4)
+    ready(0)
+    lane = lax.broadcasted_iota(jnp.int32, (1, nz), 1)
+    numbers = jnp.zeros((1, nz), F32)
+    for k in range(n_stored):
+        numbers = jnp.where(lane == n_stored * at + k, blocks[k].astype(F32), numbers)
     row = lax.broadcasted_iota(jnp.int32, (head, nz), 0)
     lines = jnp.where(row == n_stored, numbers, 0.0)
     for k in range(n_stored):
@@ -244,7 +263,7 @@
 
 def spectral_kernel(ready, every, to_spectral, to_z, spectral):
     ready(1, 2)
-    spectral[...] = mm(mm(to_spectral[...], every[...]), to_z[: every.shape[1], :])
+    spectral[...] = mm3(mm3(to_spectral[...], every[...]), to_z[: every.shape[1], :])
 
 
 def solve_kernel(
@@ -260,9 +279,11 @@
     ready(7)
     wide[:, :n_y, :] = sums[...]
     weighted = wide[...].reshape(-1, n_z) * spectral
-    inner[...] = jnp.sum(jnp.sum(weighted * spectral, axis=0, keepdims=True), axis=1, keepdims=True)
+    line = jnp.sum(weighted * spectral, axis=0, keepdims=True)
+    wide_line = jnp.concatenate([line, jnp.zeros((1, 256 - n_z), F32)], axis=1)
+    inner[...] = folded((wide_line[:, :128] + wide_line[:, 128:])[None])
     ready(4, 6)
-    local_part[...] = mm(mm(from_spectral[...], weighted), from_z[...])
+    local_part[...] = mm3(mm3(from_spectral[...], weighted), from_z[...])
 
 
 def derive(matrix, slabs):
@@ -289,9 +310,10 @@
         target[x] = mass[x] * source[x] + value + yz[x * ny : (x + 1) * ny]
 
 
-def operator_kernel(ready, direction, conductance, mass, ky, ky_t, kz, kz_t, image):
+def operator_kernel(ready, direction, conductance, mass, ky, ky_t, kz, kz_t, image, third):
     ready(0, 1, 2, 3, 4, 5, 6)
     operator(direction, conductance, mass, ky, ky_t, kz, kz_t, image)
+    third[...] = folded(direction[...] * image[...])
 
 
 def total_of(values):
@@ -326,24 +348,26 @@
         out[1, :ny] = image_direction[x]
 
 
-def terms_kernel(
-    ready, z, image, direction, image_direction, inner_local, coarse_inner, after, terms, square
-):
-    first = jnp.sum(z[...] * image[...], axis=0)
-    second = jnp.sum(z[...] * image_direction[...] + direction[...] * image[...], axis=0)
-    third = jnp.sum(direction[...] * image_direction[...], axis=0)
-    lane = lax.broadcasted_iota(jnp.int32, (1, terms.shape[2]), 1)
-    line = jnp.where(lane == 0, inner_local[...], 0.0)
-    for i, value in enumerate((first, second, third)):
-        line = jnp.where(lane == i + 1, total_of(value), line)
+def folded(values):
+    line = jnp.sum(jnp.sum(values, axis=0), axis=0, keepdims=True)
+    line = line + pltpu.roll(line, 64, 1)
+    return line + pltpu.roll(line, 32, 1)
+
+
+def terms_kernel(ready, z, image, direction, image_direction, inner_local, third, after, terms):
+    first = folded(z[...] * image[...])
+    second = folded(z[...] * image_direction[...] + direction[...] * image[...])
+    group = lax.broadcasted_iota(jnp.int32, (1, terms.shape[2]), 1) // 32
+    line = jnp.where(group == 0, inner_local[...], third[...])
+    line = jnp.where(group == 1, first, jnp.where(group == 2, second, line))
     for i in range(terms.shape[0]):
         terms[i] = line
+
+
+def assemble_length_kernel(
+    ready, image, image_direction, low, high, coarse_inner, out, to_high, to_low, square
+):
     square[...] = total_of(coarse_inner[...] * coarse_inner[...])
-
-
-def assemble_length_kernel(
-    ready, image, image_direction, low, high, out, to_high, to_low
-):
     nx, ny, nz = image.shape
     for i, ref in ((0, image), (1, image_direction)):
         out[i] = ref[...]
@@ -376,40 +400,40 @@
     to_low[...] = ends[1:2]
 
 
-def update_kernel(
-    ready, prior, terms, square, images, low, high, residual, solution, direction, z,
-    new_solution, new_residual, new_direction,
-):
-    nx, ny, nz = residual.shape
-    rows = nx * ny
-    lane1 = lax.broadcasted_iota(jnp.int32, (1, nz), 1)
-    sums = jnp.sum(terms[...], axis=0)
-
-    def term(i):
-        return jnp.sum(jnp.where(lane1 == i, sums, 0.0), axis=1, keepdims=True)
-
-    inner = term(0) + square[...]
-    ratio = inner / prior[0]
-    alpha = inner / (term(1) + ratio * term(2) + ratio * ratio * term(3))
-    new = z[...].reshape(rows, nz) + ratio * direction[...].reshape(rows, nz)
-    new_direction[...] = new.reshape(nx, ny, nz)
-    new_solution[...] = (solution[...].reshape(rows, nz) + alpha * new).reshape(nx, ny, nz)
-    image = images[0].reshape(rows, nz) + ratio * images[1].reshape(rows, nz)
+def assemble_depth_kernel(ready, images, low, high, out):
+    _, nx, ny, nz = images.shape
+    rows = 2 * nx * ny
+    image = images[...].reshape(rows, nz)
     row = lax.broadcasted_iota(jnp.int32, (8, rows), 0)
-    low_line = low[:, :rows] + ratio * low[:, rows:]
-    high_line = high[:, :rows] + ratio * high[:, rows:]
-    ends = jnp.where(row == 0, low_line, jnp.where(row == 1, high_line, 0.0))
+    ends = jnp.where(row == 0, low[...], jnp.where(row == 1, high[...], 0.0))
     row = lax.broadcasted_iota(jnp.int32, (8, nz), 0)
     lane = lax.broadcasted_iota(jnp.int32, (8, nz), 1)
     place = ((row == 0) & (lane == 0)) | ((row == 1) & (lane == nz - 1))
     outer = mm(jnp.transpose(ends), place.astype(F32))
     lane = lax.broadcasted_iota(jnp.int32, (rows, nz), 1)
-    above = pltpu.roll(image, nz - 1, 1)
-    below = pltpu.roll(image, 1, 1)
-    above = jnp.where((lane % N == N - 1) & (lane < nz - 1), above, 0.0)
-    below = jnp.where((lane % N == 0) & (lane > 0), below, 0.0)
-    image = image + above + below + outer
-    new_residual[...] = (residual[...].reshape(rows, nz) - alpha * image).reshape(nx, ny, nz)
+    above = jnp.where((lane % N == N - 1) & (lane < nz - 1), pltpu.roll(image, nz - 1, 1), 0.0)
+    below = jnp.where((lane % N == 0) & (lane > 0), pltpu.roll(image, 1, 1), 0.0)
+    out[...] = (image + above + below + outer).reshape(out.shape)
+
+
+def update_kernel(
+    ready, prior, terms, square, images, residual, solution, direction, z,
+    new_solution, new_residual, new_direction,
+):
+    lane = lax.broadcasted_iota(jnp.int32, (1, terms.shape[2]), 1)
+    sums = jnp.sum(terms[...], axis=0)
+
+    def term(i):
+        return jnp.sum(jnp.where(lane // 32 == i, sums, 0.0), axis=1, keepdims=True)
+
+    inner = term(0) + square[...]
+    ratio = inner / prior[0]
+    alpha = inner / (term(1) + ratio * term(2) + ratio * ratio * term(3))
+    ratio, alpha = ratio[None], alpha[None]
+    new = z[...] + ratio * direction[...]
+    new_direction[...] = new
+    new_solution[...] = solution[...] + alpha * new
+    new_residual[...] = residual[...] - alpha * (images[0] + ratio * images[1])
 
 
 def shifts(axis):
@@ -453,9 +477,11 @@
     me = lax.axis_index("gx").astype(jnp.int32).reshape(1)
     head = up8(xxt_values.shape[0] + 1)
     assert xxt_values.shape[0] * n_line <= nz
-    payload, ids_wide, residual, xxt_values = call(
+    payload, ids_wide, residual, xxt_values, block_numbers = call(
         coarse_kernel, "coarse_restrict", [(n_line, head + ny, nz), (ex * ey, nz)],
-        xxt_blocks, me, residual, ids, xxt_values, smem=(0, 1), load=(3,), keep=(2, 4), pin=(1,),
+        xxt_blocks, me, residual, ids, xxt_values, xxt_blocks, smem=(1,), load=(3,), keep=(2, 4, 5),
+        pin=(1,),
+        numbers=(0,),
     )
     parts = spread(payload, "gx")
 
@@ -463,9 +489,9 @@
     ky = np.kron(np.eye(nx, dtype=np.float32), np.kron(np.eye(ey, dtype=np.float32), cheb))
     kz = np.kron(np.eye(ez, dtype=np.float32), cheb)
     tables = [jnp.asarray(np.ascontiguousarray(t)) for t in (ky, ky.T, kz, kz.T)]
-    image_direction, direction, conductance, mass_term, *tables = call(
-        operator_kernel, "operator_direction", [direction.shape],
-        direction, conductance, mass_term, *tables, keep=tuple(range(7)), pin=(0,),
+    image_direction, third, direction, conductance, mass_term, *tables = call(
+        operator_kernel, "operator_direction", [direction.shape, (1, nz)],
+        direction, conductance, mass_term, *tables, keep=tuple(range(7)), pin=(0, 1),
     )
 
     face = up8(nx + 2)
@@ -527,7 +553,7 @@
         every, to_spectral, to_z, load=(1, 2), pin=(0,),
     )
     local_part, inner_local = call(
-        solve_kernel, "element_solve", [(rows, nz), (1, 1)],
+        solve_kernel, "element_solve", [(rows, nz), (1, nz)],
         spectral, z_low, z_high, to_spectral, from_spectral, to_z, from_z, inverse_eigen_sums,
         load=(3, 4, 5, 6, 7), pin=(0, 1), scratch=(pltpu.VMEM((n_x, high_y, n_z), F32),),
     )
@@ -535,18 +561,19 @@
     z, image, to_high, to_low = call(
         correct_kernel, "coarse_correct",
         [direction.shape, direction.shape, (2, 4 * ny, nz), (2, 4 * ny, nz)],
-        xxt_blocks, coarse_inner, xxt_values, ids_wide, local_part, direction,
+        block_numbers, coarse_inner, xxt_values, ids_wide, local_part, direction,
         image_direction, conductance, mass_term, *tables, smem=(0,), pin=(0, 1),
     )
     low, high = exchange(to_high, to_low, "gx")
-    terms, square = call(
-        terms_kernel, "terms", [(n_plane, 1, nz), (1, 1)],
-        z, image, direction, image_direction, inner_local, coarse_inner, low, pin=(1,),
+    (terms,) = call(
+        terms_kernel, "terms", [(n_plane, 1, nz)],
+        z, image, direction, image_direction, inner_local, third, low,
     )
     parts = spread(terms, plane)
-    images, to_high, to_low = call(
-        assemble_length_kernel, "assemble_length", [(2, nx, ny, nz), (2, 2 * nx, nz), (2, 2 * nx, nz)],
-        image, image_direction, low, high, pin=(0,),
+    images, to_high, to_low, square = call(
+        assemble_length_kernel, "assemble_length",
+        [(2, nx, ny, nz), (2, 2 * nx, nz), (2, 2 * nx, nz), (1, 1)],
+        image, image_direction, low, high, coarse_inner, pin=(0, 3),
     )
     low, high = exchange(to_high, to_low, "gy")
     (terms,) = call(spread_sum_kernel, "sum_terms", [(n_line, 1, nz)], parts, low)
@@ -556,11 +583,13 @@
         images, low, high, solution, keep=(3,), pin=(0,),
     )
     low, high = exchange(to_high, to_low, "gz")
+    (images,) = call(
+        assemble_depth_kernel, "assemble_depth", [images.shape], images, low, high, pin=(0,)
+    )
     return tuple(
         call(
             update_kernel, "update", [direction.shape] * 3,
-            prior_inner, parts, square, images, low, high, residual, solution, direction, z,
-            smem=(0,),
+            prior_inner, parts, square, images, residual, solution, direction, z, smem=(0,),
         )
     )
 

time: 137 us -> 134 us (0.978)
    pallas_call x13 -> x14, Pallas kernels: 26.4 us -> 25.1 us  [call(): pl.pallas_call(whole, out_shape=[pltpu.VMEM(o, F32) if i in pin else pltp...]
  transfers between devices with their start and end apart: 15 -> 15, of which waited for: 7 -> 8; matrix products, arithmetic and copies ran while one was open for 0% -> 0% of each run, Pallas kernels for 14% -> 14%
where the time goes in v7:
time: 134 us; the launch traced here: 133 us
  starting transfers between devices  83.6 us (62%)
  Pallas kernels  25.1 us (19%)
  waiting for transfers between devices  23 us (17%)
  between operations  1.52 us (1%)
    all_to_all x5, starting transfers between devices, spread(): return lax.all_to_all(values, axes, 0, 0, tiled=False)  59.6 us
    pallas_call x14, Pallas kernels, call(): pl.pallas_call(whole, out_shape=[pltpu.VMEM(o, F32) if i in pin else pltp...  25.1 us
    ppermute x5, starting transfers between devices, exchange(): lax.ppermute(to_high, axis, forward)  16.3 us
    all_to_all x5, waiting for transfers between devices, spread(): return lax.all_to_all(values, axes, 0, 0, tiled=False)  15.6 us
    ppermute x5, starting transfers between devices, exchange(): lax.ppermute(to_low, axis, backward)  7.72 us
    ppermute x5, waiting for transfers between devices, exchange(): lax.ppermute(to_low, axis, backward)  7.32 us
  transfers between devices with their start and end apart: 15, of which 8 were waited for; matrix products, arithmetic and copies ran while one was open for 0% of the time, Pallas kernels for 14%

profile of v7, /device:TPU:1, one launch (start us, length us, event | category | flops | bytes accessed | tf_op | source)
XLA Modules:
  0.0 133.2 jit_solution(17771140913780849684)
XLA Ops:
  0.6 1.8 %coarse_restrict.1 = (f32[16,32,128]{2,1,0:T(8,128)}, f32[4,128]{1,0:T(4,128)S(1)}, f32[16,16,128]{2,1,0:T(8,128)S(1)}, f32[8,64,128]{2,1,0:T(8,128)S(1)}, s32[8]{0:T(128)S(1)}) custom-call(s32[8]{0:T(128)} %refs_5_.3, s32[1]{0:T(128)} %bitcast.refs_1_.refs_0_, f32[16,16,128]{2,1,0:T(8,128)} %refs_2_.3, s32[4,16]{1,0:T(4,128)} %bitcast.5, ...), custom_call_target="tpu_custom_call" | custom-call | bytes 657732 | tf_op jit(solution)/shard_map/coarse_restrict/pallas_call | solution.py:119
  2.5 19.4 %all-to-all-start = ((f32[16,32,128]{2,1,0:T(8,128)}), f32[16,32,128]{2,1,0:T(8,128)S(1)}, u32[]{:S(2)}, u32[]{:S(2)}) async-start(f32[16,32,128]{2,1,0:T(8,128)} %get-tuple-element.45), calls=%async_computation | async-start | bytes 524288 | tf_op jit(solution)/shard_map/all_to_all | solution.py:451
  21.9 2.4 %operator_direction.1 = (f32[16,16,128]{2,1,0:T(8,128)S(1)}, f32[1,128]{1,0:T(1,128)S(1)}, f32[16,16,128]{2,1,0:T(8,128)S(1)}, f32[3,16,16,128]{3,2,1,0:T(8,128)...) custom-call(f32[16,16,128]{2,1,0:T(8,128)} %refs_0_.5, ...), custom_call_target="tpu_custom_call" | custom-call | bytes 1442304 | tf_op jit(solution)/shard_map/operator_direction/pallas_call | solution.py:119
  24.3 5.9 %basis_matrices.1 = (f32[480,336]{1,0:T(8,128)}, f32[256,480]{1,0:T(8,128)}, f32[136,160]{1,0:T(8,128)}, f32[160,128]{1,0:T(8,128)}) custom-call(f32[10,10]{1,0:T(8,128)} %refs_0_.6, f32[20,10]{1,0:T(8,128)} %constant.42.clone.refs_1_, f32[20,20]{1,0:T(8,128)} %constant.43.clone.refs_2_, f32[160,10]{1,0:T(8,128)} %constant.44.clone.refs_3_, ...), custom_call_target="tpu_custom_call" | custom-call | bytes 1757680 | tf_op jit(solution)/shard_map/basis_matrices/pallas_call | solution.py:119
  30.2 4.8 %all-to-all-done.refs_1_ = f32[16,32,128]{2,1,0:T(8,128)S(1)} async-done(((f32[16,32,128]{2,1,0:T(8,128)}), f32[16,32,128]{2,1,0:T(8,128)S(1)}, u32[]{:S(2)}, u32[]{:S(2)}) %all-to-all-start) | async-done | bytes 262176 | tf_op jit(solution)/shard_map/all_to_all | solution.py:451
  35.0 1.1 line_sum.1
  36.1 16.3 %all-to-all-start.1 = ((f32[64,8,128]{2,1,0:T(8,128)}), f32[64,8,128]{2,1,0:T(8,128)S(1)}, u32[]{:S(2)}, u32[]{:S(2)}) async-start(f32[64,8,128]{2,1,0:T(8,128)} %get-tuple-element.49), calls=%async_computation.1 | async-start | bytes 524288 | tf_op jit(solution)/shard_map/all_to_all | solution.py:451
  52.4 3.3 %collective-permute-start = (f32[24,128]{1,0:T(8,128)S(1)}, f32[24,128]{1,0:T(8,128)S(1)}, u32[]{:S(2)}, u32[]{:S(2)}) collective-permute-start(f32[24,128]{1,0:T(8,128)S(1)} %get-tuple-element.52), channel_id=1, source_target_pairs={{0,8},{8,16},{16,24},{24,32},{32,40},{40,48},{48,56},{1,9},{9,17},... | collective-permute-start | bytes 36872 | tf_op jit(solution)/shard_map/ppermute | solution.py:447
  55.7 1.3 collective-permute-start.1
  57.0 0.0 collective-permute-done.refs_4_
  57.0 3.6 %collective-permute-done.1.refs_5_ = f32[24,128]{1,0:T(8,128)S(1)} collective-permute-done((f32[24,128]{1,0:T(8,128)S(1)}, f32[24,128]{1,0:T(8,128)S(1)}, u32[]{:S(2)}, u32[]{:S(2)}) %collective-permute-start.1) | collective-permute-done | bytes 12320 | tf_op jit(solution)/shard_map/ppermute | solution.py:447
  60.6 4.9 %all-to-all-done.1.refs_0_ = f32[64,8,128]{2,1,0:T(8,128)S(1)} async-done(((f32[64,8,128]{2,1,0:T(8,128)}), f32[64,8,128]{2,1,0:T(8,128)S(1)}, u32[]{:S(2)}, u32[]{:S(2)}) %all-to-all-start.1) | async-done | bytes 262176 | tf_op jit(solution)/shard_map/all_to_all | solution.py:451
  65.6 0.9 plane_sum.1
  66.5 6.4 %all-to-all-start.2 = ((f32[64,8,128]{2,1,0:T(8,128)}), f32[64,8,128]{2,1,0:T(8,128)S(1)}, u32[]{:S(2)}, u32[]{:S(2)}) async-start(f32[64,8,128]{2,1,0:T(8,128)} %get-tuple-element.54), calls=%async_computation.2 | async-start | bytes 524288 | tf_op jit(solution)/shard_map/all_to_all | solution.py:451
  72.9 3.5 %collective-permute-start.2 = (f32[1,336]{1,0:T(1,128)S(1)}, f32[1,336]{1,0:T(1,128)S(1)}, u32[]{:S(2)}, u32[]{:S(2)}) collective-permute-start(f32[1,336]{1,0:T(1,128)S(1)} %get-tuple-element.60), channel_id=1, source_target_pairs={{0,1},{1,2},{2,3},{3,4},{4,5},{5,6},{6,7},{8,9},{9,10},{10,11},{11... | collective-permute-start | bytes 4040 | tf_op jit(solution)/shard_map/ppermute | solution.py:447
  76.5 1.9 %collective-permute-start.3 = (f32[1,336]{1,0:T(1,128)S(1)}, f32[1,336]{1,0:T(1,128)S(1)}, u32[]{:S(2)}, u32[]{:S(2)}) collective-permute-start(f32[1,336]{1,0:T(1,128)S(1)} %get-tuple-element.61), channel_id=1, source_target_pairs={{1,0},{2,1},{3,2},{4,3},{5,4},{6,5},{7,6},{9,8},{10,9},{11,10},{12... | collective-permute-start | bytes 4040 | tf_op jit(solution)/shard_map/ppermute | solution.py:447
  78.4 2.2 %element_spectral.1.refs_0_ = f32[480,160]{1,0:T(8,128)S(1)} custom-call(f32[336,128]{1,0:T(8,128)S(1)} %get-tuple-element.57.refs_0_, f32[480,336]{1,0:T(8,128)} %get-tuple-element.58.refs_1_.refs_3_, f32[136,160]{1,0:T(8,128)} %get-tuple-element.59.refs_2_.refs_5_), custom_call_target="tpu_custom_call" | custom-call | bytes 1211392 | tf_op jit(solution)/shard_map/element_spectral/pallas_call | solution.py:119
  80.6 0.0 collective-permute-done.2.refs_1_
  80.6 1.1 collective-permute-done.3.refs_2_
  81.7 4.0 %element_solve.1 = (f32[256,128]{1,0:T(8,128)S(1)}, f32[1,128]{1,0:T(1,128)S(1)}) custom-call(f32[480,160]{1,0:T(8,128)S(1)} %element_spectral.1.refs_0_, f32[1,336]{1,0:T(1,128)S(1)} %collective-permute-done.2.refs_1_, f32[1,336]{1,0:T(1,128)S(1)} %collective-permute-done.3.refs_2_, f32[480,336]{1,0:T(8,128)} %get-tuple-element.58.refs_1_.refs_3_, ...), custom_call_target="tpu_custom_call" | custom-call | bytes 2003072 | tf_op jit(solution)/shard_map/element_solve/pallas_call | solution.py:119
  85.7 0.4 all-to-all-done.2
  86.1 1.6 %coarse_correct.1 = (f32[16,16,128]{2,1,0:T(8,128)S(1)}, f32[16,16,128]{2,1,0:T(8,128)S(1)}, f32[2,64,128]{2,1,0:T(8,128)S(1)}, f32[2,64,128]{2,1,0:T(8,128)S(1)}) custom-call(s32[8]{0:T(128)S(1)} %get-tuple-element.44.refs_0_, f32[512,128]{1,0:T(8,128)S(1)} %bitcast.3, f32[8,64,128]{2,1,0:T(8,128)S(1)} %get-tuple-element.55.refs_2_, ...), custom_call_target="tpu_custom_call" | custom-call | bytes 2492448 | tf_op jit(solution)/shard_map/coarse_correct/pallas_call | solution.py:119
  87.7 3.1 %collective-permute-start.4 = (f32[2,64,128]{2,1,0:T(8,128)S(1)}, f32[2,64,128]{2,1,0:T(8,128)S(1)}, u32[]{:S(2)}, u32[]{:S(2)}) collective-permute-start(f32[2,64,128]{2,1,0:T(8,128)S(1)} %get-tuple-element.75), channel_id=1, source_target_pairs={{0,64},{64,128},{128,192},{192,256},{256,320},{320,384},{384,448},... | collective-permute-start | bytes 196616 | tf_op jit(solution)/shard_map/ppermute | solution.py:447
  90.8 1.3 collective-permute-start.5
  92.1 0.0 collective-permute-done.4.refs_6_.refs_2_
  92.1 0.8 terms.1
  92.9 9.8 %all-to-all-start.3 = ((f32[64,1,128]{2,1,0:T(1,128)}), f32[64,1,128]{2,1,0:T(1,128)S(1)}, u32[]{:S(2)}, u32[]{:S(2)}) async-start(f32[64,1,128]{2,1,0:T(1,128)} %terms.1), calls=%async_computation.3 | async-start | bytes 65536 | tf_op jit(solution)/shard_map/all_to_all | solution.py:451
  102.7 0.0 collective-permute-done.5.refs_3_
  102.7 0.8 assemble_length.1
  103.5 3.3 %collective-permute-start.6 = (f32[2,32,128]{2,1,0:T(8,128)S(1)}, f32[2,32,128]{2,1,0:T(8,128)S(1)}, u32[]{:S(2)}, u32[]{:S(2)}) collective-permute-start(f32[2,32,128]{2,1,0:T(8,128)S(1)} %get-tuple-element.77), channel_id=1, source_target_pairs={{0,8},{8,16},{16,24},{24,32},{32,40},{40,48},{48,56},{1,9},{9,17},... | collective-permute-start | bytes 98312 | tf_op jit(solution)/shard_map/ppermute | solution.py:447
  106.8 1.3 collective-permute-start.7
  108.1 0.0 collective-permute-done.6.refs_1_
  108.1 3.9 %all-to-all-done.3.refs_0_ = f32[64,1,128]{2,1,0:T(1,128)S(1)} async-done(((f32[64,1,128]{2,1,0:T(1,128)}), f32[64,1,128]{2,1,0:T(1,128)S(1)}, u32[]{:S(2)}, u32[]{:S(2)}) %all-to-all-start.3) | async-done | bytes 32800 | tf_op jit(solution)/shard_map/all_to_all | solution.py:451
  112.0 0.7 sum_terms.1
  112.7 7.7 %all-to-all-start.4 = ((f32[16,1,128]{2,1,0:T(1,128)}), f32[16,1,128]{2,1,0:T(1,128)S(1)}, u32[]{:S(2)}, u32[]{:S(2)}) async-start(f32[16,1,128]{2,1,0:T(1,128)} %sum_terms.1), calls=%async_computation.4 | async-start | bytes 16384 | tf_op jit(solution)/shard_map/all_to_all | solution.py:451
  120.4 0.0 collective-permute-done.7.refs_2_
  120.4 1.0 assemble_across.1
  121.4 3.0 %collective-permute-start.8 = (f32[1,512]{1,0:T(1,128)S(1)}, f32[1,512]{1,0:T(1,128)S(1)}, u32[]{:S(2)}, u32[]{:S(2)}) collective-permute-start(f32[1,512]{1,0:T(1,128)S(1)} %get-tuple-element.82), channel_id=1, source_target_pairs={{0,1},{1,2},{2,3},{3,4},{4,5},{5,6},{6,7},{8,9},{9,10},{10,11},{11... | collective-permute-start | bytes 6152 | tf_op jit(solution)/shard_map/ppermute | solution.py:447
  124.4 1.9 %collective-permute-start.9 = (f32[1,512]{1,0:T(1,128)S(1)}, f32[1,512]{1,0:T(1,128)S(1)}, u32[]{:S(2)}, u32[]{:S(2)}) collective-permute-start(f32[1,512]{1,0:T(1,128)S(1)} %get-tuple-element.83), channel_id=1, source_target_pairs={{1,0},{2,1},{3,2},{4,3},{5,4},{6,5},{7,6},{9,8},{10,9},{11,10},{12... | collective-permute-start | bytes 6152 | tf_op jit(solution)/shard_map/ppermute | solution.py:447
  127.0 0.0 collective-permute-done.8.refs_1_
  127.0 2.6 %collective-permute-done.9.refs_2_ = f32[1,512]{1,0:T(1,128)S(1)} collective-permute-done((f32[1,512]{1,0:T(1,128)S(1)}, f32[1,512]{1,0:T(1,128)S(1)}, u32[]{:S(2)}, u32[]{:S(2)}) %collective-permute-start.9) | collective-permute-done | bytes 2080 | tf_op jit(solution)/shard_map/ppermute | solution.py:447
  129.6 0.4 assemble_depth.1.refs_3_
  130.1 1.6 %all-to-all-done.4.refs_1_ = f32[16,1,128]{2,1,0:T(1,128)S(1)} async-done(((f32[16,1,128]{2,1,0:T(1,128)}), f32[16,1,128]{2,1,0:T(1,128)S(1)}, u32[]{:S(2)}, u32[]{:S(2)}) %all-to-all-start.4) | async-done | bytes 8224 | tf_op jit(solution)/shard_map/all_to_all | solution.py:451
  131.6 1.6 %update.1 = (f32[16,16,128]{2,1,0:T(8,128)}, f32[16,16,128]{2,1,0:T(8,128)}, f32[16,16,128]{2,1,0:T(8,128)}) custom-call(f32[1]{0:T(128)S(6)} %copy.30.refs_0_, f32[16,1,128]{2,1,0:T(1,128)S(1)} %all-to-all-done.4.refs_1_, f32[1,1]{1,0:T(1,128)} %get-tuple-element.78.refs_2_, f32[2,16,16,128]{3,2,1,0:T(8,128)S(1)} %assemble_depth.1.refs_3_, ...), custom_call_target="tpu_custom_call" | custom-call | bytes 1187848 | tf_op jit(solution)/shard_map/update/pallas_call | solution.py:119
Async XLA Ops:
  2.5 32.6 %all-to-all-start = ((f32[16,32,128]{2,1,0:T(8,128)}), f32[16,32,128]{2,1,0:T(8,128)S(1)}, u32[]{:S(2)}, u32[]{:S(2)}) async-start(f32[16,32,128]{2,1,0:T(8,128)} %get-tuple-element.45), calls=%async_computation | async-start | bytes 524288 | tf_op jit(solution)/shard_map/all_to_all | solution.py:451
  36.1 29.5 %all-to-all-start.1 = ((f32[64,8,128]{2,1,0:T(8,128)}), f32[64,8,128]{2,1,0:T(8,128)S(1)}, u32[]{:S(2)}, u32[]{:S(2)}) async-start(f32[64,8,128]{2,1,0:T(8,128)} %get-tuple-element.49), calls=%async_computation.1 | async-start | bytes 524288 | tf_op jit(solution)/shard_map/all_to_all | solution.py:451
  52.4 4.6 %collective-permute-start = (f32[24,128]{1,0:T(8,128)S(1)}, f32[24,128]{1,0:T(8,128)S(1)}, u32[]{:S(2)}, u32[]{:S(2)}) collective-permute-start(f32[24,128]{1,0:T(8,128)S(1)} %get-tuple-element.52), channel_id=1, source_target_pairs={{0,8},{8,16},{16,24},{24,32},{32,40},{40,48},{48,56},{1,9},{9,17},... | collective-permute-start | bytes 36872 | tf_op jit(solution)/shard_map/ppermute | solution.py:447
  55.7 4.9 %collective-permute-start.1 = (f32[24,128]{1,0:T(8,128)S(1)}, f32[24,128]{1,0:T(8,128)S(1)}, u32[]{:S(2)}, u32[]{:S(2)}) collective-permute-start(f32[24,128]{1,0:T(8,128)S(1)} %get-tuple-element.53), channel_id=1, source_target_pairs={{8,0},{16,8},{24,16},{32,24},{40,32},{48,40},{56,48},{9,1},{17,9},... | collective-permute-start | bytes 36872 | tf_op jit(solution)/shard_map/ppermute | solution.py:447
  66.5 19.6 %all-to-all-start.2 = ((f32[64,8,128]{2,1,0:T(8,128)}), f32[64,8,128]{2,1,0:T(8,128)S(1)}, u32[]{:S(2)}, u32[]{:S(2)}) async-start(f32[64,8,128]{2,1,0:T(8,128)} %get-tuple-element.54), calls=%async_computation.2 | async-start | bytes 524288 | tf_op jit(solution)/shard_map/all_to_all | solution.py:451
  72.9 7.6 %collective-permute-start.2 = (f32[1,336]{1,0:T(1,128)S(1)}, f32[1,336]{1,0:T(1,128)S(1)}, u32[]{:S(2)}, u32[]{:S(2)}) collective-permute-start(f32[1,336]{1,0:T(1,128)S(1)} %get-tuple-element.60), channel_id=1, source_target_pairs={{0,1},{1,2},{2,3},{3,4},{4,5},{5,6},{6,7},{8,9},{9,10},{10,11},{11... | collective-permute-start | bytes 4040 | tf_op jit(solution)/shard_map/ppermute | solution.py:447
  76.5 5.2 %collective-permute-start.3 = (f32[1,336]{1,0:T(1,128)S(1)}, f32[1,336]{1,0:T(1,128)S(1)}, u32[]{:S(2)}, u32[]{:S(2)}) collective-permute-start(f32[1,336]{1,0:T(1,128)S(1)} %get-tuple-element.61), channel_id=1, source_target_pairs={{1,0},{2,1},{3,2},{4,3},{5,4},{6,5},{7,6},{9,8},{10,9},{11,10},{12... | collective-permute-start | bytes 4040 | tf_op jit(solution)/shard_map/ppermute | solution.py:447
  87.7 4.4 %collective-permute-start.4 = (f32[2,64,128]{2,1,0:T(8,128)S(1)}, f32[2,64,128]{2,1,0:T(8,128)S(1)}, u32[]{:S(2)}, u32[]{:S(2)}) collective-permute-start(f32[2,64,128]{2,1,0:T(8,128)S(1)} %get-tuple-element.75), channel_id=1, source_target_pairs={{0,64},{64,128},{128,192},{192,256},{256,320},{320,384},{384,448},... | collective-permute-start | bytes 196616 | tf_op jit(solution)/shard_map/ppermute | solution.py:447
  90.8 11.9 %collective-permute-start.5 = (f32[2,64,128]{2,1,0:T(8,128)S(1)}, f32[2,64,128]{2,1,0:T(8,128)S(1)}, u32[]{:S(2)}, u32[]{:S(2)}) collective-permute-start(f32[2,64,128]{2,1,0:T(8,128)S(1)} %get-tuple-element.76), channel_id=1, source_target_pairs={{64,0},{128,64},{192,128},{256,192},{320,256},{384,320},{448,384},... | collective-permute-start | bytes 196616 | tf_op jit(solution)/shard_map/ppermute | solution.py:447
  92.9 19.1 %all-to-all-start.3 = ((f32[64,1,128]{2,1,0:T(1,128)}), f32[64,1,128]{2,1,0:T(1,128)S(1)}, u32[]{:S(2)}, u32[]{:S(2)}) async-start(f32[64,1,128]{2,1,0:T(1,128)} %terms.1), calls=%async_computation.3 | async-start | bytes 65536 | tf_op jit(solution)/shard_map/all_to_all | solution.py:451
  103.5 4.6 %collective-permute-start.6 = (f32[2,32,128]{2,1,0:T(8,128)S(1)}, f32[2,32,128]{2,1,0:T(8,128)S(1)}, u32[]{:S(2)}, u32[]{:S(2)}) collective-permute-start(f32[2,32,128]{2,1,0:T(8,128)S(1)} %get-tuple-element.77), channel_id=1, source_target_pairs={{0,8},{8,16},{16,24},{24,32},{32,40},{40,48},{48,56},{1,9},{9,17},... | collective-permute-start | bytes 98312 | tf_op jit(solution)/shard_map/ppermute | solution.py:447
  106.8 13.6 %collective-permute-start.7 = (f32[2,32,128]{2,1,0:T(8,128)S(1)}, f32[2,32,128]{2,1,0:T(8,128)S(1)}, u32[]{:S(2)}, u32[]{:S(2)}) collective-permute-start(f32[2,32,128]{2,1,0:T(8,128)S(1)} %get-tuple-element.80), channel_id=1, source_target_pairs={{8,0},{16,8},{24,16},{32,24},{40,32},{48,40},{56,48},{9,1},{17,9},... | collective-permute-start | bytes 98312 | tf_op jit(solution)/shard_map/ppermute | solution.py:447
  112.7 18.9 %all-to-all-start.4 = ((f32[16,1,128]{2,1,0:T(1,128)}), f32[16,1,128]{2,1,0:T(1,128)S(1)}, u32[]{:S(2)}, u32[]{:S(2)}) async-start(f32[16,1,128]{2,1,0:T(1,128)} %sum_terms.1), calls=%async_computation.4 | async-start | bytes 16384 | tf_op jit(solution)/shard_map/all_to_all | solution.py:451
  121.4 5.6 %collective-permute-start.8 = (f32[1,512]{1,0:T(1,128)S(1)}, f32[1,512]{1,0:T(1,128)S(1)}, u32[]{:S(2)}, u32[]{:S(2)}) collective-permute-start(f32[1,512]{1,0:T(1,128)S(1)} %get-tuple-element.82), channel_id=1, source_target_pairs={{0,1},{1,2},{2,3},{3,4},{4,5},{5,6},{6,7},{8,9},{9,10},{10,11},{11... | collective-permute-start | bytes 6152 | tf_op jit(solution)/shard_map/ppermute | solution.py:447
  124.4 5.2 %collective-permute-start.9 = (f32[1,512]{1,0:T(1,128)S(1)}, f32[1,512]{1,0:T(1,128)S(1)}, u32[]{:S(2)}, u32[]{:S(2)}) collective-permute-start(f32[1,512]{1,0:T(1,128)S(1)} %get-tuple-element.83), channel_id=1, source_target_pairs={{1,0},{2,1},{3,2},{4,3},{5,4},{6,5},{7,6},{9,8},{10,9},{11,10},{12... | collective-permute-start | bytes 6152 | tf_op jit(solution)/shard_map/ppermute | solution.py:447

commit v8 on v7

--- a/solution.py
+++ b/solution.py
@@ -144,17 +144,16 @@
     )(*args)
 
 
-def coarse_kernel(ready, blocks, me, residual, ids, values, kept, payload, ids_wide):
+def coarse_kernel(ready, blocks, me, residual, ids, values, kept, payload, ids_wide, to_high, to_low):
     nx, ny, nz = residual.shape
     ex, ey = nx // N, ny // N
     ez = ids.shape[1]
     n_stored, coarse, _ = values.shape
-    n_line, head = payload.shape[0], payload.shape[1] - ny
+    n_line, head = payload.shape[:2]
     widen = (
         lax.broadcasted_iota(jnp.int32, (ez, nz), 1) // N
         == lax.broadcasted_iota(jnp.int32, (ez, nz), 0)
     ).astype(F32)
-    payload[...] = jnp.zeros_like(payload)
     at = me[0]
     ready(3)
     wide = mm(ids[...].astype(F32), widen)
@@ -163,14 +162,8 @@
     total = jnp.zeros((coarse, nz), F32)
     ready(2)
 
-    @pl.when(at + 1 < n_line)
-    def _():
-        payload[at + 1, head:, :] = residual[nx - 2]
-
-    @pl.when(at > 0)
-    def _():
-        payload[at - 1, head:, :] = residual[1]
-
+    to_high[...] = residual[nx - 2]
+    to_low[...] = residual[1]
     for a in range(ex):
         for b in range(ey):
             part = jnp.sum(residual[a * N : a * N + N, b * N : b * N + N, :], axis=(0, 1))[None]
@@ -190,16 +183,14 @@
             row == k, jnp.sum(values[k] * coarse_residual, axis=0, keepdims=True), lines
         )
     for i in range(n_line):
-        payload[i, :head, :] = lines
+        payload[i] = lines
 
 
 def line_kernel(
-    n_stored, ready, me, parts, residual, after1, after2, dense, x_low, x_high, to_high, to_low
+    n_stored, ready, parts, residual, x_low, x_high, after1, after2, dense, to_high, to_low
 ):
     nx, ny, nz = residual.shape
     n_line = parts.shape[0]
-    head = parts.shape[1] - ny
-    at = me[0]
     rows = parts[:, :n_stored, :].reshape(n_line * n_stored, nz)
     if rows.shape[0] < nz:
         rows = jnp.concatenate([rows, jnp.zeros((nz - rows.shape[0], nz), F32)])
@@ -208,9 +199,6 @@
     block = lax.broadcasted_iota(jnp.int32, (n_blocks, nz), 0).astype(F32)
     place = (jnp.abs(block - numbers) < 0.5).astype(F32)
     dense[...] = mm(place, rows).reshape(dense.shape)
-    before, behind = jnp.maximum(at - 1, 0), jnp.minimum(at + 1, n_line - 1)
-    x_low[...] = jnp.where(at > 0, parts[before, head:, :], 0.0)
-    x_high[...] = jnp.where(at + 1 < n_line, parts[behind, head:, :], 0.0)
     for out, y in ((to_high, ny - 2), (to_low, 1)):
         out[...] = jnp.zeros_like(out)
         out[:nx] = residual[:, y, :]
@@ -477,13 +465,15 @@
     me = lax.axis_index("gx").astype(jnp.int32).reshape(1)
     head = up8(xxt_values.shape[0] + 1)
     assert xxt_values.shape[0] * n_line <= nz
-    payload, ids_wide, residual, xxt_values, block_numbers = call(
-        coarse_kernel, "coarse_restrict", [(n_line, head + ny, nz), (ex * ey, nz)],
+    payload, ids_wide, to_high, to_low, residual, xxt_values, block_numbers = call(
+        coarse_kernel, "coarse_restrict",
+        [(n_line, head, nz), (ex * ey, nz), (ny, nz), (ny, nz)],
         xxt_blocks, me, residual, ids, xxt_values, xxt_blocks, smem=(1,), load=(3,), keep=(2, 4, 5),
         pin=(1,),
         numbers=(0,),
     )
     parts = spread(payload, "gx")
+    x_low, x_high = exchange(to_high, to_low, "gx")
 
     cheb = cheb_matrix()
     ky = np.kron(np.eye(nx, dtype=np.float32), np.kron(np.eye(ey, dtype=np.float32), cheb))
@@ -534,10 +524,10 @@
         load=tuple(range(13)), store=(0, 1, 2, 3),
     )
 
-    dense, x_low, x_high, to_high, to_low = call(
+    dense, to_high, to_low = call(
         functools.partial(line_kernel, xxt_values.shape[0]), "line_sum",
-        [(n_plane, own, block), (ny, nz), (ny, nz), (face, nz), (face, nz)],
-        me, parts, residual, image_direction, from_z, smem=(0,), pin=(1, 2), idle=(4,),
+        [(n_plane, own, block), (face, nz), (face, nz)],
+        parts, residual, x_low, x_high, image_direction, from_z, idle=(5,),
     )
     parts = spread(dense, plane)
     y_low, y_high = exchange(to_high, to_low, "gy")

time: 134 us -> 137 us (1.022)
  starting transfers between devices: 83.6 us -> 91.7 us
  waiting for transfers between devices: 23 us -> 18.2 us
    all_to_all x5, waiting for transfers between devices: 15.6 us -> 10.9 us  [spread(): return lax.all_to_all(values, axes, 0, 0, tiled=False)]
    all_to_all x5, starting transfers between devices: 59.6 us -> 63.3 us  [spread(): return lax.all_to_all(values, axes, 0, 0, tiled=False)]
    ppermute x5 -> x6, starting transfers between devices: 16.3 us -> 19.4 us  [exchange(): lax.ppermute(to_high, axis, forward)]
    ppermute x5 -> x6, starting transfers between devices: 7.72 us -> 9.01 us  [exchange(): lax.ppermute(to_low, axis, backward)]
    ppermute x5 -> x6, waiting for transfers between devices: 7.32 us -> 7.32 us  [exchange(): lax.ppermute(to_low, axis, backward)]
  transfers between devices with their start and end apart: 15 -> 17, of which waited for: 8 -> 7; matrix products, arithmetic and copies ran while one was open for 0% -> 0% of each run, Pallas kernels for 14% -> 13%
where the time goes in v8:
time: 137 us; the launch traced here: 136 us
  starting transfers between devices  91.7 us (67%)
  Pallas kernels  24.9 us (18%)
  waiting for transfers between devices  18.2 us (13%)
  between operations  1.55 us (1%)
    all_to_all x5, starting transfers between devices, spread(): return lax.all_to_all(values, axes, 0, 0, tiled=False)  63.3 us
    pallas_call x14, Pallas kernels, call(): pl.pallas_call(whole, out_shape=[pltpu.VMEM(o, F32) if i in pin else pltp...  24.9 us
    ppermute x6, starting transfers between devices, exchange(): lax.ppermute(to_high, axis, forward)  19.4 us
    all_to_all x5, waiting for transfers between devices, spread(): return lax.all_to_all(values, axes, 0, 0, tiled=False)  10.9 us
    ppermute x6, starting transfers between devices, exchange(): lax.ppermute(to_low, axis, backward)  9.01 us
    ppermute x6, waiting for transfers between devices, exchange(): lax.ppermute(to_low, axis, backward)  7.32 us
  transfers between devices with their start and end apart: 17, of which 7 were waited for; matrix products, arithmetic and copies ran while one was open for 0% of the time, Pallas kernels for 13%

profile of v8, /device:TPU:1, one launch (start us, length us, event | category | flops | bytes accessed | tf_op | source)
XLA Modules:
  0.0 136.4 jit_solution(3960570086478445167)
XLA Ops:
  0.6 1.8 %coarse_restrict.1 = (f32[16,16,128]{2,1,0:T(8,128)}, f32[4,128]{1,0:T(4,128)S(1)}, f32[16,128]{1,0:T(8,128)S(1)}, f32[16,128]{1,0:T(8,128)S(1)}, f32[16,16,128]...) custom-call(s32[8]{0:T(128)} %refs_5_.3, s32[1]{0:T(128)} %bitcast.refs_1_, f32[16,16,128]{2,1,0:T(8,128)} %refs_2_.3, ...), custom_call_target="tpu_custom_call" | custom-call | bytes 543044 | tf_op jit(solution)/shard_map/coarse_restrict/pallas_call | solution.py:119
  2.4 19.4 %all-to-all-start = ((f32[16,16,128]{2,1,0:T(8,128)}), f32[16,16,128]{2,1,0:T(8,128)S(1)}, u32[]{:S(2)}, u32[]{:S(2)}) async-start(f32[16,16,128]{2,1,0:T(8,128)} %get-tuple-element.45), calls=%async_computation | async-start | bytes 262144 | tf_op jit(solution)/shard_map/all_to_all | solution.py:439
  21.9 3.3 %collective-permute-start = (f32[16,128]{1,0:T(8,128)S(1)}, f32[16,128]{1,0:T(8,128)S(1)}, u32[]{:S(2)}, u32[]{:S(2)}) collective-permute-start(f32[16,128]{1,0:T(8,128)S(1)} %get-tuple-element.47), channel_id=1, source_target_pairs={{0,64},{64,128},{128,192},{192,256},{256,320},{320,384},{384,448},... | collective-permute-start | bytes 24584 | tf_op jit(solution)/shard_map/ppermute | solution.py:435
  25.1 1.3 collective-permute-start.1
  26.4 2.4 %operator_direction.1 = (f32[16,16,128]{2,1,0:T(8,128)S(1)}, f32[1,128]{1,0:T(1,128)S(1)}, f32[16,16,128]{2,1,0:T(8,128)S(1)}, f32[3,16,16,128]{3,2,1,0:T(8,128)...) custom-call(f32[16,16,128]{2,1,0:T(8,128)} %refs_0_.5, ...), custom_call_target="tpu_custom_call" | custom-call | bytes 1442304 | tf_op jit(solution)/shard_map/operator_direction/pallas_call | solution.py:119
  28.9 5.9 %basis_matrices.1 = (f32[480,336]{1,0:T(8,128)}, f32[256,480]{1,0:T(8,128)}, f32[136,160]{1,0:T(8,128)}, f32[160,128]{1,0:T(8,128)}) custom-call(f32[10,10]{1,0:T(8,128)} %refs_0_.6, f32[20,10]{1,0:T(8,128)} %constant.42.clone.refs_1_, f32[20,20]{1,0:T(8,128)} %constant.43.clone.refs_2_, f32[160,10]{1,0:T(8,128)} %constant.44.clone.refs_3_, ...), custom_call_target="tpu_custom_call" | custom-call | bytes 1757680 | tf_op jit(solution)/shard_map/basis_matrices/pallas_call | solution.py:119
  34.7 0.0 collective-permute-done.refs_2_
  34.8 0.0 collective-permute-done.1.refs_3_
  34.8 0.0 all-to-all-done.refs_0_
  34.8 1.1 line_sum.1
  35.9 13.0 %all-to-all-start.1 = ((f32[64,8,128]{2,1,0:T(8,128)}), f32[64,8,128]{2,1,0:T(8,128)S(1)}, u32[]{:S(2)}, u32[]{:S(2)}) async-start(f32[64,8,128]{2,1,0:T(8,128)} %get-tuple-element.51), calls=%async_computation.1 | async-start | bytes 524288 | tf_op jit(solution)/shard_map/all_to_all | solution.py:439
  48.9 3.3 %collective-permute-start.2 = (f32[24,128]{1,0:T(8,128)S(1)}, f32[24,128]{1,0:T(8,128)S(1)}, u32[]{:S(2)}, u32[]{:S(2)}) collective-permute-start(f32[24,128]{1,0:T(8,128)S(1)} %get-tuple-element.52), channel_id=1, source_target_pairs={{0,8},{8,16},{16,24},{24,32},{32,40},{40,48},{48,56},{1,9},{9,17},... | collective-permute-start | bytes 36872 | tf_op jit(solution)/shard_map/ppermute | solution.py:435
  52.2 1.3 collective-permute-start.3
  53.5 0.0 collective-permute-done.2.refs_4_
  53.5 3.6 %collective-permute-done.3.refs_5_ = f32[24,128]{1,0:T(8,128)S(1)} collective-permute-done((f32[24,128]{1,0:T(8,128)S(1)}, f32[24,128]{1,0:T(8,128)S(1)}, u32[]{:S(2)}, u32[]{:S(2)}) %collective-permute-start.3) | collective-permute-done | bytes 12320 | tf_op jit(solution)/shard_map/ppermute | solution.py:435
  57.1 4.9 %all-to-all-done.1.refs_0_ = f32[64,8,128]{2,1,0:T(8,128)S(1)} async-done(((f32[64,8,128]{2,1,0:T(8,128)}), f32[64,8,128]{2,1,0:T(8,128)S(1)}, u32[]{:S(2)}, u32[]{:S(2)}) %all-to-all-start.1) | async-done | bytes 262176 | tf_op jit(solution)/shard_map/all_to_all | solution.py:439
  62.0 0.9 plane_sum.1
  63.0 6.4 %all-to-all-start.2 = ((f32[64,8,128]{2,1,0:T(8,128)}), f32[64,8,128]{2,1,0:T(8,128)S(1)}, u32[]{:S(2)}, u32[]{:S(2)}) async-start(f32[64,8,128]{2,1,0:T(8,128)} %get-tuple-element.54), calls=%async_computation.2 | async-start | bytes 524288 | tf_op jit(solution)/shard_map/all_to_all | solution.py:439
  69.4 3.5 %collective-permute-start.4 = (f32[1,336]{1,0:T(1,128)S(1)}, f32[1,336]{1,0:T(1,128)S(1)}, u32[]{:S(2)}, u32[]{:S(2)}) collective-permute-start(f32[1,336]{1,0:T(1,128)S(1)} %get-tuple-element.60), channel_id=1, source_target_pairs={{0,1},{1,2},{2,3},{3,4},{4,5},{5,6},{6,7},{8,9},{9,10},{10,11},{11... | collective-permute-start | bytes 4040 | tf_op jit(solution)/shard_map/ppermute | solution.py:435
  72.9 1.9 %collective-permute-start.5 = (f32[1,336]{1,0:T(1,128)S(1)}, f32[1,336]{1,0:T(1,128)S(1)}, u32[]{:S(2)}, u32[]{:S(2)}) collective-permute-start(f32[1,336]{1,0:T(1,128)S(1)} %get-tuple-element.61), channel_id=1, source_target_pairs={{1,0},{2,1},{3,2},{4,3},{5,4},{6,5},{7,6},{9,8},{10,9},{11,10},{12... | collective-permute-start | bytes 4040 | tf_op jit(solution)/shard_map/ppermute | solution.py:435
  74.9 2.2 %element_spectral.1.refs_0_ = f32[480,160]{1,0:T(8,128)S(1)} custom-call(f32[336,128]{1,0:T(8,128)S(1)} %get-tuple-element.57.refs_0_, f32[480,336]{1,0:T(8,128)} %get-tuple-element.58.refs_1_.refs_3_, f32[136,160]{1,0:T(8,128)} %get-tuple-element.59.refs_2_.refs_5_), custom_call_target="tpu_custom_call" | custom-call | bytes 1211392 | tf_op jit(solution)/shard_map/element_spectral/pallas_call | solution.py:119
  77.0 0.0 collective-permute-done.4.refs_1_
  77.0 1.1 collective-permute-done.5.refs_2_
  78.1 4.0 %element_solve.1 = (f32[256,128]{1,0:T(8,128)S(1)}, f32[1,128]{1,0:T(1,128)S(1)}) custom-call(f32[480,160]{1,0:T(8,128)S(1)} %element_spectral.1.refs_0_, f32[1,336]{1,0:T(1,128)S(1)} %collective-permute-done.4.refs_1_, f32[1,336]{1,0:T(1,128)S(1)} %collective-permute-done.5.refs_2_, f32[480,336]{1,0:T(8,128)} %get-tuple-element.58.refs_1_.refs_3_, ...), custom_call_target="tpu_custom_call" | custom-call | bytes 2003072 | tf_op jit(solution)/shard_map/element_solve/pallas_call | solution.py:119
  82.2 0.4 all-to-all-done.2
  82.5 1.6 %coarse_correct.1 = (f32[16,16,128]{2,1,0:T(8,128)S(1)}, f32[16,16,128]{2,1,0:T(8,128)S(1)}, f32[2,64,128]{2,1,0:T(8,128)S(1)}, f32[2,64,128]{2,1,0:T(8,128)S(1)}) custom-call(s32[8]{0:T(128)S(1)} %get-tuple-element.44.refs_0_, f32[512,128]{1,0:T(8,128)S(1)} %bitcast.3, f32[8,64,128]{2,1,0:T(8,128)S(1)} %get-tuple-element.55.refs_2_, ...), custom_call_target="tpu_custom_call" | custom-call | bytes 2492448 | tf_op jit(solution)/shard_map/coarse_correct/pallas_call | solution.py:119
  84.1 3.0 %collective-permute-start.6 = (f32[2,64,128]{2,1,0:T(8,128)S(1)}, f32[2,64,128]{2,1,0:T(8,128)S(1)}, u32[]{:S(2)}, u32[]{:S(2)}) collective-permute-start(f32[2,64,128]{2,1,0:T(8,128)S(1)} %get-tuple-element.75), channel_id=1, source_target_pairs={{0,64},{64,128},{128,192},{192,256},{256,320},{320,384},{384,448},... | collective-permute-start | bytes 196616 | tf_op jit(solution)/shard_map/ppermute | solution.py:435
  87.1 1.3 collective-permute-start.7
  88.4 0.0 collective-permute-done.6.refs_6_.refs_2_
  88.4 0.8 terms.1
  89.2 9.8 %all-to-all-start.3 = ((f32[64,1,128]{2,1,0:T(1,128)}), f32[64,1,128]{2,1,0:T(1,128)S(1)}, u32[]{:S(2)}, u32[]{:S(2)}) async-start(f32[64,1,128]{2,1,0:T(1,128)} %terms.1), calls=%async_computation.3 | async-start | bytes 65536 | tf_op jit(solution)/shard_map/all_to_all | solution.py:439
  99.0 0.0 collective-permute-done.7.refs_3_
  99.0 0.7 assemble_length.1
  99.7 3.3 %collective-permute-start.8 = (f32[2,32,128]{2,1,0:T(8,128)S(1)}, f32[2,32,128]{2,1,0:T(8,128)S(1)}, u32[]{:S(2)}, u32[]{:S(2)}) collective-permute-start(f32[2,32,128]{2,1,0:T(8,128)S(1)} %get-tuple-element.77), channel_id=1, source_target_pairs={{0,8},{8,16},{16,24},{24,32},{32,40},{40,48},{48,56},{1,9},{9,17},... | collective-permute-start | bytes 98312 | tf_op jit(solution)/shard_map/ppermute | solution.py:435
  103.0 1.3 collective-permute-start.9
  104.3 0.0 collective-permute-done.8.refs_1_
  104.3 4.0 %all-to-all-done.3.refs_0_ = f32[64,1,128]{2,1,0:T(1,128)S(1)} async-done(((f32[64,1,128]{2,1,0:T(1,128)}), f32[64,1,128]{2,1,0:T(1,128)S(1)}, u32[]{:S(2)}, u32[]{:S(2)}) %all-to-all-start.3) | async-done | bytes 32800 | tf_op jit(solution)/shard_map/all_to_all | solution.py:439
  108.3 0.7 sum_terms.1
  109.0 14.7 %all-to-all-start.4 = ((f32[16,1,128]{2,1,0:T(1,128)}), f32[16,1,128]{2,1,0:T(1,128)S(1)}, u32[]{:S(2)}, u32[]{:S(2)}) async-start(f32[16,1,128]{2,1,0:T(1,128)} %sum_terms.1), calls=%async_computation.4 | async-start | bytes 16384 | tf_op jit(solution)/shard_map/all_to_all | solution.py:439
  123.7 0.0 collective-permute-done.9.refs_2_
  123.7 1.0 assemble_across.1
  124.6 3.0 %collective-permute-start.10 = (f32[1,512]{1,0:T(1,128)S(1)}, f32[1,512]{1,0:T(1,128)S(1)}, u32[]{:S(2)}, u32[]{:S(2)}) collective-permute-start(f32[1,512]{1,0:T(1,128)S(1)} %get-tuple-element.82), channel_id=1, source_target_pairs={{0,1},{1,2},{2,3},{3,4},{4,5},{5,6},{6,7},{8,9},{9,10},{10,11},{11... | collective-permute-start | bytes 6152 | tf_op jit(solution)/shard_map/ppermute | solution.py:435
  127.7 1.9 %collective-permute-start.11 = (f32[1,512]{1,0:T(1,128)S(1)}, f32[1,512]{1,0:T(1,128)S(1)}, u32[]{:S(2)}, u32[]{:S(2)}) collective-permute-start(f32[1,512]{1,0:T(1,128)S(1)} %get-tuple-element.83), channel_id=1, source_target_pairs={{1,0},{2,1},{3,2},{4,3},{5,4},{6,5},{7,6},{9,8},{10,9},{11,10},{12... | collective-permute-start | bytes 6152 | tf_op jit(solution)/shard_map/ppermute | solution.py:435
  130.3 0.0 collective-permute-done.10.refs_1_
  130.3 2.6 %collective-permute-done.11.refs_2_ = f32[1,512]{1,0:T(1,128)S(1)} collective-permute-done((f32[1,512]{1,0:T(1,128)S(1)}, f32[1,512]{1,0:T(1,128)S(1)}, u32[]{:S(2)}, u32[]{:S(2)}) %collective-permute-start.11) | collective-permute-done | bytes 2080 | tf_op jit(solution)/shard_map/ppermute | solution.py:435
  132.9 0.4 assemble_depth.1.refs_3_
  133.3 1.6 %all-to-all-done.4.refs_1_ = f32[16,1,128]{2,1,0:T(1,128)S(1)} async-done(((f32[16,1,128]{2,1,0:T(1,128)}), f32[16,1,128]{2,1,0:T(1,128)S(1)}, u32[]{:S(2)}, u32[]{:S(2)}) %all-to-all-start.4) | async-done | bytes 8224 | tf_op jit(solution)/shard_map/all_to_all | solution.py:439
  134.9 1.5 %update.1 = (f32[16,16,128]{2,1,0:T(8,128)}, f32[16,16,128]{2,1,0:T(8,128)}, f32[16,16,128]{2,1,0:T(8,128)}) custom-call(f32[1]{0:T(128)S(6)} %copy.30.refs_0_, f32[16,1,128]{2,1,0:T(1,128)S(1)} %all-to-all-done.4.refs_1_, f32[1,1]{1,0:T(1,128)} %get-tuple-element.78.refs_2_, f32[2,16,16,128]{3,2,1,0:T(8,128)S(1)} %assemble_depth.1.refs_3_, ...), custom_call_target="tpu_custom_call" | custom-call | bytes 1187848 | tf_op jit(solution)/shard_map/update/pallas_call | solution.py:119
Async XLA Ops:
  2.4 32.3 %all-to-all-start = ((f32[16,16,128]{2,1,0:T(8,128)}), f32[16,16,128]{2,1,0:T(8,128)S(1)}, u32[]{:S(2)}, u32[]{:S(2)}) async-start(f32[16,16,128]{2,1,0:T(8,128)} %get-tuple-element.45), calls=%async_computation | async-start | bytes 262144 | tf_op jit(solution)/shard_map/all_to_all | solution.py:439
  21.9 12.9 %collective-permute-start = (f32[16,128]{1,0:T(8,128)S(1)}, f32[16,128]{1,0:T(8,128)S(1)}, u32[]{:S(2)}, u32[]{:S(2)}) collective-permute-start(f32[16,128]{1,0:T(8,128)S(1)} %get-tuple-element.47), channel_id=1, source_target_pairs={{0,64},{64,128},{128,192},{192,256},{256,320},{320,384},{384,448},... | collective-permute-start | bytes 24584 | tf_op jit(solution)/shard_map/ppermute | solution.py:435
  25.1 9.6 %collective-permute-start.1 = (f32[16,128]{1,0:T(8,128)S(1)}, f32[16,128]{1,0:T(8,128)S(1)}, u32[]{:S(2)}, u32[]{:S(2)}) collective-permute-start(f32[16,128]{1,0:T(8,128)S(1)} %get-tuple-element.48), channel_id=1, source_target_pairs={{64,0},{128,64},{192,128},{256,192},{320,256},{384,320},{448,384},... | collective-permute-start | bytes 24584 | tf_op jit(solution)/shard_map/ppermute | solution.py:435
  35.9 26.1 %all-to-all-start.1 = ((f32[64,8,128]{2,1,0:T(8,128)}), f32[64,8,128]{2,1,0:T(8,128)S(1)}, u32[]{:S(2)}, u32[]{:S(2)}) async-start(f32[64,8,128]{2,1,0:T(8,128)} %get-tuple-element.51), calls=%async_computation.1 | async-start | bytes 524288 | tf_op jit(solution)/shard_map/all_to_all | solution.py:439
  48.9 4.6 %collective-permute-start.2 = (f32[24,128]{1,0:T(8,128)S(1)}, f32[24,128]{1,0:T(8,128)S(1)}, u32[]{:S(2)}, u32[]{:S(2)}) collective-permute-start(f32[24,128]{1,0:T(8,128)S(1)} %get-tuple-element.52), channel_id=1, source_target_pairs={{0,8},{8,16},{16,24},{24,32},{32,40},{40,48},{48,56},{1,9},{9,17},... | collective-permute-start | bytes 36872 | tf_op jit(solution)/shard_map/ppermute | solution.py:435
  52.2 4.9 %collective-permute-start.3 = (f32[24,128]{1,0:T(8,128)S(1)}, f32[24,128]{1,0:T(8,128)S(1)}, u32[]{:S(2)}, u32[]{:S(2)}) collective-permute-start(f32[24,128]{1,0:T(8,128)S(1)} %get-tuple-element.53), channel_id=1, source_target_pairs={{8,0},{16,8},{24,16},{32,24},{40,32},{48,40},{56,48},{9,1},{17,9},... | collective-permute-start | bytes 36872 | tf_op jit(solution)/shard_map/ppermute | solution.py:435
  63.0 19.6 %all-to-all-start.2 = ((f32[64,8,128]{2,1,0:T(8,128)}), f32[64,8,128]{2,1,0:T(8,128)S(1)}, u32[]{:S(2)}, u32[]{:S(2)}) async-start(f32[64,8,128]{2,1,0:T(8,128)} %get-tuple-element.54), calls=%async_computation.2 | async-start | bytes 524288 | tf_op jit(solution)/shard_map/all_to_all | solution.py:439
  69.4 7.6 %collective-permute-start.4 = (f32[1,336]{1,0:T(1,128)S(1)}, f32[1,336]{1,0:T(1,128)S(1)}, u32[]{:S(2)}, u32[]{:S(2)}) collective-permute-start(f32[1,336]{1,0:T(1,128)S(1)} %get-tuple-element.60), channel_id=1, source_target_pairs={{0,1},{1,2},{2,3},{3,4},{4,5},{5,6},{6,7},{8,9},{9,10},{10,11},{11... | collective-permute-start | bytes 4040 | tf_op jit(solution)/shard_map/ppermute | solution.py:435
  72.9 5.2 %collective-permute-start.5 = (f32[1,336]{1,0:T(1,128)S(1)}, f32[1,336]{1,0:T(1,128)S(1)}, u32[]{:S(2)}, u32[]{:S(2)}) collective-permute-start(f32[1,336]{1,0:T(1,128)S(1)} %get-tuple-element.61), channel_id=1, source_target_pairs={{1,0},{2,1},{3,2},{4,3},{5,4},{6,5},{7,6},{9,8},{10,9},{11,10},{12... | collective-permute-start | bytes 4040 | tf_op jit(solution)/shard_map/ppermute | solution.py:435
  84.1 4.3 %collective-permute-start.6 = (f32[2,64,128]{2,1,0:T(8,128)S(1)}, f32[2,64,128]{2,1,0:T(8,128)S(1)}, u32[]{:S(2)}, u32[]{:S(2)}) collective-permute-start(f32[2,64,128]{2,1,0:T(8,128)S(1)} %get-tuple-element.75), channel_id=1, source_target_pairs={{0,64},{64,128},{128,192},{192,256},{256,320},{320,384},{384,448},... | collective-permute-start | bytes 196616 | tf_op jit(solution)/shard_map/ppermute | solution.py:435
  87.1 11.9 %collective-permute-start.7 = (f32[2,64,128]{2,1,0:T(8,128)S(1)}, f32[2,64,128]{2,1,0:T(8,128)S(1)}, u32[]{:S(2)}, u32[]{:S(2)}) collective-permute-start(f32[2,64,128]{2,1,0:T(8,128)S(1)} %get-tuple-element.76), channel_id=1, source_target_pairs={{64,0},{128,64},{192,128},{256,192},{320,256},{384,320},{448,384},... | collective-permute-start | bytes 196616 | tf_op jit(solution)/shard_map/ppermute | solution.py:435
  89.2 19.1 %all-to-all-start.3 = ((f32[64,1,128]{2,1,0:T(1,128)}), f32[64,1,128]{2,1,0:T(1,128)S(1)}, u32[]{:S(2)}, u32[]{:S(2)}) async-start(f32[64,1,128]{2,1,0:T(1,128)} %terms.1), calls=%async_computation.3 | async-start | bytes 65536 | tf_op jit(solution)/shard_map/all_to_all | solution.py:439
  99.7 4.6 %collective-permute-start.8 = (f32[2,32,128]{2,1,0:T(8,128)S(1)}, f32[2,32,128]{2,1,0:T(8,128)S(1)}, u32[]{:S(2)}, u32[]{:S(2)}) collective-permute-start(f32[2,32,128]{2,1,0:T(8,128)S(1)} %get-tuple-element.77), channel_id=1, source_target_pairs={{0,8},{8,16},{16,24},{24,32},{32,40},{40,48},{48,56},{1,9},{9,17},... | collective-permute-start | bytes 98312 | tf_op jit(solution)/shard_map/ppermute | solution.py:435
  103.0 20.6 %collective-permute-start.9 = (f32[2,32,128]{2,1,0:T(8,128)S(1)}, f32[2,32,128]{2,1,0:T(8,128)S(1)}, u32[]{:S(2)}, u32[]{:S(2)}) collective-permute-start(f32[2,32,128]{2,1,0:T(8,128)S(1)} %get-tuple-element.80), channel_id=1, source_target_pairs={{8,0},{16,8},{24,16},{32,24},{40,32},{48,40},{56,48},{9,1},{17,9},... | collective-permute-start | bytes 98312 | tf_op jit(solution)/shard_map/ppermute | solution.py:435
  109.0 25.9 %all-to-all-start.4 = ((f32[16,1,128]{2,1,0:T(1,128)}), f32[16,1,128]{2,1,0:T(1,128)S(1)}, u32[]{:S(2)}, u32[]{:S(2)}) async-start(f32[16,1,128]{2,1,0:T(1,128)} %sum_terms.1), calls=%async_computation.4 | async-start | bytes 16384 | tf_op jit(solution)/shard_map/all_to_all | solution.py:439
  124.6 5.6 %collective-permute-start.10 = (f32[1,512]{1,0:T(1,128)S(1)}, f32[1,512]{1,0:T(1,128)S(1)}, u32[]{:S(2)}, u32[]{:S(2)}) collective-permute-start(f32[1,512]{1,0:T(1,128)S(1)} %get-tuple-element.82), channel_id=1, source_target_pairs={{0,1},{1,2},{2,3},{3,4},{4,5},{5,6},{6,7},{8,9},{9,10},{10,11},{11... | collective-permute-start | bytes 6152 | tf_op jit(solution)/shard_map/ppermute | solution.py:435
  127.7 5.2 %collective-permute-start.11 = (f32[1,512]{1,0:T(1,128)S(1)}, f32[1,512]{1,0:T(1,128)S(1)}, u32[]{:S(2)}, u32[]{:S(2)}) collective-permute-start(f32[1,512]{1,0:T(1,128)S(1)} %get-tuple-element.83), channel_id=1, source_target_pairs={{1,0},{2,1},{3,2},{4,3},{5,4},{6,5},{7,6},{9,8},{10,9},{11,10},{12... | collective-permute-start | bytes 6152 | tf_op jit(solution)/shard_map/ppermute | solution.py:435

commit v9 on v7

--- a/solution.py
+++ b/solution.py
@@ -149,12 +149,12 @@
     ex, ey = nx // N, ny // N
     ez = ids.shape[1]
     n_stored, coarse, _ = values.shape
-    n_line, head = payload.shape[0], payload.shape[1] - ny
+    head = n_stored + 1
+    n_line = payload.shape[0] // (head + ny)
     widen = (
         lax.broadcasted_iota(jnp.int32, (ez, nz), 1) // N
         == lax.broadcasted_iota(jnp.int32, (ez, nz), 0)
     ).astype(F32)
-    payload[...] = jnp.zeros_like(payload)
     at = me[0]
     ready(3)
     wide = mm(ids[...].astype(F32), widen)
@@ -165,11 +165,13 @@
 
     @pl.when(at + 1 < n_line)
     def _():
-        payload[at + 1, head:, :] = residual[nx - 2]
+        for y in range(ny):
+            payload[(at + 1) * (head + ny) + head + y] = residual[nx - 2, y : y + 1, :]
 
     @pl.when(at > 0)
     def _():
-        payload[at - 1, head:, :] = residual[1]
+        for y in range(ny):
+            payload[(at - 1) * (head + ny) + head + y] = residual[1, y : y + 1, :]
 
     for a in range(ex):
         for b in range(ey):
@@ -183,34 +185,38 @@
     numbers = jnp.zeros((1, nz), F32)
     for k in range(n_stored):
         numbers = jnp.where(lane == n_stored * at + k, blocks[k].astype(F32), numbers)
-    row = lax.broadcasted_iota(jnp.int32, (head, nz), 0)
-    lines = jnp.where(row == n_stored, numbers, 0.0)
-    for k in range(n_stored):
-        lines = jnp.where(
-            row == k, jnp.sum(values[k] * coarse_residual, axis=0, keepdims=True), lines
-        )
+    for k in range(head):
+        if k < n_stored:
+            line = jnp.sum(values[k] * coarse_residual, axis=0, keepdims=True)
+        else:
+            line = numbers
+        for i in range(n_line):
+            payload[i * (head + ny) + k] = line
+
+
+def line_kernel(
+    n_stored, ready, me, parts, residual, after1, after2, dense, x_low, x_high, to_high, to_low, rows
+):
+    nx, ny, nz = residual.shape
+    head = n_stored + 1
+    size = head + ny
+    n_line = parts.shape[0] // size
+    at = me[0]
+    numbers = jnp.zeros((1, nz), F32)
+    if n_line * n_stored < nz:
+        rows[n_line * n_stored :, :] = jnp.zeros((nz - n_line * n_stored, nz), F32)
     for i in range(n_line):
-        payload[i, :head, :] = lines
-
-
-def line_kernel(
-    n_stored, ready, me, parts, residual, after1, after2, dense, x_low, x_high, to_high, to_low
-):
-    nx, ny, nz = residual.shape
-    n_line = parts.shape[0]
-    head = parts.shape[1] - ny
-    at = me[0]
-    rows = parts[:, :n_stored, :].reshape(n_line * n_stored, nz)
-    if rows.shape[0] < nz:
-        rows = jnp.concatenate([rows, jnp.zeros((nz - rows.shape[0], nz), F32)])
-    numbers = jnp.sum(parts[:, n_stored : n_stored + 1, :], axis=0)
+        numbers = numbers + parts[i * size + n_stored]
+        for k in range(n_stored):
+            rows[i * n_stored + k : i * n_stored + k + 1, :] = parts[i * size + k]
     n_blocks = dense.shape[0] * dense.shape[1]
     block = lax.broadcasted_iota(jnp.int32, (n_blocks, nz), 0).astype(F32)
     place = (jnp.abs(block - numbers) < 0.5).astype(F32)
-    dense[...] = mm(place, rows).reshape(dense.shape)
+    dense[...] = mm(place, rows[...]).reshape(dense.shape)
     before, behind = jnp.maximum(at - 1, 0), jnp.minimum(at + 1, n_line - 1)
-    x_low[...] = jnp.where(at > 0, parts[before, head:, :], 0.0)
-    x_high[...] = jnp.where(at + 1 < n_line, parts[behind, head:, :], 0.0)
+    for y in range(ny):
+        x_low[y : y + 1] = jnp.where(at > 0, parts[before * size + head + y], 0.0)
+        x_high[y : y + 1] = jnp.where(at + 1 < n_line, parts[behind * size + head + y], 0.0)
     for out, y in ((to_high, ny - 2), (to_low, 1)):
         out[...] = jnp.zeros_like(out)
         out[:nx] = residual[:, y, :]
@@ -475,15 +481,16 @@
 
     ids = element_coarse_index.reshape(ex * ey, ez)
     me = lax.axis_index("gx").astype(jnp.int32).reshape(1)
-    head = up8(xxt_values.shape[0] + 1)
+    head = xxt_values.shape[0] + 1
     assert xxt_values.shape[0] * n_line <= nz
     payload, ids_wide, residual, xxt_values, block_numbers = call(
-        coarse_kernel, "coarse_restrict", [(n_line, head + ny, nz), (ex * ey, nz)],
+        coarse_kernel, "coarse_restrict",
+        [(n_line * (head + ny), 1, nz), (ex * ey, nz)],
         xxt_blocks, me, residual, ids, xxt_values, xxt_blocks, smem=(1,), load=(3,), keep=(2, 4, 5),
         pin=(1,),
         numbers=(0,),
     )
-    parts = spread(payload, "gx")
+    parts = spread(payload.reshape(n_line, head + ny, 1, nz), "gx").reshape(payload.shape)
 
     cheb = cheb_matrix()
     ky = np.kron(np.eye(nx, dtype=np.float32), np.kron(np.eye(ey, dtype=np.float32), cheb))
@@ -538,6 +545,7 @@
         functools.partial(line_kernel, xxt_values.shape[0]), "line_sum",
         [(n_plane, own, block), (ny, nz), (ny, nz), (face, nz), (face, nz)],
         me, parts, residual, image_direction, from_z, smem=(0,), pin=(1, 2), idle=(4,),
+        scratch=(pltpu.VMEM((nz, nz), F32),),
     )
     parts = spread(dense, plane)
     y_low, y_high = exchange(to_high, to_low, "gy")

time: 134 us -> 132 us (0.985)
  starting transfers between devices: 83.6 us -> 81.7 us
    all_to_all x5, starting transfers between devices: 59.6 us -> 57.7 us  [spread(): return lax.all_to_all(values, axes, 0, 0, tiled=False)]
where the time goes in v9:
time: 132 us; the launch traced here: 131 us
  starting transfers between devices  81.7 us (62%)
  Pallas kernels  25.1 us (19%)
  waiting for transfers between devices  22.4 us (17%)
  between operations  1.52 us (1%)
    all_to_all x5, starting transfers between devices, spread(): return lax.all_to_all(values, axes, 0, 0, tiled=False)  57.7 us
    pallas_call x14, Pallas kernels, call(): pl.pallas_call(whole, out_shape=[pltpu.VMEM(o, F32) if i in pin else pltp...  25.1 us
    ppermute x5, starting transfers between devices, exchange(): lax.ppermute(to_high, axis, forward)  16.3 us
    all_to_all x5, waiting for transfers between devices, spread(): return lax.all_to_all(values, axes, 0, 0, tiled=False)  15.1 us
    ppermute x5, starting transfers between devices, exchange(): lax.ppermute(to_low, axis, backward)  7.72 us
    ppermute x5, waiting for transfers between devices, exchange(): lax.ppermute(to_low, axis, backward)  7.32 us
  transfers between devices with their start and end apart: 15, of which 8 were waited for; matrix products, arithmetic and copies ran while one was open for 0% of the time, Pallas kernels for 14%

profile of v9, /device:TPU:1, one launch (start us, length us, event | category | flops | bytes accessed | tf_op | source)
XLA Modules:
  0.0 130.7 jit_solution(14723132639230296523)
XLA Ops:
  0.6 1.8 %coarse_restrict.1 = (f32[400,1,128]{2,1,0:T(1,128)}, f32[4,128]{1,0:T(4,128)S(1)}, f32[16,16,128]{2,1,0:T(8,128)S(1)}, f32[8,64,128]{2,1,0:T(8,128)S(1)}, s32[8]{0:T(128)S(1)}) custom-call(s32[8]{0:T(128)} %refs_5_.3, s32[1]{0:T(128)} %bitcast.refs_1_.refs_0_, f32[16,16,128]{2,1,0:T(8,128)} %refs_2_.3, s32[4,16]{1,0:T(4,128)} %bitcast.8, ...), custom_call_target="tpu_custom_call" | custom-call | bytes 600388 | tf_op jit(solution)/shard_map/coarse_restrict/pallas_call | solution.py:119
  2.5 19.4 %all-to-all-start = ((f32[16,25,1,128]{3,2,1,0:T(1,128)}), f32[16,25,1,128]{3,2,1,0:T(1,128)S(1)}, u32[]{:S(2)}, u32[]{:S(2)}) async-start(f32[16,25,1,128]{3,2,1,0:T(1,128)} %bitcast.2), calls=%async_computation | async-start | bytes 409600 | tf_op jit(solution)/shard_map/all_to_all | solution.py:457
  21.9 2.4 %operator_direction.1 = (f32[16,16,128]{2,1,0:T(8,128)S(1)}, f32[1,128]{1,0:T(1,128)S(1)}, f32[16,16,128]{2,1,0:T(8,128)S(1)}, f32[3,16,16,128]{3,2,1,0:T(8,128)...) custom-call(f32[16,16,128]{2,1,0:T(8,128)} %refs_0_.5, ...), custom_call_target="tpu_custom_call" | custom-call | bytes 1442304 | tf_op jit(solution)/shard_map/operator_direction/pallas_call | solution.py:119
  24.3 5.9 %basis_matrices.1 = (f32[480,336]{1,0:T(8,128)}, f32[256,480]{1,0:T(8,128)}, f32[136,160]{1,0:T(8,128)}, f32[160,128]{1,0:T(8,128)}) custom-call(f32[10,10]{1,0:T(8,128)} %refs_0_.6, f32[20,10]{1,0:T(8,128)} %constant.42.clone.refs_1_, f32[20,20]{1,0:T(8,128)} %constant.43.clone.refs_2_, f32[160,10]{1,0:T(8,128)} %constant.44.clone.refs_3_, ...), custom_call_target="tpu_custom_call" | custom-call | bytes 1757680 | tf_op jit(solution)/shard_map/basis_matrices/pallas_call | solution.py:119
  30.2 4.2 %all-to-all-done = f32[16,25,1,128]{3,2,1,0:T(1,128)S(1)} async-done(((f32[16,25,1,128]{3,2,1,0:T(1,128)}), f32[16,25,1,128]{3,2,1,0:T(1,128)S(1)}, u32[]{:S(2)}, u32[]{:S(2)}) %all-to-all-start) | async-done | bytes 204832 | tf_op jit(solution)/shard_map/all_to_all | solution.py:457
  34.5 1.1 line_sum.1
  35.5 15.2 %all-to-all-start.1 = ((f32[64,8,128]{2,1,0:T(8,128)}), f32[64,8,128]{2,1,0:T(8,128)S(1)}, u32[]{:S(2)}, u32[]{:S(2)}) async-start(f32[64,8,128]{2,1,0:T(8,128)} %get-tuple-element.49), calls=%async_computation.1 | async-start | bytes 524288 | tf_op jit(solution)/shard_map/all_to_all | solution.py:457
  50.7 3.3 %collective-permute-start = (f32[24,128]{1,0:T(8,128)S(1)}, f32[24,128]{1,0:T(8,128)S(1)}, u32[]{:S(2)}, u32[]{:S(2)}) collective-permute-start(f32[24,128]{1,0:T(8,128)S(1)} %get-tuple-element.52), channel_id=1, source_target_pairs={{0,8},{8,16},{16,24},{24,32},{32,40},{40,48},{48,56},{1,9},{9,17},... | collective-permute-start | bytes 36872 | tf_op jit(solution)/shard_map/ppermute | solution.py:453
  54.0 1.3 collective-permute-start.1
  55.3 0.0 collective-permute-done.refs_4_
  55.3 3.6 %collective-permute-done.1.refs_5_ = f32[24,128]{1,0:T(8,128)S(1)} collective-permute-done((f32[24,128]{1,0:T(8,128)S(1)}, f32[24,128]{1,0:T(8,128)S(1)}, u32[]{:S(2)}, u32[]{:S(2)}) %collective-permute-start.1) | collective-permute-done | bytes 12320 | tf_op jit(solution)/shard_map/ppermute | solution.py:453
  58.9 4.9 %all-to-all-done.1.refs_0_ = f32[64,8,128]{2,1,0:T(8,128)S(1)} async-done(((f32[64,8,128]{2,1,0:T(8,128)}), f32[64,8,128]{2,1,0:T(8,128)S(1)}, u32[]{:S(2)}, u32[]{:S(2)}) %all-to-all-start.1) | async-done | bytes 262176 | tf_op jit(solution)/shard_map/all_to_all | solution.py:457
  63.9 0.9 plane_sum.1
  64.8 6.4 %all-to-all-start.2 = ((f32[64,8,128]{2,1,0:T(8,128)}), f32[64,8,128]{2,1,0:T(8,128)S(1)}, u32[]{:S(2)}, u32[]{:S(2)}) async-start(f32[64,8,128]{2,1,0:T(8,128)} %get-tuple-element.54), calls=%async_computation.2 | async-start | bytes 524288 | tf_op jit(solution)/shard_map/all_to_all | solution.py:457
  71.2 3.5 %collective-permute-start.2 = (f32[1,336]{1,0:T(1,128)S(1)}, f32[1,336]{1,0:T(1,128)S(1)}, u32[]{:S(2)}, u32[]{:S(2)}) collective-permute-start(f32[1,336]{1,0:T(1,128)S(1)} %get-tuple-element.60), channel_id=1, source_target_pairs={{0,1},{1,2},{2,3},{3,4},{4,5},{5,6},{6,7},{8,9},{9,10},{10,11},{11... | collective-permute-start | bytes 4040 | tf_op jit(solution)/shard_map/ppermute | solution.py:453
  74.8 1.9 %collective-permute-start.3 = (f32[1,336]{1,0:T(1,128)S(1)}, f32[1,336]{1,0:T(1,128)S(1)}, u32[]{:S(2)}, u32[]{:S(2)}) collective-permute-start(f32[1,336]{1,0:T(1,128)S(1)} %get-tuple-element.61), channel_id=1, source_target_pairs={{1,0},{2,1},{3,2},{4,3},{5,4},{6,5},{7,6},{9,8},{10,9},{11,10},{12... | collective-permute-start | bytes 4040 | tf_op jit(solution)/shard_map/ppermute | solution.py:453
  76.7 2.2 %element_spectral.1.refs_0_ = f32[480,160]{1,0:T(8,128)S(1)} custom-call(f32[336,128]{1,0:T(8,128)S(1)} %get-tuple-element.57.refs_0_, f32[480,336]{1,0:T(8,128)} %get-tuple-element.58.refs_1_.refs_3_, f32[136,160]{1,0:T(8,128)} %get-tuple-element.59.refs_2_.refs_5_), custom_call_target="tpu_custom_call" | custom-call | bytes 1211392 | tf_op jit(solution)/shard_map/element_spectral/pallas_call | solution.py:119
  78.9 0.0 collective-permute-done.2.refs_1_
  78.9 1.1 collective-permute-done.3.refs_2_
  80.0 4.0 %element_solve.1 = (f32[256,128]{1,0:T(8,128)S(1)}, f32[1,128]{1,0:T(1,128)S(1)}) custom-call(f32[480,160]{1,0:T(8,128)S(1)} %element_spectral.1.refs_0_, f32[1,336]{1,0:T(1,128)S(1)} %collective-permute-done.2.refs_1_, f32[1,336]{1,0:T(1,128)S(1)} %collective-permute-done.3.refs_2_, f32[480,336]{1,0:T(8,128)} %get-tuple-element.58.refs_1_.refs_3_, ...), custom_call_target="tpu_custom_call" | custom-call | bytes 2003072 | tf_op jit(solution)/shard_map/element_solve/pallas_call | solution.py:119
  84.0 0.4 all-to-all-done.2
  84.4 1.6 %coarse_correct.1 = (f32[16,16,128]{2,1,0:T(8,128)S(1)}, f32[16,16,128]{2,1,0:T(8,128)S(1)}, f32[2,64,128]{2,1,0:T(8,128)S(1)}, f32[2,64,128]{2,1,0:T(8,128)S(1)}) custom-call(s32[8]{0:T(128)S(1)} %get-tuple-element.44.refs_0_, f32[512,128]{1,0:T(8,128)S(1)} %bitcast.5, f32[8,64,128]{2,1,0:T(8,128)S(1)} %get-tuple-element.55.refs_2_, ...), custom_call_target="tpu_custom_call" | custom-call | bytes 2492448 | tf_op jit(solution)/shard_map/coarse_correct/pallas_call | solution.py:119
  86.0 3.1 %collective-permute-start.4 = (f32[2,64,128]{2,1,0:T(8,128)S(1)}, f32[2,64,128]{2,1,0:T(8,128)S(1)}, u32[]{:S(2)}, u32[]{:S(2)}) collective-permute-start(f32[2,64,128]{2,1,0:T(8,128)S(1)} %get-tuple-element.75), channel_id=1, source_target_pairs={{0,64},{64,128},{128,192},{192,256},{256,320},{320,384},{384,448},... | collective-permute-start | bytes 196616 | tf_op jit(solution)/shard_map/ppermute | solution.py:453
  89.1 1.3 collective-permute-start.5
  90.4 0.0 collective-permute-done.4.refs_6_.refs_2_
  90.4 0.8 terms.1
  91.2 9.8 %all-to-all-start.3 = ((f32[64,1,128]{2,1,0:T(1,128)}), f32[64,1,128]{2,1,0:T(1,128)S(1)}, u32[]{:S(2)}, u32[]{:S(2)}) async-start(f32[64,1,128]{2,1,0:T(1,128)} %terms.1), calls=%async_computation.3 | async-start | bytes 65536 | tf_op jit(solution)/shard_map/all_to_all | solution.py:457
  101.1 0.0 collective-permute-done.5.refs_3_
  101.1 0.8 assemble_length.1
  101.8 3.3 %collective-permute-start.6 = (f32[2,32,128]{2,1,0:T(8,128)S(1)}, f32[2,32,128]{2,1,0:T(8,128)S(1)}, u32[]{:S(2)}, u32[]{:S(2)}) collective-permute-start(f32[2,32,128]{2,1,0:T(8,128)S(1)} %get-tuple-element.77), channel_id=1, source_target_pairs={{0,8},{8,16},{16,24},{24,32},{32,40},{40,48},{48,56},{1,9},{9,17},... | collective-permute-start | bytes 98312 | tf_op jit(solution)/shard_map/ppermute | solution.py:453
  105.1 1.3 collective-permute-start.7
  106.4 0.0 collective-permute-done.6.refs_1_
  106.4 3.9 %all-to-all-done.3.refs_0_ = f32[64,1,128]{2,1,0:T(1,128)S(1)} async-done(((f32[64,1,128]{2,1,0:T(1,128)}), f32[64,1,128]{2,1,0:T(1,128)S(1)}, u32[]{:S(2)}, u32[]{:S(2)}) %all-to-all-start.3) | async-done | bytes 32800 | tf_op jit(solution)/shard_map/all_to_all | solution.py:457
  110.4 0.7 sum_terms.1
  111.0 6.9 %all-to-all-start.4 = ((f32[16,1,128]{2,1,0:T(1,128)}), f32[16,1,128]{2,1,0:T(1,128)S(1)}, u32[]{:S(2)}, u32[]{:S(2)}) async-start(f32[16,1,128]{2,1,0:T(1,128)} %sum_terms.1), calls=%async_computation.4 | async-start | bytes 16384 | tf_op jit(solution)/shard_map/all_to_all | solution.py:457
  117.9 0.0 collective-permute-done.7.refs_2_
  117.9 1.0 assemble_across.1
  118.9 3.0 %collective-permute-start.8 = (f32[1,512]{1,0:T(1,128)S(1)}, f32[1,512]{1,0:T(1,128)S(1)}, u32[]{:S(2)}, u32[]{:S(2)}) collective-permute-start(f32[1,512]{1,0:T(1,128)S(1)} %get-tuple-element.82), channel_id=1, source_target_pairs={{0,1},{1,2},{2,3},{3,4},{4,5},{5,6},{6,7},{8,9},{9,10},{10,11},{11... | collective-permute-start | bytes 6152 | tf_op jit(solution)/shard_map/ppermute | solution.py:453
  122.0 1.9 %collective-permute-start.9 = (f32[1,512]{1,0:T(1,128)S(1)}, f32[1,512]{1,0:T(1,128)S(1)}, u32[]{:S(2)}, u32[]{:S(2)}) collective-permute-start(f32[1,512]{1,0:T(1,128)S(1)} %get-tuple-element.83), channel_id=1, source_target_pairs={{1,0},{2,1},{3,2},{4,3},{5,4},{6,5},{7,6},{9,8},{10,9},{11,10},{12... | collective-permute-start | bytes 6152 | tf_op jit(solution)/shard_map/ppermute | solution.py:453
  124.5 0.0 collective-permute-done.8.refs_1_
  124.5 2.6 %collective-permute-done.9.refs_2_ = f32[1,512]{1,0:T(1,128)S(1)} collective-permute-done((f32[1,512]{1,0:T(1,128)S(1)}, f32[1,512]{1,0:T(1,128)S(1)}, u32[]{:S(2)}, u32[]{:S(2)}) %collective-permute-start.9) | collective-permute-done | bytes 2080 | tf_op jit(solution)/shard_map/ppermute | solution.py:453
  127.1 0.4 assemble_depth.1.refs_3_
  127.6 1.6 %all-to-all-done.4.refs_1_ = f32[16,1,128]{2,1,0:T(1,128)S(1)} async-done(((f32[16,1,128]{2,1,0:T(1,128)}), f32[16,1,128]{2,1,0:T(1,128)S(1)}, u32[]{:S(2)}, u32[]{:S(2)}) %all-to-all-start.4) | async-done | bytes 8224 | tf_op jit(solution)/shard_map/all_to_all | solution.py:457
  129.1 1.6 %update.1 = (f32[16,16,128]{2,1,0:T(8,128)}, f32[16,16,128]{2,1,0:T(8,128)}, f32[16,16,128]{2,1,0:T(8,128)}) custom-call(f32[1]{0:T(128)S(6)} %copy.30.refs_0_, f32[16,1,128]{2,1,0:T(1,128)S(1)} %all-to-all-done.4.refs_1_, f32[1,1]{1,0:T(1,128)} %get-tuple-element.78.refs_2_, f32[2,16,16,128]{3,2,1,0:T(8,128)S(1)} %assemble_depth.1.refs_3_, ...), custom_call_target="tpu_custom_call" | custom-call | bytes 1187848 | tf_op jit(solution)/shard_map/update/pallas_call | solution.py:119
Async XLA Ops:
  2.5 32.0 %all-to-all-start = ((f32[16,25,1,128]{3,2,1,0:T(1,128)}), f32[16,25,1,128]{3,2,1,0:T(1,128)S(1)}, u32[]{:S(2)}, u32[]{:S(2)}) async-start(f32[16,25,1,128]{3,2,1,0:T(1,128)} %bitcast.2), calls=%async_computation | async-start | bytes 409600 | tf_op jit(solution)/shard_map/all_to_all | solution.py:457
  35.5 28.3 %all-to-all-start.1 = ((f32[64,8,128]{2,1,0:T(8,128)}), f32[64,8,128]{2,1,0:T(8,128)S(1)}, u32[]{:S(2)}, u32[]{:S(2)}) async-start(f32[64,8,128]{2,1,0:T(8,128)} %get-tuple-element.49), calls=%async_computation.1 | async-start | bytes 524288 | tf_op jit(solution)/shard_map/all_to_all | solution.py:457
  50.7 4.6 %collective-permute-start = (f32[24,128]{1,0:T(8,128)S(1)}, f32[24,128]{1,0:T(8,128)S(1)}, u32[]{:S(2)}, u32[]{:S(2)}) collective-permute-start(f32[24,128]{1,0:T(8,128)S(1)} %get-tuple-element.52), channel_id=1, source_target_pairs={{0,8},{8,16},{16,24},{24,32},{32,40},{40,48},{48,56},{1,9},{9,17},... | collective-permute-start | bytes 36872 | tf_op jit(solution)/shard_map/ppermute | solution.py:453
  54.0 4.9 %collective-permute-start.1 = (f32[24,128]{1,0:T(8,128)S(1)}, f32[24,128]{1,0:T(8,128)S(1)}, u32[]{:S(2)}, u32[]{:S(2)}) collective-permute-start(f32[24,128]{1,0:T(8,128)S(1)} %get-tuple-element.53), channel_id=1, source_target_pairs={{8,0},{16,8},{24,16},{32,24},{40,32},{48,40},{56,48},{9,1},{17,9},... | collective-permute-start | bytes 36872 | tf_op jit(solution)/shard_map/ppermute | solution.py:453
  64.8 19.6 %all-to-all-start.2 = ((f32[64,8,128]{2,1,0:T(8,128)}), f32[64,8,128]{2,1,0:T(8,128)S(1)}, u32[]{:S(2)}, u32[]{:S(2)}) async-start(f32[64,8,128]{2,1,0:T(8,128)} %get-tuple-element.54), calls=%async_computation.2 | async-start | bytes 524288 | tf_op jit(solution)/shard_map/all_to_all | solution.py:457
  71.2 7.6 %collective-permute-start.2 = (f32[1,336]{1,0:T(1,128)S(1)}, f32[1,336]{1,0:T(1,128)S(1)}, u32[]{:S(2)}, u32[]{:S(2)}) collective-permute-start(f32[1,336]{1,0:T(1,128)S(1)} %get-tuple-element.60), channel_id=1, source_target_pairs={{0,1},{1,2},{2,3},{3,4},{4,5},{5,6},{6,7},{8,9},{9,10},{10,11},{11... | collective-permute-start | bytes 4040 | tf_op jit(solution)/shard_map/ppermute | solution.py:453
  74.8 5.2 %collective-permute-start.3 = (f32[1,336]{1,0:T(1,128)S(1)}, f32[1,336]{1,0:T(1,128)S(1)}, u32[]{:S(2)}, u32[]{:S(2)}) collective-permute-start(f32[1,336]{1,0:T(1,128)S(1)} %get-tuple-element.61), channel_id=1, source_target_pairs={{1,0},{2,1},{3,2},{4,3},{5,4},{6,5},{7,6},{9,8},{10,9},{11,10},{12... | collective-permute-start | bytes 4040 | tf_op jit(solution)/shard_map/ppermute | solution.py:453
  86.0 4.5 %collective-permute-start.4 = (f32[2,64,128]{2,1,0:T(8,128)S(1)}, f32[2,64,128]{2,1,0:T(8,128)S(1)}, u32[]{:S(2)}, u32[]{:S(2)}) collective-permute-start(f32[2,64,128]{2,1,0:T(8,128)S(1)} %get-tuple-element.75), channel_id=1, source_target_pairs={{0,64},{64,128},{128,192},{192,256},{256,320},{320,384},{384,448},... | collective-permute-start | bytes 196616 | tf_op jit(solution)/shard_map/ppermute | solution.py:453
  89.1 11.9 %collective-permute-start.5 = (f32[2,64,128]{2,1,0:T(8,128)S(1)}, f32[2,64,128]{2,1,0:T(8,128)S(1)}, u32[]{:S(2)}, u32[]{:S(2)}) collective-permute-start(f32[2,64,128]{2,1,0:T(8,128)S(1)} %get-tuple-element.76), channel_id=1, source_target_pairs={{64,0},{128,64},{192,128},{256,192},{320,256},{384,320},{448,384},... | collective-permute-start | bytes 196616 | tf_op jit(solution)/shard_map/ppermute | solution.py:453
  91.2 19.1 %all-to-all-start.3 = ((f32[64,1,128]{2,1,0:T(1,128)}), f32[64,1,128]{2,1,0:T(1,128)S(1)}, u32[]{:S(2)}, u32[]{:S(2)}) async-start(f32[64,1,128]{2,1,0:T(1,128)} %terms.1), calls=%async_computation.3 | async-start | bytes 65536 | tf_op jit(solution)/shard_map/all_to_all | solution.py:457
  101.8 4.6 %collective-permute-start.6 = (f32[2,32,128]{2,1,0:T(8,128)S(1)}, f32[2,32,128]{2,1,0:T(8,128)S(1)}, u32[]{:S(2)}, u32[]{:S(2)}) collective-permute-start(f32[2,32,128]{2,1,0:T(8,128)S(1)} %get-tuple-element.77), channel_id=1, source_target_pairs={{0,8},{8,16},{16,24},{24,32},{32,40},{40,48},{48,56},{1,9},{9,17},... | collective-permute-start | bytes 98312 | tf_op jit(solution)/shard_map/ppermute | solution.py:453
  105.1 12.8 %collective-permute-start.7 = (f32[2,32,128]{2,1,0:T(8,128)S(1)}, f32[2,32,128]{2,1,0:T(8,128)S(1)}, u32[]{:S(2)}, u32[]{:S(2)}) collective-permute-start(f32[2,32,128]{2,1,0:T(8,128)S(1)} %get-tuple-element.80), channel_id=1, source_target_pairs={{8,0},{16,8},{24,16},{32,24},{40,32},{48,40},{56,48},{9,1},{17,9},... | collective-permute-start | bytes 98312 | tf_op jit(solution)/shard_map/ppermute | solution.py:453
  111.0 18.1 %all-to-all-start.4 = ((f32[16,1,128]{2,1,0:T(1,128)}), f32[16,1,128]{2,1,0:T(1,128)S(1)}, u32[]{:S(2)}, u32[]{:S(2)}) async-start(f32[16,1,128]{2,1,0:T(1,128)} %sum_terms.1), calls=%async_computation.4 | async-start | bytes 16384 | tf_op jit(solution)/shard_map/all_to_all | solution.py:457
  118.9 5.6 %collective-permute-start.8 = (f32[1,512]{1,0:T(1,128)S(1)}, f32[1,512]{1,0:T(1,128)S(1)}, u32[]{:S(2)}, u32[]{:S(2)}) collective-permute-start(f32[1,512]{1,0:T(1,128)S(1)} %get-tuple-element.82), channel_id=1, source_target_pairs={{0,1},{1,2},{2,3},{3,4},{4,5},{5,6},{6,7},{8,9},{9,10},{10,11},{11... | collective-permute-start | bytes 6152 | tf_op jit(solution)/shard_map/ppermute | solution.py:453
  122.0 5.2 %collective-permute-start.9 = (f32[1,512]{1,0:T(1,128)S(1)}, f32[1,512]{1,0:T(1,128)S(1)}, u32[]{:S(2)}, u32[]{:S(2)}) collective-permute-start(f32[1,512]{1,0:T(1,128)S(1)} %get-tuple-element.83), channel_id=1, source_target_pairs={{1,0},{2,1},{3,2},{4,3},{5,4},{6,5},{7,6},{9,8},{10,9},{11,10},{12... | collective-permute-start | bytes 6152 | tf_op jit(solution)/shard_map/ppermute | solution.py:453
